TPU v7x, 32 devices: a whole 2x2x4 slice. The times are simulated.
32 devices in a mesh: head: 2 (over x), blk: 16 (over z, y, core).
Axes of the slice: x: 2, y: 2, z: 4, core: 2. Of those that a mesh axis runs over, the one named last changes fastest.
Arguments:
- layer_input: bfloat16 [2, 2048, 768], P(None, ('head', 'blk')), may hold values from -12 to 12
- segment_ids: int32 [2, 2048], P(None, ('head', 'blk')), may hold values from 0 to 3, never falling along the last dimension, each value on 1 to 1024 neighbouring positions
- token_live: int32 [2, 2048], P(None, ('head', 'blk')), may hold values 0 or 1
- w_query: bfloat16 [768, 768], P(('head', 'blk')), may hold values from -0.21875 to 0.21875
- b_query: bfloat16 [768], P(('head', 'blk')), may hold values from -1.75 to 1.75
- w_key: bfloat16 [768, 768], P(('head', 'blk')), may hold values from -0.21875 to 0.21875
- w_value: bfloat16 [768, 768], P(('head', 'blk')), may hold values from -0.21875 to 0.21875
- b_value: bfloat16 [768], P(('head', 'blk')), may hold values from -0.625 to 0.625
- w_output: bfloat16 [768, 768], P(('head', 'blk')), may hold values from -0.875 to 0.875
- b_output: bfloat16 [768], P(('head', 'blk')), may hold values from -1.25 to 1.25
- first_gain: bfloat16 [768], P(('head', 'blk')), may hold values from 0.5 to 1.5
- first_shift: bfloat16 [768], P(('head', 'blk')), may hold values from -1.25 to 1.25
- w_gate: bfloat16 [768, 3072], P(('head', 'blk')), may hold values from -0.21875 to 0.21875
- w_up: bfloat16 [768, 3072], P(('head', 'blk')), may hold values from -0.21875 to 0.21875
- w_down: bfloat16 [3072, 768], P(('head', 'blk')), may hold values from -0.109375 to 0.109375
- b_down: bfloat16 [768], P(('head', 'blk')), may hold values from -1.25 to 1.25
- second_gain: bfloat16 [768], P(('head', 'blk')), may hold values from 0.5 to 1.5
- second_shift: bfloat16 [768], P(('head', 'blk')), may hold values from -1.25 to 1.25
- output_grad: bfloat16 [2, 2048, 768], P(None, ('head', 'blk')), may hold values from -12 to 12
Outputs:
- layer_output: bfloat16 [2, 2048, 768], P(None, ('head', 'blk'))
- input_grad: bfloat16 [2, 2048, 768], P(None, ('head', 'blk'))
- grad_query: float32 [768, 768], P(('head', 'blk'))
- grad_query_bias: float32 [768], P(('head', 'blk'))
- grad_key: float32 [768, 768], P(('head', 'blk'))
- grad_value: float32 [768, 768], P(('head', 'blk'))
- grad_value_bias: float32 [768], P(('head', 'blk'))
- grad_output: float32 [768, 768], P(('head', 'blk'))
- grad_output_bias: float32 [768], P(('head', 'blk'))
- grad_first_gain: float32 [768], P(('head', 'blk'))
- grad_first_shift: float32 [768], P(('head', 'blk'))
- grad_gate: float32 [768, 3072], P(('head', 'blk'))
- grad_up: float32 [768, 3072], P(('head', 'blk'))
- grad_down: float32 [3072, 768], P(('head', 'blk'))
- grad_down_bias: float32 [768], P(('head', 'blk'))
- grad_second_gain: float32 [768], P(('head', 'blk'))
- grad_second_shift: float32 [768], P(('head', 'blk'))
Inputs may be any that keep to these rules, and one draw needn't show every extreme that they name: `segment_ids`: along each sequence the numbers never fall; each document covers 1 to 1024 tokens, and in each sequence one covers exactly 1024.
All inputs are finite; a program needn't handle non-finite values. No bound on the sum of `token_live` on one device may be relied on, other than what follows from the above.
Results may differ from a plain program's by a relative error of at most 0.039.
Values may be sent and summed in bfloat16 or wider, within the bound.
No kernel may reach another device: no remote copies, remote signals or barrier semaphores. Data moves between devices by JAX's collectives and lax.ppermute only.
A program may use at most 192 MiB of HBM per device.

v0:
```python
import math

import jax
import jax.numpy as jnp
import numpy as np
from jax import lax
from jax.sharding import PartitionSpec as P

HEADS = 12
HEAD_DIM = 64


norm_epsilon = 1e-12
masked_value = -1e30


def alibi_slopes(head_total):
    nearest = 2 ** int(math.floor(math.log2(head_total)))
    slopes = [2.0 ** (-8.0 * (head_index + 1) / nearest) for head_index in range(nearest)]
    extra_slopes = [
        2.0 ** (-8.0 * (head_index + 1) / (2 * nearest)) for head_index in range(2 * nearest)
    ]
    slopes = slopes + extra_slopes[0::2][: head_total - nearest]
    return np.array(slopes, dtype=np.float32)


def contract_rows(left_side, right_side):
    return lax.dot_general(
        left_side, right_side, (((0,), (0,)), ((), ())), preferred_element_type=jnp.float32
    )


def contract_cols(left_side, right_side):
    return lax.dot_general(
        left_side, right_side, (((1,), (1,)), ((), ())), preferred_element_type=jnp.float32
    )


def norm_forward(values, norm_gain, norm_shift):
    centred = values - jnp.mean(values, axis=-1, keepdims=True)
    inverse = lax.rsqrt(jnp.mean(centred * centred, axis=-1, keepdims=True) + norm_epsilon)
    normed = centred * inverse
    return (normed * norm_gain + norm_shift, normed, inverse)


def norm_backward(upstream, normed, inverse, norm_gain):
    scaled = upstream * norm_gain
    adjusted = (
        scaled
        - jnp.mean(scaled, axis=-1, keepdims=True)
        - normed * jnp.mean(scaled * normed, axis=-1, keepdims=True)
    )
    return (adjusted * inverse, jnp.sum(upstream * normed, axis=0), jnp.sum(upstream, axis=0))


def on_device(
    layer_input,
    segment_ids,
    token_live,
    w_query,
    b_query,
    w_key,
    w_value,
    b_value,
    w_output,
    b_output,
    first_gain,
    first_shift,
    w_gate,
    w_up,
    w_down,
    b_down,
    second_gain,
    second_shift,
    output_grad,
):
    sequences, shard_rows, model_width = layer_input.shape
    head_parts = lax.axis_size("head")
    group_total = lax.axis_size("blk")
    group_self = lax.axis_index("blk")
    head_self = lax.axis_index("head")
    query_rows = head_parts * shard_rows
    half_width = model_width // head_parts
    local_heads = HEADS // head_parts
    head_size = HEAD_DIM
    score_scale = head_size ** (-0.5)
    widest_rows = 8 * query_rows
    slopes_here = lax.dynamic_slice_in_dim(
        jnp.asarray(alibi_slopes(HEADS)), head_self * local_heads, local_heads
    )

    def positions(global_rows):
        device = global_rows // query_rows
        within = global_rows % query_rows
        return (within // shard_rows * group_total + device) * shard_rows + within % shard_rows

    def heads_view(flat_rows):
        return flat_rows.reshape(flat_rows.shape[0], flat_rows.shape[1], local_heads, head_size)

    def mask_block(query_place, key_place, query_segment, key_code):
        same_segment = query_segment[:, None, :, None] == key_code[:, None, None, :]
        same_row = (query_place[:, None] == key_place[None, :])[None, None]
        return same_segment | same_row

    def score_block(query_part, key_part, query_place, key_place):
        raw_scores = jnp.einsum(
            "bqhd,bkhd->bhqk",
            heads_view(query_part),
            heads_view(key_part),
            preferred_element_type=jnp.float32,
        )
        distance = jnp.abs(query_place[:, None] - key_place[None, :]).astype(jnp.float32)
        return raw_scores * score_scale - slopes_here[None, :, None, None] * distance[None, None]

    def fold_blocks(block_step, running, pieces):
        piece_rows = pieces[0].shape[1]
        block_rows = math.gcd(piece_rows, widest_rows)
        block_total = piece_rows // block_rows

        def to_blocks(source_array):
            shaped = source_array.reshape(
                (sequences, block_total, block_rows) + source_array.shape[2:]
            )
            return jnp.moveaxis(shaped, 1, 0)

        offsets = jnp.arange(block_total, dtype=jnp.int32) * block_rows

        def scan_step(current, packed):
            return (block_step(current, *packed[:-1], packed[-1]), None)

        result, ignored = lax.scan(
            scan_step, running, tuple((to_blocks(member) for member in pieces)) + (offsets,)
        )
        return result

    (
        full_query,
        full_key,
        full_value,
        full_output,
        gain_one,
        shift_one,
        bias_query,
        bias_value,
        bias_output,
    ) = (
        lax.all_gather(w_query, ("head", "blk"), axis=0, tiled=True),
        lax.all_gather(w_key, ("head", "blk"), axis=0, tiled=True),
        lax.all_gather(w_value, ("head", "blk"), axis=0, tiled=True),
        lax.all_gather(w_output, ("head", "blk"), axis=0, tiled=True),
        lax.all_gather(first_gain, ("head", "blk"), axis=0, tiled=True),
        lax.all_gather(first_shift, ("head", "blk"), axis=0, tiled=True),
        lax.all_gather(b_query, ("head", "blk"), axis=0, tiled=True),
        lax.all_gather(b_value, ("head", "blk"), axis=0, tiled=True),
        lax.all_gather(b_output, ("head", "blk"), axis=0, tiled=True),
    )
    full_gate, full_up, full_down, gain_two, shift_two, bias_down = (
        lax.all_gather(w_gate, ("head", "blk"), axis=0, tiled=True),
        lax.all_gather(w_up, ("head", "blk"), axis=0, tiled=True),
        lax.all_gather(w_down, ("head", "blk"), axis=0, tiled=True),
        lax.all_gather(second_gain, ("head", "blk"), axis=0, tiled=True),
        lax.all_gather(second_shift, ("head", "blk"), axis=0, tiled=True),
        lax.all_gather(b_down, ("head", "blk"), axis=0, tiled=True),
    )
    tokens = layer_input.reshape(sequences * shard_rows, model_width)
    merged_weights = jnp.concatenate([full_query, full_key, full_value], axis=1)
    merged_bias = jnp.concatenate(
        [
            bias_query.astype(jnp.float32),
            jnp.zeros((model_width,), jnp.float32),
            bias_value.astype(jnp.float32),
        ]
    )
    projected = (
        jnp.dot(tokens, merged_weights, preferred_element_type=jnp.float32) + merged_bias
    ).astype(jnp.bfloat16)
    exchanged = lax.all_to_all(
        projected.reshape(sequences, shard_rows, 3, model_width),
        "head",
        split_axis=3,
        concat_axis=1,
        tiled=True,
    )
    query_local = exchanged[:, :, 0, :]
    key_local = exchanged[:, :, 1, :]
    value_local = exchanged[:, :, 2, :]
    segs_local, live_local = (
        lax.all_gather(segment_ids, "head", axis=1, tiled=True),
        lax.all_gather(token_live, "head", axis=1, tiled=True),
    )
    code_local = jnp.where(live_local == 1, segs_local, -1)
    local_place = positions(group_self * query_rows + jnp.arange(query_rows, dtype=jnp.int32))

    def forward_block(running, key_part, value_part, code_part, first_row):
        key_place = positions(first_row + jnp.arange(key_part.shape[1], dtype=jnp.int32))
        allowed = mask_block(local_place, key_place, segs_local, code_part)
        top_now, sum_now, total_now = running
        scores = jnp.where(
            allowed, score_block(query_local, key_part, local_place, key_place), masked_value
        )
        top_new = jnp.maximum(top_now, jnp.max(scores, axis=-1))
        factor = jnp.exp(top_now - top_new)
        soft_probs = jnp.where(allowed, jnp.exp(scores - top_new[..., None]), 0.0)
        mixed_rows = jnp.einsum(
            "bhqk,bkhd->bqhd",
            soft_probs.astype(jnp.bfloat16),
            heads_view(value_part),
            preferred_element_type=jnp.float32,
        )
        factor_cols = jnp.repeat(jnp.swapaxes(factor, 1, 2), head_size, axis=2)
        return (
            top_new,
            sum_now * factor + jnp.sum(soft_probs, axis=-1),
            total_now * factor_cols + mixed_rows.reshape(total_now.shape),
        )

    start_state = (
        jnp.full((sequences, local_heads, query_rows), masked_value, jnp.float32),
        jnp.zeros((sequences, local_heads, query_rows), jnp.float32),
        jnp.zeros((sequences, query_rows, half_width), jnp.float32),
    )
    running = fold_blocks(
        forward_block,
        start_state,
        (
            lax.all_gather(key_local, "blk", axis=1, tiled=True),
            lax.all_gather(value_local, "blk", axis=1, tiled=True),
            lax.all_gather(code_local, "blk", axis=1, tiled=True),
        ),
    )
    top_all, sum_all, total_all = running
    attended = (total_all / jnp.repeat(jnp.swapaxes(sum_all, 1, 2), head_size, axis=2)).astype(
        jnp.bfloat16
    )
    log_totals = top_all + jnp.log(sum_all)
    attended_tokens = lax.all_to_all(
        attended, "head", split_axis=1, concat_axis=2, tiled=True
    ).reshape(sequences * shard_rows, model_width)
    branch = jnp.dot(
        attended_tokens, full_output, preferred_element_type=jnp.float32
    ) + bias_output.astype(jnp.float32)
    first_norm, normed_one, inverse_one = norm_forward(
        tokens.astype(jnp.float32) + branch, gain_one, shift_one
    )
    first_low = first_norm.astype(jnp.bfloat16)
    gate_rows = jnp.dot(first_low, full_gate, preferred_element_type=jnp.float32)
    up_rows = jnp.dot(first_low, full_up, preferred_element_type=jnp.float32)
    hidden_wide, gelu_pull = jax.vjp(
        lambda gate_in, up_in: jax.nn.gelu(gate_in, approximate=False) * up_in, gate_rows, up_rows
    )
    hidden = hidden_wide.astype(jnp.bfloat16)
    mixed_output = jnp.dot(
        hidden, full_down, preferred_element_type=jnp.float32
    ) + bias_down.astype(jnp.float32)
    layer_wide, normed_two, inverse_two = norm_forward(
        first_norm + mixed_output, gain_two, shift_two
    )
    layer_output = layer_wide.astype(jnp.bfloat16).reshape(layer_input.shape)
    upstream = output_grad.reshape(sequences * shard_rows, model_width).astype(jnp.float32)
    back_second, grad_gain_two, grad_shift_two = norm_backward(
        upstream, normed_two, inverse_two, gain_two
    )
    back_mixed = back_second.astype(jnp.bfloat16)
    grad_down = contract_rows(hidden, back_mixed)
    grad_down_bias = jnp.sum(back_mixed.astype(jnp.float32), axis=0)
    back_hidden = contract_cols(back_mixed, full_down)
    back_gate_wide, back_up_wide = gelu_pull(back_hidden)
    back_gate = back_gate_wide.astype(jnp.bfloat16)
    back_up = back_up_wide.astype(jnp.bfloat16)
    grad_gate = contract_rows(first_low, back_gate)
    grad_up = contract_rows(first_low, back_up)
    back_first = back_second + contract_cols(back_gate, full_gate) + contract_cols(back_up, full_up)
    back_inner, grad_gain_one, grad_shift_one = norm_backward(
        back_first, normed_one, inverse_one, gain_one
    )
    back_branch = back_inner.astype(jnp.bfloat16)
    grad_output = contract_rows(attended_tokens, back_branch)
    grad_output_bias = jnp.sum(back_branch.astype(jnp.float32), axis=0)
    back_attended = (
        contract_cols(back_branch, full_output)
        .astype(jnp.bfloat16)
        .reshape(sequences, shard_rows, model_width)
    )
    dout_local = lax.all_to_all(back_attended, "head", split_axis=2, concat_axis=1, tiled=True)
    delta_rows = jnp.swapaxes(
        jnp.sum(heads_view(dout_local.astype(jnp.float32) * attended.astype(jnp.float32)), axis=-1),
        1,
        2,
    )
    lse_all, delta_all = (
        lax.all_gather(log_totals, "blk", axis=2, tiled=True),
        lax.all_gather(delta_rows, "blk", axis=2, tiled=True),
    )

    def block_grads(
        query_part,
        dout_part,
        lse_part,
        delta_part,
        query_place,
        key_place,
        key_part,
        value_part,
        allowed,
    ):
        scores = score_block(query_part, key_part, query_place, key_place)
        soft_probs = jnp.exp(jnp.where(allowed, scores - lse_part[..., None], masked_value))
        back_prob = jnp.einsum(
            "bqhd,bkhd->bhqk",
            heads_view(dout_part),
            heads_view(value_part),
            preferred_element_type=jnp.float32,
        )
        back_scores = (soft_probs * (back_prob - delta_part[..., None])).astype(jnp.bfloat16)
        return (soft_probs, back_scores)

    def query_side_block(running, key_part, value_part, code_part, first_row):
        key_place = positions(first_row + jnp.arange(key_part.shape[1], dtype=jnp.int32))
        allowed = mask_block(local_place, key_place, segs_local, code_part)
        ignored, back_scores = block_grads(
            query_local,
            dout_local,
            log_totals,
            delta_rows,
            local_place,
            key_place,
            key_part,
            value_part,
            allowed,
        )
        query_grad_part = (
            jnp.einsum(
                "bhqk,bkhd->bqhd",
                back_scores,
                heads_view(key_part),
                preferred_element_type=jnp.float32,
            )
            * score_scale
        )
        return running + query_grad_part.reshape(running.shape)

    def key_side_block(running, query_part, dout_part, segment_part, first_row):
        piece_rows = query_part.shape[1]
        query_place = positions(first_row + jnp.arange(piece_rows, dtype=jnp.int32))
        lse_part = lax.dynamic_slice_in_dim(lse_all, first_row, piece_rows, 2)
        delta_part = lax.dynamic_slice_in_dim(delta_all, first_row, piece_rows, 2)
        allowed = mask_block(query_place, local_place, segment_part, code_local)
        soft_probs, back_scores = block_grads(
            query_part,
            dout_part,
            lse_part,
            delta_part,
            query_place,
            local_place,
            key_local,
            value_local,
            allowed,
        )
        value_grad_part = jnp.einsum(
            "bhqk,bqhd->bkhd",
            soft_probs.astype(jnp.bfloat16),
            heads_view(dout_part),
            preferred_element_type=jnp.float32,
        )
        key_grad_part = (
            jnp.einsum(
                "bhqk,bqhd->bkhd",
                back_scores,
                heads_view(query_part),
                preferred_element_type=jnp.float32,
            )
            * score_scale
        )
        return (
            running[0] + key_grad_part.reshape(running[0].shape),
            running[1] + value_grad_part.reshape(running[1].shape),
        )

    zero_rows = jnp.zeros((sequences, query_rows, half_width), jnp.float32)
    key_grad_all, value_grad_all = fold_blocks(
        key_side_block,
        (zero_rows, zero_rows),
        (
            lax.all_gather(query_local, "blk", axis=1, tiled=True),
            lax.all_gather(dout_local, "blk", axis=1, tiled=True),
            lax.all_gather(segs_local, "blk", axis=1, tiled=True),
        ),
    )
    query_grad_all = fold_blocks(
        query_side_block,
        zero_rows,
        (
            lax.all_gather(key_local, "blk", axis=1, tiled=True),
            lax.all_gather(value_local, "blk", axis=1, tiled=True),
            lax.all_gather(code_local, "blk", axis=1, tiled=True),
        ),
    )
    stacked = jnp.stack([query_grad_all, key_grad_all, value_grad_all], axis=2).astype(jnp.bfloat16)
    back_projected = lax.all_to_all(
        stacked, "head", split_axis=1, concat_axis=3, tiled=True
    ).reshape(sequences * shard_rows, 3 * model_width)
    grad_merged = contract_rows(tokens, back_projected)
    projected_sums = jnp.sum(back_projected.astype(jnp.float32), axis=0)
    input_grad = (
        (back_inner + contract_cols(back_projected, merged_weights))
        .astype(jnp.bfloat16)
        .reshape(layer_input.shape)
    )
    attn_members = (
        grad_merged[:, :model_width],
        projected_sums[:model_width],
        grad_merged[:, model_width : 2 * model_width],
        grad_merged[:, 2 * model_width :],
        projected_sums[2 * model_width :],
        grad_output,
        grad_output_bias,
        grad_gain_one,
        grad_shift_one,
    )
    mlp_members = (grad_gate, grad_up, grad_down, grad_down_bias, grad_gain_two, grad_shift_two)
    attn_sums = (
        lax.psum_scatter(attn_members[0], ("head", "blk"), scatter_dimension=0, tiled=True),
        lax.psum_scatter(attn_members[1], ("head", "blk"), scatter_dimension=0, tiled=True),
        lax.psum_scatter(attn_members[2], ("head", "blk"), scatter_dimension=0, tiled=True),
        lax.psum_scatter(attn_members[3], ("head", "blk"), scatter_dimension=0, tiled=True),
        lax.psum_scatter(attn_members[4], ("head", "blk"), scatter_dimension=0, tiled=True),
        lax.psum_scatter(attn_members[5], ("head", "blk"), scatter_dimension=0, tiled=True),
        lax.psum_scatter(attn_members[6], ("head", "blk"), scatter_dimension=0, tiled=True),
        lax.psum_scatter(attn_members[7], ("head", "blk"), scatter_dimension=0, tiled=True),
        lax.psum_scatter(attn_members[8], ("head", "blk"), scatter_dimension=0, tiled=True),
    )
    mlp_sums = (
        lax.psum_scatter(mlp_members[0], ("head", "blk"), scatter_dimension=0, tiled=True),
        lax.psum_scatter(mlp_members[1], ("head", "blk"), scatter_dimension=0, tiled=True),
        lax.psum_scatter(mlp_members[2], ("head", "blk"), scatter_dimension=0, tiled=True),
        lax.psum_scatter(mlp_members[3], ("head", "blk"), scatter_dimension=0, tiled=True),
        lax.psum_scatter(mlp_members[4], ("head", "blk"), scatter_dimension=0, tiled=True),
        lax.psum_scatter(mlp_members[5], ("head", "blk"), scatter_dimension=0, tiled=True),
    )
    return (layer_output, input_grad) + tuple(attn_sums) + tuple(mlp_sums)


def solution(mesh):
    return jax.shard_map(
        on_device,
        mesh=mesh,
        in_specs=(
            P(None, ("head", "blk"), None),
            P(None, ("head", "blk")),
            P(None, ("head", "blk")),
            P(("head", "blk"), None),
            P(("head", "blk")),
            P(("head", "blk"), None),
            P(("head", "blk"), None),
            P(("head", "blk")),
            P(("head", "blk"), None),
            P(("head", "blk")),
            P(("head", "blk")),
            P(("head", "blk")),
            P(("head", "blk"), None),
            P(("head", "blk"), None),
            P(("head", "blk"), None),
            P(("head", "blk")),
            P(("head", "blk")),
            P(("head", "blk")),
            P(None, ("head", "blk"), None),
        ),
        out_specs=(
            P(None, ("head", "blk"), None),
            P(None, ("head", "blk"), None),
            P(("head", "blk"), None),
            P(("head", "blk")),
            P(("head", "blk"), None),
            P(("head", "blk"), None),
            P(("head", "blk")),
            P(("head", "blk"), None),
            P(("head", "blk")),
            P(("head", "blk")),
            P(("head", "blk")),
            P(("head", "blk"), None),
            P(("head", "blk"), None),
            P(("head", "blk"), None),
            P(("head", "blk")),
            P(("head", "blk")),
            P(("head", "blk")),
        ),
        check_vma=False,
    )
```

profile of v0, /device:TPU:0, one launch (start us, length us, event | category | flops | bytes accessed | tf_op | source)
XLA Modules:
  0.0 1511.6 jit_solution(6978543041912007066)
XLA Ops:
  16.2 42.2 %all-reduce.17 = (bf16[768]{0:T(1024)(128)(2,1)S(1)}, bf16[768]{0:T(1024)(128)(2,1)S(1)}, bf16[768]{0:T(1024)(128)(2,1)}, bf16[768]{0:T(1024)(128)(2,1)}, bf16[7...) all-reduce(bf16[768]{0:T(1024)(128)(2,1)S(1)} %dynamic-update-slice, ...), channel_id=1, replica_groups=mesh['head'=2,'blk'=16] {'head','blk'}, use_global_device_ids=true, to_apply=%add.1 | all-reduce | flops 6144 | bytes 24576
  58.4 9.3 all-gather.17.cloned.1.call-done
  69.1 54.8 %all-gather.19.cloned.1.call-done = bf16[768,768]{1,0:T(8,128)(2,1)} async-done(((bf16[24,768]{1,0:T(8,128)(2,1)}), bf16[768,768]{1,0:T(8,128)(2,1)}) %all-gather.19.cloned.1.call-update) | async-done | bytes 1179664 | tf_op jit(solution)/shard_map/all_gather | solution.py:148
  125.2 54.6 %all-gather.21.cloned.1.call-done = bf16[768,768]{1,0:T(8,128)(2,1)} async-done(((bf16[24,768]{1,0:T(8,128)(2,1)}), bf16[768,768]{1,0:T(8,128)(2,1)}) %all-gather.21.cloned.1.call-update) | async-done | bytes 1179664 | tf_op jit(solution)/shard_map/all_gather | solution.py:149
  183.3 3.4 reshape.695
  189.8 11.8 all_to_all.66
  208.5 4.2 all-gather.3
  212.9 4.2 all-gather.4
  217.8 20.9 %all_gather.80 = s32[2,2048]{1,0:T(2,128)S(1)} all-gather(s32[2,128]{1,0:T(2,128)} %bitcast_select_fusion), channel_id=1, replica_groups=mesh['head'=2,'blk'=16] {'blk'}, dimensions={1}, use_global_device_ids=true | all-gather | bytes 17408 | tf_op jit(solution)/shard_map/all_gather | solution.py:228
  240.2 9.2 all-gather.33.cloned.1.call-done
  249.4 4.8 copy.222
  254.1 42.0 %all-gather.35.cloned.1.call-done = bf16[2,2048,1,384]{3,1,2,0:T(8,128)(2,1)} async-done(((bf16[2,128,1,384]{3,1,2,0:T(8,128)(2,1)}), bf16[2,2048,1,384]{3,1,2,0:T(8,128)(2,1)}) %all-gather.35.cloned.1.call-update) | async-done | bytes 3145744 | tf_op jit(solution)/shard_map/all_gather | solution.py:227
  296.2 4.7 copy.224
  300.9 38.0 %while.48 = (s32[]{:T(128)}, f32[2,6,128]{2,1,0:T(8,128)S(1)}, f32[2,6,128]{2,1,0:T(8,128)S(1)}, f32[2,128,384]{1,2,0:T(8,128)}, s32[2,128]{1,0:T(2,128)S(1)}, /...) while((s32[]{:T(128)}, f32[2,6,128]{2,1,0:T(8,128)S(1)}, ...), condition=%wide.region_3.4_spmd.clone, body=%wide.region_0.3_spmd.clone.sunk | while | flops 430007680 | bytes 93133680 | solution.py:131
  304.3 3.0 constant_dynamic-slice_fusion.14
  307.2 4.3 fusion.205
  311.6 3.9 fusion.207
  316.7 2.3 fusion.209
  323.3 3.0 constant_dynamic-slice_fusion.14
  326.2 4.3 fusion.205
  330.6 3.9 fusion.207
  335.7 2.3 fusion.209
  340.8 3.4 all-to-all-start.1
  345.1 4.3 all-to-all-done.1
  354.0 63.2 %all-gather.25.cloned.1.call-done = bf16[768,3072]{1,0:T(8,128)(2,1)} async-done(((bf16[24,3072]{1,0:T(8,128)(2,1)}), bf16[768,3072]{1,0:T(8,128)(2,1)}) %all-gather.25.cloned.1.call-update) | async-done | bytes 4718608 | tf_op jit(solution)/shard_map/all_gather | solution.py:158
  417.2 3.1 fusion.123
  420.3 62.1 %all-gather.27.cloned.1.call-done = bf16[768,3072]{1,0:T(8,128)(2,1)} async-done(((bf16[24,3072]{1,0:T(8,128)(2,1)}), bf16[768,3072]{1,0:T(8,128)(2,1)}) %all-gather.27.cloned.1.call-update) | async-done | bytes 4718608 | tf_op jit(solution)/shard_map/all_gather | solution.py:159
  482.4 8.1 multiply_convert_fusion.5
  490.6 57.1 %all-gather.29.cloned.1.call-done = bf16[3072,768]{1,0:T(8,128)(2,1)} async-done(((bf16[96,768]{1,0:T(8,128)(2,1)}), bf16[3072,768]{1,0:T(8,128)(2,1)}) %all-gather.29.cloned.1.call-update) | async-done | bytes 4718608 | tf_op jit(solution)/shard_map/all_gather | solution.py:160
  547.7 3.4 fusion.120
  557.7 2.3 multiply_reduce_fusion
  562.6 7.6 all_to_all.67
  571.6 20.8 %all_gather.99 = s32[2,2048]{1,0:T(2,128)} all-gather(s32[2,128]{1,0:T(2,128)S(1)} %get-tuple-element.1761), channel_id=1, replica_groups=mesh['head'=2,'blk'=16] {'blk'}, dimensions={1}, use_global_device_ids=true | all-gather | bytes 17408 | tf_op jit(solution)/shard_map/all_gather | solution.py:386
  594.1 19.5 %all_gather.100 = f32[2,6,2048]{2,1,0:T(8,128)} all-gather(f32[2,6,128]{2,1,0:T(8,128)S(1)} %log_add_fusion), channel_id=1, replica_groups=mesh['head'=2,'blk'=16] {'blk'}, dimensions={2}, use_global_device_ids=true | all-gather | bytes 104448 | tf_op jit(solution)/shard_map/all_gather | solution.py:291
  618.2 21.1 %all_gather.102 = f32[2,6,2048]{2,1,0:T(8,128)} all-gather(f32[2,6,128]{2,1,0:T(8,128)S(1)} %bitcast.345), channel_id=1, replica_groups=mesh['head'=2,'blk'=16] {'blk'}, dimensions={2}, use_global_device_ids=true | all-gather | bytes 104448 | tf_op jit(solution)/shard_map/all_gather | solution.py:292
  639.4 40.8 %while.49 = (s32[]{:T(128)}, f32[2,128,384]{1,2,0:T(8,128)}, bf16[2,2,1024,384]{2,3,1,0:T(8,128)(2,1)}, s32[2,128]{1,0:T(2,128)}, s32[2,2,1024]{2,1,0:T(2,128)S(...) while((s32[]{:T(128)}, f32[2,128,384]{1,2,0:T(8,128)}, ...), condition=%wide.region_14.15_spmd.clone, body=%wide.region_13.14_spmd.clone.sunk | while | flops 617169280 | bytes 33766336 | solution.py:131
  639.4 2.3 constant_dynamic-slice_fusion.15
  641.7 3.7 fusion.216
  650.3 7.6 fusion.219
  662.0 3.7 fusion.216
  670.6 7.6 fusion.219
  681.9 70.7 %while.50 = (s32[]{:T(128)}, f32[2,128,384]{1,2,0:T(8,128)}, f32[2,128,384]{1,2,0:T(8,128)}, bf16[2,2,1024,384]{3,2,0,1:T(8,128)(2,1)}, s32[2,2,1024]{2,1,0:T(2,...) while((s32[]{:T(128)}, f32[2,128,384]{1,2,0:T(8,128)}, ...), condition=%wide.region_16.17_spmd.clone, body=%wide.region_15.16_spmd.clone.sunk | while | flops 826556800 | bytes 67034164 | solution.py:131
  687.5 5.0 fusion.227
  699.4 5.2 fusion.230
  706.2 9.0 fusion.231
  722.8 5.0 fusion.227
  734.7 5.2 fusion.230
  741.4 9.0 fusion.231
  750.4 2.2 bitcast_add_fusion.9
  756.6 12.0 all_to_all.68
  770.8 2.6 fusion.116
  773.4 3.0 copy.258
  776.5 3.1 copy.260
  782.8 5.1 fusion.124
  789.1 5.0 fusion.125
  795.4 5.0 fusion.110
  801.1 37.6 %all-reduce.16 = (f32[768]{0:T(1024)S(1)}, f32[768]{0:T(1024)S(1)}, f32[768]{0:T(1024)S(1)}, f32[768]{0:T(1024)S(1)}, f32[768]{0:T(1024)S(1)}, /*index=5*/f32[768]{0:T(1024)S(1)}, f32[768]{0:T(1024)S(1)}, f32[768]{0:T(1024)S(1)}) all-reduce(f32[768]{0:T(1024)S(1)} %slice.35, ...), channel_id=6, replica_groups=mesh['head'=2,'blk'=16] {'head','blk'}, use_global_device_ids=true, to_apply=%region_19.20.clone | all-reduce | flops 6144 | bytes 49152
  843.3 4.0 fusion.97
  847.3 24.8 %reduce-scatter.22.cloned.1.call-done = f32[24,768]{1,0:T(8,128)} async-done(((f32[768,768]{1,0:T(8,128)}), f32[24,768]{1,0:T(8,128)}) %reduce-scatter.22.cloned.1.call-update) | async-done | bytes 73744
  872.1 103.7 %reduce-scatter.24.cloned.1.call-done = f32[24,768]{1,0:T(8,128)} async-done(((f32[768,768]{1,0:T(8,128)}), f32[24,768]{1,0:T(8,128)}) %reduce-scatter.24.cloned.1.call-update) | async-done | bytes 73744
  975.8 104.7 %reduce-scatter.26.cloned.1.call-done = f32[24,768]{1,0:T(8,128)} async-done(((f32[768,768]{1,0:T(8,128)}), f32[24,768]{1,0:T(8,128)}) %reduce-scatter.26.cloned.1.call-update) | async-done | bytes 73744
  1080.5 140.8 %reduce-scatter.16.cloned.1.call-done = f32[24,3072]{1,0:T(8,128)} async-done(((f32[768,3072]{1,0:T(8,128)}), f32[24,3072]{1,0:T(8,128)}) %reduce-scatter.16.cloned.1.call-update) | async-done | bytes 294928 | tf_op jit(solution)/shard_map/reduce_scatter | solution.py:433
  1221.3 142.3 %reduce-scatter.18.cloned.1.call-done = f32[24,3072]{1,0:T(8,128)} async-done(((f32[768,3072]{1,0:T(8,128)}), f32[24,3072]{1,0:T(8,128)}) %reduce-scatter.18.cloned.1.call-update) | async-done | bytes 294928 | tf_op jit(solution)/shard_map/reduce_scatter | solution.py:434
  1363.6 141.0 %reduce-scatter.20.cloned.1.call-done = f32[96,768]{1,0:T(8,128)} async-done(((f32[3072,768]{1,0:T(8,128)}), f32[96,768]{1,0:T(8,128)}) %reduce-scatter.20.cloned.1.call-update) | async-done | bytes 294928 | tf_op jit(solution)/shard_map/reduce_scatter | solution.py:435
  (390 shorter events, 122.4 us)
Async XLA Ops:
  7.2 60.5 %all-gather.17.cloned.1.call-start = ((), (), s32[]{:S(2)}) async-start(), calls=%async_computation.11 | async-start | bytes 1216512 | tf_op jit(solution)/shard_map/all_gather | solution.py:147
  7.9 115.9 %all-gather.19.cloned.1.call-start = ((), (), s32[]{:S(2)}) async-start(), calls=%async_computation.12 | async-start | bytes 1216512 | tf_op jit(solution)/shard_map/all_gather | solution.py:148
  8.7 171.1 %all-gather.21.cloned.1.call-start = ((), (), s32[]{:S(2)}) async-start(), calls=%async_computation.13 | async-start | bytes 1216512 | tf_op jit(solution)/shard_map/all_gather | solution.py:149
  9.4 240.0 %all-gather.33.cloned.1.call-start = ((), (), s32[]{:S(2)}) async-start(), calls=%async_computation.23 | async-start | bytes 3342336 | tf_op jit(solution)/shard_map/all_gather | solution.py:226
  202.4 6.1 copy-start.56
  202.4 10.4 copy-start.57
  202.4 14.8 copy-start.61
  202.4 36.3 %copy-start.25 = (bf16[2,64,768]{2,1,0:T(8,128)(2,1)S(1)}, bf16[2,64,768]{2,1,0:T(8,128)(2,1)}, u32[]{:S(2)}) copy-start(bf16[2,64,768]{2,1,0:T(8,128)(2,1)} %param.44) | copy-start | bytes 589828
  205.1 49.1 %copy-start.27 = (bf16[2,128,1,384]{3,1,2,0:T(8,128)(2,1)}, bf16[2,128,1,384]{3,1,2,0:T(8,128)(2,1)S(1)}, u32[]{:S(2)}) copy-start(bf16[2,128,1,384]{3,1,2,0:T(8,128)(2,1)S(1)} %get-tuple-element.1297) | copy-start | bytes 589828
  205.1 91.1 %all-gather.35.cloned.1.call-start = ((), (), s32[]{:S(2)}) async-start(), calls=%async_computation.24 | async-start | bytes 3342336 | tf_op jit(solution)/shard_map/all_gather | solution.py:227
  205.7 146.2 %all-gather.23.cloned.1.call-start = ((), (), s32[]{:S(2)}) async-start(), calls=%async_computation.14 | async-start | bytes 1216512 | tf_op jit(solution)/shard_map/all_gather | solution.py:150
  206.2 210.9 %all-gather.25.cloned.1.call-start = ((), (), s32[]{:S(2)}) async-start(), calls=%async_computation.15 | async-start | bytes 4866048 | tf_op jit(solution)/shard_map/all_gather | solution.py:158
  207.0 275.4 %all-gather.27.cloned.1.call-start = ((), (), s32[]{:S(2)}) async-start(), calls=%async_computation.16 | async-start | bytes 4866048 | tf_op jit(solution)/shard_map/all_gather | solution.py:159
  207.7 340.0 %all-gather.29.cloned.1.call-start = ((), (), s32[]{:S(2)}) async-start(), calls=%async_computation.17 | async-start | bytes 4866048 | tf_op jit(solution)/shard_map/all_gather | solution.py:160
  300.8 43.5 %copy-start.55 = (bf16[768]{0:T(1024)(128)(2,1)S(1)}, bf16[768]{0:T(1024)(128)(2,1)}, u32[]{:S(2)}) copy-start(bf16[768]{0:T(1024)(128)(2,1)} %get-tuple-element.1272) | copy-start | bytes 4612
  300.8 43.5 %copy-start.54 = (bf16[768]{0:T(1024)(128)(2,1)S(1)}, bf16[768]{0:T(1024)(128)(2,1)}, u32[]{:S(2)}) copy-start(bf16[768]{0:T(1024)(128)(2,1)} %get-tuple-element.1269) | copy-start | bytes 4612
  300.8 43.5 %copy-start.53 = (bf16[768]{0:T(1024)(128)(2,1)S(1)}, bf16[768]{0:T(1024)(128)(2,1)}, u32[]{:S(2)}) copy-start(bf16[768]{0:T(1024)(128)(2,1)} %get-tuple-element.1270) | copy-start | bytes 4612
  300.8 43.5 %copy-start.52 = (bf16[768]{0:T(1024)(128)(2,1)S(1)}, bf16[768]{0:T(1024)(128)(2,1)}, u32[]{:S(2)}) copy-start(bf16[768]{0:T(1024)(128)(2,1)} %get-tuple-element.1271) | copy-start | bytes 4612
  300.9 43.6 %copy-start.51 = (bf16[768]{0:T(1024)(128)(2,1)S(1)}, bf16[768]{0:T(1024)(128)(2,1)}, u32[]{:S(2)}) copy-start(bf16[768]{0:T(1024)(128)(2,1)} %get-tuple-element.1273) | copy-start | bytes 4612
  311.6 4.6 copy-start
  311.6 5.1 copy-start.2
  330.6 4.6 copy-start
  330.6 5.1 copy-start.2
  338.9 14.7 copy-start.40
  338.9 14.7 copy-start.58
  338.9 232.7 %copy-start.38 = (s32[2,128]{1,0:T(2,128)}, s32[2,128]{1,0:T(2,128)S(1)}, u32[]{:S(2)}) copy-start(s32[2,128]{1,0:T(2,128)S(1)} %get-tuple-element.1761) | copy-start | bytes 3076
  338.9 13.0 copy-start.36
  339.9 11.9 copy-start.31
  340.8 8.6 all-to-all-start.1
  344.2 337.7 %all-gather.37.cloned.1.call-start = ((), (), s32[]{:S(2)}) async-start(), calls=%async_computation.25 | async-start | bytes 3342336 | tf_op jit(solution)/shard_map/all_gather | solution.py:384
  344.8 337.1 %all-gather.31.cloned.1.call-start = ((), (), s32[]{:S(2)}) async-start(), calls=%async_computation.18 | async-start | bytes 3342336 | tf_op jit(solution)/shard_map/all_gather | solution.py:385
  354.0 128.5 %copy-start.23 = (bf16[128,768]{1,0:T(8,128)(2,1)}, bf16[128,768]{1,0:T(8,128)(2,1)S(1)}, u32[]{:S(2)}) copy-start(bf16[128,768]{1,0:T(8,128)(2,1)S(1)} %fusion.106) | copy-start | bytes 589828
  490.6 60.5 %copy-start.21 = (bf16[128,3072]{1,0:T(8,128)(2,1)}, bf16[128,3072]{1,0:T(8,128)(2,1)S(1)}, u32[]{:S(2)}) copy-start(bf16[128,3072]{1,0:T(8,128)(2,1)S(1)} %get-tuple-element.1281) | copy-start | bytes 2359300
  547.7 5.9 slice-start.2
  547.7 3.6 copy-start.26
  547.7 5.9 slice-start.3
  547.7 5.9 copy-start.34
  552.1 5.6 slice-start.4
  553.6 4.1 slice-start.5
  560.8 52.7 %copy-start.18 = (f32[128,768]{1,0:T(8,128)}, f32[128,768]{1,0:T(8,128)S(1)}, u32[]{:S(2)}) copy-start(f32[128,768]{1,0:T(8,128)S(1)} %get-tuple-element.1280) | copy-start | bytes 1179652
  561.9 30.5 %copy-start.29 = (bf16[2,128,1,384]{3,1,2,0:T(8,128)(2,1)S(1)}, bf16[2,128,1,384]{3,1,2,0:T(8,128)(2,1)}, u32[]{:S(2)}) copy-start(bf16[2,128,1,384]{3,1,2,0:T(8,128)(2,1)} %get-tuple-element.1298) | copy-start | bytes 589828
  561.9 31.4 %copy-start.28 = (bf16[2,128,1,384]{3,1,2,0:T(8,128)(2,1)S(1)}, bf16[2,128,1,384]{3,1,2,0:T(8,128)(2,1)}, u32[]{:S(2)}) copy-start(bf16[2,128,1,384]{3,1,2,0:T(8,128)(2,1)} %get-tuple-element.1296) | copy-start | bytes 589828
  571.5 275.8 %reduce-scatter.14.cloned.1.call-start = ((), (), s32[]{:S(2)}) async-start(), calls=%async_computation.19 | async-start | bytes 2433024 | tf_op jit(solution)/shard_map/reduce_scatter | solution.py:427
  594.1 19.5 %copy-start.43 = (f32[2,6,128]{2,1,0:T(8,128)}, f32[2,6,128]{2,1,0:T(8,128)S(1)}, u32[]{:S(2)}) copy-start(f32[2,6,128]{2,1,0:T(8,128)S(1)} %log_add_fusion) | copy-start | bytes 18436
  615.5 23.9 %copy-start.7 = (bf16[2,128,1,384]{1,3,0,2:T(8,128)(2,1)S(1)}, bf16[2,128,1,384]{1,3,0,2:T(8,128)(2,1)}, u32[]{:S(2)}) copy-start(bf16[2,128,1,384]{1,3,0,2:T(8,128)(2,1)} %get-tuple-element.1731) | copy-start | bytes 589828
  615.5 256.6 %reduce-scatter.22.cloned.1.call-start = ((), (), s32[]{:S(2)}) async-start(), calls=%async_computation.26 | async-start | bytes 2433024
  641.7 3.8 copy-start.59
  641.7 5.2 copy-start.41
  661.9 3.8 copy-start.59
  662.0 5.2 copy-start.41
  687.5 5.0 copy-start.3
  687.5 5.0 copy-start.60
  687.5 9.4 copy-start.42
  699.4 5.2 copy-start.5
  722.8 5.0 copy-start.3
  722.8 5.0 copy-start.60
  722.8 9.4 copy-start.42
  734.7 5.2 copy-start.5
  776.5 199.3 %reduce-scatter.24.cloned.1.call-start = ((), (), s32[]{:S(2)}) async-start(), calls=%async_computation.27 | async-start | bytes 2433024
  779.6 300.9 %reduce-scatter.26.cloned.1.call-start = ((), (), s32[]{:S(2)}) async-start(), calls=%async_computation.28 | async-start | bytes 2433024
  781.7 439.6 %reduce-scatter.16.cloned.1.call-start = ((), (), s32[]{:S(2)}) async-start(), calls=%async_computation.20 | async-start | bytes 9732096 | tf_op jit(solution)/shard_map/reduce_scatter | solution.py:433
  788.0 575.7 %reduce-scatter.18.cloned.1.call-start = ((), (), s32[]{:S(2)}) async-start(), calls=%async_computation.21 | async-start | bytes 9732096 | tf_op jit(solution)/shard_map/reduce_scatter | solution.py:434
  794.1 710.5 %reduce-scatter.20.cloned.1.call-start = ((), (), s32[]{:S(2)}) async-start(), calls=%async_computation.22 | async-start | bytes 9732096 | tf_op jit(solution)/shard_map/reduce_scatter | solution.py:435
  800.4 43.0 %copy-start.19 = (f32[128,768]{1,0:T(8,128)S(1)}, f32[128,768]{1,0:T(8,128)}, u32[]{:S(2)}) copy-start(f32[128,768]{1,0:T(8,128)} %copy-done.18) | copy-start | bytes 1179652
  (39 other events, 71.7 us)
Sparse Core Ops, SparseCore 0:
  10.9 56.7 all-gather.16
  70.6 53.1 all-gather.18
  126.7 52.9 all-gather.20
  205.2 44.1 all-gather.32
  252.1 44.0 all-gather.34
  298.9 52.9 all-gather.22
  354.8 62.3 all-gather.24
  420.1 62.3 all-gather.26
  485.4 62.3 all-gather.28
  550.4 44.1 all-gather.36
  596.9 44.6 all-gather.30
  647.3 98.0 reduce-scatter.13
  776.6 95.4 reduce-scatter.21
  877.8 97.9 reduce-scatter.23
  982.4 98.1 reduce-scatter.25
  1086.9 134.3 reduce-scatter.15
  1228.6 134.9 reduce-scatter.17
  1369.9 134.5 reduce-scatter.19
where the time goes:
time: 1520 us; the launch traced here: 1510 us
  waiting for transfers between devices  1020 us (67%)
  blocking collectives  202 us (13%)
  matrix products  121 us (8%)
  local copies, waits for them, and re-layouts  101 us (7%)
  other arithmetic  40.9 us (3%)
    unnamed x21, waiting for transfers between devices  239 us
    reduce_scatter x1, waiting for transfers between devices, on_device(): lax.psum_scatter(mlp_members[1], ('head', 'blk'), scatter_dimension=0, ti...  142 us
    reduce_scatter x1, waiting for transfers between devices, on_device(): lax.psum_scatter(mlp_members[2], ('head', 'blk'), scatter_dimension=0, ti...  141 us
    reduce_scatter x1, waiting for transfers between devices, on_device(): lax.psum_scatter(mlp_members[0], ('head', 'blk'), scatter_dimension=0, ti...  141 us
    unnamed x2, blocking collectives  79.8 us
    all_gather x1, waiting for transfers between devices, on_device(): lax.all_gather(w_gate, ('head', 'blk'), axis=0, tiled=True)  63.2 us
    all_gather x1, waiting for transfers between devices, on_device(): lax.all_gather(w_up, ('head', 'blk'), axis=0, tiled=True)  62.1 us
    all_gather x1, waiting for transfers between devices, on_device(): lax.all_gather(w_down, ('head', 'blk'), axis=0, tiled=True)  57.1 us
  transfers between devices with their start and end apart: 19, of which 16 were waited for; matrix products, arithmetic and copies ran while one was open for 16% of the time, Pallas kernels for 0%

commit v1 on v0

v1 whole, which is shorter than its diff:
```python
import functools
import math

import jax
import jax.numpy as jnp
import numpy as np
from jax import lax
from jax.experimental import pallas as pl
from jax.experimental.pallas import tpu as pltpu
from jax.sharding import Mesh
from jax.sharding import PartitionSpec as P

HEADS = 12
HEAD_DIM = 64
FEATS = 4
SLOTS = 4
PACK = 4 * HEAD_DIM
BLOCK = 256

norm_epsilon = 1e-12
masked_value = -1e30
f32 = jnp.float32
bf16 = jnp.bfloat16


def alibi_slopes(head_total):
    nearest = 2 ** int(math.floor(math.log2(head_total)))
    slopes = [2.0 ** (-8.0 * (index + 1) / nearest) for index in range(nearest)]
    extra = [2.0 ** (-8.0 * (index + 1) / (2 * nearest)) for index in range(2 * nearest)]
    slopes = slopes + extra[0::2][: head_total - nearest]
    return np.array(slopes, dtype=np.float32)


def dot(left, right, left_dim=1, right_dim=0):
    return lax.dot_general(
        left, right, (((left_dim,), (right_dim,)), ((), ())), preferred_element_type=f32
    )


def swap(values, axis, step=1):
    size = lax.axis_size(axis)
    return lax.ppermute(values, axis, [(i, i ^ step) for i in range(size)])


def in_order(parts, me):
    if len(parts) == 2:
        mine, other = parts
        return jnp.stack([jnp.where(me == 0, mine, other), jnp.where(me == 0, other, mine)])
    return jnp.take(jnp.stack(parts), jnp.arange(len(parts)) ^ me, axis=0)


def gather_axis(values, axis):
    size = lax.axis_size(axis)
    parts = [values] + [swap(values, axis, k) for k in range(1, size)]
    return in_order(parts, lax.axis_index(axis))


def scatter_axis(values, axis):
    size = lax.axis_size(axis)
    me = lax.axis_index(axis)

    def pick(k):
        if size == 2:
            return jnp.where((me ^ k) == 0, values[0], values[1])
        return lax.dynamic_index_in_dim(values, me ^ k, 0, keepdims=False)

    total = pick(0)
    for k in range(1, size):
        total = total + swap(pick(k).astype(bf16), axis, k).astype(f32)
    return total


def gather_feats(values):
    return [values] + [swap(values, "f", k) for k in range(1, FEATS)]


def scatter_feats(values):
    rows = values.shape[0] // FEATS
    total = values[:rows]
    for k in range(1, FEATS):
        total = total + swap(values[k * rows : (k + 1) * rows].astype(bf16), "f", k).astype(f32)
    return total


def all_to_all(values, axes):
    return lax.all_to_all(values, axes, split_axis=0, concat_axis=0, tiled=True)


def place(unit, side, feat, core, rows):
    return (((unit * 2 + side) * FEATS + feat) * 2 + core) * rows


def unpack_qkv(qkv_ref, q_s, k_s, v_s, feat):
    slots, feats, sides, rows, _ = qkv_ref.shape
    for slot in range(slots):
        for k in range(feats):
            for side in range(sides):
                start = pl.multiple_of(place(slot // 2, side, feat ^ k, slot % 2, rows), rows)
                here = pl.ds(start, rows)
                piece = qkv_ref[slot, k, side]
                q_s[here, :] = piece[:, :HEAD_DIM] * (HEAD_DIM**-0.5)
                k_s[here, :] = piece[:, HEAD_DIM : 2 * HEAD_DIM]
                v_s[here, :] = piece[:, 2 * HEAD_DIM : 3 * HEAD_DIM]


def spread_codes(code_ref, code_s):
    for start in range(0, code_ref.shape[1], 128):
        row = code_ref[:, start : start + 128]
        code_s[start : start + 128, :] = jnp.transpose(jnp.broadcast_to(row, (128, 128)))


def distance_tile():
    rows = lax.broadcasted_iota(jnp.int32, (BLOCK, BLOCK), 0)
    cols = lax.broadcasted_iota(jnp.int32, (BLOCK, BLOCK), 1)
    return (cols - rows).astype(f32)


def score_tile(q_part, k_part, code_part, seg_part, tile, offset, slope):
    distance = tile + offset
    scores = dot(k_part, q_part, 1, 1) - slope * jnp.abs(distance)
    codes = jnp.concatenate([code_part] * (BLOCK // 128), axis=1)
    allowed = (codes == seg_part) | (distance == 0.0)
    return scores, allowed


def attend_kernel(
    table_ref, slope_ref, qkv_ref, seg_ref, code_ref, out_ref, lse_ref, ot_ref,
    q_s, k_s, v_s, o_s, code_s,
):
    slope = slope_ref[0, 0]
    unpack_qkv(qkv_ref, q_s, k_s, v_s, table_ref[2, 0])
    spread_codes(code_ref, code_s)
    tile = distance_tile()
    units = qkv_ref.shape[0] // 2
    rows = qkv_ref.shape[3]
    if qkv_ref.shape[0] > SLOTS:
        o_s[...] = jnp.zeros_like(o_s)
        ot_ref[...] = jnp.zeros_like(ot_ref)
        lse_ref[...] = jnp.zeros_like(lse_ref)

    def query_step(i, carry):
        here = pl.ds(pl.multiple_of(i * BLOCK, BLOCK), BLOCK)
        q_part = q_s[here, :]
        seg_part = seg_ref[:, here]

        def key_step(j, state):
            top, total, mixed = state
            there = pl.ds(pl.multiple_of(j * BLOCK, BLOCK), BLOCK)
            offset = ((i - j) * BLOCK).astype(f32)
            scores, allowed = score_tile(
                q_part, k_s[there, :], code_s[there, :], seg_part, tile, offset, slope
            )
            scores = jnp.where(allowed, scores, masked_value)
            top_new = jnp.maximum(top, jnp.max(scores, axis=0, keepdims=True))
            probs = jnp.exp(scores - top_new)
            factor = jnp.exp(top - top_new)
            total = total * factor + jnp.sum(probs, axis=0, keepdims=True)
            mixed = mixed * factor + dot(v_s[there, :], probs.astype(bf16), 0, 0)
            return top_new, total, mixed

        top, total, mixed = lax.fori_loop(
            table_ref[0, i],
            table_ref[1, i],
            key_step,
            (
                jnp.full((1, BLOCK), masked_value, f32),
                jnp.zeros((1, BLOCK), f32),
                jnp.zeros((HEAD_DIM, BLOCK), f32),
            ),
        )
        mixed = mixed / total
        ot_ref[:, here] = mixed
        lse_ref[:, here] = top + jnp.log(total)
        o_s[here, :] = jnp.transpose(mixed)
        return carry

    lax.fori_loop(table_ref[2, 1], table_ref[2, 2], query_step, 0)
    for unit in range(units):
        for feat in range(FEATS):
            for core in range(2):
                starts = [place(unit, side, feat, core, rows) for side in range(2)]
                sides = [o_s[start : start + rows, :] for start in starts]
                out_ref[(unit * FEATS + feat) * 2 + core] = jnp.concatenate(sides, axis=1).astype(bf16)


def attend_back_kernel(
    table_ref, slope_ref, qkv_ref, dout_ref, ot_ref, lse_ref, seg_ref, code_ref, dqkv_ref,
    q_s, k_s, v_s, do_s, code_s, delta_s, dq_s, dk_s, dv_s,
):
    slope = slope_ref[0, 0]
    feat_self = table_ref[2, 0]
    first, last = table_ref[2, 1], table_ref[2, 2]
    slots, feats, sides, rows, _ = qkv_ref.shape
    unpack_qkv(qkv_ref, q_s, k_s, v_s, feat_self)
    spread_codes(code_ref, code_s)
    tile = distance_tile()
    for unit in range(slots // 2):
        for feat in range(FEATS):
            for core in range(2):
                piece = dout_ref[(unit * FEATS + feat) * 2 + core]
                for side in range(2):
                    start = place(unit, side, feat, core, rows)
                    do_s[start : start + rows, :] = piece[:, side * HEAD_DIM : (side + 1) * HEAD_DIM]
    dq_s[...] = jnp.zeros_like(dq_s)

    def delta_step(i, carry):
        here = pl.ds(pl.multiple_of(i * BLOCK, BLOCK), BLOCK)
        turned = jnp.transpose(do_s[here, :].astype(f32))
        delta_s[:, here] = jnp.sum(turned * ot_ref[:, here], axis=0, keepdims=True)
        return carry

    lax.fori_loop(first, last, delta_step, 0)

    def key_step(j, carry):
        there = pl.ds(pl.multiple_of(j * BLOCK, BLOCK), BLOCK)
        k_part, v_part, code_part = k_s[there, :], v_s[there, :], code_s[there, :]

        def query_step(i, state):
            dk, dv = state
            here = pl.ds(pl.multiple_of(i * BLOCK, BLOCK), BLOCK)
            q_part, do_part = q_s[here, :], do_s[here, :]
            offset = ((i - j) * BLOCK).astype(f32)
            scores, allowed = score_tile(
                q_part, k_part, code_part, seg_ref[:, here], tile, offset, slope
            )
            probs = jnp.exp(jnp.where(allowed, scores - lse_ref[:, here], masked_value))
            back_probs = dot(v_part, do_part, 1, 1)
            back_scores = (probs * (back_probs - delta_s[:, here])).astype(bf16)
            dv = dv + dot(probs.astype(bf16), do_part)
            dk = dk + dot(back_scores, q_part)
            dq_s[here, :] += dot(back_scores, k_part, 0, 0)
            return dk, dv

        zero = jnp.zeros((BLOCK, HEAD_DIM), f32)
        dk, dv = lax.fori_loop(
            jnp.maximum(table_ref[0, j], first),
            jnp.minimum(table_ref[1, j], last),
            query_step,
            (zero, zero),
        )
        dk_s[there, :] = dk
        dv_s[there, :] = dv
        return carry

    lax.fori_loop(0, q_s.shape[0] // BLOCK, key_step, 0)
    for slot in range(slots):
        for k in range(feats):
            for side in range(sides):
                start = pl.multiple_of(place(slot // 2, side, feat_self ^ k, slot % 2, rows), rows)
                here = pl.ds(start, rows)
                dqkv_ref[slot, k, side] = jnp.concatenate(
                    [
                        dq_s[here, :] * (HEAD_DIM**-0.5),
                        dk_s[here, :],
                        dv_s[here, :],
                        jnp.zeros((rows, HEAD_DIM), f32),
                    ],
                    axis=1,
                ).astype(bf16)


def attend(table, slope, qkv, seg_row, code_row):
    slots, feats, sides, rows, _ = qkv.shape
    length = slots * feats * sides * rows
    vmem = pl.BlockSpec(memory_space=pltpu.VMEM)
    smem = pl.BlockSpec(memory_space=pltpu.SMEM)
    return pl.pallas_call(
        attend_kernel,
        out_shape=(
            jax.ShapeDtypeStruct((slots * feats, rows, 2 * HEAD_DIM), bf16),
            jax.ShapeDtypeStruct((1, length), f32),
            jax.ShapeDtypeStruct((HEAD_DIM, length), f32),
        ),
        in_specs=[smem, smem, vmem, vmem, vmem],
        out_specs=(vmem, vmem, vmem),
        scratch_shapes=[pltpu.VMEM((length, HEAD_DIM), bf16)] * 3
        + [pltpu.VMEM((length, HEAD_DIM), f32), pltpu.VMEM((length, 128), f32)],
        name="attend",
    )(table, slope, qkv, seg_row, code_row)


def attend_back(table, slope, qkv, dout, o_turned, lse, seg_row, code_row):
    slots, feats, sides, rows, _ = qkv.shape
    length = slots * feats * sides * rows
    vmem = pl.BlockSpec(memory_space=pltpu.VMEM)
    smem = pl.BlockSpec(memory_space=pltpu.SMEM)
    return pl.pallas_call(
        attend_back_kernel,
        out_shape=jax.ShapeDtypeStruct(qkv.shape, bf16),
        in_specs=[smem, smem] + [vmem] * 6,
        out_specs=vmem,
        scratch_shapes=[pltpu.VMEM((length, HEAD_DIM), bf16)] * 4
        + [pltpu.VMEM((length, 128), f32), pltpu.VMEM((1, length), f32)]
        + [pltpu.VMEM((length, HEAD_DIM), f32)] * 3,
        name="attend_back",
    )(table, slope, qkv, dout, o_turned, lse, seg_row, code_row)


def norm_forward(values, gain, shift):
    centred = values - jnp.mean(values, axis=-1, keepdims=True)
    inverse = lax.rsqrt(jnp.mean(centred * centred, axis=-1, keepdims=True) + norm_epsilon)
    normed = centred * inverse
    return normed * gain + shift, normed, inverse


def norm_backward(upstream, normed, inverse, gain):
    scaled = upstream * gain
    adjusted = (
        scaled
        - jnp.mean(scaled, axis=-1, keepdims=True)
        - normed * jnp.mean(scaled * normed, axis=-1, keepdims=True)
    )
    return adjusted * inverse, jnp.sum(upstream * normed, axis=0), jnp.sum(upstream, axis=0)


def on_device(
    layer_input, segment_ids, token_live, w_query, b_query, w_key, w_value, b_value,
    w_output, b_output, first_gain, first_shift, w_gate, w_up, w_down, b_down,
    second_gain, second_shift, output_grad,
):
    units = lax.axis_size("u")
    unit, side, feat, core = (lax.axis_index(name) for name in ("u", "s", "f", "c"))
    devices = units * 2 * FEATS * 2
    sequences, rows, width = layer_input.shape
    length = rows * devices
    w_rows = w_query.shape[0]
    down_rows, ff_part = w_down.shape[0], w_gate.shape[1] // FEATS
    slots = units * 2
    heads = HEADS // FEATS
    head_width = heads * HEAD_DIM
    ranges = slots // SLOTS
    local = 2 * rows
    group = FEATS * local

    def exchange_sides(values):
        kept = jnp.where(side == 0, values[0], values[1])
        got = swap(jnp.where(side == 0, values[1], values[0]), "s")
        return kept, got

    def to_tokens(values):
        kept, got = exchange_sides(values)
        return jnp.concatenate(
            [jnp.where(side == 0, kept, got), jnp.where(side == 0, got, kept)], axis=0
        )

    def from_tokens(values):
        kept, got = exchange_sides(values.reshape(2, rows, width))
        return jnp.stack([jnp.where(side == 0, kept, got), jnp.where(side == 0, got, kept)])

    tokens = to_tokens(layer_input)
    token_parts = gather_feats(tokens)

    codes = jnp.where(token_live == 1, segment_ids, -1)
    vectors = jnp.stack(
        [b_query, b_value, b_output, first_gain, first_shift, b_down, second_gain, second_shift],
        axis=1,
    )
    seg_lanes = jnp.pad(
        jnp.concatenate([segment_ids, codes], axis=0).astype(bf16),
        ((0, w_rows - 2 * sequences), (0, HEAD_DIM - rows)),
    )
    vec_lanes = jnp.pad(vectors, ((0, 0), (0, HEAD_DIM - vectors.shape[1])))
    extra = jnp.stack([jnp.zeros_like(seg_lanes), seg_lanes, vec_lanes], axis=1)
    by_head = [w.reshape(w_rows, FEATS, heads, HEAD_DIM) for w in (w_query, w_key, w_value)]
    by_head.append(jnp.broadcast_to(extra[:, None], by_head[0].shape))
    half = heads * PACK // 2
    early = jnp.concatenate(by_head, axis=-1).reshape(w_rows, FEATS, 2, half)
    early = jnp.broadcast_to(
        early.transpose(1, 2, 0, 3)[None], (slots, FEATS, 2, w_rows, half)
    ).reshape(devices * w_rows, half)
    early_mine = all_to_all(early, ("u", "s", "f", "c"))
    early_other = swap(early_mine, "c")
    w_attn = jnp.concatenate(
        [
            jnp.where(core == 0, early_mine, early_other),
            jnp.where(core == 0, early_other, early_mine),
        ],
        axis=1,
    )

    gate_cols = w_gate.reshape(w_rows, slots, FEATS, 2 * down_rows).transpose(2, 0, 1, 3)
    up_cols = w_up.reshape(w_rows, slots, FEATS, 2 * down_rows).transpose(2, 0, 1, 3)
    late = jnp.concatenate(
        [
            jnp.broadcast_to(w_output[None], (FEATS, w_rows, width)),
            gate_cols.reshape(FEATS, w_rows, ff_part),
            up_cols.reshape(FEATS, w_rows, ff_part),
        ],
        axis=-1,
    )
    late_half = late.shape[-1] // 2
    late = late.reshape(FEATS, w_rows, 2, late_half).transpose(0, 2, 1, 3)
    late = all_to_all(late.reshape(FEATS * 2 * w_rows, late_half), ("f", "c"))
    late_rows = late.shape[0]
    late = jnp.concatenate([late, jnp.pad(w_down, ((0, 0), (0, late_half - width)))], axis=0)
    late = gather_axis(gather_axis(late, "s"), "u")
    late_other = swap(late, "c")
    late_zero = jnp.where(core == 0, late, late_other)
    late_one = jnp.where(core == 0, late_other, late)

    def upper(values):
        return values[:, :, :late_rows].reshape(width, late_half)

    late_zero_top, late_one_top = upper(late_zero), upper(late_one)
    full_output = late_zero_top[:, :width]
    full_gate = jnp.concatenate(
        [late_zero_top[:, width:], late_one_top[:, : ff_part - (late_half - width)]], axis=1
    )
    full_up = late_one_top[:, late_half - ff_part :]
    full_down = jnp.stack(
        [late_zero[:, :, late_rows:, :width], late_one[:, :, late_rows:, :width]], axis=2
    ).reshape(ff_part, width)

    vec_start = heads * PACK - HEAD_DIM
    params = w_attn[:, vec_start : vec_start + 8].astype(f32).T
    bias_output, gain_one, shift_one, bias_down, gain_two, shift_two = (
        params[index] for index in range(2, 8)
    )
    bias_parts = [
        lax.dynamic_slice_in_dim(params[index], feat * head_width, head_width).reshape(heads, 1, HEAD_DIM)
        for index in (0, 1)
    ]
    no_bias = jnp.zeros_like(bias_parts[0])
    attn_bias = jnp.concatenate([bias_parts[0], no_bias, bias_parts[1], no_bias], axis=1).reshape(
        heads * PACK
    )
    seg_start = 2 * PACK - HEAD_DIM
    seg_all = w_attn.reshape(devices, w_rows, heads * PACK)[
        :, : 2 * sequences, seg_start : seg_start + rows
    ]
    seg_all = seg_all.astype(f32).reshape(devices, 2, sequences, rows)
    seg_here = jnp.where(side == 0, seg_all[:, :, 0], seg_all[:, :, 1])
    seg_row = seg_here[:, 0].reshape(1, length)
    code_row = seg_here[:, 1].reshape(1, length)

    tokens_group = jnp.concatenate(token_parts, axis=0)
    projected = (dot(tokens_group, w_attn) + attn_bias).astype(bf16)
    pieces = [projected[:, h * PACK : (h + 1) * PACK] for h in range(heads)]
    sent = jnp.concatenate([pieces[min(slot % SLOTS, heads - 1)] for slot in range(slots)], axis=0)
    qkv = all_to_all(sent, ("u", "c")).reshape(slots, FEATS, 2, rows, PACK)

    blocks = length // BLOCK
    slot_self = unit * 2 + core
    range_self = slot_self // SLOTS
    head_self = feat * heads + jnp.minimum(slot_self % SLOTS, heads - 1)
    slope = jnp.asarray(alibi_slopes(HEADS))[head_self].reshape(1, 1)
    seg_blocks = seg_row.reshape(blocks, BLOCK)
    seg_low, seg_high = seg_blocks[:, 0], seg_blocks[:, -1]
    key_low = jnp.sum(seg_high[None, :] < seg_low[:, None], axis=1, dtype=jnp.int32)
    key_high = jnp.sum(seg_low[None, :] <= seg_high[:, None], axis=1, dtype=jnp.int32)
    own = jnp.stack(
        [feat, range_self * (blocks // ranges), (range_self + 1) * (blocks // ranges)]
    ).astype(jnp.int32)
    table = jnp.stack([key_low, key_high, jnp.pad(own, (0, blocks - 3))])
    out_blocks, lse, o_turned = attend(table, slope, qkv, seg_row, code_row)

    heads_in = all_to_all(out_blocks.reshape(-1, 2 * HEAD_DIM), ("u", "f", "c"))
    heads_in = heads_in.reshape(units, FEATS, 2, rows, 2, HEAD_DIM).transpose(4, 3, 1, 0, 2, 5)
    heads_in = heads_in.reshape(2, rows, FEATS, ranges, SLOTS, HEAD_DIM)
    my_range = (unit * 2) // SLOTS
    if ranges > 1:
        heads_in = lax.dynamic_index_in_dim(heads_in, my_range, 3, keepdims=False)
    else:
        heads_in = heads_in[:, :, :, 0]
    attended = heads_in[:, :, :, :heads].reshape(local, width)

    branch = dot(attended, full_output) + bias_output
    first_norm, normed_one, inverse_one = norm_forward(
        tokens.astype(f32) + branch, gain_one, shift_one
    )
    first_low = jnp.concatenate(gather_feats(first_norm.astype(bf16)), axis=0)
    gate_rows = dot(first_low, full_gate)
    up_rows = dot(first_low, full_up)
    spread = 0.5 * (1.0 + lax.erf(gate_rows * (0.5**0.5)))
    gelu = gate_rows * spread
    hidden = (gelu * up_rows).astype(bf16)
    mixed = scatter_feats(dot(hidden, full_down)) + bias_down
    layer_wide, normed_two, inverse_two = norm_forward(first_norm + mixed, gain_two, shift_two)
    layer_output = from_tokens(layer_wide.astype(bf16))

    upstream = to_tokens(output_grad).astype(f32)
    back_second, grad_gain_two, grad_shift_two = norm_backward(
        upstream, normed_two, inverse_two, gain_two
    )
    back_low = back_second.astype(bf16)
    grad_down_bias = jnp.sum(back_low.astype(f32), axis=0)
    back_mixed = jnp.concatenate(gather_feats(back_low), axis=0)
    back_hidden = dot(back_mixed, full_down, 1, 1)
    density = jnp.exp(-0.5 * gate_rows * gate_rows) * (1.0 / math.sqrt(2.0 * math.pi))
    back_gate = (back_hidden * up_rows * (spread + gate_rows * density)).astype(bf16)
    back_up = (back_hidden * gelu).astype(bf16)
    back_first = back_second + scatter_feats(
        dot(back_gate, full_gate, 1, 1) + dot(back_up, full_up, 1, 1)
    )

    def reduce_units(values, stages):
        for axis in stages:
            values = scatter_axis(values, axis)
        return values

    grad_down = dot(hidden, back_mixed, 0, 0).reshape(units, 2, 2, down_rows, width)
    grad_down = scatter_axis(jnp.moveaxis(grad_down, 2, 0), "c")
    grad_down = scatter_axis(scatter_axis(jnp.moveaxis(grad_down, 1, 0), "s"), "u")
    grad_ff = jnp.concatenate(
        [dot(first_low, back_gate, 0, 0), dot(first_low, back_up, 0, 0)], axis=1
    ).reshape(units, 2, FEATS, 2, w_rows, 2 * ff_part)
    grad_ff = scatter_axis(jnp.moveaxis(grad_ff, 3, 0), "c")
    grad_ff = scatter_axis(scatter_axis(jnp.moveaxis(grad_ff, 1, 0), "s"), "u")
    grad_ff = all_to_all(grad_ff.astype(bf16).reshape(FEATS * w_rows, 2 * ff_part), ("f",))
    grad_ff = grad_ff.astype(f32).reshape(FEATS, w_rows, 2, slots, 2 * down_rows)
    grad_ff = grad_ff.transpose(2, 1, 3, 0, 4).reshape(2, w_rows, FEATS * ff_part)

    back_inner, grad_gain_one, grad_shift_one = norm_backward(
        back_first, normed_one, inverse_one, gain_one
    )
    back_branch = back_inner.astype(bf16)
    grad_output_bias = jnp.sum(back_branch.astype(f32), axis=0)
    grad_output = dot(attended, back_branch, 0, 0)
    back_attended = dot(back_branch, full_output, 1, 1).astype(bf16)
    back_attended = back_attended.reshape(2, rows, FEATS, heads, HEAD_DIM)
    back_attended = jnp.concatenate([back_attended, back_attended[:, :, :, :1]], axis=3)
    back_attended = back_attended.transpose(3, 2, 1, 0, 4).reshape(
        2, 2, FEATS, rows, 2 * HEAD_DIM
    )
    back_attended = jnp.broadcast_to(
        back_attended.transpose(0, 2, 1, 3, 4)[None],
        (ranges, 2, FEATS, 2, rows, 2 * HEAD_DIM),
    )
    dout = all_to_all(back_attended.reshape(-1, 2 * HEAD_DIM), ("u", "f", "c"))
    dout = dout.reshape(slots * FEATS, rows, 2 * HEAD_DIM)
    dqkv = attend_back(table, slope, qkv, dout, o_turned, lse, seg_row, code_row)
    dqkv = all_to_all(dqkv.reshape(-1, PACK), ("u", "c")).reshape(ranges, SLOTS, group, PACK)
    dqkv = dqkv[:, :heads]
    if ranges > 1:
        dqkv = jnp.sum(dqkv.astype(f32), axis=0).astype(bf16)
    else:
        dqkv = dqkv[0]
    back_projected = dqkv.transpose(1, 0, 2).reshape(group, heads * PACK)
    partial_input = scatter_feats(dot(back_projected, w_attn, 1, 1))
    input_grad = from_tokens((back_inner + partial_input).astype(bf16))

    sums = jnp.sum(back_projected.astype(f32), axis=0).reshape(heads, 4, HEAD_DIM)

    def placed(values):
        return lax.dynamic_update_slice_in_dim(
            jnp.zeros((width,), f32), values.reshape(head_width), feat * head_width, 0
        )

    vector_grads = jnp.stack(
        [
            placed(sums[:, 0]), placed(sums[:, 2]), grad_output_bias, grad_gain_one,
            grad_shift_one, grad_down_bias, grad_gain_two, grad_shift_two,
        ],
        axis=1,
    )
    grad_attn = dot(tokens_group, back_projected, 0, 0)
    grad_attn = grad_attn + jnp.pad(vector_grads, ((0, 0), (vec_start, HEAD_DIM - 8)))
    grad_attn = jnp.concatenate([grad_attn, grad_output], axis=1)
    attn_cols = heads * PACK + width
    grad_attn = grad_attn.reshape(slots * FEATS, 2, w_rows, attn_cols)
    grad_attn = scatter_axis(jnp.moveaxis(grad_attn, 1, 0), "c").astype(bf16)
    grad_attn = all_to_all(grad_attn.reshape(-1, attn_cols), ("u", "s", "f"))
    grad_attn = jnp.sum(grad_attn.reshape(slots, FEATS, w_rows, attn_cols).astype(f32), axis=0)
    grad_output = jnp.sum(grad_attn[:, :, heads * PACK :], axis=0)
    vectors_out = jnp.sum(grad_attn[:, :, vec_start : vec_start + 8], axis=0)
    grad_attn = grad_attn[:, :, : heads * PACK].reshape(FEATS, w_rows, heads, 4, HEAD_DIM)
    grad_query, grad_key, grad_value = (
        grad_attn[:, :, :, index].transpose(1, 0, 2, 3).reshape(w_rows, width) for index in range(3)
    )
    return (
        layer_output, input_grad, grad_query, vectors_out[:, 0], grad_key, grad_value,
        vectors_out[:, 1], grad_output, vectors_out[:, 2], vectors_out[:, 3], vectors_out[:, 4],
        grad_ff[0], grad_ff[1], grad_down, vectors_out[:, 5], vectors_out[:, 6], vectors_out[:, 7],
    )


def solution(mesh):
    devices = mesh.devices
    names = ("u", "s", "f", "c")
    inner = Mesh(devices.reshape(devices.size // (4 * FEATS), 2, FEATS, 2), names)
    tokens, matrix, vector = P(None, names, None), P(names, None), P(names)
    ids = P(None, names)
    return jax.shard_map(
        on_device,
        mesh=inner,
        in_specs=(
            tokens, ids, ids, matrix, vector, matrix, matrix, vector, matrix, vector, vector,
            vector, matrix, matrix, matrix, vector, vector, vector, tokens,
        ),
        out_specs=(
            tokens, tokens, matrix, vector, matrix, matrix, vector, matrix, vector, vector,
            vector, matrix, matrix, matrix, vector, vector, vector,
        ),
        check_vma=False,
    )
```

time: 1520 us -> 397 us (0.26)
  waiting for transfers between devices: 1020 us -> 148 us
  blocking collectives: 202 us -> 0 us
  matrix products: 121 us -> 22.6 us
  starting transfers between devices: 4.34 us -> 66.9 us
  local copies, waits for them, and re-layouts: 101 us -> 51.6 us
  Pallas kernels: 0 us -> 47.7 us
    reduce_scatter x4 -> x0, waiting for transfers between devices: 424 us -> none  [the longest x1 142 us: on_device(): lax.psum_scatter(mlp_members[1], ('head', 'blk'), scatter_dimension=0, ti...]
    all_gather x11 -> x0, waiting for transfers between devices: 355 us -> none  [the longest x1 63.2 us: on_device(): lax.all_gather(w_gate, ('head', 'blk'), axis=0, tiled=True)]
    unnamed x21 -> x0, waiting for transfers between devices: 239 us -> none
    ppermute x0 -> x33, waiting for transfers between devices: none -> 104 us  [swap(): return lax.ppermute(values, axis, [(i, i ^ step) for i in range(size)])]
    dot_general x29 -> x15, matrix products: 121 us -> 22.6 us  [dot(): lax.dot_general(left, right, (((left_dim,), (right_dim,)), ((), ())), pre...]
    all_gather x6 -> x0, blocking collectives: 90.8 us -> none  [the longest x1 21.1 us: on_device(): lax.all_gather(delta_rows, 'blk', axis=2, tiled=True)]
    unnamed x2 -> x0, blocking collectives: 79.8 us -> none
    pallas_call x0 -> x2, Pallas kernels: none -> 47.7 us  [the longest x1 26.7 us: attend_back(): pl.pallas_call(attend_back_kernel, out_shape=jax.ShapeDtypeStruct(qkv.sha...]
  transfers between devices with their start and end apart: 19 -> 41, of which waited for: 16 -> 26; matrix products, arithmetic and copies ran while one was open for 16% -> 26% of each run, Pallas kernels for 0% -> 12%
where the time goes in v1:
time: 397 us; the launch traced here: 391 us
  waiting for transfers between devices  148 us (37%)
  starting transfers between devices  66.9 us (17%)
  local copies, waits for them, and re-layouts  51.6 us (13%)
  other arithmetic  51.2 us (13%)
  Pallas kernels  47.7 us (12%)
  matrix products  22.6 us (6%)
    ppermute x33, waiting for transfers between devices, swap(): return lax.ppermute(values, axis, [(i, i ^ step) for i in range(size)])  104 us
    all_to_all x8, waiting for transfers between devices, all_to_all(): return lax.all_to_all(values, axes, split_axis=0, concat_axis=0, tiled=True)  44.5 us
    ppermute x33, starting transfers between devices, swap(): return lax.ppermute(values, axis, [(i, i ^ step) for i in range(size)])  33.9 us
    all_to_all x8, starting transfers between devices, all_to_all(): return lax.all_to_all(values, axes, split_axis=0, concat_axis=0, tiled=True)  33 us
    pallas_call x1, Pallas kernels, attend_back(): pl.pallas_call(attend_back_kernel, out_shape=jax.ShapeDtypeStruct(qkv.sha...  26.7 us
    dot_general x15, matrix products, dot(): lax.dot_general(left, right, (((left_dim,), (right_dim,)), ((), ())), pre...  22.6 us
    pallas_call x1, Pallas kernels, attend(): pl.pallas_call(attend_kernel, out_shape=(jax.ShapeDtypeStruct((slots * fe...  21 us
    convert_element_type x7, other arithmetic, scatter_axis(): total = total + swap(pick(k).astype(bf16), axis, k).astype(f32)  9.4 us
  transfers between devices with their start and end apart: 41, of which 26 were waited for; matrix products, arithmetic and copies ran while one was open for 26% of the time, Pallas kernels for 12%

profile of v1, /device:TPU:0, one launch (start us, length us, event | category | flops | bytes accessed | tf_op | source)
XLA Modules:
  0.0 391.0 jit_solution(7817481608379341587)
XLA Ops:
  4.6 5.4 %all-to-all-start.3 = ((bf16[8,24,1152]{2,1,0:T(8,128)(2,1)}), bf16[8,24,1152]{2,1,0:T(8,128)(2,1)S(1)}, u32[]{:S(2)}, u32[]{:S(2)}) async-start(bf16[8,24,1152]{2,1,0:T(8,128)(2,1)} %bitcast.33), calls=%async_computation.3 | async-start | bytes 884736 | tf_op jit(solution)/shard_map/all_to_all | solution.py:86
  10.0 2.7 collective-permute-start
  12.6 7.4 %all-to-all-done.3 = bf16[8,24,1152]{2,1,0:T(8,128)(2,1)S(1)} async-done(((bf16[8,24,1152]{2,1,0:T(8,128)(2,1)}), bf16[8,24,1152]{2,1,0:T(8,128)(2,1)S(1)}, u32[]{:S(2)}, u32[]{:S(2)}) %all-to-all-start.3) | async-done | bytes 442400 | tf_op jit(solution)/shard_map/all_to_all | solution.py:86
  23.4 4.4 %all-to-all-start = ((bf16[32,24,384]{2,1,0:T(8,128)(2,1)}), bf16[32,24,384]{2,1,0:T(8,128)(2,1)S(1)}, u32[]{:S(2)}, u32[]{:S(2)}) async-start(bf16[32,24,384]{2,1,0:T(8,128)(2,1)} %bitcast.13), calls=%async_computation | async-start | bytes 1179648 | tf_op jit(solution)/shard_map/all_to_all | solution.py:86
  28.4 29.8 %collective-permute-done.5 = bf16[288,1152]{1,0:T(8,128)(2,1)S(1)} collective-permute-done((bf16[288,1152]{1,0:T(8,128)(2,1)S(1)}, bf16[288,1152]{1,0:T(8,128)(2,1)S(1)}, u32[]{:S(2)}, u32[]{:S(2)}) %collective-permute-start.5) | collective-permute-done | bytes 663584 | tf_op jit(solution)/shard_map/ppermute | solution.py:42
  61.5 3.9 all-to-all-done
  67.0 2.1 collective-permute-start.4
  69.0 3.7 collective-permute-done.2
  75.4 2.9 collective-permute-done.4
  80.0 10.9 %collective-permute-done.6 = bf16[2,288,1152]{2,1,0:T(8,128)(2,1)} collective-permute-done((bf16[2,288,1152]{2,1,0:T(8,128)(2,1)S(1)}, bf16[2,288,1152]{2,1,0:T(8,128)(2,1)}, u32[]{:S(2)}, u32[]{:S(2)}) %collective-permute-start.6) | collective-permute-done | bytes 1327136 | tf_op jit(solution)/shard_map/ppermute | solution.py:42
  90.8 1.6 select_bitcast_fusion.1
  92.4 1.8 pad_maximum_fusion.2
  94.3 2.7 slice_reduce_fusion.1
  98.4 2.1 add_convert_fusion
  101.6 4.2 %all-to-all-start.1 = ((bf16[4,512,256]{2,1,0:T(8,128)(2,1)}), bf16[4,512,256]{2,1,0:T(8,128)(2,1)}, u32[]{:S(2)}, u32[]{:S(2)}) async-start(bf16[4,512,256]{2,1,0:T(8,128)(2,1)} %bitcast.218), calls=%async_computation.1 | async-start | bytes 2097152 | tf_op jit(solution)/shard_map/all_to_all | solution.py:86
  109.6 10.8 %all-to-all-done.1 = bf16[4,512,256]{2,1,0:T(8,128)(2,1)} async-done(((bf16[4,512,256]{2,1,0:T(8,128)(2,1)}), bf16[4,512,256]{2,1,0:T(8,128)(2,1)}, u32[]{:S(2)}, u32[]{:S(2)}) %all-to-all-start.1) | async-done | bytes 1048608 | tf_op jit(solution)/shard_map/all_to_all | solution.py:86
  120.4 21.0 %attend.1 = (bf16[16,64,128]{2,1,0:T(8,128)(2,1)}, f32[1,2048]{1,0:T(1,128)}, f32[64,2048]{1,0:T(8,128)}) custom-call(s32[3,8]{1,0:T(4,128)} %pad_add_fusion.1.table_ref, f32[1,1]{1,0:T(1,128)} %bitcast.25.slope_ref, bf16[4,4,2,64,256]{4,3,2,1,0:T(8,128)(2,1)} %bitcast.28.qkv_ref, f32[1,2048]{1,0:T(1,128)} %reshape_squeeze.12.seg_ref, ...), custom_call_target="tpu_custom_call" | custom-call | tf_op jit(solution)/shard_map/attend/pallas_call | solution.py:267
  141.3 3.7 all-to-all-start.2
  145.7 8.0 %all-to-all-done.2 = bf16[16,64,128]{2,1,0:T(8,128)(2,1)S(1)} async-done(((bf16[16,64,128]{2,1,0:T(8,128)(2,1)}), bf16[16,64,128]{2,1,0:T(8,128)(2,1)S(1)}, u32[]{:S(2)}, u32[]{:S(2)}) %all-to-all-start.2) | async-done | bytes 262176 | tf_op jit(solution)/shard_map/all_to_all | solution.py:86
  154.8 2.4 broadcast_select_fusion.1
  159.7 2.8 collective-permute-start.8
  163.0 4.7 %collective-permute-done.10 = bf16[128,768]{1,0:T(8,128)(2,1)S(1)} collective-permute-done((bf16[128,768]{1,0:T(8,128)(2,1)S(1)}, bf16[128,768]{1,0:T(8,128)(2,1)S(1)}, u32[]{:S(2)}, u32[]{:S(2)}) %collective-permute-start.10) | collective-permute-done | bytes 196640 | tf_op jit(solution)/shard_map/ppermute | solution.py:42
  167.7 1.9 collective-permute-done.9
  171.1 2.5 multiply_convert_fusion.1
  176.0 2.0 collective-permute-start.12
  179.0 6.6 %collective-permute-done.11 = bf16[128,768]{1,0:T(8,128)(2,1)S(1)} collective-permute-done((bf16[128,768]{1,0:T(8,128)(2,1)S(1)}, bf16[128,768]{1,0:T(8,128)(2,1)S(1)}, u32[]{:S(2)}, u32[]{:S(2)}) %collective-permute-start.11) | collective-permute-done | bytes 196640 | tf_op jit(solution)/shard_map/ppermute | solution.py:42
  188.4 1.8 collective-permute-start.17
  193.1 3.5 collective-permute-done.18
  198.8 4.2 %multiply_convert_fusion = (bf16[512,768]{1,0:T(8,128)(2,1)S(1)}, bf16[512,768]{1,0:T(8,128)(2,1)S(1)}) fusion(f32[512,768]{1,0:T(8,128)} %get-tuple-element.59, f32[512,768]{1,0:T(8,128)} %copy-done.78, f32[512,768]{1,0:T(8,128)} %get-tuple-element.108, bf16[768,768]{1,0:T(8,128)(2,1)} %bitcast.217, bf16[128,768]{1,0:T(8,128)(2,1)} %copy-done.73, ...), kind=kOutput, calls=%fused_computation.22 | convolution fusion | flops 612237312 | bytes 8257536 | tf_op jit(solution)/shard_map/dot_general | solution.py:35
  203.9 2.1 fusion.81
  208.4 1.9 collective-permute-start.20
  210.3 1.7 fusion.50
  215.4 2.5 pad_maximum_fusion.1
  217.8 6.2 %copy.220 = f32[768,1536]{1,0:T(8,128)} copy(f32[768,1536]{0,1:T(8,128)} %pad_maximum_fusion.1) | data formatting | bytes 9437184 | tf_op jit(solution)/shard_map/concatenate | solution.py:504
  224.2 3.6 fusion.10
  228.6 1.9 multiply_reduce_fusion
  232.4 1.7 maximum_bitcast_fusion
  234.1 3.5 copy.210
  239.6 3.5 all-to-all-start.4
  243.2 1.9 fusion.58
  246.7 4.1 %all-to-all-done.4.dout_ref = bf16[16,64,128]{2,1,0:T(8,128)(2,1)S(1)} async-done(((bf16[16,64,128]{2,1,0:T(8,128)(2,1)}), bf16[16,64,128]{2,1,0:T(8,128)(2,1)S(1)}, u32[]{:S(2)}, u32[]{:S(2)}) %all-to-all-start.4) | async-done | bytes 262176 | tf_op jit(solution)/shard_map/all_to_all | solution.py:86
  251.5 26.7 %attend_back.1 = bf16[4,4,2,64,256]{4,3,2,1,0:T(8,128)(2,1)} custom-call(s32[3,8]{1,0:T(4,128)} %pad_add_fusion.1.table_ref, f32[1,1]{1,0:T(1,128)} %bitcast.25.slope_ref, bf16[4,4,2,64,256]{4,3,2,1,0:T(8,128)(2,1)} %bitcast.28.qkv_ref, bf16[16,64,128]{2,1,0:T(8,128)(2,1)} %copy-done.17, f32[64,2048]{1,0:T(8,128)} %get-tuple-element.21.ot_ref, ...), custom_call_target="tpu_custom_call" | custom-call | tf_op jit(solution)/shard_map/attend_back/pallas_call | solution.py:287
  278.3 2.3 copy.212
  280.6 3.5 all-to-all-start.5
  284.1 3.3 fusion
  289.8 8.8 %all-to-all-done.5 = bf16[4,512,256]{1,2,0:T(8,128)(2,1)S(1)} async-done(((bf16[4,512,256]{1,2,0:T(8,128)(2,1)}), bf16[4,512,256]{1,2,0:T(8,128)(2,1)S(1)}, u32[]{:S(2)}, u32[]{:S(2)}) %all-to-all-start.5) | async-done | bytes 1048608 | tf_op jit(solution)/shard_map/all_to_all | solution.py:86
  300.4 2.3 pad_add_fusion
  302.7 2.5 pad_maximum_fusion
  305.1 6.1 %copy.213 = f32[768,1536]{1,0:T(8,128)} copy(f32[768,1536]{0,1:T(8,128)} %pad_maximum_fusion) | data formatting | bytes 9437184 | tf_op jit(solution)/shard_map/concatenate | solution.py:558
  311.2 3.8 fusion.9
  314.9 3.6 collective-permute-done.28
  319.9 1.6 collective-permute-start.29
  322.9 6.0 %collective-permute-done.29 = bf16[4,24,1536]{2,1,0:T(8,128)(2,1)S(1)} collective-permute-done((bf16[4,24,1536]{2,1,0:T(8,128)(2,1)S(1)}, bf16[4,24,1536]{2,1,0:T(8,128)(2,1)S(1)}, u32[]{:S(2)}, u32[]{:S(2)}) %collective-permute-start.29) | collective-permute-done | bytes 294944 | tf_op jit(solution)/shard_map/ppermute | solution.py:42
  329.7 3.5 all-to-all-start.7
  333.2 4.4 %fusion.1 = bf16[16,24,1536]{2,1,0:T(8,128)(2,1)} fusion(bf16[16,24,1536]{2,1,0:T(8,128)(2,1)} %collective-permute-done.26, f32[2,16,24,1536]{3,2,0,1:T(8,128)} %bitcast.202, pred[]{:T(512)S(6)} %eq.19), kind=kLoop, calls=%fused_computation.10 | loop fusion | flops 2359296 | bytes 7077889 | tf_op jit(solution)/shard_map/convert_element_type | solution.py:561
  337.6 1.6 all-to-all-done.7
  339.2 4.7 %all-to-all-start.6 = ((bf16[16,24,1536]{2,1,0:T(8,128)(2,1)}), bf16[16,24,1536]{2,1,0:T(8,128)(2,1)S(1)}, u32[]{:S(2)}, u32[]{:S(2)}) async-start(bf16[16,24,1536]{2,1,0:T(8,128)(2,1)} %fusion.1), calls=%async_computation.6 | async-start | bytes 2359296 | tf_op jit(solution)/shard_map/all_to_all | solution.py:86
  346.4 2.1 collective-permute-start.22
  350.0 2.0 collective-permute-start.32
  352.1 9.1 %collective-permute-done.22 = bf16[128,768]{1,0:T(8,128)(2,1)S(1)} collective-permute-done((bf16[128,768]{1,0:T(8,128)(2,1)S(1)}, bf16[128,768]{1,0:T(8,128)(2,1)S(1)}, u32[]{:S(2)}, u32[]{:S(2)}) %collective-permute-start.22) | collective-permute-done | bytes 196640 | tf_op jit(solution)/shard_map/ppermute | solution.py:42
  361.2 9.6 %collective-permute-done.24 = bf16[128,768]{1,0:T(8,128)(2,1)S(1)} collective-permute-done((bf16[128,768]{1,0:T(8,128)(2,1)S(1)}, bf16[128,768]{1,0:T(8,128)(2,1)S(1)}, u32[]{:S(2)}, u32[]{:S(2)}) %collective-permute-start.24) | collective-permute-done | bytes 196640 | tf_op jit(solution)/shard_map/ppermute | solution.py:42
  370.8 3.1 collective-permute-done.23
  374.0 3.6 collective-permute-start.25
  378.3 3.1 collective-permute-done.25
  (362 shorter events, 75.1 us)
Async XLA Ops:
  3.3 16.7 %copy-start.24 = (bf16[96,768]{1,0:T(8,128)(2,1)S(1)}, bf16[96,768]{1,0:T(8,128)(2,1)}, u32[]{:S(2)}) copy-start(bf16[96,768]{1,0:T(8,128)(2,1)} %param.34) | copy-start | bytes 442372
  3.6 17.5 %copy-start.57 = (s32[2,64]{1,0:T(2,128)S(1)}, s32[2,64]{1,0:T(2,128)}, u32[]{:S(2)}) copy-start(s32[2,64]{1,0:T(2,128)} %param.21) | copy-start | bytes 1540
  3.6 17.4 %copy-start.58 = (s32[2,64]{1,0:T(2,128)S(1)}, s32[2,64]{1,0:T(2,128)}, u32[]{:S(2)}) copy-start(s32[2,64]{1,0:T(2,128)} %param.22) | copy-start | bytes 1540
  3.7 17.6 %copy-start.59 = (bf16[24]{0:T(256)(128)(2,1)S(1)}, bf16[24]{0:T(256)(128)(2,1)}, u32[]{:S(2)}) copy-start(bf16[24]{0:T(256)(128)(2,1)} %param.24) | copy-start | bytes 148
  3.7 17.6 %copy-start.60 = (bf16[24]{0:T(256)(128)(2,1)S(1)}, bf16[24]{0:T(256)(128)(2,1)}, u32[]{:S(2)}) copy-start(bf16[24]{0:T(256)(128)(2,1)} %param.27) | copy-start | bytes 148
  3.7 17.6 %copy-start.61 = (bf16[24]{0:T(256)(128)(2,1)S(1)}, bf16[24]{0:T(256)(128)(2,1)}, u32[]{:S(2)}) copy-start(bf16[24]{0:T(256)(128)(2,1)} %param.29) | copy-start | bytes 148
  3.7 17.6 %copy-start.62 = (bf16[24]{0:T(256)(128)(2,1)S(1)}, bf16[24]{0:T(256)(128)(2,1)}, u32[]{:S(2)}) copy-start(bf16[24]{0:T(256)(128)(2,1)} %param.30) | copy-start | bytes 148
  3.7 17.6 %copy-start.63 = (bf16[24]{0:T(256)(128)(2,1)S(1)}, bf16[24]{0:T(256)(128)(2,1)}, u32[]{:S(2)}) copy-start(bf16[24]{0:T(256)(128)(2,1)} %param.31) | copy-start | bytes 148
  3.7 17.6 %copy-start.64 = (bf16[24]{0:T(256)(128)(2,1)S(1)}, bf16[24]{0:T(256)(128)(2,1)}, u32[]{:S(2)}) copy-start(bf16[24]{0:T(256)(128)(2,1)} %param.35) | copy-start | bytes 148
  3.7 17.6 %copy-start.65 = (bf16[24]{0:T(256)(128)(2,1)S(1)}, bf16[24]{0:T(256)(128)(2,1)}, u32[]{:S(2)}) copy-start(bf16[24]{0:T(256)(128)(2,1)} %param.36) | copy-start | bytes 148
  3.7 17.6 %copy-start.66 = (bf16[24]{0:T(256)(128)(2,1)S(1)}, bf16[24]{0:T(256)(128)(2,1)}, u32[]{:S(2)}) copy-start(bf16[24]{0:T(256)(128)(2,1)} %param.37) | copy-start | bytes 148
  4.5 17.0 %copy-start.37 = (bf16[24,768]{1,0:T(8,128)(2,1)S(1)}, bf16[24,768]{1,0:T(8,128)(2,1)}, u32[]{:S(2)}) copy-start(bf16[24,768]{1,0:T(8,128)(2,1)} %param.23) | copy-start | bytes 110596
  4.5 17.1 %copy-start.38 = (bf16[24,768]{1,0:T(8,128)(2,1)S(1)}, bf16[24,768]{1,0:T(8,128)(2,1)}, u32[]{:S(2)}) copy-start(bf16[24,768]{1,0:T(8,128)(2,1)} %param.25) | copy-start | bytes 110596
  4.5 17.3 %copy-start.39 = (bf16[24,768]{1,0:T(8,128)(2,1)S(1)}, bf16[24,768]{1,0:T(8,128)(2,1)}, u32[]{:S(2)}) copy-start(bf16[24,768]{1,0:T(8,128)(2,1)} %param.26) | copy-start | bytes 110596
  4.6 15.5 %all-to-all-start.3 = ((bf16[8,24,1152]{2,1,0:T(8,128)(2,1)}), bf16[8,24,1152]{2,1,0:T(8,128)(2,1)S(1)}, u32[]{:S(2)}, u32[]{:S(2)}) async-start(bf16[8,24,1152]{2,1,0:T(8,128)(2,1)} %bitcast.33), calls=%async_computation.3 | async-start | bytes 884736 | tf_op jit(solution)/shard_map/all_to_all | solution.py:86
  10.0 50.2 %collective-permute-start = (bf16[64,768]{1,0:T(8,128)(2,1)S(1)}, bf16[64,768]{1,0:T(8,128)(2,1)S(1)}, u32[]{:S(2)}, u32[]{:S(2)}) collective-permute-start(bf16[64,768]{1,0:T(8,128)(2,1)S(1)} %select_bitcast_fusion.9), channel_id=1, source_target_pairs={{0,8},{8,0},{1,9},{9,1},{2,10},{10,2},{3,11},{11,3},{4,12},{12,4},... | collective-permute-start | bytes 294920 | tf_op jit(solution)/shard_map/ppermute | solution.py:42
  20.1 38.1 %collective-permute-start.5 = (bf16[288,1152]{1,0:T(8,128)(2,1)S(1)}, bf16[288,1152]{1,0:T(8,128)(2,1)S(1)}, u32[]{:S(2)}, u32[]{:S(2)}) collective-permute-start(bf16[288,1152]{1,0:T(8,128)(2,1)S(1)} %fusion.21), channel_id=1, source_target_pairs={{0,8},{8,0},{1,9},{9,1},{2,10},{10,2},{3,11},{11,3},{4,12},{12,4},... | collective-permute-start | bytes 1990664 | tf_op jit(solution)/shard_map/ppermute | solution.py:42
  23.4 42.0 %all-to-all-start = ((bf16[32,24,384]{2,1,0:T(8,128)(2,1)}), bf16[32,24,384]{2,1,0:T(8,128)(2,1)S(1)}, u32[]{:S(2)}, u32[]{:S(2)}) async-start(bf16[32,24,384]{2,1,0:T(8,128)(2,1)} %bitcast.13), calls=%async_computation | async-start | bytes 1179648 | tf_op jit(solution)/shard_map/all_to_all | solution.py:86
  58.6 32.2 %collective-permute-start.6 = (bf16[2,288,1152]{2,1,0:T(8,128)(2,1)S(1)}, bf16[2,288,1152]{2,1,0:T(8,128)(2,1)}, u32[]{:S(2)}, u32[]{:S(2)}) collective-permute-start(bf16[2,288,1152]{2,1,0:T(8,128)(2,1)S(1)} %pad_maximum_fusion.3), channel_id=1, source_target_pairs={{0,16},{16,0},{1,17},{17,1},{2,18},{18,2},{3,19},{19,3},{4,20},{20... | collective-permute-start | bytes 3981320 | tf_op jit(solution)/shard_map/ppermute | solution.py:42
  61.5 18.4 %copy-start.29 = (bf16[64,768]{1,0:T(8,128)(2,1)}, bf16[64,768]{1,0:T(8,128)(2,1)S(1)}, u32[]{:S(2)}) copy-start(bf16[64,768]{1,0:T(8,128)(2,1)S(1)} %get-tuple-element.61) | copy-start | bytes 294916
  65.4 13.6 %collective-permute-start.1 = (bf16[768,384]{1,0:T(8,128)(2,1)S(1)}, bf16[768,384]{1,0:T(8,128)(2,1)S(1)}, u32[]{:S(2)}, u32[]{:S(2)}) collective-permute-start(bf16[768,384]{1,0:T(8,128)(2,1)S(1)} %bitcast.223), channel_id=1, source_target_pairs={{0,1},{1,0},{2,3},{3,2},{4,5},{5,4},{6,7},{7,6},{8,9},{9,8},{10,11... | collective-permute-start | bytes 1769480 | tf_op jit(solution)/shard_map/ppermute | solution.py:42
  65.4 7.4 %collective-permute-start.2 = (bf16[128,768]{1,0:T(8,128)(2,1)S(1)}, bf16[128,768]{1,0:T(8,128)(2,1)S(1)}, u32[]{:S(2)}, u32[]{:S(2)}) collective-permute-start(bf16[128,768]{1,0:T(8,128)(2,1)S(1)} %pad_maximum_fusion.14), channel_id=1, source_target_pairs={{0,2},{2,0},{4,6},{6,4},{1,3},{3,1},{5,7},{7,5},{8,10},{10,8},{12,... | collective-permute-start | bytes 589832 | tf_op jit(solution)/shard_map/ppermute | solution.py:42
  66.9 7.7 %collective-permute-start.3 = (bf16[128,768]{1,0:T(8,128)(2,1)S(1)}, bf16[128,768]{1,0:T(8,128)(2,1)S(1)}, u32[]{:S(2)}, u32[]{:S(2)}) collective-permute-start(bf16[128,768]{1,0:T(8,128)(2,1)S(1)} %pad_maximum_fusion.14), channel_id=1, source_target_pairs={{0,4},{2,6},{4,0},{6,2},{1,5},{3,7},{5,1},{7,3},{8,12},{10,14},{12... | collective-permute-start | bytes 589832 | tf_op jit(solution)/shard_map/ppermute | solution.py:42
  67.0 11.3 %collective-permute-start.4 = (bf16[128,768]{1,0:T(8,128)(2,1)S(1)}, bf16[128,768]{1,0:T(8,128)(2,1)S(1)}, u32[]{:S(2)}, u32[]{:S(2)}) collective-permute-start(bf16[128,768]{1,0:T(8,128)(2,1)S(1)} %pad_maximum_fusion.14), channel_id=1, source_target_pairs={{0,6},{2,4},{4,2},{6,0},{1,7},{3,5},{5,3},{7,1},{8,14},{10,12},{12... | collective-permute-start | bytes 589832 | tf_op jit(solution)/shard_map/ppermute | solution.py:42
  73.5 17.3 %copy-start.10 = (bf16[1,288,1152]{2,1,0:T(8,128)(2,1)S(1)}, bf16[1,288,1152]{2,1,0:T(8,128)(2,1)}, u32[]{:S(2)}) copy-start(bf16[1,288,1152]{2,1,0:T(8,128)(2,1)} %copy-done.9) | copy-start | bytes 1990660
  73.5 17.3 %copy-start.12 = (bf16[1,288,1152]{2,1,0:T(8,128)(2,1)S(1)}, bf16[1,288,1152]{2,1,0:T(8,128)(2,1)}, u32[]{:S(2)}) copy-start(bf16[1,288,1152]{2,1,0:T(8,128)(2,1)} %copy-done.11) | copy-start | bytes 1990660
  80.0 25.9 %copy-start.5 = (bf16[768,384]{1,0:T(8,128)(2,1)}, bf16[768,384]{1,0:T(8,128)(2,1)S(1)}, u32[]{:S(2)}) copy-start(bf16[768,384]{1,0:T(8,128)(2,1)S(1)} %get-tuple-element.73) | copy-start | bytes 1769476
  94.2 60.6 %collective-permute-start.7 = (bf16[2,2,288,1152]{3,2,1,0:T(8,128)(2,1)}, bf16[2,2,288,1152]{3,2,1,0:T(8,128)(2,1)}, u32[]{:S(2)}, u32[]{:S(2)}) collective-permute-start(bf16[2,2,288,1152]{3,2,1,0:T(8,128)(2,1)} %pad_maximum_fusion.2), channel_id=1, source_target_pairs={{0,1},{1,0},{2,3},{3,2},{4,5},{5,4},{6,7},{7,6},{8,9},{9,8},{10,11... | collective-permute-start | bytes 7962632 | tf_op jit(solution)/shard_map/ppermute | solution.py:42
  101.6 18.8 %all-to-all-start.1 = ((bf16[4,512,256]{2,1,0:T(8,128)(2,1)}), bf16[4,512,256]{2,1,0:T(8,128)(2,1)}, u32[]{:S(2)}, u32[]{:S(2)}) async-start(bf16[4,512,256]{2,1,0:T(8,128)(2,1)} %bitcast.218), calls=%async_computation.1 | async-start | bytes 2097152 | tf_op jit(solution)/shard_map/all_to_all | solution.py:86
  107.0 38.0 %copy-start.20 = (bf16[2,64,768]{2,1,0:T(8,128)(2,1)S(1)}, bf16[2,64,768]{2,1,0:T(8,128)(2,1)}, u32[]{:S(2)}) copy-start(bf16[2,64,768]{2,1,0:T(8,128)(2,1)} %param.38) | copy-start | bytes 589828
  141.3 12.4 %all-to-all-start.2 = ((bf16[16,64,128]{2,1,0:T(8,128)(2,1)}), bf16[16,64,128]{2,1,0:T(8,128)(2,1)S(1)}, u32[]{:S(2)}, u32[]{:S(2)}) async-start(bf16[16,64,128]{2,1,0:T(8,128)(2,1)} %get-tuple-element.20), calls=%async_computation.2 | async-start | bytes 524288 | tf_op jit(solution)/shard_map/all_to_all | solution.py:86
  145.7 32.3 %collective-permute-start.15 = (bf16[64,768]{1,0:T(8,128)(2,1)}, bf16[64,768]{1,0:T(8,128)(2,1)}, u32[]{:S(2)}, u32[]{:S(2)}) collective-permute-start(bf16[64,768]{1,0:T(8,128)(2,1)} %select_bitcast_fusion.6), channel_id=1, source_target_pairs={{0,8},{8,0},{1,9},{9,1},{2,10},{10,2},{3,11},{11,3},{4,12},{12,4},... | collective-permute-start | bytes 294920 | tf_op jit(solution)/shard_map/ppermute | solution.py:42
  158.5 28.3 %copy-start.41 = (f32[128]{0:T(128)}, f32[128]{0:T(128)S(1)}, u32[]{:S(2)}) copy-start(f32[128]{0:T(128)S(1)} %broadcast_multiply_fusion.5) | copy-start | bytes 1540
  158.7 28.1 %copy-start.46 = (f32[128]{0:T(128)}, f32[128]{0:T(128)S(1)}, u32[]{:S(2)}) copy-start(f32[128]{0:T(128)S(1)} %add_rsqrt_fusion.1) | copy-start | bytes 1540
  158.9 8.8 %collective-permute-start.10 = (bf16[128,768]{1,0:T(8,128)(2,1)S(1)}, bf16[128,768]{1,0:T(8,128)(2,1)S(1)}, u32[]{:S(2)}, u32[]{:S(2)}) collective-permute-start(bf16[128,768]{1,0:T(8,128)(2,1)S(1)} %fusion.44), channel_id=1, source_target_pairs={{0,6},{2,4},{4,2},{6,0},{1,7},{3,5},{5,3},{7,1},{8,14},{10,12},{12... | collective-permute-start | bytes 589832 | tf_op jit(solution)/shard_map/ppermute | solution.py:42
  159.0 10.7 %collective-permute-start.9 = (bf16[128,768]{1,0:T(8,128)(2,1)S(1)}, bf16[128,768]{1,0:T(8,128)(2,1)S(1)}, u32[]{:S(2)}, u32[]{:S(2)}) collective-permute-start(bf16[128,768]{1,0:T(8,128)(2,1)S(1)} %fusion.44), channel_id=1, source_target_pairs={{0,4},{2,6},{4,0},{6,2},{1,5},{3,7},{5,1},{7,3},{8,12},{10,14},{12... | collective-permute-start | bytes 589832 | tf_op jit(solution)/shard_map/ppermute | solution.py:42
  159.7 10.5 %collective-permute-start.8 = (bf16[128,768]{1,0:T(8,128)(2,1)S(1)}, bf16[128,768]{1,0:T(8,128)(2,1)S(1)}, u32[]{:S(2)}, u32[]{:S(2)}) collective-permute-start(bf16[128,768]{1,0:T(8,128)(2,1)S(1)} %fusion.44), channel_id=1, source_target_pairs={{0,2},{2,0},{4,6},{6,4},{1,3},{3,1},{5,7},{7,5},{8,10},{10,8},{12,... | collective-permute-start | bytes 589832 | tf_op jit(solution)/shard_map/ppermute | solution.py:42
  174.5 11.1 %collective-permute-start.11 = (bf16[128,768]{1,0:T(8,128)(2,1)S(1)}, bf16[128,768]{1,0:T(8,128)(2,1)S(1)}, u32[]{:S(2)}, u32[]{:S(2)}) collective-permute-start(bf16[128,768]{1,0:T(8,128)(2,1)S(1)} %get-tuple-element.82), channel_id=1, source_target_pairs={{0,2},{2,0},{4,6},{6,4},{1,3},{3,1},{5,7},{7,5},{8,10},{10,8},{12,... | collective-permute-start | bytes 589832 | tf_op jit(solution)/shard_map/ppermute | solution.py:42
  175.4 10.2 %collective-permute-start.13 = (bf16[128,768]{1,0:T(8,128)(2,1)S(1)}, bf16[128,768]{1,0:T(8,128)(2,1)S(1)}, u32[]{:S(2)}, u32[]{:S(2)}) collective-permute-start(bf16[128,768]{1,0:T(8,128)(2,1)S(1)} %get-tuple-element.83), channel_id=1, source_target_pairs={{0,6},{2,4},{4,2},{6,0},{1,7},{3,5},{5,3},{7,1},{8,14},{10,12},{12... | collective-permute-start | bytes 589832 | tf_op jit(solution)/shard_map/ppermute | solution.py:42
  176.0 10.8 %collective-permute-start.12 = (bf16[128,768]{1,0:T(8,128)(2,1)S(1)}, bf16[128,768]{1,0:T(8,128)(2,1)S(1)}, u32[]{:S(2)}, u32[]{:S(2)}) collective-permute-start(bf16[128,768]{1,0:T(8,128)(2,1)S(1)} %get-tuple-element.84), channel_id=1, source_target_pairs={{0,4},{2,6},{4,0},{6,2},{1,5},{3,7},{5,1},{7,3},{8,12},{10,14},{12... | collective-permute-start | bytes 589832 | tf_op jit(solution)/shard_map/ppermute | solution.py:42
  187.8 15.3 %copy-start.34 = (bf16[128,768]{1,0:T(8,128)(2,1)}, bf16[128,768]{1,0:T(8,128)(2,1)S(1)}, u32[]{:S(2)}) copy-start(bf16[128,768]{1,0:T(8,128)(2,1)S(1)} %get-tuple-element.52) | copy-start | bytes 589828
  187.8 8.8 %collective-permute-start.18 = (bf16[128,768]{1,0:T(8,128)(2,1)S(1)}, bf16[128,768]{1,0:T(8,128)(2,1)S(1)}, u32[]{:S(2)}, u32[]{:S(2)}) collective-permute-start(bf16[128,768]{1,0:T(8,128)(2,1)S(1)} %get-tuple-element.52), channel_id=1, source_target_pairs={{0,6},{2,4},{4,2},{6,0},{1,7},{3,5},{5,3},{7,1},{8,14},{10,12},{12... | collective-permute-start | bytes 589832 | tf_op jit(solution)/shard_map/ppermute | solution.py:42
  188.4 9.7 %collective-permute-start.17 = (bf16[128,768]{1,0:T(8,128)(2,1)S(1)}, bf16[128,768]{1,0:T(8,128)(2,1)S(1)}, u32[]{:S(2)}, u32[]{:S(2)}) collective-permute-start(bf16[128,768]{1,0:T(8,128)(2,1)S(1)} %get-tuple-element.52), channel_id=1, source_target_pairs={{0,4},{2,6},{4,0},{6,2},{1,5},{3,7},{5,1},{7,3},{8,12},{10,14},{12... | collective-permute-start | bytes 589832 | tf_op jit(solution)/shard_map/ppermute | solution.py:42
  190.2 8.6 %collective-permute-start.16 = (bf16[128,768]{1,0:T(8,128)(2,1)S(1)}, bf16[128,768]{1,0:T(8,128)(2,1)}, u32[]{:S(2)}, u32[]{:S(2)}) collective-permute-start(bf16[128,768]{1,0:T(8,128)(2,1)S(1)} %get-tuple-element.52), channel_id=1, source_target_pairs={{0,2},{2,0},{4,6},{6,4},{1,3},{3,1},{5,7},{7,5},{8,10},{10,8},{12,... | collective-permute-start | bytes 589832 | tf_op jit(solution)/shard_map/ppermute | solution.py:42
  206.8 21.0 %collective-permute-start.19 = (bf16[128,768]{1,0:T(8,128)(2,1)}, bf16[128,768]{1,0:T(8,128)(2,1)S(1)}, u32[]{:S(2)}, u32[]{:S(2)}) collective-permute-start(bf16[128,768]{1,0:T(8,128)(2,1)} %get-tuple-element.79), channel_id=1, source_target_pairs={{0,2},{2,0},{4,6},{6,4},{1,3},{3,1},{5,7},{7,5},{8,10},{10,8},{12,... | collective-permute-start | bytes 589832 | tf_op jit(solution)/shard_map/ppermute | solution.py:42
  207.9 20.0 %collective-permute-start.21 = (bf16[128,768]{1,0:T(8,128)(2,1)}, bf16[128,768]{1,0:T(8,128)(2,1)}, u32[]{:S(2)}, u32[]{:S(2)}) collective-permute-start(bf16[128,768]{1,0:T(8,128)(2,1)} %get-tuple-element.80), channel_id=1, source_target_pairs={{0,6},{2,4},{4,2},{6,0},{1,7},{3,5},{5,3},{7,1},{8,14},{10,12},{12... | collective-permute-start | bytes 589832 | tf_op jit(solution)/shard_map/ppermute | solution.py:42
  208.4 19.5 %collective-permute-start.20 = (bf16[128,768]{1,0:T(8,128)(2,1)}, bf16[128,768]{1,0:T(8,128)(2,1)}, u32[]{:S(2)}, u32[]{:S(2)}) collective-permute-start(bf16[128,768]{1,0:T(8,128)(2,1)} %get-tuple-element.81), channel_id=1, source_target_pairs={{0,4},{2,6},{4,0},{6,2},{1,5},{3,7},{5,1},{7,3},{8,12},{10,14},{12... | collective-permute-start | bytes 589832 | tf_op jit(solution)/shard_map/ppermute | solution.py:42
  213.2 108.3 %collective-permute-start.30 = (bf16[2,2,96,768]{3,2,0,1:T(8,128)(2,1)}, bf16[2,2,96,768]{3,2,0,1:T(8,128)(2,1)}, u32[]{:S(2)}, u32[]{:S(2)}) collective-permute-start(bf16[2,2,96,768]{3,2,0,1:T(8,128)(2,1)} %fusion.23), channel_id=1, source_target_pairs={{0,1},{1,0},{2,3},{3,2},{4,5},{5,4},{6,7},{7,6},{8,9},{9,8},{10,11... | collective-permute-start | bytes 1769480 | tf_op jit(solution)/shard_map/ppermute | solution.py:42
  227.8 56.3 %collective-permute-start.27 = (bf16[2,2,4,24,1536]{4,3,2,1,0:T(8,128)(2,1)}, bf16[2,2,4,24,1536]{4,3,2,1,0:T(8,128)(2,1)}, u32[]{:S(2)}, u32[]{:S(2)}) collective-permute-start(bf16[2,2,4,24,1536]{4,3,2,1,0:T(8,128)(2,1)} %fusion.10), channel_id=1, source_target_pairs={{0,1},{1,0},{2,3},{3,2},{4,5},{5,4},{6,7},{7,6},{8,9},{9,8},{10,11... | collective-permute-start | bytes 3538952 | tf_op jit(solution)/shard_map/ppermute | solution.py:42
  232.1 13.0 %collective-permute-start.14 = (bf16[64,768]{1,0:T(8,128)(2,1)}, bf16[64,768]{1,0:T(8,128)(2,1)}, u32[]{:S(2)}, u32[]{:S(2)}) collective-permute-start(bf16[64,768]{1,0:T(8,128)(2,1)} %broadcast_select_fusion.8), channel_id=1, source_target_pairs={{0,8},{8,0},{1,9},{9,1},{2,10},{10,2},{3,11},{11,3},{4,12},{12,4},... | collective-permute-start | bytes 294920 | tf_op jit(solution)/shard_map/ppermute | solution.py:42
  239.6 11.2 %all-to-all-start.4 = ((bf16[16,64,128]{2,1,0:T(8,128)(2,1)}), bf16[16,64,128]{2,1,0:T(8,128)(2,1)S(1)}, u32[]{:S(2)}, u32[]{:S(2)}) async-start(bf16[16,64,128]{2,1,0:T(8,128)(2,1)} %bitcast.228), calls=%async_computation.4 | async-start | bytes 524288 | tf_op jit(solution)/shard_map/all_to_all | solution.py:86
  280.6 18.0 %all-to-all-start.5 = ((bf16[4,512,256]{1,2,0:T(8,128)(2,1)}), bf16[4,512,256]{1,2,0:T(8,128)(2,1)S(1)}, u32[]{:S(2)}, u32[]{:S(2)}) async-start(bf16[4,512,256]{1,2,0:T(8,128)(2,1)} %copy.212), calls=%async_computation.5 | async-start | bytes 2097152 | tf_op jit(solution)/shard_map/all_to_all | solution.py:86
  289.8 28.7 %collective-permute-start.28 = (bf16[2,4,24,1536]{3,2,1,0:T(8,128)(2,1)}, bf16[2,4,24,1536]{3,2,1,0:T(8,128)(2,1)}, u32[]{:S(2)}, u32[]{:S(2)}) collective-permute-start(bf16[2,4,24,1536]{3,2,1,0:T(8,128)(2,1)} %fusion.22), channel_id=1, source_target_pairs={{0,8},{8,0},{1,9},{9,1},{2,10},{10,2},{3,11},{11,3},{4,12},{12,4},... | collective-permute-start | bytes 1769480 | tf_op jit(solution)/shard_map/ppermute | solution.py:42
  314.9 18.2 %collective-permute-start.26 = (bf16[16,24,1536]{2,1,0:T(8,128)(2,1)}, bf16[16,24,1536]{2,1,0:T(8,128)(2,1)}, u32[]{:S(2)}, u32[]{:S(2)}) collective-permute-start(bf16[16,24,1536]{2,1,0:T(8,128)(2,1)} %fusion.9), channel_id=1, source_target_pairs={{0,1},{1,0},{2,3},{3,2},{4,5},{5,4},{6,7},{7,6},{8,9},{9,8},{10,11... | collective-permute-start | bytes 3538952 | tf_op jit(solution)/shard_map/ppermute | solution.py:42
  319.9 9.0 %collective-permute-start.29 = (bf16[4,24,1536]{2,1,0:T(8,128)(2,1)S(1)}, bf16[4,24,1536]{2,1,0:T(8,128)(2,1)S(1)}, u32[]{:S(2)}, u32[]{:S(2)}) collective-permute-start(bf16[4,24,1536]{2,1,0:T(8,128)(2,1)S(1)} %fusion.45), channel_id=1, source_target_pairs={{0,16},{16,0},{1,17},{17,1},{2,18},{18,2},{3,19},{19,3},{4,20},{20... | collective-permute-start | bytes 884744 | tf_op jit(solution)/shard_map/ppermute | solution.py:42
  322.8 21.1 %collective-permute-start.31 = (bf16[2,96,768]{2,1,0:T(8,128)(2,1)S(1)}, bf16[2,96,768]{2,1,0:T(8,128)(2,1)}, u32[]{:S(2)}, u32[]{:S(2)}) collective-permute-start(bf16[2,96,768]{2,1,0:T(8,128)(2,1)S(1)} %fusion.46), channel_id=1, source_target_pairs={{0,8},{8,0},{1,9},{9,1},{2,10},{10,2},{3,11},{11,3},{4,12},{12,4},... | collective-permute-start | bytes 884744 | tf_op jit(solution)/shard_map/ppermute | solution.py:42
  329.7 9.4 %all-to-all-start.7 = ((bf16[4,24,1536]{2,1,0:T(8,128)(2,1)}), bf16[4,24,1536]{2,1,0:T(8,128)(2,1)S(1)}, u32[]{:S(2)}, u32[]{:S(2)}) async-start(bf16[4,24,1536]{2,1,0:T(8,128)(2,1)} %fusion.24), calls=%async_computation.7 | async-start | bytes 589824 | tf_op jit(solution)/shard_map/all_to_all | solution.py:86
  339.2 46.4 %all-to-all-start.6 = ((bf16[16,24,1536]{2,1,0:T(8,128)(2,1)}), bf16[16,24,1536]{2,1,0:T(8,128)(2,1)S(1)}, u32[]{:S(2)}, u32[]{:S(2)}) async-start(bf16[16,24,1536]{2,1,0:T(8,128)(2,1)} %fusion.1), calls=%async_computation.6 | async-start | bytes 2359296 | tf_op jit(solution)/shard_map/all_to_all | solution.py:86
  346.3 27.5 %copy-start.8 = (f32[128,768]{1,0:T(8,128)S(1)}, f32[128,768]{1,0:T(8,128)}, u32[]{:S(2)}) copy-start(f32[128,768]{1,0:T(8,128)} %copy-done.7) | copy-start | bytes 1179652
  346.4 14.8 %collective-permute-start.22 = (bf16[128,768]{1,0:T(8,128)(2,1)S(1)}, bf16[128,768]{1,0:T(8,128)(2,1)S(1)}, u32[]{:S(2)}, u32[]{:S(2)}) collective-permute-start(bf16[128,768]{1,0:T(8,128)(2,1)S(1)} %get-tuple-element.76), channel_id=1, source_target_pairs={{0,2},{2,0},{4,6},{6,4},{1,3},{3,1},{5,7},{7,5},{8,10},{10,8},{12,... | collective-permute-start | bytes 589832 | tf_op jit(solution)/shard_map/ppermute | solution.py:42
  348.5 22.3 %collective-permute-start.24 = (bf16[128,768]{1,0:T(8,128)(2,1)S(1)}, bf16[128,768]{1,0:T(8,128)(2,1)S(1)}, u32[]{:S(2)}, u32[]{:S(2)}) collective-permute-start(bf16[128,768]{1,0:T(8,128)(2,1)S(1)} %get-tuple-element.77), channel_id=1, source_target_pairs={{0,6},{2,4},{4,2},{6,0},{1,7},{3,5},{5,3},{7,1},{8,14},{10,12},{12... | collective-permute-start | bytes 589832 | tf_op jit(solution)/shard_map/ppermute | solution.py:42
  349.9 23.9 %collective-permute-start.23 = (bf16[128,768]{1,0:T(8,128)(2,1)S(1)}, bf16[128,768]{1,0:T(8,128)(2,1)S(1)}, u32[]{:S(2)}, u32[]{:S(2)}) collective-permute-start(bf16[128,768]{1,0:T(8,128)(2,1)S(1)} %get-tuple-element.78), channel_id=1, source_target_pairs={{0,4},{2,6},{4,0},{6,2},{1,5},{3,7},{5,1},{7,3},{8,12},{10,14},{12... | collective-permute-start | bytes 589832 | tf_op jit(solution)/shard_map/ppermute | solution.py:42
  350.0 27.5 %collective-permute-start.32 = (bf16[96,768]{1,0:T(8,128)(2,1)S(1)}, bf16[96,768]{1,0:T(8,128)(2,1)S(1)}, u32[]{:S(2)}, u32[]{:S(2)}) collective-permute-start(bf16[96,768]{1,0:T(8,128)(2,1)S(1)} %fusion.49), channel_id=1, source_target_pairs={{0,16},{16,0},{1,17},{17,1},{2,18},{18,2},{3,19},{19,3},{4,20},{20... | collective-permute-start | bytes 442376 | tf_op jit(solution)/shard_map/ppermute | solution.py:42
  374.0 7.4 %collective-permute-start.25 = (bf16[64,768]{1,0:T(8,128)(2,1)S(1)}, bf16[64,768]{1,0:T(8,128)(2,1)S(1)}, u32[]{:S(2)}, u32[]{:S(2)}) collective-permute-start(bf16[64,768]{1,0:T(8,128)(2,1)S(1)} %broadcast_select_fusion.6), channel_id=1, source_target_pairs={{0,8},{8,0},{1,9},{9,1},{2,10},{10,2},{3,11},{11,3},{4,12},{12,4},... | collective-permute-start | bytes 294920 | tf_op jit(solution)/shard_map/ppermute | solution.py:42
  (56 other events, 272.5 us)

commit v2 on v1

v2 whole, which is shorter than its diff:
```python
import functools
import math

import jax
import jax.numpy as jnp
import numpy as np
from jax import lax
from jax.experimental import pallas as pl
from jax.experimental.pallas import tpu as pltpu
from jax.sharding import Mesh
from jax.sharding import PartitionSpec as P

HEADS = 12
HEAD_DIM = 64
FEATS = 4
SLOTS = 4
PACK = 4 * HEAD_DIM
BLOCK = 256

norm_epsilon = 1e-12
masked_value = -1e30
f32 = jnp.float32
bf16 = jnp.bfloat16


def alibi_slopes(head_total):
    nearest = 2 ** int(math.floor(math.log2(head_total)))
    slopes = [2.0 ** (-8.0 * (index + 1) / nearest) for index in range(nearest)]
    extra = [2.0 ** (-8.0 * (index + 1) / (2 * nearest)) for index in range(2 * nearest)]
    slopes = slopes + extra[0::2][: head_total - nearest]
    return np.array(slopes, dtype=np.float32)


def dot(left, right, left_dim=1, right_dim=0):
    return lax.dot_general(
        left, right, (((left_dim,), (right_dim,)), ((), ())), preferred_element_type=f32
    )


def swap(values, axis, step=1):
    size = lax.axis_size(axis)
    return lax.ppermute(values, axis, [(i, i ^ step) for i in range(size)])


def in_order(parts, me):
    if len(parts) == 2:
        mine, other = parts
        return jnp.stack([jnp.where(me == 0, mine, other), jnp.where(me == 0, other, mine)])
    return jnp.take(jnp.stack(parts), jnp.arange(len(parts)) ^ me, axis=0)


def gather_axis(values, axis):
    size = lax.axis_size(axis)
    parts = [values] + [swap(values, axis, k) for k in range(1, size)]
    return in_order(parts, lax.axis_index(axis))


def scatter_axis(values, axis):
    size = lax.axis_size(axis)
    me = lax.axis_index(axis)

    def pick(k):
        if size == 2:
            return jnp.where((me ^ k) == 0, values[0], values[1])
        return lax.dynamic_index_in_dim(values, me ^ k, 0, keepdims=False)

    total = pick(0)
    for k in range(1, size):
        total = total + swap(pick(k).astype(bf16), axis, k).astype(f32)
    return total


def gather_feats(values):
    return [values] + [swap(values, "f", k) for k in range(1, FEATS)]


def scatter_feats(values):
    rows = values.shape[0] // FEATS
    total = values[:rows]
    for k in range(1, FEATS):
        total = total + swap(values[k * rows : (k + 1) * rows].astype(bf16), "f", k).astype(f32)
    return total


def all_to_all(values, axes):
    return lax.all_to_all(values, axes, split_axis=0, concat_axis=0, tiled=True)


def place(unit, side, feat, core, rows):
    return (((unit * 2 + side) * FEATS + feat) * 2 + core) * rows


def unpack_qkv(qkv_ref, nat_s, feat, rows):
    slots, lines, _ = qkv_ref.shape
    group = 2 * FEATS * rows
    nothing = jnp.zeros((rows, HEAD_DIM), bf16)
    for slot in range(slots):
        for k in range(FEATS):
            for side in range(2):
                here = pl.ds(
                    pl.multiple_of(place(slot // 2, side, feat ^ k, slot % 2, rows), rows), rows
                )
                start = (2 * k + side) * rows
                nat_s[here, :128] = qkv_ref[slot, start : start + rows, :]
                start = group + (2 * (k % 2) + side) * rows
                lanes = slice((k // 2) * HEAD_DIM, (k // 2 + 1) * HEAD_DIM)
                value = qkv_ref[slot, start : start + rows, lanes]
                nat_s[here, 128:] = jnp.concatenate([value, nothing], axis=1)


def turn(values):
    return jnp.transpose(values.astype(f32))


def spread_codes(code_ref, code_s):
    for start in range(0, code_ref.shape[1], 128):
        row = code_ref[:, start : start + 128]
        code_s[start : start + 128, :] = jnp.transpose(jnp.broadcast_to(row, (128, 128)))


def distance_tile():
    rows = lax.broadcasted_iota(jnp.int32, (BLOCK, BLOCK), 0)
    cols = lax.broadcasted_iota(jnp.int32, (BLOCK, BLOCK), 1)
    return (cols - rows).astype(f32)


def span(index):
    return pl.ds(pl.multiple_of(index * BLOCK, BLOCK), BLOCK)


def even_range(low, high, first, last):
    low, high = jnp.maximum(low, first), jnp.minimum(high, last)
    high = jnp.maximum(low, high)
    odd = (high - low) % 2
    up = odd * (high < last).astype(jnp.int32)
    low = low - (odd - up)
    return low, (high + up - low) // 2


def score_tile(qk_part, qz_part, code_part, seg_part, offset, slope):
    distance = distance_tile() + offset
    scores = dot(qk_part, qz_part) - slope * jnp.abs(distance)
    codes = jnp.concatenate([code_part] * (BLOCK // 128), axis=1)
    allowed = (codes == seg_part) | (distance == 0.0)
    return jnp.where(allowed, scores, masked_value)


def attend_kernel(
    table_ref, slope_ref, qkv_ref, seg_ref, code_ref, out_ref, lse_ref, ot_ref,
    nat_s, qz_s, vt_s, o_s, code_s,
):
    slope = slope_ref[0, 0]
    units = qkv_ref.shape[0] // 2
    rows = out_ref.shape[1]
    unpack_qkv(qkv_ref, nat_s, table_ref[2, 0], rows)
    spread_codes(code_ref, code_s)
    length = nat_s.shape[0]
    blocks = length // BLOCK
    qz_s[:HEAD_DIM, :] = jnp.zeros((HEAD_DIM, length), bf16)
    for start in range(0, length, 128):
        here = slice(start, start + 128)
        qk_turned = turn(nat_s[here, :128])
        qz_s[HEAD_DIM:, here] = (qk_turned[:HEAD_DIM] * (HEAD_DIM**-0.5)).astype(bf16)
        vt_s[:, here] = turn(nat_s[here, 128:])[:HEAD_DIM].astype(bf16)
    if qkv_ref.shape[0] > SLOTS:
        o_s[...] = jnp.zeros_like(o_s)
        ot_ref[...] = jnp.zeros_like(ot_ref)
        lse_ref[...] = jnp.zeros_like(lse_ref)

    def query_step(i, carry):
        here = span(i)
        qz_part = qz_s[:, here]
        seg_part = seg_ref[:, here]
        low, pairs = even_range(table_ref[0, i], table_ref[1, i], 0, blocks)

        def key_step(pair, state):
            top, total, mixed = state
            keys = [low + 2 * pair, low + 2 * pair + 1]
            scores = [
                score_tile(
                    nat_s[span(j), :128], qz_part, code_s[span(j), :], seg_part,
                    ((i - j) * BLOCK).astype(f32), slope,
                )
                for j in keys
            ]
            tops = [jnp.max(values, axis=0, keepdims=True) for values in scores]
            top_new = jnp.maximum(top, jnp.maximum(tops[0], tops[1]))
            factor = jnp.exp(top - top_new)
            total, mixed = total * factor, mixed * factor
            for j, values in zip(keys, scores):
                probs = jnp.exp(values - top_new)
                total = total + jnp.sum(probs, axis=0, keepdims=True)
                mixed = mixed + dot(vt_s[:, span(j)], probs.astype(bf16))
            return top_new, total, mixed

        top, total, mixed = lax.fori_loop(
            0,
            pairs,
            key_step,
            (
                jnp.full((1, BLOCK), masked_value, f32),
                jnp.zeros((1, BLOCK), f32),
                jnp.zeros((HEAD_DIM, BLOCK), f32),
            ),
        )
        mixed = mixed / total
        ot_ref[:, here] = mixed
        lse_ref[:, here] = top + jnp.log(total)
        o_s[here, :] = jnp.transpose(mixed)
        return carry

    lax.fori_loop(table_ref[2, 1], table_ref[2, 2], query_step, 0)
    for unit in range(units):
        for feat in range(FEATS):
            for core in range(2):
                starts = [place(unit, side, feat, core, rows) for side in range(2)]
                sides = [o_s[start : start + rows, :] for start in starts]
                out_ref[(unit * FEATS + feat) * 2 + core] = jnp.concatenate(sides, axis=1).astype(bf16)


def attend_back_kernel(
    table_ref, slope_ref, qkv_ref, dout_ref, ot_ref, lse_ref, seg_ref, code_ref, dqkv_ref,
    nat_s, qz_s, kt_s, do_s, dz_s, code_s, delta_s, dqt_s, dq_s, dk_s, dv_s,
):
    slope = slope_ref[0, 0]
    feat_self = table_ref[2, 0]
    first, last = table_ref[2, 1], table_ref[2, 2]
    slots, rows = qkv_ref.shape[0], dout_ref.shape[1]
    group = 2 * FEATS * rows
    length = nat_s.shape[0]
    blocks = length // BLOCK
    unpack_qkv(qkv_ref, nat_s, feat_self, rows)
    spread_codes(code_ref, code_s)
    for unit in range(slots // 2):
        for feat in range(FEATS):
            for core in range(2):
                piece = dout_ref[(unit * FEATS + feat) * 2 + core]
                for side in range(2):
                    start = place(unit, side, feat, core, rows)
                    do_s[start : start + rows, :] = piece[:, side * HEAD_DIM : (side + 1) * HEAD_DIM]
    zero_half = jnp.zeros((HEAD_DIM, length), bf16)
    qz_s[:HEAD_DIM, :] = zero_half
    dz_s[HEAD_DIM:, :] = zero_half
    dqt_s[...] = jnp.zeros_like(dqt_s)
    for start in range(0, length, 128):
        here = slice(start, start + 128)
        qk_turned = turn(nat_s[here, :128])
        qz_s[HEAD_DIM:, here] = (qk_turned[:HEAD_DIM] * (HEAD_DIM**-0.5)).astype(bf16)
        kt_s[:, here] = qk_turned[HEAD_DIM:].astype(bf16)
        do_turned = turn(do_s[here, :])
        dz_s[:HEAD_DIM, here] = do_turned.astype(bf16)
        delta_s[:, here] = jnp.sum(do_turned * ot_ref[:, here], axis=0, keepdims=True)

    def key_step(j, carry):
        there = span(j)
        qk_part, vx_part = nat_s[there, :128], nat_s[there, 128:]
        code_part, kt_part = code_s[there, :], kt_s[:, there]
        low, pairs = even_range(table_ref[0, j], table_ref[1, j], first, last)

        def query_step(pair, state):
            dk, dv = state
            for i in (low + 2 * pair, low + 2 * pair + 1):
                here = span(i)
                scores = score_tile(
                    qk_part, qz_s[:, here], code_part, seg_ref[:, here],
                    ((i - j) * BLOCK).astype(f32), slope,
                )
                probs = jnp.exp(scores - lse_ref[:, here])
                back_probs = dot(vx_part, dz_s[:, here])
                back_scores = (probs * (back_probs - delta_s[:, here])).astype(bf16)
                dv = dv + dot(probs.astype(bf16), do_s[here, :])
                dk = dk + dot(back_scores, nat_s[here, :HEAD_DIM])
                dqt_s[:, here] += dot(kt_part, back_scores)
            return dk, dv

        zero = jnp.zeros((BLOCK, HEAD_DIM), f32)
        dk, dv = lax.fori_loop(0, pairs, query_step, (zero, zero))
        dk_s[there, :] = dk
        dv_s[there, :] = dv
        return carry

    lax.fori_loop(0, blocks, key_step, 0)
    for start in range(0, length, 128):
        here = slice(start, start + 128)
        dq_s[here, :] = jnp.transpose(dqt_s[:, here])
    for slot in range(slots):
        for k in range(FEATS):
            for side in range(2):
                here = pl.ds(
                    pl.multiple_of(place(slot // 2, side, feat_self ^ k, slot % 2, rows), rows), rows
                )
                start = (2 * k + side) * rows
                both = jnp.concatenate([dq_s[here, :], dk_s[here, :]], axis=1) * (HEAD_DIM**-0.5)
                dqkv_ref[slot, start : start + rows, :] = both.astype(bf16)
                start = group + (2 * (k % 2) + side) * rows
                lanes = slice((k // 2) * HEAD_DIM, (k // 2 + 1) * HEAD_DIM)
                dqkv_ref[slot, start : start + rows, lanes] = dv_s[here, :].astype(bf16)


def attend(table, slope, qkv, seg_row, code_row):
    slots, length = qkv.shape[0], seg_row.shape[1]
    rows = length // (slots * FEATS * 2)
    vmem = pl.BlockSpec(memory_space=pltpu.VMEM)
    smem = pl.BlockSpec(memory_space=pltpu.SMEM)
    return pl.pallas_call(
        attend_kernel,
        out_shape=(
            jax.ShapeDtypeStruct((slots * FEATS, rows, 2 * HEAD_DIM), bf16),
            jax.ShapeDtypeStruct((1, length), f32),
            jax.ShapeDtypeStruct((HEAD_DIM, length), f32),
        ),
        in_specs=[smem, smem, vmem, vmem, vmem],
        out_specs=(vmem, vmem, vmem),
        scratch_shapes=[
            pltpu.VMEM((length, PACK), bf16),
            pltpu.VMEM((2 * HEAD_DIM, length), bf16),
            pltpu.VMEM((HEAD_DIM, length), bf16),
            pltpu.VMEM((length, HEAD_DIM), f32),
            pltpu.VMEM((length, 128), f32),
        ],
        name="attend",
    )(table, slope, qkv, seg_row, code_row)


def attend_back(table, slope, qkv, dout, o_turned, lse, seg_row, code_row):
    slots, length = qkv.shape[0], seg_row.shape[1]
    rows = length // (slots * FEATS * 2)
    vmem = pl.BlockSpec(memory_space=pltpu.VMEM)
    smem = pl.BlockSpec(memory_space=pltpu.SMEM)
    return pl.pallas_call(
        attend_back_kernel,
        out_shape=jax.ShapeDtypeStruct(qkv.shape, bf16),
        in_specs=[smem, smem] + [vmem] * 6,
        out_specs=vmem,
        scratch_shapes=[
            pltpu.VMEM((length, PACK), bf16),
            pltpu.VMEM((2 * HEAD_DIM, length), bf16),
            pltpu.VMEM((HEAD_DIM, length), bf16),
            pltpu.VMEM((length, HEAD_DIM), bf16),
            pltpu.VMEM((2 * HEAD_DIM, length), bf16),
            pltpu.VMEM((length, 128), f32),
            pltpu.VMEM((1, length), f32),
            pltpu.VMEM((HEAD_DIM, length), f32),
            pltpu.VMEM((length, HEAD_DIM), f32),
            pltpu.VMEM((length, HEAD_DIM), f32),
            pltpu.VMEM((length, HEAD_DIM), f32),
        ],
        name="attend_back",
    )(table, slope, qkv, dout, o_turned, lse, seg_row, code_row)


def norm_forward(values, gain, shift):
    centred = values - jnp.mean(values, axis=-1, keepdims=True)
    inverse = lax.rsqrt(jnp.mean(centred * centred, axis=-1, keepdims=True) + norm_epsilon)
    normed = centred * inverse
    return normed * gain + shift, normed, inverse


def norm_backward(upstream, normed, inverse, gain):
    scaled = upstream * gain
    adjusted = (
        scaled
        - jnp.mean(scaled, axis=-1, keepdims=True)
        - normed * jnp.mean(scaled * normed, axis=-1, keepdims=True)
    )
    sums = [jnp.sum(upstream * normed, axis=0, keepdims=True), jnp.sum(upstream, axis=0, keepdims=True)]
    return adjusted * inverse, sums[0], sums[1]


def call(kernel, shapes, name, where, scratch=(), aliases={}):
    spaces = {"s": pltpu.SMEM, "v": pltpu.VMEM}
    return pl.pallas_call(
        kernel,
        out_shape=shapes,
        in_specs=[pl.BlockSpec(memory_space=spaces[key]) for key in where],
        out_specs=tuple(pl.BlockSpec(memory_space=pltpu.VMEM) for _ in shapes),
        scratch_shapes=list(scratch),
        input_output_aliases=aliases,
        name=name,
    )


def pack_kernel(query_ref, key_ref, value_ref, *refs, heads):
    vector_refs, (seg_ref, live_ref, out_ref, vec_s) = refs[:-4], refs[-4:]
    w_rows = query_ref.shape[0]
    sequences, rows = seg_ref.shape
    vec_s[...] = jnp.zeros_like(vec_s)
    for index, ref in enumerate(vector_refs):
        vec_s[index : index + 1, :w_rows] = ref[...].astype(f32)
    columns = jnp.transpose(vec_s[...])[:w_rows, :HEAD_DIM]
    seg = seg_ref[...]
    codes = jnp.where(live_ref[...] == 1, seg, -1)
    lines = jnp.concatenate([seg.astype(f32), codes.astype(f32)], axis=0)
    lines = jnp.concatenate([lines, jnp.zeros((w_rows - 2 * sequences, rows), f32)], axis=0)
    if rows < HEAD_DIM:
        lines = jnp.concatenate([lines, jnp.zeros((w_rows, HEAD_DIM - rows), f32)], axis=1)
    half = heads * 2 * HEAD_DIM
    for feat in range(FEATS):
        pair, single = [], []
        for h in range(heads):
            lanes = slice((feat * heads + h) * HEAD_DIM, (feat * heads + h + 1) * HEAD_DIM)
            pair += [query_ref[:, lanes].astype(f32), key_ref[:, lanes].astype(f32)]
            single.append(value_ref[:, lanes].astype(f32))
        single += [lines, columns, jnp.zeros((w_rows, HEAD_DIM), f32)]
        for core, pieces in ((0, pair), (1, single)):
            wide = jnp.concatenate(pieces, axis=1).astype(bf16)
            for slot in range(out_ref.shape[0]):
                out_ref[slot, feat, core] = wide


def pack_late_kernel(place_ref, w_ref, gate_ref, up_ref, kept_ref, sent_ref, *, slots):
    half = w_ref.shape[1] // 2
    cols = gate_ref.shape[1] // (FEATS * slots)

    def write(core, source_ref, target_ref):
        for feat in range(FEATS):
            pieces = [w_ref[:, core * half : (core + 1) * half]]
            for slot in range(slots):
                start = (slot * FEATS + feat) * cols
                pieces.append(source_ref[:, start : start + cols])
            target_ref[feat] = jnp.concatenate([p.astype(f32) for p in pieces], axis=1).astype(bf16)

    @pl.when(place_ref[0] == 0)
    def _():
        write(0, gate_ref, kept_ref)
        write(1, up_ref, sent_ref)

    @pl.when(place_ref[0] == 1)
    def _():
        write(0, gate_ref, sent_ref)
        write(1, up_ref, kept_ref)


def route_kernel(place_ref, kept_ref, got_ref, *out_refs):
    rows = kept_ref.shape[1]
    first, second = pl.ds(0, rows), pl.ds(rows, rows)
    for k in range(FEATS):
        target = place_ref[2] ^ k
        kept, got = kept_ref[target].astype(f32), got_ref[target].astype(f32)
        first_core = place_ref[0] == 0
        both = [jnp.where(first_core, kept, got), jnp.where(first_core, got, kept)]
        out_refs[k][...] = jnp.concatenate(both, axis=0).astype(bf16)


def piece_row(place_ref, index, piece_rows):
    member = (place_ref[3] ^ (index // 2)) * 2 + (place_ref[1] ^ (index % 2))
    return pl.multiple_of(member * piece_rows, 16)


def qkv_kernel(place_ref, mine_ref, other_ref, *refs, w_rows, rows, heads, pieces):
    token_refs = refs[:FEATS]
    sent_ref, w_ref, params_ref, seg_ref, code_ref, wide_s, vec_s = refs[FEATS:]
    first_core = place_ref[0] == 0
    side, feat = place_ref[1], place_ref[2]
    half = mine_ref.shape[1]
    mine, other = mine_ref[...], other_ref[...]
    w_ref[:, :half] = jnp.where(first_core, mine, other)
    w_ref[:, half:] = jnp.where(first_core, other, mine)
    vec_s[...] = w_ref[:, 2 * half - 128 :].astype(f32)
    wide_s[...] = w_ref[:, 2 * half - 256 : 2 * half - 128].astype(f32)
    head_width = heads * HEAD_DIM
    own = vec_s[pl.ds(pl.multiple_of(feat * head_width, HEAD_DIM), head_width), :]
    own = jnp.concatenate([own, jnp.zeros((256 - head_width, 128), f32)], axis=0)
    own = jnp.concatenate([jnp.transpose(own[:128]), jnp.transpose(own[128:])], axis=1)
    local = token_refs[0].shape[0]
    group = FEATS * local
    rest = jnp.zeros((1, half - head_width), f32)
    value_bias = jnp.concatenate([own[1:2, :head_width], rest], axis=1)
    for k in range(FEATS):
        tokens = token_refs[k][...]
        values = (dot(tokens, w_ref[:, half:]) + value_bias).astype(bf16)
        pairs = dot(tokens, w_ref[:, :half])
        for h in range(heads):
            bias = own[0:1, h * HEAD_DIM : (h + 1) * HEAD_DIM]
            bias = jnp.concatenate([bias, jnp.zeros((1, HEAD_DIM), f32)], axis=1)
            made = (pairs[:, 2 * h * HEAD_DIM : 2 * (h + 1) * HEAD_DIM] + bias).astype(bf16)
            value = values[:, h * HEAD_DIM : (h + 1) * HEAD_DIM]
            start = group + (k % 2) * local
            lanes = slice((k // 2) * HEAD_DIM, (k // 2 + 1) * HEAD_DIM)
            for slot in range(pieces):
                if min(slot % SLOTS, heads - 1) == h:
                    sent_ref[slot, k * local : (k + 1) * local, :] = made
                    sent_ref[slot, start : start + local, lanes] = value
    for start in range(0, w_ref.shape[0], 128):
        turned = jnp.transpose(vec_s[start : start + 128, :])
        params_ref[:, start : start + 128] = turned[:8]
    devices = w_ref.shape[0] // w_rows
    for ref, row in ((seg_ref, 0), (code_ref, 2)):
        for device in range(0, devices, 2):
            lines = []
            for start in (device * w_rows + row, (device + 1) * w_rows + row):
                pair = wide_s[start : start + 2, HEAD_DIM : HEAD_DIM + rows]
                lines.append(jnp.where(side == 0, pair[:1], pair[1:]))
            ref[:, device * rows : (device + 2) * rows] = jnp.concatenate(lines, axis=1)


def split_rows(first_core, values, kept_ref, sent_ref, lanes, rows):
    def write(first, second):
        for block in range(values.shape[0] // (2 * rows)):
            start = 2 * rows * block
            first[block, :, lanes] = values[start : start + rows].astype(bf16)
            second[block, :, lanes] = values[start + rows : start + 2 * rows].astype(bf16)

    @pl.when(first_core)
    def _():
        write(kept_ref, sent_ref)

    @pl.when(jnp.logical_not(first_core))
    def _():
        write(sent_ref, kept_ref)


def collect_kernel(dqkv_ref, out_ref, *, heads):
    half = heads * 2 * HEAD_DIM
    group = out_ref.shape[0]
    quarter = group // 2
    out_ref[:, half + heads * HEAD_DIM :] = jnp.zeros((group, half - heads * HEAD_DIM), bf16)
    for h in range(heads):
        out_ref[:, 2 * h * HEAD_DIM : 2 * (h + 1) * HEAD_DIM] = dqkv_ref[h, :group, :]
        lanes = slice(half + h * HEAD_DIM, half + (h + 1) * HEAD_DIM)
        out_ref[:quarter, lanes] = dqkv_ref[h, group:, :HEAD_DIM]
        out_ref[quarter:, lanes] = dqkv_ref[h, group:, HEAD_DIM:]


def grad_qkv_kernel(place_ref, *refs, heads, w_rows):
    token_refs = refs[:FEATS]
    back_ref, sums_ref, kept_ref, sent_ref, wide_s, vec_s = refs[FEATS:]
    first_core = place_ref[0] == 0
    width = wide_s.shape[1]
    wide_s[...] = jnp.zeros_like(wide_s)
    wide_s[2 : 2 + sums_ref.shape[0], :] = sums_ref[...]
    for start in range(0, width, 128):
        vec_s[start : start + 128, :] = jnp.transpose(wide_s[:, start : start + 128])
    head_width = heads * HEAD_DIM
    half = 2 * head_width
    tokens = jnp.concatenate([ref[...] for ref in token_refs], axis=0)
    back = back_ref[...]
    sums = jnp.sum(back.astype(f32), axis=0, keepdims=True)
    queries = [sums[:, 2 * h * HEAD_DIM : (2 * h + 1) * HEAD_DIM] for h in range(heads)]
    none = jnp.zeros((1, 256 - head_width), f32)
    own = jnp.concatenate(
        [
            jnp.concatenate(queries + [none], axis=1),
            sums[:, half : half + 256],
            jnp.zeros((126, 256), f32),
        ],
        axis=0,
    )
    own = jnp.concatenate([jnp.transpose(own[:, :128]), jnp.transpose(own[:, 128:])], axis=0)
    here = pl.ds(pl.multiple_of(place_ref[2] * head_width, HEAD_DIM), head_width)
    vec_s[here, :] += own[:head_width]
    grad = dot(tokens, back, 0, 0)
    grad = jnp.concatenate([grad[:, : 2 * half - 128], grad[:, 2 * half - 128 :] + vec_s[...]], axis=1)
    split_rows(first_core, grad, kept_ref, sent_ref, slice(None), w_rows)


def place_first_kernel(place_ref, *refs, pieces, down_rows):
    mine_refs, other_refs = refs[:pieces], refs[pieces : 2 * pieces]
    out_ref, down_ref = refs[2 * pieces :]
    out_rows, half = mine_refs[0].shape
    out_rows = out_rows - 2 * down_rows
    feat_rows = out_rows // FEATS

    def fill(cores):
        for index in range(pieces):
            for core in range(2):
                ref = cores[core][index]
                columns = slice(core * half, (core + 1) * half)
                for k in range(FEATS):
                    start = piece_row(place_ref, index, out_rows) + (place_ref[2] ^ k) * feat_rows
                    here = pl.ds(pl.multiple_of(start, 4), feat_rows)
                    out_ref[here, columns] = ref[k * feat_rows : (k + 1) * feat_rows, :]
                start = piece_row(place_ref, index, 2 * down_rows) + core * down_rows
                here = pl.ds(pl.multiple_of(start, 8), down_rows)
                down_ref[here, :half] = ref[out_rows : out_rows + down_rows, :]
                down_ref[here, half:] = ref[out_rows + down_rows :, :]

    @pl.when(place_ref[0] == 0)
    def _():
        fill((mine_refs, other_refs))

    @pl.when(place_ref[0] == 1)
    def _():
        fill((other_refs, mine_refs))


def place_second_kernel(place_ref, *refs, indices):
    pieces = len(indices)
    mine_refs, other_refs = refs[:pieces], refs[pieces : 2 * pieces]
    gate_ref, up_ref = refs[-2:]
    rows = mine_refs[0].shape[0]
    feat_rows = rows // FEATS

    def fill(gate_refs, up_refs):
        for position, index in enumerate(indices):
            for k in range(FEATS):
                start = piece_row(place_ref, index, rows) + (place_ref[2] ^ k) * feat_rows
                here = pl.ds(pl.multiple_of(start, 4), feat_rows)
                source = slice(k * feat_rows, (k + 1) * feat_rows)
                gate_ref[here, :] = gate_refs[position][source, :]
                up_ref[here, :] = up_refs[position][source, :]

    @pl.when(place_ref[0] == 0)
    def _():
        fill(mine_refs, other_refs)

    @pl.when(place_ref[0] == 1)
    def _():
        fill(other_refs, mine_refs)


def join_kernel(
    heads_ref, tokens_ref, w_ref, params_ref,
    attended_ref, norm_ref, low_ref, normed_ref, inverse_ref, *, heads,
):
    sides = []
    for side in range(2):
        lanes = slice(side * HEAD_DIM, (side + 1) * HEAD_DIM)
        pieces = [
            heads_ref[((h // 2) * FEATS + feat) * 2 + h % 2][:, lanes]
            for feat in range(FEATS)
            for h in range(heads)
        ]
        sides.append(jnp.concatenate(pieces, axis=1))
    attended = jnp.concatenate(sides, axis=0)
    attended_ref[...] = attended
    branch = dot(attended, w_ref[...])
    first, normed, inverse = norm_forward(
        tokens_ref[...].astype(f32) + branch + params_ref[2:3, :],
        params_ref[3:4, :],
        params_ref[4:5, :],
    )
    norm_ref[...] = first
    low_ref[...] = first.astype(bf16)
    normed_ref[...] = normed
    inverse_ref[...] = inverse


def part_kernel(
    place_ref, second_ref, own_ref, got_a_ref, got_b_ref, got_c_ref, normed_ref, inverse_ref,
    params_ref, w_ref, attended_ref,
    inner_ref, dout_ref, kept_ref, sent_ref, sums_ref, *, heads, rows,
):
    back_first = second_ref[...] + own_ref[...].astype(f32) + got_a_ref[...].astype(f32)
    back_first = back_first + got_b_ref[...].astype(f32) + got_c_ref[...].astype(f32)
    inner, gain_sum, shift_sum = norm_backward(
        back_first, normed_ref[...], inverse_ref[...], params_ref[3:4, :]
    )
    inner_ref[...] = inner
    branch = inner.astype(bf16)
    sums_ref[...] = jnp.concatenate(
        [jnp.sum(branch.astype(f32), axis=0, keepdims=True), gain_sum, shift_sum], axis=0
    )
    back = dot(branch, w_ref[...], 1, 1).astype(bf16)
    for slot in range(SLOTS):
        for feat in range(FEATS):
            start = (feat * heads + min(slot, heads - 1)) * HEAD_DIM
            piece = back[:, start : start + HEAD_DIM]
            dout_ref[((slot // 2) * FEATS + feat) * 2 + slot % 2] = jnp.concatenate(
                [piece[:rows], piece[rows:]], axis=1
            )
    half = branch.shape[1] // 2
    grad = dot(attended_ref[...], branch, 0, 0).astype(bf16)
    first_core = place_ref[0] == 0
    kept_ref[...] = jnp.where(first_core, grad[:, :half], grad[:, half:])
    sent_ref[...] = jnp.where(first_core, grad[:, half:], grad[:, :half])


def finish_kernel(parts_ref, query_ref, key_ref, value_ref, *refs, heads):
    vector_refs, vec_s = refs[:-1], refs[-1]
    groups = parts_ref.shape[0] // FEATS
    vec_s[...] = jnp.zeros_like(vec_s)
    w_rows = parts_ref.shape[1]
    half = heads * 2 * HEAD_DIM
    head_width = heads * HEAD_DIM
    vectors = jnp.zeros((w_rows, 128), f32)
    for feat in range(FEATS):
        total = parts_ref[feat].astype(f32)
        for group in range(1, groups):
            total = total + parts_ref[group * FEATS + feat].astype(f32)
        lanes = slice(feat * head_width, (feat + 1) * head_width)
        for index, ref in enumerate((query_ref, key_ref)):
            starts = [(2 * h + index) * HEAD_DIM for h in range(heads)]
            ref[:, lanes] = jnp.concatenate([total[:, at : at + HEAD_DIM] for at in starts], axis=1)
        value_ref[:, lanes] = total[:, half : half + head_width]
        vectors = vectors + total[:, 2 * half - 128 :]
    vec_s[:w_rows, :] = vectors
    turned = jnp.transpose(vec_s[...])
    for index, ref in enumerate(vector_refs):
        ref[...] = turned[index : index + 1, :w_rows]


def fold_kernel(
    place_ref, ff_kept_ref, ff_got_ref, down_kept_ref, down_got_ref, out_kept_ref, out_got_ref, *refs,
    units,
):
    ff_refs, down_refs, out_refs = refs[:2], refs[2 : 2 + units], refs[2 + units :]
    rows = ff_kept_ref.shape[0] // (2 * units)
    for k, ref in enumerate(ff_refs):
        for unit in range(units):
            start = (unit * 2 + (place_ref[1] ^ k)) * rows
            here = pl.ds(pl.multiple_of(start, 16), rows)
            value = ff_kept_ref[here, :].astype(f32) + ff_got_ref[here, :].astype(f32)
            ref[unit] = value.astype(bf16)
    for kept_ref, got_ref, moved_refs in (
        (down_kept_ref, down_got_ref, down_refs),
        (out_kept_ref, out_got_ref, out_refs),
    ):
        rows = kept_ref.shape[0] // units
        for k, ref in enumerate(moved_refs):
            here = pl.ds(pl.multiple_of((place_ref[3] ^ k) * rows, 16), rows)
            value = kept_ref[here, :].astype(f32) + got_ref[here, :].astype(f32)
            ref[...] = value.astype(bf16)


def finish_late_kernel(place_ref, *refs, ff_part):
    part_refs, (kept_ref, sent_ref) = refs[:FEATS], refs[FEATS:]
    w_rows = kept_ref.shape[0]
    total = part_refs[0][:, ff_part:].astype(f32)
    for part in part_refs[1:]:
        total = total + part[:, ff_part:].astype(f32)
    for core in range(2):

        @pl.when(place_ref[0] == core)
        def _():
            for ref, rows in (
                (kept_ref, slice(core * w_rows, (core + 1) * w_rows)),
                (sent_ref, slice((1 - core) * w_rows, (2 - core) * w_rows)),
            ):
                ref[:, FEATS * ff_part :] = total[rows].astype(bf16)
                for k in range(FEATS):
                    lanes = pl.ds(pl.multiple_of((place_ref[2] ^ k) * ff_part, 128), ff_part)
                    ref[:, lanes] = part_refs[k][rows, :ff_part]


def finish_wide_kernel(
    place_ref, kept_ref, got_ref, down_kept_ref, down_got_ref,
    gate_ref, up_ref, out_ref, down_ref, *, slots,
):
    total = gate_ref.shape[1]
    cols = total // (FEATS * slots)
    half = out_ref.shape[1] // 2

    def write(first, second, down_first, down_second):
        for source, target in ((first, gate_ref), (second, up_ref)):
            for slot in range(slots):
                pieces = []
                for feat in range(FEATS):
                    start = (feat * slots + slot) * cols
                    pieces.append(source[:, start : start + cols].astype(f32))
                start = slot * FEATS * cols
                target[:, start : start + FEATS * cols] = jnp.concatenate(pieces, axis=1)
        out_ref[:, :half] = first[:, total:].astype(f32)
        out_ref[:, half:] = second[:, total:].astype(f32)
        down_ref[:, :half] = down_first[...].astype(f32)
        down_ref[:, half:] = down_second[...].astype(f32)

    @pl.when(place_ref[0] == 0)
    def _():
        write(kept_ref, got_ref, down_kept_ref, down_got_ref)

    @pl.when(place_ref[0] == 1)
    def _():
        write(got_ref, kept_ref, down_got_ref, down_kept_ref)


def after(values, *others):
    return lax.optimization_barrier((values,) + others)[0]


def tie(*values):
    return lax.optimization_barrier(values)


def on_device(
    layer_input, segment_ids, token_live, w_query, b_query, w_key, w_value, b_value,
    w_output, b_output, first_gain, first_shift, w_gate, w_up, w_down, b_down,
    second_gain, second_shift, output_grad,
):
    units = lax.axis_size("u")
    unit, side, feat, core = (lax.axis_index(name) for name in ("u", "s", "f", "c"))
    devices = units * 2 * FEATS * 2
    sequences, rows, width = layer_input.shape
    length = rows * devices
    w_rows = w_query.shape[0]
    down_rows, ff_part = w_down.shape[0], w_gate.shape[1] // FEATS
    slots = units * 2
    heads = HEADS // FEATS
    head_width = heads * HEAD_DIM
    ranges = slots // SLOTS
    local = 2 * rows
    group = FEATS * local
    here = jnp.stack([core, side, feat, unit]).astype(jnp.int32)
    parts = slots

    def exchange_sides(values):
        kept = jnp.where(side == 0, values[0], values[1])
        got = swap(jnp.where(side == 0, values[1], values[0]), "s")
        return kept, got

    def to_tokens(values):
        kept, got = exchange_sides(values)
        return jnp.concatenate(
            [jnp.where(side == 0, kept, got), jnp.where(side == 0, got, kept)], axis=0
        )

    def from_tokens(values):
        kept, got = exchange_sides(values.reshape(2, rows, width))
        return jnp.stack([jnp.where(side == 0, kept, got), jnp.where(side == 0, got, kept)])

    def to_group(blocks):
        return all_to_all(blocks.reshape(-1, blocks.shape[-1]), ("f", "c"))

    def from_units(own, other_side, pin=None):
        pieces = [own, other_side]
        for k in range(1, units):
            for piece in (own, other_side):
                pieces.append(swap(piece if pin is None else after(piece, pin), "u", k))
        return pieces

    tokens = to_tokens(layer_input)

    vectors = [
        values.reshape(1, w_rows)
        for values in (
            b_query, b_value, b_output, first_gain, first_shift, b_down, second_gain, second_shift
        )
    ]
    half = heads * 2 * HEAD_DIM
    (early,) = call(
        functools.partial(pack_kernel, heads=heads),
        (jax.ShapeDtypeStruct((slots, FEATS, 2, w_rows, half), bf16),),
        "pack_attn",
        "v" * 13,
        [pltpu.VMEM((128, 128), f32)],
    )(w_query, w_key, w_value, *vectors, segment_ids, token_live)
    early, tokens = tie(early, tokens)
    early_mine = all_to_all(early.reshape(-1, half), ("u", "s", "f", "c"))
    token_parts = gather_feats(tokens)

    late_cols = width // 2 + ff_part
    late_shape = jax.ShapeDtypeStruct((FEATS, w_rows, late_cols), bf16)
    late_kept, late_sent = call(
        functools.partial(pack_late_kernel, slots=slots), (late_shape, late_shape), "pack_late", "svvv"
    )(here, w_output, w_gate, w_up)
    routed = call(
        route_kernel,
        (jax.ShapeDtypeStruct((2 * w_rows, late_cols), bf16),) * FEATS,
        "route_late",
        "svv",
    )(here, late_kept, swap(late_sent, "c"))
    out_half = width // 2
    late_feats = [routed[0]] + [swap(routed[k], "f", k) for k in range(1, FEATS)]
    early_mine, *token_parts = tie(early_mine, *token_parts)
    early_other = swap(early_mine, "c")
    here_qkv, *late_feats = tie(here, *late_feats)
    first_own = jnp.concatenate(
        [piece[:, :out_half] for piece in late_feats] + [w_down[:, :out_half], w_down[:, out_half:]]
    )
    second_own = jnp.concatenate([piece[:, out_half:] for piece in late_feats])
    others = range(1, units)

    sent, w_attn, params, seg_row, code_row = call(
        functools.partial(qkv_kernel, w_rows=w_rows, rows=rows, heads=heads, pieces=parts),
        (
            jax.ShapeDtypeStruct((slots, group * 3 // 2, 2 * HEAD_DIM), bf16),
            jax.ShapeDtypeStruct((width, 2 * half), bf16),
            jax.ShapeDtypeStruct((8, width), f32),
            jax.ShapeDtypeStruct((1, length), f32),
            jax.ShapeDtypeStruct((1, length), f32),
        ),
        "qkv",
        "s" + "v" * (2 + FEATS),
        [pltpu.VMEM((width, 128), f32)] * 2,
    )(here_qkv, early_mine, early_other, *token_parts)
    qkv = all_to_all(sent.reshape(-1, 2 * HEAD_DIM), ("u", "c"))
    first_side = swap(first_own, "s")
    first_units = [swap(first_own, "u", k) for k in others]
    first_swaps = [swap(piece, "c") for piece in [first_own, first_side] + first_units]
    second_swaps = [swap(second_own, "c")]
    qkv, first_side, second_swaps[0], *moved = tie(
        qkv, first_side, second_swaps[0], *first_units, *first_swaps
    )
    first_units, first_swaps = moved[: units - 1], moved[units - 1 :]
    qkv = qkv.reshape(sent.shape)

    blocks = length // BLOCK
    slot_self = unit * 2 + core
    range_self = slot_self // SLOTS
    head_self = feat * heads + jnp.minimum(slot_self % SLOTS, heads - 1)
    slope = jnp.asarray(alibi_slopes(HEADS))[head_self].reshape(1, 1)
    seg_blocks = seg_row.reshape(blocks, BLOCK)
    seg_low, seg_high = seg_blocks[:, 0], seg_blocks[:, -1]
    key_low = jnp.sum(seg_high[None, :] < seg_low[:, None], axis=1, dtype=jnp.int32)
    key_high = jnp.sum(seg_low[None, :] <= seg_high[:, None], axis=1, dtype=jnp.int32)
    own = jnp.stack(
        [feat, range_self * (blocks // ranges), (range_self + 1) * (blocks // ranges)]
    ).astype(jnp.int32)
    table = jnp.stack([key_low, key_high, jnp.pad(own, (0, blocks - 3))])
    second_side = swap(second_own, "s")
    second_units = [swap(second_own, "u", k) for k in others]
    first_far = [swap(first_side, "u", k) for k in others]
    out_blocks, lse, o_turned = attend(table, slope, qkv, seg_row, code_row)
    out_blocks, second_side, *moved = tie(out_blocks, second_side, *second_units, *first_far)
    second_units, first_far = moved[: units - 1], moved[units - 1 :]
    second_far = [swap(second_side, "u", k) for k in others]
    first_swaps += [swap(piece, "c") for piece in first_far]
    second_swaps += [swap(piece, "c") for piece in [second_side] + second_units]

    def by_distance(own, other_side, near, far):
        pieces = [own, other_side]
        for index in range(units - 1):
            pieces += [near[index], far[index]]
        return pieces

    first_pieces = by_distance(first_own, first_side, first_units, first_far)
    first_others = by_distance(
        first_swaps[0], first_swaps[1], first_swaps[2 : 1 + units], first_swaps[1 + units :]
    )
    aligned = w_rows % 8 == 0

    def in_rows(pieces, feats):
        cols = pieces[0].shape[1]
        values = jnp.stack(pieces).reshape(units, 2, feats, -1, cols)
        values = jnp.take(values, jnp.arange(units) ^ unit, axis=0)
        values = jnp.take(values, jnp.arange(2) ^ side, axis=1)
        if feats == FEATS:
            values = jnp.take(values, jnp.arange(FEATS) ^ feat, axis=2)
        return values.reshape(-1, cols)

    def by_core(mine, others_):
        mine, others_ = in_rows(mine, FEATS), in_rows(others_, FEATS)
        return jnp.where(core == 0, mine, others_), jnp.where(core == 0, others_, mine)

    if aligned:
        full_output, full_down = call(
            functools.partial(place_first_kernel, pieces=parts, down_rows=down_rows),
            (
                jax.ShapeDtypeStruct((width, width), bf16),
                jax.ShapeDtypeStruct((ff_part, width), bf16),
            ),
            "place_first",
            "s" + "v" * 2 * parts,
        )(here, *first_pieces, *first_others)
    else:
        out_rows = 2 * FEATS * w_rows
        full_output = jnp.concatenate(
            by_core([p[:out_rows] for p in first_pieces], [p[:out_rows] for p in first_others]), axis=1
        )

        def down_of(pieces):
            return in_rows(
                [
                    jnp.concatenate([p[out_rows : out_rows + down_rows], p[out_rows + down_rows :]], axis=1)
                    for p in pieces
                ],
                1,
            ).reshape(slots, down_rows, width)

        down_mine, down_others = down_of(first_pieces), down_of(first_others)
        full_down = jnp.stack(
            [jnp.where(core == 0, down_mine, down_others), jnp.where(core == 0, down_others, down_mine)],
            axis=1,
        ).reshape(ff_part, width)

    heads_in = all_to_all(out_blocks.reshape(-1, 2 * HEAD_DIM), ("u", "f", "c"))
    heads_in, *second_swaps[1:] = tie(heads_in, *second_swaps[1:])
    heads_in = heads_in.reshape(ranges, SLOTS * FEATS, rows, 2 * HEAD_DIM)
    if ranges > 1:
        heads_in = lax.dynamic_index_in_dim(heads_in, unit * 2 // SLOTS, 0, keepdims=False)
    else:
        heads_in = heads_in[0]
    attended, first_norm, first_low_own, normed_one, inverse_one = call(
        functools.partial(join_kernel, heads=heads),
        (
            jax.ShapeDtypeStruct((local, width), bf16),
            jax.ShapeDtypeStruct((local, width), f32),
            jax.ShapeDtypeStruct((local, width), bf16),
            jax.ShapeDtypeStruct((local, width), f32),
            jax.ShapeDtypeStruct((local, 1), f32),
        ),
        "join_heads",
        "vvvv",
    )(heads_in, tokens, full_output, params)

    first_low_own, *second_far = tie(first_low_own, *second_far)
    second_swaps += [swap(piece, "c") for piece in second_far]
    ff_square = jax.ShapeDtypeStruct((width, ff_part), bf16)
    indices = [0, 1] + [2 * k for k in others] + [2 * k + 1 for k in others]
    second_pieces = [second_own, second_side, *second_units, *second_far]
    if aligned:
        full_gate, full_up = call(
            functools.partial(place_second_kernel, indices=indices),
            (ff_square, ff_square),
            "place_second",
            "s" + "v" * 2 * parts,
        )(here, *second_pieces, *second_swaps)
    else:
        order = [indices.index(position) for position in range(parts)]
        full_gate, full_up = by_core(
            [second_pieces[position] for position in order],
            [second_swaps[position] for position in order],
        )
    low_parts = gather_feats(first_low_own)
    full_gate, full_up, *low_parts = tie(full_gate, full_up, *low_parts)
    first_low = jnp.concatenate(low_parts, axis=0)
    gate_rows = dot(first_low, full_gate)
    up_rows = dot(first_low, full_up)
    spread = 0.5 * (1.0 + lax.erf(gate_rows * (0.5**0.5)))
    gelu = gate_rows * spread
    hidden = (gelu * up_rows).astype(bf16)
    partial_mixed = dot(hidden, full_down).astype(bf16).reshape(FEATS, local, width)
    partial_mixed, gate_kept, up_kept = tie(partial_mixed, gate_rows, up_rows)
    mixed_got = [swap(partial_mixed[k], "f", k) for k in range(1, FEATS)]
    spread = 0.5 * (1.0 + lax.erf(gate_kept * (0.5**0.5)))
    density = jnp.exp(-0.5 * gate_kept * gate_kept) * (1.0 / math.sqrt(2.0 * math.pi))
    gate_factor = (up_kept * (spread + gate_kept * density)).astype(bf16)
    up_factor = (gate_kept * spread).astype(bf16)
    bias_down, gate_factor, up_factor = tie(params[5], gate_factor, up_factor)
    mixed = partial_mixed[0].astype(f32) + bias_down
    for piece in mixed_got:
        mixed = mixed + piece.astype(f32)
    gain_two = params[6]
    layer_wide, normed_two, inverse_two = norm_forward(first_norm + mixed, gain_two, params[7])

    upstream = to_tokens(after(output_grad, out_blocks)).astype(f32)
    back_second, grad_gain_two, grad_shift_two = norm_backward(
        upstream, normed_two, inverse_two, gain_two
    )
    back_low = back_second.astype(bf16)
    grad_down_bias = jnp.sum(back_low.astype(f32), axis=0, keepdims=True)
    back_mixed = jnp.concatenate(gather_feats(back_low), axis=0)
    back_hidden = dot(back_mixed, full_down, 1, 1)
    back_gate = (back_hidden * gate_factor.astype(f32)).astype(bf16)
    back_up = (back_hidden * up_factor.astype(f32)).astype(bf16)
    partial_first = (dot(back_gate, full_gate, 1, 1) + dot(back_up, full_up, 1, 1)).astype(bf16)
    partial_first = partial_first.reshape(FEATS, local, width)
    partial_got = [swap(partial_first[k], "f", k) for k in range(1, FEATS)]
    partial_got[0], back_gate, back_up, back_mixed = tie(partial_got[0], back_gate, back_up, back_mixed)
    half_width = width // 2

    def chosen(first, second):
        return jnp.where(core == 0, first, second)

    left, right = back_mixed[:, :half_width], back_mixed[:, half_width:]

    def outer(rows_side, cols_side):
        return dot(cols_side, rows_side, 0, 0).astype(bf16).T

    ff_sent = outer(first_low, chosen(back_up, back_gate))
    down_sent = outer(hidden, chosen(right, left))
    ff_kept = outer(first_low, chosen(back_gate, back_up))
    down_kept = outer(hidden, chosen(left, right))
    here_join, ff_sent, down_sent, ff_kept, down_kept = tie(here, ff_sent, down_sent, ff_kept, down_kept)
    ff_got, down_got = None, None
    inner_shape = jax.ShapeDtypeStruct((local, width), f32)
    back_inner, dout_blocks, out_kept, out_sent, sums_one = call(
        functools.partial(part_kernel, heads=heads, rows=rows),
        (
            inner_shape,
            jax.ShapeDtypeStruct((SLOTS * FEATS, rows, 2 * HEAD_DIM), bf16),
            jax.ShapeDtypeStruct((width, half_width), bf16),
            jax.ShapeDtypeStruct((width, half_width), bf16),
            jax.ShapeDtypeStruct((3, width), f32),
        ),
        "back_join",
        "s" + "v" * 10,
    )(
        here_join, back_second, partial_first[0], *partial_got, normed_one, inverse_one, params,
        full_output, attended,
    )
    dout_sent = jnp.broadcast_to(dout_blocks[None], (ranges,) + dout_blocks.shape)
    dout = all_to_all(dout_sent.reshape(-1, 2 * HEAD_DIM), ("u", "f", "c"))
    dout = dout.reshape(slots * FEATS, rows, 2 * HEAD_DIM)

    def fold(values, axis):
        return scatter_axis(values, axis).astype(bf16)

    def added(kept, got):
        return (kept.astype(f32) + got.astype(f32)).astype(bf16)

    out_got = swap(out_sent, "c")
    ff_got, down_got = swap(after(ff_sent, dout_blocks), "c"), swap(after(down_sent, dout_blocks), "c")
    ff_rows, down_half = 2 * FEATS * w_rows, width // units
    ff_shape = jax.ShapeDtypeStruct((units, ff_rows, ff_part), bf16)
    half_shape = jax.ShapeDtypeStruct((down_half, half_width), bf16)
    folded = call(
        functools.partial(fold_kernel, units=units),
        (ff_shape,) * 2 + (half_shape,) * (2 * units),
        "fold_cores",
        "s" + "v" * 6,
    )(after(here, dout), ff_kept, ff_got, down_kept, down_got, out_kept, out_got)
    grad_ff, ff_moved = folded[0], [swap(folded[1], "s")]
    grad_down = folded[2]
    down_moved = [swap(folded[2 + k], "u", k) for k in range(1, units)]
    grad_out = folded[2 + units]
    out_moved = [swap(folded[2 + units + k], "u", k) for k in range(1, units)]

    def parts_of(values, axis):
        size, me = lax.axis_size(axis), lax.axis_index(axis)
        if size == 2:
            return [jnp.where(me == 0, values[0], values[1]), jnp.where(me == 0, values[1], values[0])]
        return [lax.dynamic_index_in_dim(values, me ^ k, 0, keepdims=False) for k in range(size)]

    def send(values, axis):
        own, *rest = parts_of(values, axis)
        return own, [swap(piece, axis, k + 1) for k, piece in enumerate(rest)]

    def total(own, got):
        result = own.astype(f32)
        for piece in got:
            result = result + piece.astype(f32)
        return result

    dout, grad_ff, grad_down, grad_out = tie(dout, grad_ff, grad_down, grad_out)
    dqkv = attend_back(table, slope, qkv, dout, o_turned, lse, seg_row, code_row)
    dqkv, *moved = tie(dqkv, *ff_moved, *down_moved, *out_moved)
    ff_moved, down_moved, out_moved = moved[:1], moved[1:units], moved[units:]
    grad_ff = total(grad_ff, ff_moved).astype(bf16)
    grad_down = total(grad_down, down_moved).astype(bf16).reshape(2, 2 * down_rows, half_width)
    grad_out = total(grad_out, out_moved).astype(bf16).reshape(2, FEATS * 2 * w_rows, half_width)
    grad_ff, ff_moved = send(grad_ff, "u")
    grad_down, down_moved = send(grad_down, "s")
    dqkv = all_to_all(dqkv.reshape(-1, 2 * HEAD_DIM), ("u", "c"))
    dqkv, *moved = tie(dqkv, *ff_moved, *down_moved)
    ff_moved, down_moved = moved[:-1], moved[-1:]
    grad_out, out_moved = send(after(grad_out, dqkv), "s")
    layer_wide_low = after(layer_wide.astype(bf16), dqkv)
    dqkv = dqkv.reshape(ranges, SLOTS, group * 3 // 2, 2 * HEAD_DIM)
    if ranges > 1:
        dqkv = jnp.sum(dqkv.astype(f32), axis=0).astype(bf16)
    else:
        dqkv = dqkv[0]
    vector_sums = jnp.concatenate([sums_one, grad_down_bias, grad_gain_two, grad_shift_two], axis=0)
    (back_projected,) = call(
        functools.partial(collect_kernel, heads=heads),
        (jax.ShapeDtypeStruct((group, 2 * half), bf16),),
        "collect",
        "v",
    )(dqkv)
    attn_shape = jax.ShapeDtypeStruct((slots * FEATS, w_rows, 2 * half), bf16)
    attn_kept, attn_sent = call(
        functools.partial(grad_qkv_kernel, heads=heads, w_rows=w_rows),
        (attn_shape, attn_shape),
        "grad_qkv",
        "s" + "v" * (FEATS + 2),
        [pltpu.VMEM((128, width), f32), pltpu.VMEM((width, 128), f32)],
    )(here, *token_parts, back_projected, vector_sums)
    attn_sent, back_projected = tie(attn_sent, back_projected)
    partial_input = dot(back_projected, w_attn, 1, 1).astype(bf16).reshape(FEATS, local, width)
    input_got = [swap(partial_input[k], "f", k) for k in range(1, FEATS)]
    grad_attn = added(after(attn_kept, partial_input), swap(attn_sent, "c"))
    back_inner, grad_attn, grad_ff = tie(back_inner, grad_attn, grad_ff)
    grad_attn = all_to_all(grad_attn.reshape(-1, 2 * half), ("u", "s", "f"))
    grad_ff = total(grad_ff, ff_moved)
    grad_out = total(grad_out, out_moved)
    grad_down = total(grad_down, down_moved).reshape(2, down_rows, half_width)
    grad_late = jnp.concatenate([grad_ff, grad_out], axis=1).astype(bf16)
    grad_late = grad_late.reshape(FEATS, 2 * w_rows, ff_part + half_width)

    input_sum = back_inner + partial_input[0].astype(f32)
    for piece in input_got:
        input_sum = input_sum + piece.astype(f32)
    input_grad = from_tokens(input_sum.astype(bf16))
    layer_output = from_tokens(layer_wide_low)

    late_got = [lax.dynamic_index_in_dim(grad_late, feat, 0, keepdims=False)]
    late_got += [
        swap(lax.dynamic_index_in_dim(grad_late, feat ^ k, 0, keepdims=False), "f", k)
        for k in range(1, FEATS)
    ]
    wide_shape = jax.ShapeDtypeStruct((w_rows, FEATS * ff_part + half_width), bf16)
    wide_kept, wide_sent = call(
        functools.partial(finish_late_kernel, ff_part=ff_part),
        (wide_shape, wide_shape),
        "finish_late",
        "s" + "v" * FEATS,
    )(here, *late_got)
    wide_got = swap(wide_sent, "c")
    down_kept = chosen(grad_down[0], grad_down[1])
    down_got = swap(chosen(grad_down[1], grad_down[0]).astype(bf16), "c")
    ff_out_shape = jax.ShapeDtypeStruct((w_rows, FEATS * ff_part), f32)
    grad_gate, grad_up, grad_output, grad_down = call(
        functools.partial(finish_wide_kernel, slots=slots),
        (
            ff_out_shape,
            ff_out_shape,
            jax.ShapeDtypeStruct((w_rows, width), f32),
            jax.ShapeDtypeStruct((down_rows, width), f32),
        ),
        "finish_wide",
        "svvvv",
    )(here, wide_kept, wide_got, down_kept, down_got)
    matrix_shape = jax.ShapeDtypeStruct((w_rows, width), f32)
    grad_query, grad_key, grad_value, *vectors_out = call(
        functools.partial(finish_kernel, heads=heads),
        (matrix_shape,) * 3 + (jax.ShapeDtypeStruct((1, w_rows), f32),) * 8,
        "finish",
        "v",
        [pltpu.VMEM((128, 128), f32)],
    )(grad_attn.reshape(slots * FEATS, w_rows, 2 * half))
    vectors_out = [values.reshape(w_rows) for values in vectors_out]
    return (
        layer_output, input_grad, grad_query, vectors_out[0], grad_key, grad_value,
        vectors_out[1], grad_output, vectors_out[2], vectors_out[3], vectors_out[4],
        grad_gate, grad_up, grad_down, vectors_out[5], vectors_out[6], vectors_out[7],
    )


def solution(mesh):
    devices = mesh.devices
    names = ("u", "s", "f", "c")
    inner = Mesh(devices.reshape(devices.size // (4 * FEATS), 2, FEATS, 2), names)
    tokens, matrix, vector = P(None, names, None), P(names, None), P(names)
    ids = P(None, names)
    return jax.shard_map(
        on_device,
        mesh=inner,
        in_specs=(
            tokens, ids, ids, matrix, vector, matrix, matrix, vector, matrix, vector, vector,
            vector, matrix, matrix, matrix, vector, vector, vector, tokens,
        ),
        out_specs=(
            tokens, tokens, matrix, vector, matrix, matrix, vector, matrix, vector, vector,
            vector, matrix, matrix, matrix, vector, vector, vector,
        ),
        check_vma=False,
    )
```

time: 397 us -> 289 us (0.73); the launches traced: 391 us -> 287 us
  waiting for transfers between devices: 148 us -> 88 us
  local copies, waits for them, and re-layouts: 51.6 us -> 12.7 us
  other arithmetic: 51.2 us -> 15.1 us
  Pallas kernels: 47.7 us -> 73.5 us
  blocking collectives: 0 us -> 11.9 us
  matrix products: 22.6 us -> 13.6 us
  starting transfers between devices: 66.9 us -> 71 us
    all_to_all x8 -> x5, waiting for transfers between devices: 44.5 us -> 4.82 us  [all_to_all(): return lax.all_to_all(values, axes, split_axis=0, concat_axis=0, tiled=True)]
    pallas_call x1 -> x15, Pallas kernels: 21 us -> 53.9 us  [the longest x1 15.7 us: attend(): pl.pallas_call(attend_kernel, out_shape=(jax.ShapeDtypeStruct((slots * FE...]
    ppermute x33 -> x56, waiting for transfers between devices: 104 us -> 83.2 us  [swap(): return lax.ppermute(values, axis, [(i, i ^ step) for i in range(size)])]
    ppermute x33 -> x56, starting transfers between devices: 33.9 us -> 50.4 us  [swap(): return lax.ppermute(values, axis, [(i, i ^ step) for i in range(size)])]
    concatenate x5 -> x2, local copies, waits for them, and re-layouts: 13.1 us -> 0.03 us  [the longest x1 0.02 us: on_device(): jnp.concatenate([piece[:, :out_half] for piece in late_feats] + [w_down[:...]
    all_to_all x8 -> x5, starting transfers between devices: 33 us -> 20.6 us  [all_to_all(): return lax.all_to_all(values, axes, split_axis=0, concat_axis=0, tiled=True)]
    all_to_all x0 -> x1, blocking collectives: none -> 11.9 us  [all_to_all(): return lax.all_to_all(values, axes, split_axis=0, concat_axis=0, tiled=True)]
    convert_element_type x11 -> x7, other arithmetic: 14.8 us -> 4.02 us  [the longest x1 1.23 us: on_device(): input_grad = from_tokens(input_sum.astype(bf16))]
  transfers between devices with their start and end apart: 41 -> 61, of which waited for: 26 -> 28; matrix products, arithmetic and copies ran while one was open for 26% -> 8% of each run, Pallas kernels for 12% -> 22%
where the time goes in v2:
time: 289 us; the launch traced here: 287 us
  waiting for transfers between devices  88 us (30%)
  Pallas kernels  73.5 us (25%)
  starting transfers between devices  71 us (25%)
  other arithmetic  15.1 us (5%)
  matrix products  13.6 us (5%)
  local copies, waits for them, and re-layouts  12.7 us (4%)
  blocking collectives  11.9 us (4%)
    ppermute x56, waiting for transfers between devices, swap(): return lax.ppermute(values, axis, [(i, i ^ step) for i in range(size)])  83.2 us
    ppermute x56, starting transfers between devices, swap(): return lax.ppermute(values, axis, [(i, i ^ step) for i in range(size)])  50.4 us
    all_to_all x5, starting transfers between devices, all_to_all(): return lax.all_to_all(values, axes, split_axis=0, concat_axis=0, tiled=True)  20.6 us
    pallas_call x1, Pallas kernels, attend_back(): pl.pallas_call(attend_back_kernel, out_shape=jax.ShapeDtypeStruct(qkv.sha...  19.6 us
    pallas_call x1, Pallas kernels, attend(): pl.pallas_call(attend_kernel, out_shape=(jax.ShapeDtypeStruct((slots * FE...  15.7 us
    dot_general x11, matrix products, dot(): lax.dot_general(left, right, (((left_dim,), (right_dim,)), ((), ())), pre...  13.6 us
    all_to_all x1, blocking collectives, all_to_all(): return lax.all_to_all(values, axes, split_axis=0, concat_axis=0, tiled=True)  11.9 us
    unnamed x114, local copies, waits for them, and re-layouts  9.69 us
  transfers between devices with their start and end apart: 61, of which 28 were waited for; matrix products, arithmetic and copies ran while one was open for 8% of the time, Pallas kernels for 22%

profile of v2, /device:TPU:0, one launch (start us, length us, event | category | flops | bytes accessed | tf_op | source)
XLA Modules:
  0.0 287.5 jit_solution(10170218534691518624)
XLA Ops:
  1.6 4.1 %collective-permute-start.4 = (bf16[64,768]{1,0:T(8,128)(2,1)S(1)}, bf16[64,768]{1,0:T(8,128)(2,1)S(1)}, u32[]{:S(2)}, u32[]{:S(2)}) collective-permute-start(bf16[64,768]{1,0:T(8,128)(2,1)S(1)} %select_bitcast_fusion.8), channel_id=1, source_target_pairs={{0,8},{8,0},{1,9},{9,1},{2,10},{10,2},{3,11},{11,3},{4,12},{12,4},... | collective-permute-start | bytes 294920 | tf_op jit(solution)/shard_map/ppermute | solution.py:42
  5.7 1.9 pack_attn.1
  7.6 3.0 %collective-permute-done.4 = bf16[64,768]{1,0:T(8,128)(2,1)S(1)} collective-permute-done((bf16[64,768]{1,0:T(8,128)(2,1)S(1)}, bf16[64,768]{1,0:T(8,128)(2,1)S(1)}, u32[]{:S(2)}, u32[]{:S(2)}) %collective-permute-start.4) | collective-permute-done | bytes 98336 | tf_op jit(solution)/shard_map/ppermute | solution.py:42
  11.6 5.8 %all-to-all-start = ((bf16[32,24,384]{2,1,0:T(8,128)(2,1)}), bf16[32,24,384]{2,1,0:T(8,128)(2,1)S(1)}, u32[]{:S(2)}, u32[]{:S(2)}) async-start(bf16[32,24,384]{2,1,0:T(8,128)(2,1)} %bitcast.105), calls=%async_computation | async-start | bytes 1179648 | tf_op jit(solution)/shard_map/all_to_all | solution.py:86
  18.0 1.9 pack_late.1
  20.2 1.4 collective-permute-done.got_ref
  22.3 1.8 route_late.1
  24.1 1.8 collective-permute-start.1
  25.9 1.5 collective-permute-start.2
  27.6 2.7 collective-permute-start.7
  32.0 2.4 collective-permute-done.2
  34.4 2.5 collective-permute-done.3
  37.7 3.4 %collective-permute-done.7.refs_3_ = bf16[128,768]{1,0:T(8,128)(2,1)S(1)} collective-permute-done((bf16[128,768]{1,0:T(8,128)(2,1)S(1)}, bf16[128,768]{1,0:T(8,128)(2,1)S(1)}, u32[]{:S(2)}, u32[]{:S(2)}) %collective-permute-start.7) | collective-permute-done | bytes 196640 | tf_op jit(solution)/shard_map/ppermute | solution.py:42
  41.1 3.5 %collective-permute-done.6.refs_2_ = bf16[128,768]{1,0:T(8,128)(2,1)S(1)} collective-permute-done((bf16[128,768]{1,0:T(8,128)(2,1)S(1)}, bf16[128,768]{1,0:T(8,128)(2,1)S(1)}, u32[]{:S(2)}, u32[]{:S(2)}) %collective-permute-start.6) | collective-permute-done | bytes 196640 | tf_op jit(solution)/shard_map/ppermute | solution.py:42
  44.8 1.5 collective-permute-start.11
  46.3 1.7 collective-permute-start.9
  48.9 3.3 %qkv.1 = (bf16[4,768,128]{2,1,0:T(8,128)(2,1)}, bf16[768,768]{1,0:T(8,128)(2,1)}, f32[8,768]{1,0:T(8,128)}, f32[1,2048]{1,0:T(1,128)}, f32[1,2048]{1,0:T(1,128)}) custom-call(s32[4]{0:T(128)} %pad_add_fusion.1.place_ref, bf16[768,384]{1,0:T(8,128)(2,1)} %bitcast.107, bf16[768,384]{1,0:T(8,128)(2,1)} %copy-done.18, bf16[128,768]{1,0:T(8,128)(2,1)} %copy-done.3, ...), custom_call_target="tpu_custom_call" | custom-call | tf_op jit(solution)/shard_map/qkv/pallas_call | solution.py:863
  52.1 3.6 %all-to-all-start.1 = ((bf16[4,768,128]{2,1,0:T(8,128)(2,1)}), bf16[4,768,128]{2,1,0:T(8,128)(2,1)S(1)}, u32[]{:S(2)}, u32[]{:S(2)}) async-start(bf16[4,768,128]{2,1,0:T(8,128)(2,1)} %get-tuple-element.156), calls=%async_computation.1 | async-start | bytes 1572864 | tf_op jit(solution)/shard_map/all_to_all | solution.py:86
  57.0 5.3 %collective-permute-done.9.refs_1_ = bf16[384,384]{1,0:T(8,128)(2,1)S(1)} collective-permute-done((bf16[384,384]{1,0:T(8,128)(2,1)S(1)}, bf16[384,384]{1,0:T(8,128)(2,1)S(1)}, u32[]{:S(2)}, u32[]{:S(2)}) %collective-permute-start.9) | collective-permute-done | bytes 294944 | tf_op jit(solution)/shard_map/ppermute | solution.py:42
  64.9 3.0 %all-to-all-done.1 = bf16[4,768,128]{2,1,0:T(8,128)(2,1)S(1)} async-done(((bf16[4,768,128]{2,1,0:T(8,128)(2,1)}), bf16[4,768,128]{2,1,0:T(8,128)(2,1)S(1)}, u32[]{:S(2)}, u32[]{:S(2)}) %all-to-all-start.1) | async-done | bytes 786464 | tf_op jit(solution)/shard_map/all_to_all | solution.py:86
  69.0 15.7 %attend.1 = (bf16[16,64,128]{2,1,0:T(8,128)(2,1)}, f32[1,2048]{1,0:T(1,128)}, f32[64,2048]{1,0:T(8,128)}) custom-call(s32[3,8]{1,0:T(4,128)} %pad_add_fusion.table_ref, f32[1,1]{1,0:T(1,128)} %bitcast.23.slope_ref, bf16[4,768,128]{2,1,0:T(8,128)(2,1)} %copy-done, f32[1,2048]{1,0:T(1,128)} %get-tuple-element.155.seg_ref, f32[1,2048]{1,0:T(1,128)} %get-tuple-element.162.code_ref), custom_call_target="tpu_custom_call" | custom-call | tf_op jit(solution)/shard_map/attend/pallas_call | solution.py:305
  84.7 4.1 %all-to-all-start.2 = ((bf16[16,64,128]{2,1,0:T(8,128)(2,1)}), bf16[16,64,128]{2,1,0:T(8,128)(2,1)S(1)}, u32[]{:S(2)}, u32[]{:S(2)}) async-start(bf16[16,64,128]{2,1,0:T(8,128)(2,1)} %get-tuple-element.165), calls=%async_computation.2 | async-start | bytes 524288 | tf_op jit(solution)/shard_map/all_to_all | solution.py:86
  89.7 1.7 collective-permute-start.21
  92.5 3.3 %place_first.1 = (bf16[768,768]{1,0:T(8,128)(2,1)}, bf16[768,768]{1,0:T(8,128)(2,1)}) custom-call(s32[4]{0:T(128)} %pad_add_fusion.1.place_ref, bf16[384,384]{1,0:T(8,128)(2,1)} %copy-done.21, bf16[384,384]{1,0:T(8,128)(2,1)} %copy-done.24, bf16[384,384]{1,0:T(8,128)(2,1)} %copy-done.23, bf16[384,384]{1,0:T(8,128)(2,1)} %collective-permute-done.17.refs_3_, ...), custom_call_target="tpu_custom_call" | custom-call | tf_op jit(solution)/shard_map/place_first/pallas_call | solution.py:936
  95.8 1.8 all-to-all-done.2
  98.4 3.0 %join_heads.1 = (bf16[128,768]{1,0:T(8,128)(2,1)}, f32[128,768]{1,0:T(8,128)}, bf16[128,768]{1,0:T(8,128)(2,1)}, f32[128,768]{1,0:T(8,128)}, f32[128,1]{1,0:T(8,128)}) custom-call(bf16[16,64,128]{2,1,0:T(8,128)(2,1)} %copy-done.9, bf16[128,768]{1,0:T(8,128)(2,1)} %copy-done.3, bf16[768,768]{1,0:T(8,128)(2,1)} %get-tuple-element.174.w_ref, ...), custom_call_target="tpu_custom_call" | custom-call | tf_op jit(solution)/shard_map/join_heads/pallas_call | solution.py:973
  102.3 2.1 collective-permute-start.25
  106.7 3.4 %place_second.1 = (bf16[768,768]{1,0:T(8,128)(2,1)}, bf16[768,768]{1,0:T(8,128)(2,1)}) custom-call(s32[4]{0:T(128)} %pad_add_fusion.1.place_ref, bf16[192,768]{1,0:T(8,128)(2,1)} %copy-done.6, bf16[192,768]{1,0:T(8,128)(2,1)} %collective-permute-done.15.refs_1_, bf16[192,768]{1,0:T(8,128)(2,1)} %collective-permute-done.16.refs_2_, ...), custom_call_target="tpu_custom_call" | custom-call | tf_op jit(solution)/shard_map/place_second/pallas_call | solution.py:992
  111.3 3.5 %collective-permute-done.24 = bf16[128,768]{1,0:T(8,128)(2,1)S(1)} collective-permute-done((bf16[128,768]{1,0:T(8,128)(2,1)}, bf16[128,768]{1,0:T(8,128)(2,1)S(1)}, u32[]{:S(2)}, u32[]{:S(2)}) %collective-permute-start.24) | collective-permute-done | bytes 196640 | tf_op jit(solution)/shard_map/ppermute | solution.py:42
  119.7 1.5 collective-permute-start.28
  122.8 6.8 %collective-permute-done.26 = bf16[128,768]{1,0:T(8,128)(2,1)S(1)} collective-permute-done((bf16[128,768]{1,0:T(8,128)(2,1)S(1)}, bf16[128,768]{1,0:T(8,128)(2,1)S(1)}, u32[]{:S(2)}, u32[]{:S(2)}) %collective-permute-start.26) | collective-permute-done | bytes 196640 | tf_op jit(solution)/shard_map/ppermute | solution.py:42
  132.5 2.0 collective-permute-start.32
  136.0 5.2 %collective-permute-done.32 = bf16[128,768]{1,0:T(8,128)(2,1)S(1)} collective-permute-done((bf16[128,768]{1,0:T(8,128)(2,1)S(1)}, bf16[128,768]{1,0:T(8,128)(2,1)S(1)}, u32[]{:S(2)}, u32[]{:S(2)}) %collective-permute-start.32) | collective-permute-done | bytes 196640 | tf_op jit(solution)/shard_map/ppermute | solution.py:42
  141.2 1.8 collective-permute-done.31
  148.1 1.5 collective-permute-start.35
  150.5 6.9 %collective-permute-done.33.got_a_ref = bf16[128,768]{1,0:T(8,128)(2,1)S(1)} collective-permute-done((bf16[128,768]{1,0:T(8,128)(2,1)}, bf16[128,768]{1,0:T(8,128)(2,1)S(1)}, u32[]{:S(2)}, u32[]{:S(2)}) %collective-permute-start.33) | collective-permute-done | bytes 196640 | tf_op jit(solution)/shard_map/ppermute | solution.py:42
  157.4 1.8 convolution_convert_fusion.ff_kept_ref
  159.2 1.9 convolution_convert_fusion.1
  161.1 1.5 convolution_convert_fusion.5
  162.6 1.4 convolution_convert_fusion.4.down_kept_ref
  164.8 3.9 %back_join.1 = (f32[128,768]{1,0:T(8,128)}, bf16[16,64,128]{2,1,0:T(8,128)(2,1)}, bf16[768,384]{1,0:T(8,128)(2,1)}, bf16[768,384]{1,0:T(8,128)(2,1)}, f32[3,768]{1,0:T(4,128)}) custom-call(s32[4]{0:T(128)} %pad_add_fusion.1.place_ref, f32[128,768]{1,0:T(8,128)} %get-tuple-element.276.second_ref, bf16[128,768]{1,0:T(8,128)(2,1)} %get-tuple-element.288.own_ref, ...), custom_call_target="tpu_custom_call" | custom-call | tf_op jit(solution)/shard_map/back_join/pallas_call | solution.py:1057
  169.3 11.9 %all_to_all.51.dout_ref = bf16[16,64,128]{2,1,0:T(8,128)(2,1)} all-to-all(bf16[16,64,128]{2,1,0:T(8,128)(2,1)} %get-tuple-element.207), channel_id=1, replica_groups=mesh['u'=2,'s'=2,'f'=4,'c'=2] {'u','f','c'}, dimensions={0} | all-to-all | bytes 524288 | tf_op jit(solution)/shard_map/all_to_all | solution.py:86
  182.7 4.1 %fold_cores.1 = (bf16[2,192,768]{2,1,0:T(8,128)(2,1)}, bf16[2,192,768]{2,1,0:T(8,128)(2,1)}, bf16[384,384]{1,0:T(8,128)(2,1)}, bf16[384,384]{1,0:T(8,128)(2,1)},...) custom-call(s32[4]{0:T(128)} %pad_add_fusion.1.place_ref, bf16[768,768]{1,0:T(8,128)(2,1)} %convolution_convert_fusion.ff_kept_ref, ...), custom_call_target="tpu_custom_call" | custom-call | tf_op jit(solution)/shard_map/fold_cores/pallas_call | solution.py:1087
  188.2 1.3 collective-permute-start.41
  190.2 19.6 %attend_back.1 = bf16[4,768,128]{2,1,0:T(8,128)(2,1)} custom-call(s32[3,8]{1,0:T(4,128)} %pad_add_fusion.table_ref, f32[1,1]{1,0:T(1,128)} %bitcast.23.slope_ref, bf16[4,768,128]{2,1,0:T(8,128)(2,1)} %copy-done, bf16[16,64,128]{2,1,0:T(8,128)(2,1)} %all_to_all.51.dout_ref, f32[64,2048]{1,0:T(8,128)} %get-tuple-element.221.ot_ref, ...), custom_call_target="tpu_custom_call" | custom-call | tf_op jit(solution)/shard_map/attend_back/pallas_call | solution.py:330
  209.8 5.3 %collective-permute-done.39 = bf16[2,192,768]{2,1,0:T(8,128)(2,1)S(1)} collective-permute-done((bf16[2,192,768]{2,1,0:T(8,128)(2,1)}, bf16[2,192,768]{2,1,0:T(8,128)(2,1)S(1)}, u32[]{:S(2)}, u32[]{:S(2)}) %collective-permute-start.39) | collective-permute-done | bytes 589856 | tf_op jit(solution)/shard_map/ppermute | solution.py:42
  215.1 3.5 %all-to-all-start.4 = ((bf16[4,768,128]{2,1,0:T(8,128)(2,1)}), bf16[4,768,128]{2,1,0:T(8,128)(2,1)S(1)}, u32[]{:S(2)}, u32[]{:S(2)}) async-start(bf16[4,768,128]{2,1,0:T(8,128)(2,1)} %attend_back.1), calls=%async_computation.4 | async-start | bytes 1572864 | tf_op jit(solution)/shard_map/all_to_all | solution.py:86
  218.8 2.0 collective-permute-start.42
  221.1 7.8 %collective-permute-done.43 = bf16[192,384]{1,0:T(8,128)(2,1)S(1)} collective-permute-done((bf16[192,384]{1,0:T(8,128)(2,1)S(1)}, bf16[192,384]{1,0:T(8,128)(2,1)S(1)}, u32[]{:S(2)}, u32[]{:S(2)}) %collective-permute-start.43) | collective-permute-done | bytes 147488 | tf_op jit(solution)/shard_map/ppermute | solution.py:42
  229.0 7.5 %collective-permute-done.42 = bf16[192,768]{1,0:T(8,128)(2,1)S(1)} collective-permute-done((bf16[192,768]{1,0:T(8,128)(2,1)S(1)}, bf16[192,768]{1,0:T(8,128)(2,1)S(1)}, u32[]{:S(2)}, u32[]{:S(2)}) %collective-permute-start.42) | collective-permute-done | bytes 294944 | tf_op jit(solution)/shard_map/ppermute | solution.py:42
  238.7 3.0 %collective-permute-start.50 = (bf16[192,384]{1,0:T(8,128)(2,1)S(1)}, bf16[192,384]{1,0:T(8,128)(2,1)S(1)}, u32[]{:S(2)}, u32[]{:S(2)}) collective-permute-start(bf16[192,384]{1,0:T(8,128)(2,1)S(1)} %select_bitcast_fusion.2), channel_id=1, source_target_pairs={{0,8},{8,0},{1,9},{9,1},{2,10},{10,2},{3,11},{11,3},{4,12},{12,4},... | collective-permute-start | bytes 442376 | tf_op jit(solution)/shard_map/ppermute | solution.py:42
  241.7 2.2 collect.1.refs_4_
  243.9 3.5 %grad_qkv.1 = (bf16[16,24,768]{2,1,0:T(8,128)(2,1)}, bf16[16,24,768]{2,1,0:T(8,128)(2,1)}) custom-call(s32[4]{0:T(128)} %pad_add_fusion.1.place_ref, bf16[128,768]{1,0:T(8,128)(2,1)} %copy-done.3, bf16[128,768]{1,0:T(8,128)(2,1)} %copy-done.13, bf16[128,768]{1,0:T(8,128)(2,1)} %copy-done.12, bf16[128,768]{1,0:T(8,128)(2,1)} %copy-done.11, ...), custom_call_target="tpu_custom_call" | custom-call | tf_op jit(solution)/shard_map/grad_qkv/pallas_call | solution.py:1142
  247.4 2.1 convolution_convert_fusion.2
  251.7 2.4 collective-permute-start.47
  255.2 3.6 %all-to-all-start.5 = ((bf16[16,24,768]{2,1,0:T(8,128)(2,1)}), bf16[16,24,768]{2,1,0:T(8,128)(2,1)S(1)}, u32[]{:S(2)}, u32[]{:S(2)}) async-start(bf16[16,24,768]{2,1,0:T(8,128)(2,1)} %add_convert_fusion.1), calls=%async_computation.5 | async-start | bytes 1179648 | tf_op jit(solution)/shard_map/all_to_all | solution.py:86
  258.8 2.5 collective-permute-done.46
  261.3 3.2 %collective-permute-done.47 = bf16[128,768]{1,0:T(8,128)(2,1)} collective-permute-done((bf16[128,768]{1,0:T(8,128)(2,1)S(1)}, bf16[128,768]{1,0:T(8,128)(2,1)}, u32[]{:S(2)}, u32[]{:S(2)}) %collective-permute-start.47) | collective-permute-done | bytes 196640 | tf_op jit(solution)/shard_map/ppermute | solution.py:42
  267.6 2.6 collective-permute-start.52
  270.8 4.1 %collective-permute-done.53.refs_3_ = bf16[48,1152]{1,0:T(8,128)(2,1)S(1)} collective-permute-done((bf16[48,1152]{1,0:T(8,128)(2,1)S(1)}, bf16[48,1152]{1,0:T(8,128)(2,1)S(1)}, u32[]{:S(2)}, u32[]{:S(2)}) %collective-permute-start.53) | collective-permute-done | bytes 110624 | tf_op jit(solution)/shard_map/ppermute | solution.py:42
  275.0 2.6 collective-permute-done.52.refs_2_
  278.2 1.8 finish_late.1
  282.3 2.2 finish_wide.1
  285.4 1.9 finish.1
  (259 shorter events, 54.1 us)
Async XLA Ops:
  1.6 9.0 %collective-permute-start.4 = (bf16[64,768]{1,0:T(8,128)(2,1)S(1)}, bf16[64,768]{1,0:T(8,128)(2,1)S(1)}, u32[]{:S(2)}, u32[]{:S(2)}) collective-permute-start(bf16[64,768]{1,0:T(8,128)(2,1)S(1)} %select_bitcast_fusion.8), channel_id=1, source_target_pairs={{0,8},{8,0},{1,9},{9,1},{2,10},{10,2},{3,11},{11,3},{4,12},{12,4},... | collective-permute-start | bytes 294920 | tf_op jit(solution)/shard_map/ppermute | solution.py:42
  11.6 33.0 %all-to-all-start = ((bf16[32,24,384]{2,1,0:T(8,128)(2,1)}), bf16[32,24,384]{2,1,0:T(8,128)(2,1)S(1)}, u32[]{:S(2)}, u32[]{:S(2)}) async-start(bf16[32,24,384]{2,1,0:T(8,128)(2,1)} %bitcast.105), calls=%async_computation | async-start | bytes 1179648 | tf_op jit(solution)/shard_map/all_to_all | solution.py:86
  19.9 1.7 collective-permute-start
  24.1 6.7 %collective-permute-start.1 = (bf16[48,1152]{1,0:T(8,128)(2,1)}, bf16[48,1152]{1,0:T(8,128)(2,1)S(1)}, u32[]{:S(2)}, u32[]{:S(2)}) collective-permute-start(bf16[48,1152]{1,0:T(8,128)(2,1)} %get-tuple-element.144), channel_id=1, source_target_pairs={{0,2},{2,0},{4,6},{6,4},{1,3},{3,1},{5,7},{7,5},{8,10},{10,8},{12,... | collective-permute-start | bytes 331784 | tf_op jit(solution)/shard_map/ppermute | solution.py:42
  25.9 8.5 %collective-permute-start.2 = (bf16[48,1152]{1,0:T(8,128)(2,1)}, bf16[48,1152]{1,0:T(8,128)(2,1)S(1)}, u32[]{:S(2)}, u32[]{:S(2)}) collective-permute-start(bf16[48,1152]{1,0:T(8,128)(2,1)} %get-tuple-element.145), channel_id=1, source_target_pairs={{0,4},{2,6},{4,0},{6,2},{1,5},{3,7},{5,1},{7,3},{8,12},{10,14},{12... | collective-permute-start | bytes 331784 | tf_op jit(solution)/shard_map/ppermute | solution.py:42
  27.4 9.6 %collective-permute-start.3 = (bf16[48,1152]{1,0:T(8,128)(2,1)}, bf16[48,1152]{1,0:T(8,128)(2,1)S(1)}, u32[]{:S(2)}, u32[]{:S(2)}) collective-permute-start(bf16[48,1152]{1,0:T(8,128)(2,1)} %get-tuple-element.146), channel_id=1, source_target_pairs={{0,6},{2,4},{4,2},{6,0},{1,7},{3,5},{5,3},{7,1},{8,14},{10,12},{12... | collective-permute-start | bytes 331784 | tf_op jit(solution)/shard_map/ppermute | solution.py:42
  27.6 13.5 %collective-permute-start.7 = (bf16[128,768]{1,0:T(8,128)(2,1)S(1)}, bf16[128,768]{1,0:T(8,128)(2,1)S(1)}, u32[]{:S(2)}, u32[]{:S(2)}) collective-permute-start(bf16[128,768]{1,0:T(8,128)(2,1)S(1)} %pad_maximum_fusion.2.refs_0_.tokens_ref), channel_id=1, source_target_pairs={{0,6},{2,4},{4,2},{6,0},{1,7},{3,5},{5,3},{7,1},{8,14},{10,12},{12... | collective-permute-start | bytes 589832 | tf_op jit(solution)/shard_map/ppermute | solution.py:42
  30.3 14.3 %collective-permute-start.6 = (bf16[128,768]{1,0:T(8,128)(2,1)S(1)}, bf16[128,768]{1,0:T(8,128)(2,1)S(1)}, u32[]{:S(2)}, u32[]{:S(2)}) collective-permute-start(bf16[128,768]{1,0:T(8,128)(2,1)S(1)} %pad_maximum_fusion.2.refs_0_.tokens_ref), channel_id=1, source_target_pairs={{0,4},{2,6},{4,0},{6,2},{1,5},{3,7},{5,1},{7,3},{8,12},{10,14},{12... | collective-permute-start | bytes 589832 | tf_op jit(solution)/shard_map/ppermute | solution.py:42
  30.9 13.7 %collective-permute-start.5 = (bf16[128,768]{1,0:T(8,128)(2,1)S(1)}, bf16[128,768]{1,0:T(8,128)(2,1)S(1)}, u32[]{:S(2)}, u32[]{:S(2)}) collective-permute-start(bf16[128,768]{1,0:T(8,128)(2,1)S(1)} %pad_maximum_fusion.2.refs_0_.tokens_ref), channel_id=1, source_target_pairs={{0,2},{2,0},{4,6},{6,4},{1,3},{3,1},{5,7},{7,5},{8,10},{10,8},{12,... | collective-permute-start | bytes 589832 | tf_op jit(solution)/shard_map/ppermute | solution.py:42
  44.6 3.4 %collective-permute-start.8 = (bf16[768,384]{1,0:T(8,128)(2,1)S(1)}, bf16[768,384]{1,0:T(8,128)(2,1)S(1)}, u32[]{:S(2)}, u32[]{:S(2)}) collective-permute-start(bf16[768,384]{1,0:T(8,128)(2,1)S(1)} %bitcast.106), channel_id=1, source_target_pairs={{0,1},{1,0},{2,3},{3,2},{4,5},{5,4},{6,7},{7,6},{8,9},{9,8},{10,11... | collective-permute-start | bytes 1769480 | tf_op jit(solution)/shard_map/ppermute | solution.py:42
  44.8 47.7 %copy-start.21 = (bf16[384,384]{1,0:T(8,128)(2,1)}, bf16[384,384]{1,0:T(8,128)(2,1)S(1)}, u32[]{:S(2)}) copy-start(bf16[384,384]{1,0:T(8,128)(2,1)S(1)} %slice_dynamic-update-slice_fusion.refs_0_) | copy-start | bytes 884740
  44.8 11.8 %collective-permute-start.11 = (bf16[384,384]{1,0:T(8,128)(2,1)S(1)}, bf16[384,384]{1,0:T(8,128)(2,1)S(1)}, u32[]{:S(2)}, u32[]{:S(2)}) collective-permute-start(bf16[384,384]{1,0:T(8,128)(2,1)S(1)} %slice_dynamic-update-slice_fusion.refs_0_), channel_id=1, source_target_pairs={{0,16},{16,0},{1,17},{17,1},{2,18},{18,2},{3,19},{19,3},{4,20},{20... | collective-permute-start | bytes 884744 | tf_op jit(solution)/shard_map/ppermute | solution.py:42
  46.3 16.0 %collective-permute-start.9 = (bf16[384,384]{1,0:T(8,128)(2,1)S(1)}, bf16[384,384]{1,0:T(8,128)(2,1)S(1)}, u32[]{:S(2)}, u32[]{:S(2)}) collective-permute-start(bf16[384,384]{1,0:T(8,128)(2,1)S(1)} %slice_dynamic-update-slice_fusion.refs_0_), channel_id=1, source_target_pairs={{0,8},{8,0},{1,9},{9,1},{2,10},{10,2},{3,11},{11,3},{4,12},{12,4},... | collective-permute-start | bytes 884744 | tf_op jit(solution)/shard_map/ppermute | solution.py:42
  52.1 15.7 %all-to-all-start.1 = ((bf16[4,768,128]{2,1,0:T(8,128)(2,1)}), bf16[4,768,128]{2,1,0:T(8,128)(2,1)S(1)}, u32[]{:S(2)}, u32[]{:S(2)}) async-start(bf16[4,768,128]{2,1,0:T(8,128)(2,1)} %get-tuple-element.156), calls=%async_computation.1 | async-start | bytes 1572864 | tf_op jit(solution)/shard_map/all_to_all | solution.py:86
  55.9 8.9 %collective-permute-start.12 = (bf16[384,384]{1,0:T(8,128)(2,1)S(1)}, bf16[384,384]{1,0:T(8,128)(2,1)S(1)}, u32[]{:S(2)}, u32[]{:S(2)}) collective-permute-start(bf16[384,384]{1,0:T(8,128)(2,1)S(1)} %slice_dynamic-update-slice_fusion.refs_0_), channel_id=1, source_target_pairs={{0,1},{1,0},{2,3},{3,2},{4,5},{5,4},{6,7},{7,6},{8,9},{9,8},{10,11... | collective-permute-start | bytes 884744 | tf_op jit(solution)/shard_map/ppermute | solution.py:42
  56.4 49.5 %copy-start.6 = (bf16[192,768]{1,0:T(8,128)(2,1)}, bf16[192,768]{1,0:T(8,128)(2,1)S(1)}, u32[]{:S(2)}) copy-start(bf16[192,768]{1,0:T(8,128)(2,1)S(1)} %pad_maximum_fusion.1.refs_0_) | copy-start | bytes 884740
  56.4 8.4 %collective-permute-start.10 = (bf16[192,768]{1,0:T(8,128)(2,1)S(1)}, bf16[192,768]{1,0:T(8,128)(2,1)S(1)}, u32[]{:S(2)}, u32[]{:S(2)}) collective-permute-start(bf16[192,768]{1,0:T(8,128)(2,1)S(1)} %pad_maximum_fusion.1.refs_0_), channel_id=1, source_target_pairs={{0,1},{1,0},{2,3},{3,2},{4,5},{5,4},{6,7},{7,6},{8,9},{9,8},{10,11... | collective-permute-start | bytes 884744 | tf_op jit(solution)/shard_map/ppermute | solution.py:42
  56.5 8.3 %collective-permute-start.14 = (bf16[384,384]{1,0:T(8,128)(2,1)S(1)}, bf16[384,384]{1,0:T(8,128)(2,1)S(1)}, u32[]{:S(2)}, u32[]{:S(2)}) collective-permute-start(bf16[384,384]{1,0:T(8,128)(2,1)S(1)} %collective-permute-done.11.refs_2_), channel_id=1, source_target_pairs={{0,1},{1,0},{2,3},{3,2},{4,5},{5,4},{6,7},{7,6},{8,9},{9,8},{10,11... | collective-permute-start | bytes 884744 | tf_op jit(solution)/shard_map/ppermute | solution.py:42
  62.3 2.6 collective-permute-start.13
  63.0 21.7 %collective-permute-start.16 = (bf16[192,768]{1,0:T(8,128)(2,1)S(1)}, bf16[192,768]{1,0:T(8,128)(2,1)}, u32[]{:S(2)}, u32[]{:S(2)}) collective-permute-start(bf16[192,768]{1,0:T(8,128)(2,1)S(1)} %pad_maximum_fusion.1.refs_0_), channel_id=1, source_target_pairs={{0,16},{16,0},{1,17},{17,1},{2,18},{18,2},{3,19},{19,3},{4,20},{20... | collective-permute-start | bytes 884744 | tf_op jit(solution)/shard_map/ppermute | solution.py:42
  64.8 19.9 %collective-permute-start.15 = (bf16[192,768]{1,0:T(8,128)(2,1)S(1)}, bf16[192,768]{1,0:T(8,128)(2,1)}, u32[]{:S(2)}, u32[]{:S(2)}) collective-permute-start(bf16[192,768]{1,0:T(8,128)(2,1)S(1)} %pad_maximum_fusion.1.refs_0_), channel_id=1, source_target_pairs={{0,8},{8,0},{1,9},{9,1},{2,10},{10,2},{3,11},{11,3},{4,12},{12,4},... | collective-permute-start | bytes 884744 | tf_op jit(solution)/shard_map/ppermute | solution.py:42
  64.9 41.1 %copy-start.22 = (bf16[192,768]{1,0:T(8,128)(2,1)}, bf16[192,768]{1,0:T(8,128)(2,1)S(1)}, u32[]{:S(2)}) copy-start(bf16[192,768]{1,0:T(8,128)(2,1)S(1)} %collective-permute-done.10.refs_4_) | copy-start | bytes 884740
  67.9 16.8 %collective-permute-start.17 = (bf16[384,384]{1,0:T(8,128)(2,1)S(1)}, bf16[384,384]{1,0:T(8,128)(2,1)}, u32[]{:S(2)}, u32[]{:S(2)}) collective-permute-start(bf16[384,384]{1,0:T(8,128)(2,1)S(1)} %collective-permute-done.9.refs_1_), channel_id=1, source_target_pairs={{0,16},{16,0},{1,17},{17,1},{2,18},{18,2},{3,19},{19,3},{4,20},{20... | collective-permute-start | bytes 884744 | tf_op jit(solution)/shard_map/ppermute | solution.py:42
  84.7 13.0 %all-to-all-start.2 = ((bf16[16,64,128]{2,1,0:T(8,128)(2,1)}), bf16[16,64,128]{2,1,0:T(8,128)(2,1)S(1)}, u32[]{:S(2)}, u32[]{:S(2)}) async-start(bf16[16,64,128]{2,1,0:T(8,128)(2,1)} %get-tuple-element.165), calls=%async_computation.2 | async-start | bytes 524288 | tf_op jit(solution)/shard_map/all_to_all | solution.py:86
  88.8 3.7 %collective-permute-start.20 = (bf16[384,384]{1,0:T(8,128)(2,1)}, bf16[384,384]{1,0:T(8,128)(2,1)}, u32[]{:S(2)}, u32[]{:S(2)}) collective-permute-start(bf16[384,384]{1,0:T(8,128)(2,1)} %collective-permute-done.17.refs_3_), channel_id=1, source_target_pairs={{0,1},{1,0},{2,3},{3,2},{4,5},{5,4},{6,7},{7,6},{8,9},{9,8},{10,11... | collective-permute-start | bytes 884744 | tf_op jit(solution)/shard_map/ppermute | solution.py:42
  89.2 6.6 %collective-permute-start.19 = (bf16[192,768]{1,0:T(8,128)(2,1)}, bf16[192,768]{1,0:T(8,128)(2,1)S(1)}, u32[]{:S(2)}, u32[]{:S(2)}) collective-permute-start(bf16[192,768]{1,0:T(8,128)(2,1)} %collective-permute-done.16.refs_2_), channel_id=1, source_target_pairs={{0,1},{1,0},{2,3},{3,2},{4,5},{5,4},{6,7},{7,6},{8,9},{9,8},{10,11... | collective-permute-start | bytes 884744 | tf_op jit(solution)/shard_map/ppermute | solution.py:42
  89.3 6.5 %collective-permute-start.18 = (bf16[192,768]{1,0:T(8,128)(2,1)}, bf16[192,768]{1,0:T(8,128)(2,1)S(1)}, u32[]{:S(2)}, u32[]{:S(2)}) collective-permute-start(bf16[192,768]{1,0:T(8,128)(2,1)} %collective-permute-done.15.refs_1_), channel_id=1, source_target_pairs={{0,1},{1,0},{2,3},{3,2},{4,5},{5,4},{6,7},{7,6},{8,9},{9,8},{10,11... | collective-permute-start | bytes 884744 | tf_op jit(solution)/shard_map/ppermute | solution.py:42
  89.7 11.7 %collective-permute-start.21 = (bf16[192,768]{1,0:T(8,128)(2,1)}, bf16[192,768]{1,0:T(8,128)(2,1)}, u32[]{:S(2)}, u32[]{:S(2)}) collective-permute-start(bf16[192,768]{1,0:T(8,128)(2,1)} %collective-permute-done.15.refs_1_), channel_id=1, source_target_pairs={{0,16},{16,0},{1,17},{17,1},{2,18},{18,2},{3,19},{19,3},{4,20},{20... | collective-permute-start | bytes 884744 | tf_op jit(solution)/shard_map/ppermute | solution.py:42
  91.4 14.5 %collective-permute-start.29 = (bf16[64,768]{1,0:T(8,128)(2,1)S(1)}, bf16[64,768]{1,0:T(8,128)(2,1)S(1)}, u32[]{:S(2)}, u32[]{:S(2)}) collective-permute-start(bf16[64,768]{1,0:T(8,128)(2,1)S(1)} %select_bitcast_fusion.7), channel_id=1, source_target_pairs={{0,8},{8,0},{1,9},{9,1},{2,10},{10,2},{3,11},{11,3},{4,12},{12,4},... | collective-permute-start | bytes 294920 | tf_op jit(solution)/shard_map/ppermute | solution.py:42
  101.4 4.5 %collective-permute-start.22 = (bf16[192,768]{1,0:T(8,128)(2,1)}, bf16[192,768]{1,0:T(8,128)(2,1)S(1)}, u32[]{:S(2)}, u32[]{:S(2)}) collective-permute-start(bf16[192,768]{1,0:T(8,128)(2,1)} %collective-permute-done.21.refs_3_), channel_id=1, source_target_pairs={{0,1},{1,0},{2,3},{3,2},{4,5},{5,4},{6,7},{7,6},{8,9},{9,8},{10,11... | collective-permute-start | bytes 884744 | tf_op jit(solution)/shard_map/ppermute | solution.py:42
  102.3 8.9 %collective-permute-start.25 = (bf16[128,768]{1,0:T(8,128)(2,1)}, bf16[128,768]{1,0:T(8,128)(2,1)S(1)}, u32[]{:S(2)}, u32[]{:S(2)}) collective-permute-start(bf16[128,768]{1,0:T(8,128)(2,1)} %get-tuple-element.185), channel_id=1, source_target_pairs={{0,6},{2,4},{4,2},{6,0},{1,7},{3,5},{5,3},{7,1},{8,14},{10,12},{12... | collective-permute-start | bytes 589832 | tf_op jit(solution)/shard_map/ppermute | solution.py:42
  104.4 10.3 %collective-permute-start.24 = (bf16[128,768]{1,0:T(8,128)(2,1)}, bf16[128,768]{1,0:T(8,128)(2,1)S(1)}, u32[]{:S(2)}, u32[]{:S(2)}) collective-permute-start(bf16[128,768]{1,0:T(8,128)(2,1)} %get-tuple-element.185), channel_id=1, source_target_pairs={{0,4},{2,6},{4,0},{6,2},{1,5},{3,7},{5,1},{7,3},{8,12},{10,14},{12... | collective-permute-start | bytes 589832 | tf_op jit(solution)/shard_map/ppermute | solution.py:42
  105.0 10.0 %collective-permute-start.23 = (bf16[128,768]{1,0:T(8,128)(2,1)}, bf16[128,768]{1,0:T(8,128)(2,1)S(1)}, u32[]{:S(2)}, u32[]{:S(2)}) collective-permute-start(bf16[128,768]{1,0:T(8,128)(2,1)} %get-tuple-element.185), channel_id=1, source_target_pairs={{0,2},{2,0},{4,6},{6,4},{1,3},{3,1},{5,7},{7,5},{8,10},{10,8},{12,... | collective-permute-start | bytes 589832 | tf_op jit(solution)/shard_map/ppermute | solution.py:42
  118.5 11.1 %collective-permute-start.26 = (bf16[128,768]{1,0:T(8,128)(2,1)S(1)}, bf16[128,768]{1,0:T(8,128)(2,1)S(1)}, u32[]{:S(2)}, u32[]{:S(2)}) collective-permute-start(bf16[128,768]{1,0:T(8,128)(2,1)S(1)} %get-tuple-element.290), channel_id=1, source_target_pairs={{0,2},{2,0},{4,6},{6,4},{1,3},{3,1},{5,7},{7,5},{8,10},{10,8},{12,... | collective-permute-start | bytes 589832 | tf_op jit(solution)/shard_map/ppermute | solution.py:42
  119.7 9.9 %collective-permute-start.28 = (bf16[128,768]{1,0:T(8,128)(2,1)S(1)}, bf16[128,768]{1,0:T(8,128)(2,1)S(1)}, u32[]{:S(2)}, u32[]{:S(2)}) collective-permute-start(bf16[128,768]{1,0:T(8,128)(2,1)S(1)} %get-tuple-element.291), channel_id=1, source_target_pairs={{0,6},{2,4},{4,2},{6,0},{1,7},{3,5},{5,3},{7,1},{8,14},{10,12},{12... | collective-permute-start | bytes 589832 | tf_op jit(solution)/shard_map/ppermute | solution.py:42
  121.2 9.6 %collective-permute-start.27 = (bf16[128,768]{1,0:T(8,128)(2,1)S(1)}, bf16[128,768]{1,0:T(8,128)(2,1)S(1)}, u32[]{:S(2)}, u32[]{:S(2)}) collective-permute-start(bf16[128,768]{1,0:T(8,128)(2,1)S(1)} %get-tuple-element.292), channel_id=1, source_target_pairs={{0,4},{2,6},{4,0},{6,2},{1,5},{3,7},{5,1},{7,3},{8,12},{10,14},{12... | collective-permute-start | bytes 589832 | tf_op jit(solution)/shard_map/ppermute | solution.py:42
  132.5 8.7 %collective-permute-start.32 = (bf16[128,768]{1,0:T(8,128)(2,1)S(1)}, bf16[128,768]{1,0:T(8,128)(2,1)S(1)}, u32[]{:S(2)}, u32[]{:S(2)}) collective-permute-start(bf16[128,768]{1,0:T(8,128)(2,1)S(1)} %get-tuple-element.275), channel_id=1, source_target_pairs={{0,6},{2,4},{4,2},{6,0},{1,7},{3,5},{5,3},{7,1},{8,14},{10,12},{12... | collective-permute-start | bytes 589832 | tf_op jit(solution)/shard_map/ppermute | solution.py:42
  134.5 8.5 %collective-permute-start.31 = (bf16[128,768]{1,0:T(8,128)(2,1)S(1)}, bf16[128,768]{1,0:T(8,128)(2,1)S(1)}, u32[]{:S(2)}, u32[]{:S(2)}) collective-permute-start(bf16[128,768]{1,0:T(8,128)(2,1)S(1)} %get-tuple-element.275), channel_id=1, source_target_pairs={{0,4},{2,6},{4,0},{6,2},{1,5},{3,7},{5,1},{7,3},{8,12},{10,14},{12... | collective-permute-start | bytes 589832 | tf_op jit(solution)/shard_map/ppermute | solution.py:42
  135.1 8.2 %collective-permute-start.30 = (bf16[128,768]{1,0:T(8,128)(2,1)S(1)}, bf16[128,768]{1,0:T(8,128)(2,1)S(1)}, u32[]{:S(2)}, u32[]{:S(2)}) collective-permute-start(bf16[128,768]{1,0:T(8,128)(2,1)S(1)} %get-tuple-element.275), channel_id=1, source_target_pairs={{0,2},{2,0},{4,6},{6,4},{1,3},{3,1},{5,7},{7,5},{8,10},{10,8},{12,... | collective-permute-start | bytes 589832 | tf_op jit(solution)/shard_map/ppermute | solution.py:42
  147.0 10.4 %collective-permute-start.33 = (bf16[128,768]{1,0:T(8,128)(2,1)}, bf16[128,768]{1,0:T(8,128)(2,1)S(1)}, u32[]{:S(2)}, u32[]{:S(2)}) collective-permute-start(bf16[128,768]{1,0:T(8,128)(2,1)} %get-tuple-element.289), channel_id=1, source_target_pairs={{0,2},{2,0},{4,6},{6,4},{1,3},{3,1},{5,7},{7,5},{8,10},{10,8},{12,... | collective-permute-start | bytes 589832 | tf_op jit(solution)/shard_map/ppermute | solution.py:42
  148.1 15.9 %collective-permute-start.35 = (bf16[128,768]{1,0:T(8,128)(2,1)S(1)}, bf16[128,768]{1,0:T(8,128)(2,1)S(1)}, u32[]{:S(2)}, u32[]{:S(2)}) collective-permute-start(bf16[128,768]{1,0:T(8,128)(2,1)S(1)} %get-tuple-element.286), channel_id=1, source_target_pairs={{0,6},{2,4},{4,2},{6,0},{1,7},{3,5},{5,3},{7,1},{8,14},{10,12},{12... | collective-permute-start | bytes 589832 | tf_op jit(solution)/shard_map/ppermute | solution.py:42
  149.6 14.4 %collective-permute-start.34 = (bf16[128,768]{1,0:T(8,128)(2,1)S(1)}, bf16[128,768]{1,0:T(8,128)(2,1)S(1)}, u32[]{:S(2)}, u32[]{:S(2)}) collective-permute-start(bf16[128,768]{1,0:T(8,128)(2,1)S(1)} %get-tuple-element.287), channel_id=1, source_target_pairs={{0,4},{2,6},{4,0},{6,2},{1,5},{3,7},{5,1},{7,3},{8,12},{10,14},{12... | collective-permute-start | bytes 589832 | tf_op jit(solution)/shard_map/ppermute | solution.py:42
  168.7 12.5 %collective-permute-start.36 = (bf16[768,768]{1,0:T(8,128)(2,1)}, bf16[768,768]{1,0:T(8,128)(2,1)S(1)}, u32[]{:S(2)}, u32[]{:S(2)}) collective-permute-start(bf16[768,768]{1,0:T(8,128)(2,1)} %convolution_convert_fusion.1), channel_id=1, source_target_pairs={{0,1},{1,0},{2,3},{3,2},{4,5},{5,4},{6,7},{7,6},{8,9},{9,8},{10,11... | collective-permute-start | bytes 3538952 | tf_op jit(solution)/shard_map/ppermute | solution.py:42
  168.7 12.5 %collective-permute-start.37 = (bf16[768,384]{1,0:T(8,128)(2,1)}, bf16[768,384]{1,0:T(8,128)(2,1)S(1)}, u32[]{:S(2)}, u32[]{:S(2)}) collective-permute-start(bf16[768,384]{1,0:T(8,128)(2,1)} %convolution_convert_fusion.5), channel_id=1, source_target_pairs={{0,1},{1,0},{2,3},{3,2},{4,5},{5,4},{6,7},{7,6},{8,9},{9,8},{10,11... | collective-permute-start | bytes 1769480 | tf_op jit(solution)/shard_map/ppermute | solution.py:42
  169.2 12.0 %collective-permute-start.38 = (bf16[768,384]{1,0:T(8,128)(2,1)}, bf16[768,384]{1,0:T(8,128)(2,1)S(1)}, u32[]{:S(2)}, u32[]{:S(2)}) collective-permute-start(bf16[768,384]{1,0:T(8,128)(2,1)} %get-tuple-element.216), channel_id=1, source_target_pairs={{0,1},{1,0},{2,3},{3,2},{4,5},{5,4},{6,7},{7,6},{8,9},{9,8},{10,11... | collective-permute-start | bytes 1769480 | tf_op jit(solution)/shard_map/ppermute | solution.py:42
  186.8 28.3 %collective-permute-start.39 = (bf16[2,192,768]{2,1,0:T(8,128)(2,1)}, bf16[2,192,768]{2,1,0:T(8,128)(2,1)S(1)}, u32[]{:S(2)}, u32[]{:S(2)}) collective-permute-start(bf16[2,192,768]{2,1,0:T(8,128)(2,1)} %get-tuple-element.223), channel_id=1, source_target_pairs={{0,8},{8,0},{1,9},{9,1},{2,10},{10,2},{3,11},{11,3},{4,12},{12,4},... | collective-permute-start | bytes 1769480 | tf_op jit(solution)/shard_map/ppermute | solution.py:42
  187.6 22.3 %collective-permute-start.40 = (bf16[384,384]{1,0:T(8,128)(2,1)}, bf16[384,384]{1,0:T(8,128)(2,1)S(1)}, u32[]{:S(2)}, u32[]{:S(2)}) collective-permute-start(bf16[384,384]{1,0:T(8,128)(2,1)} %get-tuple-element.224), channel_id=1, source_target_pairs={{0,16},{16,0},{1,17},{17,1},{2,18},{18,2},{3,19},{19,3},{4,20},{20... | collective-permute-start | bytes 884744 | tf_op jit(solution)/shard_map/ppermute | solution.py:42
  188.2 21.6 %collective-permute-start.41 = (bf16[384,384]{1,0:T(8,128)(2,1)}, bf16[384,384]{1,0:T(8,128)(2,1)S(1)}, u32[]{:S(2)}, u32[]{:S(2)}) collective-permute-start(bf16[384,384]{1,0:T(8,128)(2,1)} %get-tuple-element.225), channel_id=1, source_target_pairs={{0,16},{16,0},{1,17},{17,1},{2,18},{18,2},{3,19},{19,3},{4,20},{20... | collective-permute-start | bytes 884744 | tf_op jit(solution)/shard_map/ppermute | solution.py:42
  215.1 21.4 %all-to-all-start.4 = ((bf16[4,768,128]{2,1,0:T(8,128)(2,1)}), bf16[4,768,128]{2,1,0:T(8,128)(2,1)S(1)}, u32[]{:S(2)}, u32[]{:S(2)}) async-start(bf16[4,768,128]{2,1,0:T(8,128)(2,1)} %attend_back.1), calls=%async_computation.4 | async-start | bytes 1572864 | tf_op jit(solution)/shard_map/all_to_all | solution.py:86
  218.8 17.7 %collective-permute-start.42 = (bf16[192,768]{1,0:T(8,128)(2,1)S(1)}, bf16[192,768]{1,0:T(8,128)(2,1)S(1)}, u32[]{:S(2)}, u32[]{:S(2)}) collective-permute-start(bf16[192,768]{1,0:T(8,128)(2,1)S(1)} %get-tuple-element.294), channel_id=1, source_target_pairs={{0,16},{16,0},{1,17},{17,1},{2,18},{18,2},{3,19},{19,3},{4,20},{20... | collective-permute-start | bytes 884744 | tf_op jit(solution)/shard_map/ppermute | solution.py:42
  221.0 8.0 %collective-permute-start.43 = (bf16[192,384]{1,0:T(8,128)(2,1)S(1)}, bf16[192,384]{1,0:T(8,128)(2,1)S(1)}, u32[]{:S(2)}, u32[]{:S(2)}) collective-permute-start(bf16[192,384]{1,0:T(8,128)(2,1)S(1)} %broadcast_select_fusion), channel_id=1, source_target_pairs={{0,8},{8,0},{1,9},{9,1},{2,10},{10,2},{3,11},{11,3},{4,12},{12,4},... | collective-permute-start | bytes 442376 | tf_op jit(solution)/shard_map/ppermute | solution.py:42
  238.0 42.8 %collective-permute-start.55 = (bf16[96,384]{1,0:T(8,128)(2,1)}, bf16[96,384]{1,0:T(8,128)(2,1)}, u32[]{:S(2)}, u32[]{:S(2)}) collective-permute-start(bf16[96,384]{1,0:T(8,128)(2,1)} %select_convert_fusion), channel_id=1, source_target_pairs={{0,1},{1,0},{2,3},{3,2},{4,5},{5,4},{6,7},{7,6},{8,9},{9,8},{10,11... | collective-permute-start | bytes 221192 | tf_op jit(solution)/shard_map/ppermute | solution.py:42
  238.7 11.6 %collective-permute-start.44 = (bf16[64,768]{1,0:T(8,128)(2,1)}, bf16[64,768]{1,0:T(8,128)(2,1)}, u32[]{:S(2)}, u32[]{:S(2)}) collective-permute-start(bf16[64,768]{1,0:T(8,128)(2,1)} %broadcast_select_fusion.5), channel_id=1, source_target_pairs={{0,8},{8,0},{1,9},{9,1},{2,10},{10,2},{3,11},{11,3},{4,12},{12,4},... | collective-permute-start | bytes 294920 | tf_op jit(solution)/shard_map/ppermute | solution.py:42
  238.7 13.0 %collective-permute-start.50 = (bf16[192,384]{1,0:T(8,128)(2,1)S(1)}, bf16[192,384]{1,0:T(8,128)(2,1)S(1)}, u32[]{:S(2)}, u32[]{:S(2)}) collective-permute-start(bf16[192,384]{1,0:T(8,128)(2,1)S(1)} %select_bitcast_fusion.2), channel_id=1, source_target_pairs={{0,8},{8,0},{1,9},{9,1},{2,10},{10,2},{3,11},{11,3},{4,12},{12,4},... | collective-permute-start | bytes 442376 | tf_op jit(solution)/shard_map/ppermute | solution.py:42
  247.4 6.8 %collective-permute-start.45 = (bf16[16,24,768]{2,1,0:T(8,128)(2,1)}, bf16[16,24,768]{2,1,0:T(8,128)(2,1)S(1)}, u32[]{:S(2)}, u32[]{:S(2)}) collective-permute-start(bf16[16,24,768]{2,1,0:T(8,128)(2,1)} %get-tuple-element.237), channel_id=1, source_target_pairs={{0,1},{1,0},{2,3},{3,2},{4,5},{5,4},{6,7},{7,6},{8,9},{9,8},{10,11... | collective-permute-start | bytes 1769480 | tf_op jit(solution)/shard_map/ppermute | solution.py:42
  249.6 11.7 %collective-permute-start.46 = (bf16[128,768]{1,0:T(8,128)(2,1)S(1)}, bf16[128,768]{1,0:T(8,128)(2,1)}, u32[]{:S(2)}, u32[]{:S(2)}) collective-permute-start(bf16[128,768]{1,0:T(8,128)(2,1)S(1)} %get-tuple-element.283), channel_id=1, source_target_pairs={{0,2},{2,0},{4,6},{6,4},{1,3},{3,1},{5,7},{7,5},{8,10},{10,8},{12,... | collective-permute-start | bytes 589832 | tf_op jit(solution)/shard_map/ppermute | solution.py:42
  250.3 11.0 %collective-permute-start.48 = (bf16[128,768]{1,0:T(8,128)(2,1)S(1)}, bf16[128,768]{1,0:T(8,128)(2,1)}, u32[]{:S(2)}, u32[]{:S(2)}) collective-permute-start(bf16[128,768]{1,0:T(8,128)(2,1)S(1)} %get-tuple-element.284), channel_id=1, source_target_pairs={{0,6},{2,4},{4,2},{6,0},{1,7},{3,5},{5,3},{7,1},{8,14},{10,12},{12... | collective-permute-start | bytes 589832 | tf_op jit(solution)/shard_map/ppermute | solution.py:42
  251.7 12.8 %collective-permute-start.47 = (bf16[128,768]{1,0:T(8,128)(2,1)S(1)}, bf16[128,768]{1,0:T(8,128)(2,1)}, u32[]{:S(2)}, u32[]{:S(2)}) collective-permute-start(bf16[128,768]{1,0:T(8,128)(2,1)S(1)} %get-tuple-element.285), channel_id=1, source_target_pairs={{0,4},{2,6},{4,0},{6,2},{1,5},{3,7},{5,1},{7,3},{8,12},{10,14},{12... | collective-permute-start | bytes 589832 | tf_op jit(solution)/shard_map/ppermute | solution.py:42
  255.2 29.3 %all-to-all-start.5 = ((bf16[16,24,768]{2,1,0:T(8,128)(2,1)}), bf16[16,24,768]{2,1,0:T(8,128)(2,1)S(1)}, u32[]{:S(2)}, u32[]{:S(2)}) async-start(bf16[16,24,768]{2,1,0:T(8,128)(2,1)} %add_convert_fusion.1), calls=%async_computation.5 | async-start | bytes 1179648 | tf_op jit(solution)/shard_map/all_to_all | solution.py:86
  265.8 14.3 %collective-permute-start.49 = (bf16[64,768]{1,0:T(8,128)(2,1)S(1)}, bf16[64,768]{1,0:T(8,128)(2,1)S(1)}, u32[]{:S(2)}, u32[]{:S(2)}) collective-permute-start(bf16[64,768]{1,0:T(8,128)(2,1)S(1)} %broadcast_select_fusion.3), channel_id=1, source_target_pairs={{0,8},{8,0},{1,9},{9,1},{2,10},{10,2},{3,11},{11,3},{4,12},{12,4},... | collective-permute-start | bytes 294920 | tf_op jit(solution)/shard_map/ppermute | solution.py:42
  266.6 8.3 %collective-permute-start.53 = (bf16[48,1152]{1,0:T(8,128)(2,1)S(1)}, bf16[48,1152]{1,0:T(8,128)(2,1)S(1)}, u32[]{:S(2)}, u32[]{:S(2)}) collective-permute-start(bf16[48,1152]{1,0:T(8,128)(2,1)S(1)} %get-tuple-element.295), channel_id=1, source_target_pairs={{0,6},{2,4},{4,2},{6,0},{1,7},{3,5},{5,3},{7,1},{8,14},{10,12},{12... | collective-permute-start | bytes 331784 | tf_op jit(solution)/shard_map/ppermute | solution.py:42
  266.7 8.4 %collective-permute-start.51 = (bf16[48,1152]{1,0:T(8,128)(2,1)S(1)}, bf16[48,1152]{1,0:T(8,128)(2,1)S(1)}, u32[]{:S(2)}, u32[]{:S(2)}) collective-permute-start(bf16[48,1152]{1,0:T(8,128)(2,1)S(1)} %get-tuple-element.297), channel_id=1, source_target_pairs={{0,2},{2,0},{4,6},{6,4},{1,3},{3,1},{5,7},{7,5},{8,10},{10,8},{12,... | collective-permute-start | bytes 331784 | tf_op jit(solution)/shard_map/ppermute | solution.py:42
  267.6 10.0 %collective-permute-start.52 = (bf16[48,1152]{1,0:T(8,128)(2,1)S(1)}, bf16[48,1152]{1,0:T(8,128)(2,1)S(1)}, u32[]{:S(2)}, u32[]{:S(2)}) collective-permute-start(bf16[48,1152]{1,0:T(8,128)(2,1)S(1)} %get-tuple-element.298), channel_id=1, source_target_pairs={{0,4},{2,6},{4,0},{6,2},{1,5},{3,7},{5,1},{7,3},{8,12},{10,14},{12... | collective-permute-start | bytes 331784 | tf_op jit(solution)/shard_map/ppermute | solution.py:42
  280.1 1.6 collective-permute-start.54
  (49 other events, 434.3 us)

commit v3 on v2

--- a/solution.py
+++ b/solution.py
@@ -404,8 +404,7 @@
         single += [lines, columns, jnp.zeros((w_rows, HEAD_DIM), f32)]
         for core, pieces in ((0, pair), (1, single)):
             wide = jnp.concatenate(pieces, axis=1).astype(bf16)
-            for slot in range(out_ref.shape[0]):
-                out_ref[slot, feat, core] = wide
+            out_ref[feat, core] = wide
 
 
 def pack_late_kernel(place_ref, w_ref, gate_ref, up_ref, kept_ref, sent_ref, *, slots):
@@ -447,15 +446,18 @@
     return pl.multiple_of(member * piece_rows, 16)
 
 
-def qkv_kernel(place_ref, mine_ref, other_ref, *refs, w_rows, rows, heads, pieces):
-    token_refs = refs[:FEATS]
-    sent_ref, w_ref, params_ref, seg_ref, code_ref, wide_s, vec_s = refs[FEATS:]
+def qkv_kernel(place_ref, *refs, w_rows, rows, heads, pieces):
+    mine_refs, other_refs = refs[:pieces], refs[pieces : 2 * pieces]
+    token_refs = refs[2 * pieces : 2 * pieces + FEATS]
+    sent_ref, w_ref, params_ref, seg_ref, code_ref, wide_s, vec_s = refs[2 * pieces + FEATS :]
     first_core = place_ref[0] == 0
     side, feat = place_ref[1], place_ref[2]
-    half = mine_ref.shape[1]
-    mine, other = mine_ref[...], other_ref[...]
-    w_ref[:, :half] = jnp.where(first_core, mine, other)
-    w_ref[:, half:] = jnp.where(first_core, other, mine)
+    piece_rows, half = mine_refs[0].shape
+    for index in range(pieces):
+        here = pl.ds(piece_row(place_ref, index, piece_rows), piece_rows)
+        mine, other = mine_refs[index][...], other_refs[index][...]
+        w_ref[here, :half] = jnp.where(first_core, mine, other)
+        w_ref[here, half:] = jnp.where(first_core, other, mine)
     vec_s[...] = w_ref[:, 2 * half - 128 :].astype(f32)
     wide_s[...] = w_ref[:, 2 * half - 256 : 2 * half - 128].astype(f32)
     head_width = heads * HEAD_DIM
@@ -510,29 +512,25 @@
         write(sent_ref, kept_ref)
 
 
-def collect_kernel(dqkv_ref, out_ref, *, heads):
-    half = heads * 2 * HEAD_DIM
-    group = out_ref.shape[0]
-    quarter = group // 2
-    out_ref[:, half + heads * HEAD_DIM :] = jnp.zeros((group, half - heads * HEAD_DIM), bf16)
-    for h in range(heads):
-        out_ref[:, 2 * h * HEAD_DIM : 2 * (h + 1) * HEAD_DIM] = dqkv_ref[h, :group, :]
-        lanes = slice(half + h * HEAD_DIM, half + (h + 1) * HEAD_DIM)
-        out_ref[:quarter, lanes] = dqkv_ref[h, group:, :HEAD_DIM]
-        out_ref[quarter:, lanes] = dqkv_ref[h, group:, HEAD_DIM:]
-
-
 def grad_qkv_kernel(place_ref, *refs, heads, w_rows):
     token_refs = refs[:FEATS]
-    back_ref, sums_ref, kept_ref, sent_ref, wide_s, vec_s = refs[FEATS:]
+    dqkv_ref, sums_ref, back_ref, kept_ref, sent_ref, wide_s, vec_s = refs[FEATS:]
     first_core = place_ref[0] == 0
+    head_width = heads * HEAD_DIM
+    half = 2 * head_width
+    group = back_ref.shape[0]
+    quarter = group // 2
+    back_ref[:, half + head_width :] = jnp.zeros((group, half - head_width), bf16)
+    for h in range(heads):
+        back_ref[:, 2 * h * HEAD_DIM : 2 * (h + 1) * HEAD_DIM] = dqkv_ref[h, :group, :]
+        lanes = slice(half + h * HEAD_DIM, half + (h + 1) * HEAD_DIM)
+        back_ref[:quarter, lanes] = dqkv_ref[h, group:, :HEAD_DIM]
+        back_ref[quarter:, lanes] = dqkv_ref[h, group:, HEAD_DIM:]
     width = wide_s.shape[1]
     wide_s[...] = jnp.zeros_like(wide_s)
     wide_s[2 : 2 + sums_ref.shape[0], :] = sums_ref[...]
     for start in range(0, width, 128):
         vec_s[start : start + 128, :] = jnp.transpose(wide_s[:, start : start + 128])
-    head_width = heads * HEAD_DIM
-    half = 2 * head_width
     tokens = jnp.concatenate([ref[...] for ref in token_refs], axis=0)
     back = back_ref[...]
     sums = jnp.sum(back.astype(f32), axis=0, keepdims=True)
@@ -829,14 +827,26 @@
     half = heads * 2 * HEAD_DIM
     (early,) = call(
         functools.partial(pack_kernel, heads=heads),
-        (jax.ShapeDtypeStruct((slots, FEATS, 2, w_rows, half), bf16),),
+        (jax.ShapeDtypeStruct((FEATS, 2, w_rows, half), bf16),),
         "pack_attn",
         "v" * 13,
         [pltpu.VMEM((128, 128), f32)],
     )(w_query, w_key, w_value, *vectors, segment_ids, token_live)
-    early, tokens = tie(early, tokens)
-    early_mine = all_to_all(early.reshape(-1, half), ("u", "s", "f", "c"))
     token_parts = gather_feats(tokens)
+    early_own = all_to_all(early.reshape(-1, half), ("f", "c"))
+    others = range(1, units)
+    early_side = swap(early_own, "s")
+    early_near = [swap(early_own, "u", k) for k in others]
+    early_far = [swap(early_side, "u", k) for k in others]
+
+    def by_distance(own, other_side, near, far):
+        pieces = [own, other_side]
+        for index in range(units - 1):
+            pieces += [near[index], far[index]]
+        return pieces
+
+    early_pieces = by_distance(early_own, early_side, early_near, early_far)
+    early_others = [swap(piece, "c") for piece in early_pieces]
 
     late_cols = width // 2 + ff_part
     late_shape = jax.ShapeDtypeStruct((FEATS, w_rows, late_cols), bf16)
@@ -848,11 +858,10 @@
         (jax.ShapeDtypeStruct((2 * w_rows, late_cols), bf16),) * FEATS,
         "route_late",
         "svv",
-    )(here, late_kept, swap(late_sent, "c"))
+    )(here, late_kept, swap(after(late_sent, early_own), "c"))
     out_half = width // 2
+    routed = [after(piece, token_parts[1]) for piece in routed]
     late_feats = [routed[0]] + [swap(routed[k], "f", k) for k in range(1, FEATS)]
-    early_mine, *token_parts = tie(early_mine, *token_parts)
-    early_other = swap(early_mine, "c")
     here_qkv, *late_feats = tie(here, *late_feats)
     first_own = jnp.concatenate(
         [piece[:, :out_half] for piece in late_feats] + [w_down[:, :out_half], w_down[:, out_half:]]
@@ -870,9 +879,9 @@
             jax.ShapeDtypeStruct((1, length), f32),
         ),
         "qkv",
-        "s" + "v" * (2 + FEATS),
+        "s" + "v" * (2 * parts + FEATS),
         [pltpu.VMEM((width, 128), f32)] * 2,
-    )(here_qkv, early_mine, early_other, *token_parts)
+    )(here_qkv, *early_pieces, *early_others, *token_parts)
     qkv = all_to_all(sent.reshape(-1, 2 * HEAD_DIM), ("u", "c"))
     first_side = swap(first_own, "s")
     first_units = [swap(first_own, "u", k) for k in others]
@@ -906,12 +915,6 @@
     second_far = [swap(second_side, "u", k) for k in others]
     first_swaps += [swap(piece, "c") for piece in first_far]
     second_swaps += [swap(piece, "c") for piece in [second_side] + second_units]
-
-    def by_distance(own, other_side, near, far):
-        pieces = [own, other_side]
-        for index in range(units - 1):
-            pieces += [near[index], far[index]]
-        return pieces
 
     first_pieces = by_distance(first_own, first_side, first_units, first_far)
     first_others = by_distance(
@@ -1052,7 +1055,6 @@
     ff_kept = outer(first_low, chosen(back_gate, back_up))
     down_kept = outer(hidden, chosen(left, right))
     here_join, ff_sent, down_sent, ff_kept, down_kept = tie(here, ff_sent, down_sent, ff_kept, down_kept)
-    ff_got, down_got = None, None
     inner_shape = jax.ShapeDtypeStruct((local, width), f32)
     back_inner, dout_blocks, out_kept, out_sent, sums_one = call(
         functools.partial(part_kernel, heads=heads, rows=rows),
@@ -1080,21 +1082,7 @@
         return (kept.astype(f32) + got.astype(f32)).astype(bf16)
 
     out_got = swap(out_sent, "c")
-    ff_got, down_got = swap(after(ff_sent, dout_blocks), "c"), swap(after(down_sent, dout_blocks), "c")
-    ff_rows, down_half = 2 * FEATS * w_rows, width // units
-    ff_shape = jax.ShapeDtypeStruct((units, ff_rows, ff_part), bf16)
-    half_shape = jax.ShapeDtypeStruct((down_half, half_width), bf16)
-    folded = call(
-        functools.partial(fold_kernel, units=units),
-        (ff_shape,) * 2 + (half_shape,) * (2 * units),
-        "fold_cores",
-        "s" + "v" * 6,
-    )(after(here, dout), ff_kept, ff_got, down_kept, down_got, out_kept, out_got)
-    grad_ff, ff_moved = folded[0], [swap(folded[1], "s")]
-    grad_down = folded[2]
-    down_moved = [swap(folded[2 + k], "u", k) for k in range(1, units)]
-    grad_out = folded[2 + units]
-    out_moved = [swap(folded[2 + units + k], "u", k) for k in range(1, units)]
+    ff_got, down_got = (swap(after(values, *partial_got), "c") for values in (ff_sent, down_sent))
 
     def parts_of(values, axis):
         size, me = lax.axis_size(axis), lax.axis_index(axis)
@@ -1112,63 +1100,73 @@
             result = result + piece.astype(f32)
         return result
 
-    dout, grad_ff, grad_down, grad_out = tie(dout, grad_ff, grad_down, grad_out)
+    def sides(values):
+        return jnp.moveaxis(values.reshape(units, 2, -1, values.shape[-1]), 1, 0)
+
+    def by_unit(values):
+        return values.reshape(units, -1, values.shape[-1])
+
+    def part(values, member):
+        return lax.dynamic_index_in_dim(values, member, 0, keepdims=False)
+
+    def send_sum(kept, got, axis):
+        me = lax.axis_index(axis)
+        moved = [
+            swap(added(part(kept, me ^ k), part(got, me ^ k)), axis, k)
+            for k in range(1, lax.axis_size(axis))
+        ]
+        return [part(kept, me), part(got, me)], moved
+
+    ff_own, ff_moved = send_sum(sides(ff_kept), sides(ff_got), "s")
+    down_own, down_moved = send_sum(by_unit(down_kept), by_unit(down_got), "u")
+    out_own, out_moved = send_sum(by_unit(out_kept), by_unit(out_got), "u")
     dqkv = attend_back(table, slope, qkv, dout, o_turned, lse, seg_row, code_row)
     dqkv, *moved = tie(dqkv, *ff_moved, *down_moved, *out_moved)
     ff_moved, down_moved, out_moved = moved[:1], moved[1:units], moved[units:]
-    grad_ff = total(grad_ff, ff_moved).astype(bf16)
-    grad_down = total(grad_down, down_moved).astype(bf16).reshape(2, 2 * down_rows, half_width)
-    grad_out = total(grad_out, out_moved).astype(bf16).reshape(2, FEATS * 2 * w_rows, half_width)
-    grad_ff, ff_moved = send(grad_ff, "u")
+    grad_down = total(down_own[0], down_own[1:] + down_moved).astype(bf16).reshape(2, 2 * down_rows, -1)
+    grad_out = total(out_own[0], out_own[1:] + out_moved).astype(bf16).reshape(2, FEATS * 2 * w_rows, -1)
     grad_down, down_moved = send(grad_down, "s")
     dqkv = all_to_all(dqkv.reshape(-1, 2 * HEAD_DIM), ("u", "c"))
-    dqkv, *moved = tie(dqkv, *ff_moved, *down_moved)
-    ff_moved, down_moved = moved[:-1], moved[-1:]
+    dqkv, down_moved[0] = tie(dqkv, down_moved[0])
+    grad_ff = total(ff_own[0], ff_own[1:] + ff_moved).astype(bf16)
+    grad_ff, ff_moved = send(after(grad_ff, dqkv), "u")
     grad_out, out_moved = send(after(grad_out, dqkv), "s")
-    layer_wide_low = after(layer_wide.astype(bf16), dqkv)
     dqkv = dqkv.reshape(ranges, SLOTS, group * 3 // 2, 2 * HEAD_DIM)
     if ranges > 1:
         dqkv = jnp.sum(dqkv.astype(f32), axis=0).astype(bf16)
     else:
         dqkv = dqkv[0]
     vector_sums = jnp.concatenate([sums_one, grad_down_bias, grad_gain_two, grad_shift_two], axis=0)
-    (back_projected,) = call(
-        functools.partial(collect_kernel, heads=heads),
-        (jax.ShapeDtypeStruct((group, 2 * half), bf16),),
-        "collect",
-        "v",
-    )(dqkv)
     attn_shape = jax.ShapeDtypeStruct((slots * FEATS, w_rows, 2 * half), bf16)
-    attn_kept, attn_sent = call(
+    back_projected, attn_kept, attn_sent = call(
         functools.partial(grad_qkv_kernel, heads=heads, w_rows=w_rows),
-        (attn_shape, attn_shape),
+        (jax.ShapeDtypeStruct((group, 2 * half), bf16), attn_shape, attn_shape),
         "grad_qkv",
         "s" + "v" * (FEATS + 2),
         [pltpu.VMEM((128, width), f32), pltpu.VMEM((width, 128), f32)],
-    )(here, *token_parts, back_projected, vector_sums)
+    )(here, *token_parts, dqkv, vector_sums)
     attn_sent, back_projected = tie(attn_sent, back_projected)
     partial_input = dot(back_projected, w_attn, 1, 1).astype(bf16).reshape(FEATS, local, width)
+    grad_attn = added(attn_kept, swap(attn_sent, "c"))
+    grad_attn, partial_input = tie(grad_attn, partial_input)
+    grad_attn = grad_attn.reshape(-1, 2 * half)
+    grad_down = total(grad_down, down_moved).reshape(2, down_rows, half_width)
+    layer_wide_low = after(layer_wide.astype(bf16), grad_attn)
+    grad_attn = all_to_all(grad_attn, ("u", "s", "f"))
     input_got = [swap(partial_input[k], "f", k) for k in range(1, FEATS)]
-    grad_attn = added(after(attn_kept, partial_input), swap(attn_sent, "c"))
-    back_inner, grad_attn, grad_ff = tie(back_inner, grad_attn, grad_ff)
-    grad_attn = all_to_all(grad_attn.reshape(-1, 2 * half), ("u", "s", "f"))
     grad_ff = total(grad_ff, ff_moved)
     grad_out = total(grad_out, out_moved)
-    grad_down = total(grad_down, down_moved).reshape(2, down_rows, half_width)
     grad_late = jnp.concatenate([grad_ff, grad_out], axis=1).astype(bf16)
     grad_late = grad_late.reshape(FEATS, 2 * w_rows, ff_part + half_width)
-
+    late_got = [lax.dynamic_index_in_dim(grad_late, feat ^ k, 0, keepdims=False) for k in range(FEATS)]
+    back_inner, *late_got = tie(back_inner, *late_got)
+    late_got = late_got[:1] + [swap(late_got[k], "f", k) for k in range(1, FEATS)]
     input_sum = back_inner + partial_input[0].astype(f32)
     for piece in input_got:
         input_sum = input_sum + piece.astype(f32)
     input_grad = from_tokens(input_sum.astype(bf16))
     layer_output = from_tokens(layer_wide_low)
 
-    late_got = [lax.dynamic_index_in_dim(grad_late, feat, 0, keepdims=False)]
-    late_got += [
-        swap(lax.dynamic_index_in_dim(grad_late, feat ^ k, 0, keepdims=False), "f", k)
-        for k in range(1, FEATS)
-    ]
     wide_shape = jax.ShapeDtypeStruct((w_rows, FEATS * ff_part + half_width), bf16)
     wide_kept, wide_sent = call(
         functools.partial(finish_late_kernel, ff_part=ff_part),

time: 289 us -> 269 us (0.931)
  Pallas kernels: 73.5 us -> 60.6 us
  waiting for transfers between devices: 88 us -> 76 us
  blocking collectives: 11.9 us -> 0 us
  other arithmetic: 15.1 us -> 24.7 us
  starting transfers between devices: 71 us -> 77.9 us
    ppermute x56 -> x62, waiting for transfers between devices: 83.2 us -> 71.2 us  [swap(): return lax.ppermute(values, axis, [(i, i ^ step) for i in range(size)])]
    all_to_all x1 -> x0, blocking collectives: 11.9 us -> none  [all_to_all(): return lax.all_to_all(values, axes, split_axis=0, concat_axis=0, tiled=True)]
    pallas_call x3 -> x1, Pallas kernels: 9.79 us -> 3.83 us  [on_device(): call(functools.partial(grad_qkv_kernel, heads=heads, w_rows=w_rows), (jax...]
    convert_element_type x1 -> x4, other arithmetic: 1 us -> 5.5 us  [added(): return (kept.astype(f32) + got.astype(f32)).astype(bf16)]
    all_to_all x5 -> x6, starting transfers between devices: 20.6 us -> 24.9 us  [all_to_all(): return lax.all_to_all(values, axes, split_axis=0, concat_axis=0, tiled=True)]
    pallas_call x1, Pallas kernels: 19.6 us -> 15.7 us  [attend_back(): pl.pallas_call(attend_back_kernel, out_shape=jax.ShapeDtypeStruct(qkv.sha...]
    convert_element_type x3, other arithmetic: 0.29 us -> 3.73 us  [the longest x1 1.33 us: on_device(): grad_ff = total(ff_own[0], ff_own[1:] + ff_moved).astype(bf16)]
    pallas_call x1, Pallas kernels: 15.7 us -> 12.6 us  [attend(): pl.pallas_call(attend_kernel, out_shape=(jax.ShapeDtypeStruct((slots * FE...]
  transfers between devices with their start and end apart: 61 -> 68, of which waited for: 28 -> 27; matrix products, arithmetic and copies ran while one was open for 8% -> 12% of each run, Pallas kernels for 22% -> 22%
where the time goes in v3:
time: 269 us; the launch traced here: 266 us
  starting transfers between devices  77.9 us (29%)
  waiting for transfers between devices  76 us (28%)
  Pallas kernels  60.6 us (23%)
  other arithmetic  24.7 us (9%)
  matrix products  12.9 us (5%)
  local copies, waits for them, and re-layouts  12.1 us (4%)
    ppermute x62, waiting for transfers between devices, swap(): return lax.ppermute(values, axis, [(i, i ^ step) for i in range(size)])  71.2 us
    ppermute x62, starting transfers between devices, swap(): return lax.ppermute(values, axis, [(i, i ^ step) for i in range(size)])  53 us
    all_to_all x6, starting transfers between devices, all_to_all(): return lax.all_to_all(values, axes, split_axis=0, concat_axis=0, tiled=True)  24.9 us
    pallas_call x1, Pallas kernels, attend_back(): pl.pallas_call(attend_back_kernel, out_shape=jax.ShapeDtypeStruct(qkv.sha...  15.7 us
    dot_general x11, matrix products, dot(): lax.dot_general(left, right, (((left_dim,), (right_dim,)), ((), ())), pre...  12.9 us
    pallas_call x1, Pallas kernels, attend(): pl.pallas_call(attend_kernel, out_shape=(jax.ShapeDtypeStruct((slots * FE...  12.6 us
    unnamed x130, local copies, waits for them, and re-layouts  9.01 us
    convert_element_type x4, other arithmetic, added(): return (kept.astype(f32) + got.astype(f32)).astype(bf16)  5.5 us
  transfers between devices with their start and end apart: 68, of which 27 were waited for; matrix products, arithmetic and copies ran while one was open for 12% of the time, Pallas kernels for 22%

profile of v3, /device:TPU:0, one launch (start us, length us, event | category | flops | bytes accessed | tf_op | source)
XLA Modules:
  0.0 265.9 jit_solution(1622343307795515690)
XLA Ops:
  1.7 4.1 %collective-permute-start.1 = (bf16[64,768]{1,0:T(8,128)(2,1)S(1)}, bf16[64,768]{1,0:T(8,128)(2,1)S(1)}, u32[]{:S(2)}, u32[]{:S(2)}) collective-permute-start(bf16[64,768]{1,0:T(8,128)(2,1)S(1)} %select_bitcast_fusion.7), channel_id=1, source_target_pairs={{0,8},{8,0},{1,9},{9,1},{2,10},{10,2},{3,11},{11,3},{4,12},{12,4},... | collective-permute-start | bytes 294920 | tf_op jit(solution)/shard_map/ppermute | solution.py:42
  5.8 1.7 pack_attn.1
  7.5 3.8 %all-to-all-start = ((bf16[8,24,384]{2,1,0:T(8,128)(2,1)}), bf16[8,24,384]{2,1,0:T(8,128)(2,1)S(1)}, u32[]{:S(2)}, u32[]{:S(2)}) async-start(bf16[8,24,384]{2,1,0:T(8,128)(2,1)} %bitcast.161), calls=%async_computation | async-start | bytes 294912 | tf_op jit(solution)/shard_map/all_to_all | solution.py:86
  11.9 1.9 pack_late.1
  14.7 1.9 all-to-all-done
  19.0 1.8 route_late.1
  20.8 3.2 %collective-permute-done.2.refs_9_.refs_1_ = bf16[128,768]{1,0:T(8,128)(2,1)S(1)} collective-permute-done((bf16[128,768]{1,0:T(8,128)(2,1)S(1)}, bf16[128,768]{1,0:T(8,128)(2,1)S(1)}, u32[]{:S(2)}, u32[]{:S(2)}) %collective-permute-start.2) | collective-permute-done | bytes 196640 | tf_op jit(solution)/shard_map/ppermute | solution.py:42
  31.1 1.9 collective-permute-done.4
  32.9 1.5 collective-permute-start.7
  35.8 1.8 collective-permute-done.14.refs_11_.refs_3_
  37.7 1.7 collective-permute-done.7.refs_2_
  39.4 1.6 collective-permute-done.8.refs_3_
  41.0 1.6 collective-permute-start.17
  44.0 3.4 %qkv.1 = (bf16[4,768,128]{2,1,0:T(8,128)(2,1)}, bf16[768,768]{1,0:T(8,128)(2,1)}, f32[8,768]{1,0:T(8,128)}, f32[1,2048]{1,0:T(1,128)}, f32[1,2048]{1,0:T(1,128)}) custom-call(s32[4]{0:T(128)} %pad_add_fusion.1.place_ref, bf16[192,384]{1,0:T(8,128)(2,1)} %bitcast.156, bf16[192,384]{1,0:T(8,128)(2,1)} %copy-done.39, bf16[192,384]{1,0:T(8,128)(2,1)} %copy-done.41, ...), custom_call_target="tpu_custom_call" | custom-call | tf_op jit(solution)/shard_map/qkv/pallas_call | solution.py:872
  47.4 3.6 %all-to-all-start.1 = ((bf16[4,768,128]{2,1,0:T(8,128)(2,1)}), bf16[4,768,128]{2,1,0:T(8,128)(2,1)S(1)}, u32[]{:S(2)}, u32[]{:S(2)}) async-start(bf16[4,768,128]{2,1,0:T(8,128)(2,1)} %get-tuple-element.145), calls=%async_computation.1 | async-start | bytes 1572864 | tf_op jit(solution)/shard_map/all_to_all | solution.py:86
  52.3 6.6 %collective-permute-done.15.refs_1_ = bf16[384,384]{1,0:T(8,128)(2,1)S(1)} collective-permute-done((bf16[384,384]{1,0:T(8,128)(2,1)S(1)}, bf16[384,384]{1,0:T(8,128)(2,1)S(1)}, u32[]{:S(2)}, u32[]{:S(2)}) %collective-permute-start.15) | collective-permute-done | bytes 294944 | tf_op jit(solution)/shard_map/ppermute | solution.py:42
  64.1 12.6 %attend.1 = (bf16[16,64,128]{2,1,0:T(8,128)(2,1)}, f32[1,2048]{1,0:T(1,128)}, f32[64,2048]{1,0:T(8,128)}) custom-call(s32[3,8]{1,0:T(4,128)} %pad_add_fusion.table_ref, f32[1,1]{1,0:T(1,128)} %bitcast.23.slope_ref, bf16[4,768,128]{2,1,0:T(8,128)(2,1)} %copy-done, f32[1,2048]{1,0:T(1,128)} %get-tuple-element.144.seg_ref, f32[1,2048]{1,0:T(1,128)} %get-tuple-element.151.code_ref), custom_call_target="tpu_custom_call" | custom-call | tf_op jit(solution)/shard_map/attend/pallas_call | solution.py:305
  76.8 4.7 %all-to-all-start.2 = ((bf16[16,64,128]{2,1,0:T(8,128)(2,1)}), bf16[16,64,128]{2,1,0:T(8,128)(2,1)S(1)}, u32[]{:S(2)}, u32[]{:S(2)}) async-start(bf16[16,64,128]{2,1,0:T(8,128)(2,1)} %get-tuple-element.154), calls=%async_computation.2 | async-start | bytes 524288 | tf_op jit(solution)/shard_map/all_to_all | solution.py:86
  82.4 1.7 collective-permute-start.27
  84.1 1.7 collective-permute-start.36
  85.9 3.4 %place_first.1 = (bf16[768,768]{1,0:T(8,128)(2,1)}, bf16[768,768]{1,0:T(8,128)(2,1)}) custom-call(s32[4]{0:T(128)} %pad_add_fusion.1.place_ref, bf16[384,384]{1,0:T(8,128)(2,1)} %copy-done.22, bf16[384,384]{1,0:T(8,128)(2,1)} %copy-done.25, bf16[384,384]{1,0:T(8,128)(2,1)} %copy-done.24, bf16[384,384]{1,0:T(8,128)(2,1)} %collective-permute-done.23.refs_3_, ...), custom_call_target="tpu_custom_call" | custom-call | tf_op jit(solution)/shard_map/place_first/pallas_call | solution.py:939
  89.3 1.7 all-to-all-done.2
  91.7 3.0 %join_heads.1 = (bf16[128,768]{1,0:T(8,128)(2,1)}, f32[128,768]{1,0:T(8,128)}, bf16[128,768]{1,0:T(8,128)(2,1)}, f32[128,768]{1,0:T(8,128)}, f32[128,1]{1,0:T(8,128)}) custom-call(bf16[16,64,128]{2,1,0:T(8,128)(2,1)} %copy-done.8, bf16[128,768]{1,0:T(8,128)(2,1)} %copy-done.2, bf16[768,768]{1,0:T(8,128)(2,1)} %get-tuple-element.163.w_ref, ...), custom_call_target="tpu_custom_call" | custom-call | tf_op jit(solution)/shard_map/join_heads/pallas_call | solution.py:976
  95.7 1.5 collective-permute-start.31
  97.8 1.5 collective-permute-start.29
  100.0 3.3 %place_second.1 = (bf16[768,768]{1,0:T(8,128)(2,1)}, bf16[768,768]{1,0:T(8,128)(2,1)}) custom-call(s32[4]{0:T(128)} %pad_add_fusion.1.place_ref, bf16[192,768]{1,0:T(8,128)(2,1)} %copy-done.4, bf16[192,768]{1,0:T(8,128)(2,1)} %collective-permute-done.21.refs_1_, bf16[192,768]{1,0:T(8,128)(2,1)} %collective-permute-done.22.refs_2_, ...), custom_call_target="tpu_custom_call" | custom-call | tf_op jit(solution)/shard_map/place_second/pallas_call | solution.py:995
  104.6 2.9 %collective-permute-done.30 = bf16[128,768]{1,0:T(8,128)(2,1)S(1)} collective-permute-done((bf16[128,768]{1,0:T(8,128)(2,1)}, bf16[128,768]{1,0:T(8,128)(2,1)S(1)}, u32[]{:S(2)}, u32[]{:S(2)}) %collective-permute-start.30) | collective-permute-done | bytes 196640 | tf_op jit(solution)/shard_map/ppermute | solution.py:42
  112.5 1.5 collective-permute-start.34
  114.0 1.4 collective-permute-start.33
  116.2 6.8 %collective-permute-done.32 = bf16[128,768]{1,0:T(8,128)(2,1)S(1)} collective-permute-done((bf16[128,768]{1,0:T(8,128)(2,1)S(1)}, bf16[128,768]{1,0:T(8,128)(2,1)S(1)}, u32[]{:S(2)}, u32[]{:S(2)}) %collective-permute-start.32) | collective-permute-done | bytes 196640 | tf_op jit(solution)/shard_map/ppermute | solution.py:42
  125.9 1.5 collective-permute-start.39
  127.9 1.5 collective-permute-start.37
  129.4 5.2 %collective-permute-done.39 = bf16[128,768]{1,0:T(8,128)(2,1)S(1)} collective-permute-done((bf16[128,768]{1,0:T(8,128)(2,1)S(1)}, bf16[128,768]{1,0:T(8,128)(2,1)S(1)}, u32[]{:S(2)}, u32[]{:S(2)}) %collective-permute-start.39) | collective-permute-done | bytes 196640 | tf_op jit(solution)/shard_map/ppermute | solution.py:42
  141.1 1.5 collective-permute-start.42
  142.6 1.4 collective-permute-start.41
  145.1 6.2 %collective-permute-done.40.got_a_ref = bf16[128,768]{1,0:T(8,128)(2,1)S(1)} collective-permute-done((bf16[128,768]{1,0:T(8,128)(2,1)}, bf16[128,768]{1,0:T(8,128)(2,1)S(1)}, u32[]{:S(2)}, u32[]{:S(2)}) %collective-permute-start.40) | collective-permute-done | bytes 196640 | tf_op jit(solution)/shard_map/ppermute | solution.py:42
  152.1 1.9 convolution_convert_fusion.1
  154.0 1.4 convolution_convert_fusion.5
  155.4 1.4 convolution_convert_fusion.4
  157.6 3.9 %back_join.1 = (f32[128,768]{1,0:T(8,128)}, bf16[16,64,128]{2,1,0:T(8,128)(2,1)}, bf16[768,384]{1,0:T(8,128)(2,1)}, bf16[768,384]{1,0:T(8,128)(2,1)}, f32[3,768]{1,0:T(4,128)}) custom-call(s32[4]{0:T(128)} %pad_add_fusion.1.place_ref, f32[128,768]{1,0:T(8,128)} %get-tuple-element.258.second_ref, bf16[128,768]{1,0:T(8,128)(2,1)} %get-tuple-element.270.own_ref, ...), custom_call_target="tpu_custom_call" | custom-call | tf_op jit(solution)/shard_map/back_join/pallas_call | solution.py:1059
  162.7 4.3 %all-to-all-start.3 = ((bf16[16,64,128]{2,1,0:T(8,128)(2,1)}), bf16[16,64,128]{2,1,0:T(8,128)(2,1)S(1)}, u32[]{:S(2)}, u32[]{:S(2)}) async-start(bf16[16,64,128]{2,1,0:T(8,128)(2,1)} %get-tuple-element.200), calls=%async_computation.3 | async-start | bytes 524288 | tf_op jit(solution)/shard_map/all_to_all | solution.py:86
  168.0 2.2 collective-permute-start.44
  170.2 1.8 fusion.38
  172.0 1.6 collective-permute-start.46
  173.6 1.7 fusion.39
  177.8 15.7 %attend_back.1 = bf16[4,768,128]{2,1,0:T(8,128)(2,1)} custom-call(s32[3,8]{1,0:T(4,128)} %pad_add_fusion.table_ref, f32[1,1]{1,0:T(1,128)} %bitcast.23.slope_ref, bf16[4,768,128]{2,1,0:T(8,128)(2,1)} %copy-done, bf16[16,64,128]{2,1,0:T(8,128)(2,1)} %copy-done.7, f32[64,2048]{1,0:T(8,128)} %get-tuple-element.201.ot_ref, ...), custom_call_target="tpu_custom_call" | custom-call | tf_op jit(solution)/shard_map/attend_back/pallas_call | solution.py:330
  193.6 3.9 %collective-permute-done.44 = bf16[2,192,768]{2,1,0:T(8,128)(2,1)S(1)} collective-permute-done((bf16[2,192,768]{2,1,0:T(8,128)(2,1)}, bf16[2,192,768]{2,1,0:T(8,128)(2,1)S(1)}, u32[]{:S(2)}, u32[]{:S(2)}) %collective-permute-start.44) | collective-permute-done | bytes 589856 | tf_op jit(solution)/shard_map/ppermute | solution.py:42
  198.2 3.5 %all-to-all-start.4 = ((bf16[4,768,128]{2,1,0:T(8,128)(2,1)}), bf16[4,768,128]{2,1,0:T(8,128)(2,1)S(1)}, u32[]{:S(2)}, u32[]{:S(2)}) async-start(bf16[4,768,128]{2,1,0:T(8,128)(2,1)} %attend_back.1), calls=%async_computation.4 | async-start | bytes 1572864 | tf_op jit(solution)/shard_map/all_to_all | solution.py:86
  205.6 7.7 %collective-permute-done.49 = bf16[192,384]{1,0:T(8,128)(2,1)S(1)} collective-permute-done((bf16[192,384]{1,0:T(8,128)(2,1)S(1)}, bf16[192,384]{1,0:T(8,128)(2,1)S(1)}, u32[]{:S(2)}, u32[]{:S(2)}) %collective-permute-start.49) | collective-permute-done | bytes 147488 | tf_op jit(solution)/shard_map/ppermute | solution.py:42
  214.1 1.7 collective-permute-start.50
  215.9 3.8 %grad_qkv.1 = (bf16[512,768]{1,0:T(8,128)(2,1)}, bf16[16,24,768]{2,1,0:T(8,128)(2,1)}, bf16[16,24,768]{2,1,0:T(8,128)(2,1)}) custom-call(s32[4]{0:T(128)} %pad_add_fusion.1.place_ref, bf16[128,768]{1,0:T(8,128)(2,1)} %copy-done.2, bf16[128,768]{1,0:T(8,128)(2,1)} %copy-done.10, bf16[128,768]{1,0:T(8,128)(2,1)} %copy-done.12, bf16[128,768]{1,0:T(8,128)(2,1)} %copy-done.11, ...), custom_call_target="tpu_custom_call" | custom-call | tf_op jit(solution)/shard_map/grad_qkv/pallas_call | solution.py:1141
  219.7 2.4 convolution_convert_fusion.2
  222.2 1.8 collective-permute-done.51
  226.8 1.6 collective-permute-start.57
  231.3 5.0 %all-to-all-start.5 = ((bf16[16,24,768]{2,1,0:T(8,128)(2,1)}), bf16[16,24,768]{2,1,0:T(8,128)(2,1)S(1)}, u32[]{:S(2)}, u32[]{:S(2)}) async-start(bf16[16,24,768]{2,1,0:T(8,128)(2,1)} %add_convert_fusion.1), calls=%async_computation.5 | async-start | bytes 1179648 | tf_op jit(solution)/shard_map/all_to_all | solution.py:86
  236.3 2.0 collective-permute-start.53
  238.3 1.5 collective-permute-start.55
  240.5 1.8 finish_late.1
  242.9 7.7 %collective-permute-done.53 = bf16[128,768]{1,0:T(8,128)(2,1)S(1)} collective-permute-done((bf16[128,768]{1,0:T(8,128)(2,1)S(1)}, bf16[128,768]{1,0:T(8,128)(2,1)S(1)}, u32[]{:S(2)}, u32[]{:S(2)}) %collective-permute-start.53) | collective-permute-done | bytes 196640 | tf_op jit(solution)/shard_map/ppermute | solution.py:42
  250.6 3.4 %collective-permute-done.55 = bf16[128,768]{1,0:T(8,128)(2,1)S(1)} collective-permute-done((bf16[128,768]{1,0:T(8,128)(2,1)S(1)}, bf16[128,768]{1,0:T(8,128)(2,1)S(1)}, u32[]{:S(2)}, u32[]{:S(2)}) %collective-permute-start.55) | collective-permute-done | bytes 196640 | tf_op jit(solution)/shard_map/ppermute | solution.py:42
  253.9 1.8 collective-permute-done.54
  255.9 2.7 %collective-permute-start.56 = (bf16[64,768]{1,0:T(8,128)(2,1)S(1)}, bf16[64,768]{1,0:T(8,128)(2,1)S(1)}, u32[]{:S(2)}, u32[]{:S(2)}) collective-permute-start(bf16[64,768]{1,0:T(8,128)(2,1)S(1)} %broadcast_select_fusion.3), channel_id=1, source_target_pairs={{0,8},{8,0},{1,9},{9,1},{2,10},{10,2},{3,11},{11,3},{4,12},{12,4},... | collective-permute-start | bytes 294920 | tf_op jit(solution)/shard_map/ppermute | solution.py:42
  259.9 2.2 finish_wide.1
  263.8 1.9 finish.1
  (289 shorter events, 64.7 us)
Async XLA Ops:
  1.7 12.1 %collective-permute-start.1 = (bf16[64,768]{1,0:T(8,128)(2,1)S(1)}, bf16[64,768]{1,0:T(8,128)(2,1)S(1)}, u32[]{:S(2)}, u32[]{:S(2)}) collective-permute-start(bf16[64,768]{1,0:T(8,128)(2,1)S(1)} %select_bitcast_fusion.7), channel_id=1, source_target_pairs={{0,8},{8,0},{1,9},{9,1},{2,10},{10,2},{3,11},{11,3},{4,12},{12,4},... | collective-permute-start | bytes 294920 | tf_op jit(solution)/shard_map/ppermute | solution.py:42
  7.5 9.1 %all-to-all-start = ((bf16[8,24,384]{2,1,0:T(8,128)(2,1)}), bf16[8,24,384]{2,1,0:T(8,128)(2,1)S(1)}, u32[]{:S(2)}, u32[]{:S(2)}) async-start(bf16[8,24,384]{2,1,0:T(8,128)(2,1)} %bitcast.161), calls=%async_computation | async-start | bytes 294912 | tf_op jit(solution)/shard_map/all_to_all | solution.py:86
  16.6 7.4 %collective-permute-start.2 = (bf16[128,768]{1,0:T(8,128)(2,1)S(1)}, bf16[128,768]{1,0:T(8,128)(2,1)S(1)}, u32[]{:S(2)}, u32[]{:S(2)}) collective-permute-start(bf16[128,768]{1,0:T(8,128)(2,1)S(1)} %pad_maximum_fusion.2.refs_8_.tokens_ref.refs_0_), channel_id=1, source_target_pairs={{0,2},{2,0},{4,6},{6,4},{1,3},{3,1},{5,7},{7,5},{8,10},{10,8},{12,... | collective-permute-start | bytes 589832 | tf_op jit(solution)/shard_map/ppermute | solution.py:42
  17.6 11.0 %collective-permute-start.6 = (bf16[192,384]{1,0:T(8,128)(2,1)S(1)}, bf16[192,384]{1,0:T(8,128)(2,1)S(1)}, u32[]{:S(2)}, u32[]{:S(2)}) collective-permute-start(bf16[192,384]{1,0:T(8,128)(2,1)S(1)} %bitcast.153), channel_id=1, source_target_pairs={{0,8},{8,0},{1,9},{9,1},{2,10},{10,2},{3,11},{11,3},{4,12},{12,4},... | collective-permute-start | bytes 442376 | tf_op jit(solution)/shard_map/ppermute | solution.py:42
  24.0 7.1 %collective-permute-start.5 = (bf16[48,1152]{1,0:T(8,128)(2,1)}, bf16[48,1152]{1,0:T(8,128)(2,1)S(1)}, u32[]{:S(2)}, u32[]{:S(2)}) collective-permute-start(bf16[48,1152]{1,0:T(8,128)(2,1)} %get-tuple-element.142), channel_id=1, source_target_pairs={{0,6},{2,4},{4,2},{6,0},{1,7},{3,5},{5,3},{7,1},{8,14},{10,12},{12... | collective-permute-start | bytes 331784 | tf_op jit(solution)/shard_map/ppermute | solution.py:42
  25.1 7.8 %collective-permute-start.4 = (bf16[48,1152]{1,0:T(8,128)(2,1)}, bf16[48,1152]{1,0:T(8,128)(2,1)S(1)}, u32[]{:S(2)}, u32[]{:S(2)}) collective-permute-start(bf16[48,1152]{1,0:T(8,128)(2,1)} %get-tuple-element.140), channel_id=1, source_target_pairs={{0,4},{2,6},{4,0},{6,2},{1,5},{3,7},{5,1},{7,3},{8,12},{10,14},{12... | collective-permute-start | bytes 331784 | tf_op jit(solution)/shard_map/ppermute | solution.py:42
  26.4 8.0 %collective-permute-start.3 = (bf16[48,1152]{1,0:T(8,128)(2,1)}, bf16[48,1152]{1,0:T(8,128)(2,1)S(1)}, u32[]{:S(2)}, u32[]{:S(2)}) collective-permute-start(bf16[48,1152]{1,0:T(8,128)(2,1)} %get-tuple-element.138), channel_id=1, source_target_pairs={{0,2},{2,0},{4,6},{6,4},{1,3},{3,1},{5,7},{7,5},{8,10},{10,8},{12,... | collective-permute-start | bytes 331784 | tf_op jit(solution)/shard_map/ppermute | solution.py:42
  27.5 10.2 %collective-permute-start.14 = (bf16[128,768]{1,0:T(8,128)(2,1)S(1)}, bf16[128,768]{1,0:T(8,128)(2,1)S(1)}, u32[]{:S(2)}, u32[]{:S(2)}) collective-permute-start(bf16[128,768]{1,0:T(8,128)(2,1)S(1)} %pad_maximum_fusion.2.refs_8_.tokens_ref.refs_0_), channel_id=1, source_target_pairs={{0,6},{2,4},{4,2},{6,0},{1,7},{3,5},{5,3},{7,1},{8,14},{10,12},{12... | collective-permute-start | bytes 589832 | tf_op jit(solution)/shard_map/ppermute | solution.py:42
  28.6 12.3 %collective-permute-start.13 = (bf16[128,768]{1,0:T(8,128)(2,1)S(1)}, bf16[128,768]{1,0:T(8,128)(2,1)S(1)}, u32[]{:S(2)}, u32[]{:S(2)}) collective-permute-start(bf16[128,768]{1,0:T(8,128)(2,1)S(1)} %pad_maximum_fusion.2.refs_8_.tokens_ref.refs_0_), channel_id=1, source_target_pairs={{0,4},{2,6},{4,0},{6,2},{1,5},{3,7},{5,1},{7,3},{8,12},{10,14},{12... | collective-permute-start | bytes 589832 | tf_op jit(solution)/shard_map/ppermute | solution.py:42
  31.1 11.5 %collective-permute-start.9 = (bf16[192,384]{1,0:T(8,128)(2,1)S(1)}, bf16[192,384]{1,0:T(8,128)(2,1)S(1)}, u32[]{:S(2)}, u32[]{:S(2)}) collective-permute-start(bf16[192,384]{1,0:T(8,128)(2,1)S(1)} %bitcast.154), channel_id=1, source_target_pairs={{0,1},{1,0},{2,3},{3,2},{4,5},{5,4},{6,7},{7,6},{8,9},{9,8},{10,11... | collective-permute-start | bytes 442376 | tf_op jit(solution)/shard_map/ppermute | solution.py:42
  32.9 6.4 %collective-permute-start.7 = (bf16[192,384]{1,0:T(8,128)(2,1)S(1)}, bf16[192,384]{1,0:T(8,128)(2,1)S(1)}, u32[]{:S(2)}, u32[]{:S(2)}) collective-permute-start(bf16[192,384]{1,0:T(8,128)(2,1)S(1)} %bitcast.155), channel_id=1, source_target_pairs={{0,16},{16,0},{1,17},{17,1},{2,18},{18,2},{3,19},{19,3},{4,20},{20... | collective-permute-start | bytes 442376 | tf_op jit(solution)/shard_map/ppermute | solution.py:42
  34.5 6.5 %collective-permute-start.8 = (bf16[192,384]{1,0:T(8,128)(2,1)S(1)}, bf16[192,384]{1,0:T(8,128)(2,1)S(1)}, u32[]{:S(2)}, u32[]{:S(2)}) collective-permute-start(bf16[192,384]{1,0:T(8,128)(2,1)S(1)} %collective-permute-done.6.refs_1_), channel_id=1, source_target_pairs={{0,16},{16,0},{1,17},{17,1},{2,18},{18,2},{3,19},{19,3},{4,20},{20... | collective-permute-start | bytes 442376 | tf_op jit(solution)/shard_map/ppermute | solution.py:42
  37.7 4.9 %collective-permute-start.10 = (bf16[192,384]{1,0:T(8,128)(2,1)S(1)}, bf16[192,384]{1,0:T(8,128)(2,1)S(1)}, u32[]{:S(2)}, u32[]{:S(2)}) collective-permute-start(bf16[192,384]{1,0:T(8,128)(2,1)S(1)} %collective-permute-done.6.refs_1_), channel_id=1, source_target_pairs={{0,1},{1,0},{2,3},{3,2},{4,5},{5,4},{6,7},{7,6},{8,9},{9,8},{10,11... | collective-permute-start | bytes 442376 | tf_op jit(solution)/shard_map/ppermute | solution.py:42
  41.0 10.8 %collective-permute-start.17 = (bf16[384,384]{1,0:T(8,128)(2,1)S(1)}, bf16[384,384]{1,0:T(8,128)(2,1)S(1)}, u32[]{:S(2)}, u32[]{:S(2)}) collective-permute-start(bf16[384,384]{1,0:T(8,128)(2,1)S(1)} %slice_dynamic-update-slice_fusion.refs_0_), channel_id=1, source_target_pairs={{0,16},{16,0},{1,17},{17,1},{2,18},{18,2},{3,19},{19,3},{4,20},{20... | collective-permute-start | bytes 884744 | tf_op jit(solution)/shard_map/ppermute | solution.py:42
  42.6 16.3 %collective-permute-start.15 = (bf16[384,384]{1,0:T(8,128)(2,1)S(1)}, bf16[384,384]{1,0:T(8,128)(2,1)S(1)}, u32[]{:S(2)}, u32[]{:S(2)}) collective-permute-start(bf16[384,384]{1,0:T(8,128)(2,1)S(1)} %slice_dynamic-update-slice_fusion.refs_0_), channel_id=1, source_target_pairs={{0,8},{8,0},{1,9},{9,1},{2,10},{10,2},{3,11},{11,3},{4,12},{12,4},... | collective-permute-start | bytes 884744 | tf_op jit(solution)/shard_map/ppermute | solution.py:42
  47.4 15.3 %all-to-all-start.1 = ((bf16[4,768,128]{2,1,0:T(8,128)(2,1)}), bf16[4,768,128]{2,1,0:T(8,128)(2,1)S(1)}, u32[]{:S(2)}, u32[]{:S(2)}) async-start(bf16[4,768,128]{2,1,0:T(8,128)(2,1)} %get-tuple-element.145), calls=%async_computation.1 | async-start | bytes 1572864 | tf_op jit(solution)/shard_map/all_to_all | solution.py:86
  51.1 10.2 %collective-permute-start.18 = (bf16[384,384]{1,0:T(8,128)(2,1)S(1)}, bf16[384,384]{1,0:T(8,128)(2,1)S(1)}, u32[]{:S(2)}, u32[]{:S(2)}) collective-permute-start(bf16[384,384]{1,0:T(8,128)(2,1)S(1)} %slice_dynamic-update-slice_fusion.refs_0_), channel_id=1, source_target_pairs={{0,1},{1,0},{2,3},{3,2},{4,5},{5,4},{6,7},{7,6},{8,9},{9,8},{10,11... | collective-permute-start | bytes 884744 | tf_op jit(solution)/shard_map/ppermute | solution.py:42
  51.7 9.8 %collective-permute-start.16 = (bf16[192,768]{1,0:T(8,128)(2,1)S(1)}, bf16[192,768]{1,0:T(8,128)(2,1)S(1)}, u32[]{:S(2)}, u32[]{:S(2)}) collective-permute-start(bf16[192,768]{1,0:T(8,128)(2,1)S(1)} %pad_maximum_fusion.1.refs_0_), channel_id=1, source_target_pairs={{0,1},{1,0},{2,3},{3,2},{4,5},{5,4},{6,7},{7,6},{8,9},{9,8},{10,11... | collective-permute-start | bytes 884744 | tf_op jit(solution)/shard_map/ppermute | solution.py:42
  51.8 9.6 %collective-permute-start.20 = (bf16[384,384]{1,0:T(8,128)(2,1)S(1)}, bf16[384,384]{1,0:T(8,128)(2,1)S(1)}, u32[]{:S(2)}, u32[]{:S(2)}) collective-permute-start(bf16[384,384]{1,0:T(8,128)(2,1)S(1)} %collective-permute-done.17.refs_2_), channel_id=1, source_target_pairs={{0,1},{1,0},{2,3},{3,2},{4,5},{5,4},{6,7},{7,6},{8,9},{9,8},{10,11... | collective-permute-start | bytes 884744 | tf_op jit(solution)/shard_map/ppermute | solution.py:42
  59.6 17.2 %collective-permute-start.22 = (bf16[192,768]{1,0:T(8,128)(2,1)S(1)}, bf16[192,768]{1,0:T(8,128)(2,1)}, u32[]{:S(2)}, u32[]{:S(2)}) collective-permute-start(bf16[192,768]{1,0:T(8,128)(2,1)S(1)} %pad_maximum_fusion.1.refs_0_), channel_id=1, source_target_pairs={{0,16},{16,0},{1,17},{17,1},{2,18},{18,2},{3,19},{19,3},{4,20},{20... | collective-permute-start | bytes 884744 | tf_op jit(solution)/shard_map/ppermute | solution.py:42
  61.4 15.4 %collective-permute-start.21 = (bf16[192,768]{1,0:T(8,128)(2,1)S(1)}, bf16[192,768]{1,0:T(8,128)(2,1)}, u32[]{:S(2)}, u32[]{:S(2)}) collective-permute-start(bf16[192,768]{1,0:T(8,128)(2,1)S(1)} %pad_maximum_fusion.1.refs_0_), channel_id=1, source_target_pairs={{0,8},{8,0},{1,9},{9,1},{2,10},{10,2},{3,11},{11,3},{4,12},{12,4},... | collective-permute-start | bytes 884744 | tf_op jit(solution)/shard_map/ppermute | solution.py:42
  62.7 14.1 %collective-permute-start.23 = (bf16[384,384]{1,0:T(8,128)(2,1)S(1)}, bf16[384,384]{1,0:T(8,128)(2,1)}, u32[]{:S(2)}, u32[]{:S(2)}) collective-permute-start(bf16[384,384]{1,0:T(8,128)(2,1)S(1)} %collective-permute-done.15.refs_1_), channel_id=1, source_target_pairs={{0,16},{16,0},{1,17},{17,1},{2,18},{18,2},{3,19},{19,3},{4,20},{20... | collective-permute-start | bytes 884744 | tf_op jit(solution)/shard_map/ppermute | solution.py:42
  76.8 14.2 %all-to-all-start.2 = ((bf16[16,64,128]{2,1,0:T(8,128)(2,1)}), bf16[16,64,128]{2,1,0:T(8,128)(2,1)S(1)}, u32[]{:S(2)}, u32[]{:S(2)}) async-start(bf16[16,64,128]{2,1,0:T(8,128)(2,1)} %get-tuple-element.154), calls=%async_computation.2 | async-start | bytes 524288 | tf_op jit(solution)/shard_map/all_to_all | solution.py:86
  81.5 4.3 %collective-permute-start.26 = (bf16[384,384]{1,0:T(8,128)(2,1)}, bf16[384,384]{1,0:T(8,128)(2,1)}, u32[]{:S(2)}, u32[]{:S(2)}) collective-permute-start(bf16[384,384]{1,0:T(8,128)(2,1)} %collective-permute-done.23.refs_3_), channel_id=1, source_target_pairs={{0,1},{1,0},{2,3},{3,2},{4,5},{5,4},{6,7},{7,6},{8,9},{9,8},{10,11... | collective-permute-start | bytes 884744 | tf_op jit(solution)/shard_map/ppermute | solution.py:42
  81.9 7.3 %collective-permute-start.25 = (bf16[192,768]{1,0:T(8,128)(2,1)}, bf16[192,768]{1,0:T(8,128)(2,1)S(1)}, u32[]{:S(2)}, u32[]{:S(2)}) collective-permute-start(bf16[192,768]{1,0:T(8,128)(2,1)} %collective-permute-done.22.refs_2_), channel_id=1, source_target_pairs={{0,1},{1,0},{2,3},{3,2},{4,5},{5,4},{6,7},{7,6},{8,9},{9,8},{10,11... | collective-permute-start | bytes 884744 | tf_op jit(solution)/shard_map/ppermute | solution.py:42
  82.1 7.2 %collective-permute-start.24 = (bf16[192,768]{1,0:T(8,128)(2,1)}, bf16[192,768]{1,0:T(8,128)(2,1)}, u32[]{:S(2)}, u32[]{:S(2)}) collective-permute-start(bf16[192,768]{1,0:T(8,128)(2,1)} %collective-permute-done.21.refs_1_), channel_id=1, source_target_pairs={{0,1},{1,0},{2,3},{3,2},{4,5},{5,4},{6,7},{7,6},{8,9},{9,8},{10,11... | collective-permute-start | bytes 884744 | tf_op jit(solution)/shard_map/ppermute | solution.py:42
  82.4 12.3 %collective-permute-start.27 = (bf16[192,768]{1,0:T(8,128)(2,1)}, bf16[192,768]{1,0:T(8,128)(2,1)}, u32[]{:S(2)}, u32[]{:S(2)}) collective-permute-start(bf16[192,768]{1,0:T(8,128)(2,1)} %collective-permute-done.21.refs_1_), channel_id=1, source_target_pairs={{0,16},{16,0},{1,17},{17,1},{2,18},{18,2},{3,19},{19,3},{4,20},{20... | collective-permute-start | bytes 884744 | tf_op jit(solution)/shard_map/ppermute | solution.py:42
  84.1 15.1 %collective-permute-start.36 = (bf16[64,768]{1,0:T(8,128)(2,1)S(1)}, bf16[64,768]{1,0:T(8,128)(2,1)S(1)}, u32[]{:S(2)}, u32[]{:S(2)}) collective-permute-start(bf16[64,768]{1,0:T(8,128)(2,1)S(1)} %select_bitcast_fusion.4), channel_id=1, source_target_pairs={{0,8},{8,0},{1,9},{9,1},{2,10},{10,2},{3,11},{11,3},{4,12},{12,4},... | collective-permute-start | bytes 294920 | tf_op jit(solution)/shard_map/ppermute | solution.py:42
  94.7 4.5 %collective-permute-start.28 = (bf16[192,768]{1,0:T(8,128)(2,1)}, bf16[192,768]{1,0:T(8,128)(2,1)S(1)}, u32[]{:S(2)}, u32[]{:S(2)}) collective-permute-start(bf16[192,768]{1,0:T(8,128)(2,1)} %collective-permute-done.27.refs_3_), channel_id=1, source_target_pairs={{0,1},{1,0},{2,3},{3,2},{4,5},{5,4},{6,7},{7,6},{8,9},{9,8},{10,11... | collective-permute-start | bytes 884744 | tf_op jit(solution)/shard_map/ppermute | solution.py:42
  95.7 8.9 %collective-permute-start.31 = (bf16[128,768]{1,0:T(8,128)(2,1)}, bf16[128,768]{1,0:T(8,128)(2,1)S(1)}, u32[]{:S(2)}, u32[]{:S(2)}) collective-permute-start(bf16[128,768]{1,0:T(8,128)(2,1)} %get-tuple-element.174), channel_id=1, source_target_pairs={{0,6},{2,4},{4,2},{6,0},{1,7},{3,5},{5,3},{7,1},{8,14},{10,12},{12... | collective-permute-start | bytes 589832 | tf_op jit(solution)/shard_map/ppermute | solution.py:42
  97.2 10.3 %collective-permute-start.30 = (bf16[128,768]{1,0:T(8,128)(2,1)}, bf16[128,768]{1,0:T(8,128)(2,1)S(1)}, u32[]{:S(2)}, u32[]{:S(2)}) collective-permute-start(bf16[128,768]{1,0:T(8,128)(2,1)} %get-tuple-element.174), channel_id=1, source_target_pairs={{0,4},{2,6},{4,0},{6,2},{1,5},{3,7},{5,1},{7,3},{8,12},{10,14},{12... | collective-permute-start | bytes 589832 | tf_op jit(solution)/shard_map/ppermute | solution.py:42
  97.8 10.6 %collective-permute-start.29 = (bf16[128,768]{1,0:T(8,128)(2,1)}, bf16[128,768]{1,0:T(8,128)(2,1)S(1)}, u32[]{:S(2)}, u32[]{:S(2)}) collective-permute-start(bf16[128,768]{1,0:T(8,128)(2,1)} %get-tuple-element.174), channel_id=1, source_target_pairs={{0,2},{2,0},{4,6},{6,4},{1,3},{3,1},{5,7},{7,5},{8,10},{10,8},{12,... | collective-permute-start | bytes 589832 | tf_op jit(solution)/shard_map/ppermute | solution.py:42
  111.9 11.1 %collective-permute-start.32 = (bf16[128,768]{1,0:T(8,128)(2,1)S(1)}, bf16[128,768]{1,0:T(8,128)(2,1)S(1)}, u32[]{:S(2)}, u32[]{:S(2)}) collective-permute-start(bf16[128,768]{1,0:T(8,128)(2,1)S(1)} %get-tuple-element.272), channel_id=1, source_target_pairs={{0,2},{2,0},{4,6},{6,4},{1,3},{3,1},{5,7},{7,5},{8,10},{10,8},{12,... | collective-permute-start | bytes 589832 | tf_op jit(solution)/shard_map/ppermute | solution.py:42
  112.5 10.4 %collective-permute-start.34 = (bf16[128,768]{1,0:T(8,128)(2,1)S(1)}, bf16[128,768]{1,0:T(8,128)(2,1)S(1)}, u32[]{:S(2)}, u32[]{:S(2)}) collective-permute-start(bf16[128,768]{1,0:T(8,128)(2,1)S(1)} %get-tuple-element.273), channel_id=1, source_target_pairs={{0,6},{2,4},{4,2},{6,0},{1,7},{3,5},{5,3},{7,1},{8,14},{10,12},{12... | collective-permute-start | bytes 589832 | tf_op jit(solution)/shard_map/ppermute | solution.py:42
  114.0 10.2 %collective-permute-start.33 = (bf16[128,768]{1,0:T(8,128)(2,1)S(1)}, bf16[128,768]{1,0:T(8,128)(2,1)S(1)}, u32[]{:S(2)}, u32[]{:S(2)}) collective-permute-start(bf16[128,768]{1,0:T(8,128)(2,1)S(1)} %get-tuple-element.274), channel_id=1, source_target_pairs={{0,4},{2,6},{4,0},{6,2},{1,5},{3,7},{5,1},{7,3},{8,12},{10,14},{12... | collective-permute-start | bytes 589832 | tf_op jit(solution)/shard_map/ppermute | solution.py:42
  125.9 8.7 %collective-permute-start.39 = (bf16[128,768]{1,0:T(8,128)(2,1)S(1)}, bf16[128,768]{1,0:T(8,128)(2,1)S(1)}, u32[]{:S(2)}, u32[]{:S(2)}) collective-permute-start(bf16[128,768]{1,0:T(8,128)(2,1)S(1)} %get-tuple-element.257), channel_id=1, source_target_pairs={{0,6},{2,4},{4,2},{6,0},{1,7},{3,5},{5,3},{7,1},{8,14},{10,12},{12... | collective-permute-start | bytes 589832 | tf_op jit(solution)/shard_map/ppermute | solution.py:42
  127.4 8.4 %collective-permute-start.38 = (bf16[128,768]{1,0:T(8,128)(2,1)S(1)}, bf16[128,768]{1,0:T(8,128)(2,1)S(1)}, u32[]{:S(2)}, u32[]{:S(2)}) collective-permute-start(bf16[128,768]{1,0:T(8,128)(2,1)S(1)} %get-tuple-element.257), channel_id=1, source_target_pairs={{0,4},{2,6},{4,0},{6,2},{1,5},{3,7},{5,1},{7,3},{8,12},{10,14},{12... | collective-permute-start | bytes 589832 | tf_op jit(solution)/shard_map/ppermute | solution.py:42
  127.9 8.8 %collective-permute-start.37 = (bf16[128,768]{1,0:T(8,128)(2,1)S(1)}, bf16[128,768]{1,0:T(8,128)(2,1)S(1)}, u32[]{:S(2)}, u32[]{:S(2)}) collective-permute-start(bf16[128,768]{1,0:T(8,128)(2,1)S(1)} %get-tuple-element.257), channel_id=1, source_target_pairs={{0,2},{2,0},{4,6},{6,4},{1,3},{3,1},{5,7},{7,5},{8,10},{10,8},{12,... | collective-permute-start | bytes 589832 | tf_op jit(solution)/shard_map/ppermute | solution.py:42
  140.5 10.7 %collective-permute-start.40 = (bf16[128,768]{1,0:T(8,128)(2,1)}, bf16[128,768]{1,0:T(8,128)(2,1)S(1)}, u32[]{:S(2)}, u32[]{:S(2)}) collective-permute-start(bf16[128,768]{1,0:T(8,128)(2,1)} %get-tuple-element.271), channel_id=1, source_target_pairs={{0,2},{2,0},{4,6},{6,4},{1,3},{3,1},{5,7},{7,5},{8,10},{10,8},{12,... | collective-permute-start | bytes 589832 | tf_op jit(solution)/shard_map/ppermute | solution.py:42
  141.1 15.8 %collective-permute-start.42 = (bf16[128,768]{1,0:T(8,128)(2,1)}, bf16[128,768]{1,0:T(8,128)(2,1)S(1)}, u32[]{:S(2)}, u32[]{:S(2)}) collective-permute-start(bf16[128,768]{1,0:T(8,128)(2,1)} %get-tuple-element.268), channel_id=1, source_target_pairs={{0,6},{2,4},{4,2},{6,0},{1,7},{3,5},{5,3},{7,1},{8,14},{10,12},{12... | collective-permute-start | bytes 589832 | tf_op jit(solution)/shard_map/ppermute | solution.py:42
  142.6 14.3 %collective-permute-start.41 = (bf16[128,768]{1,0:T(8,128)(2,1)}, bf16[128,768]{1,0:T(8,128)(2,1)S(1)}, u32[]{:S(2)}, u32[]{:S(2)}) collective-permute-start(bf16[128,768]{1,0:T(8,128)(2,1)} %get-tuple-element.269), channel_id=1, source_target_pairs={{0,4},{2,6},{4,0},{6,2},{1,5},{3,7},{5,1},{7,3},{8,12},{10,14},{12... | collective-permute-start | bytes 589832 | tf_op jit(solution)/shard_map/ppermute | solution.py:42
  156.9 10.1 %collective-permute-start.43 = (bf16[768,768]{1,0:T(8,128)(2,1)}, bf16[768,768]{1,0:T(8,128)(2,1)S(1)}, u32[]{:S(2)}, u32[]{:S(2)}) collective-permute-start(bf16[768,768]{1,0:T(8,128)(2,1)} %convolution_convert_fusion.1), channel_id=1, source_target_pairs={{0,1},{1,0},{2,3},{3,2},{4,5},{5,4},{6,7},{7,6},{8,9},{9,8},{10,11... | collective-permute-start | bytes 3538952 | tf_op jit(solution)/shard_map/ppermute | solution.py:42
  157.2 12.9 %collective-permute-start.45 = (bf16[768,384]{1,0:T(8,128)(2,1)}, bf16[768,384]{1,0:T(8,128)(2,1)}, u32[]{:S(2)}, u32[]{:S(2)}) collective-permute-start(bf16[768,384]{1,0:T(8,128)(2,1)} %convolution_convert_fusion.5), channel_id=1, source_target_pairs={{0,1},{1,0},{2,3},{3,2},{4,5},{5,4},{6,7},{7,6},{8,9},{9,8},{10,11... | collective-permute-start | bytes 1769480 | tf_op jit(solution)/shard_map/ppermute | solution.py:42
  161.5 12.1 %collective-permute-start.47 = (bf16[768,384]{1,0:T(8,128)(2,1)}, bf16[768,384]{1,0:T(8,128)(2,1)}, u32[]{:S(2)}, u32[]{:S(2)}) collective-permute-start(bf16[768,384]{1,0:T(8,128)(2,1)} %get-tuple-element.207), channel_id=1, source_target_pairs={{0,1},{1,0},{2,3},{3,2},{4,5},{5,4},{6,7},{7,6},{8,9},{9,8},{10,11... | collective-permute-start | bytes 1769480 | tf_op jit(solution)/shard_map/ppermute | solution.py:42
  162.5 13.3 %collective-permute-start.35 = (bf16[64,768]{1,0:T(8,128)(2,1)}, bf16[64,768]{1,0:T(8,128)(2,1)S(1)}, u32[]{:S(2)}, u32[]{:S(2)}) collective-permute-start(bf16[64,768]{1,0:T(8,128)(2,1)} %broadcast_select_fusion.5), channel_id=1, source_target_pairs={{0,8},{8,0},{1,9},{9,1},{2,10},{10,2},{3,11},{11,3},{4,12},{12,4},... | collective-permute-start | bytes 294920 | tf_op jit(solution)/shard_map/ppermute | solution.py:42
  162.7 14.4 %all-to-all-start.3 = ((bf16[16,64,128]{2,1,0:T(8,128)(2,1)}), bf16[16,64,128]{2,1,0:T(8,128)(2,1)S(1)}, u32[]{:S(2)}, u32[]{:S(2)}) async-start(bf16[16,64,128]{2,1,0:T(8,128)(2,1)} %get-tuple-element.200), calls=%async_computation.3 | async-start | bytes 524288 | tf_op jit(solution)/shard_map/all_to_all | solution.py:86
  168.0 29.5 %collective-permute-start.44 = (bf16[2,192,768]{2,1,0:T(8,128)(2,1)}, bf16[2,192,768]{2,1,0:T(8,128)(2,1)S(1)}, u32[]{:S(2)}, u32[]{:S(2)}) collective-permute-start(bf16[2,192,768]{2,1,0:T(8,128)(2,1)} %fusion.11), channel_id=1, source_target_pairs={{0,8},{8,0},{1,9},{9,1},{2,10},{10,2},{3,11},{11,3},{4,12},{12,4},... | collective-permute-start | bytes 1769480 | tf_op jit(solution)/shard_map/ppermute | solution.py:42
  172.0 21.6 %collective-permute-start.46 = (bf16[384,384]{1,0:T(8,128)(2,1)}, bf16[384,384]{1,0:T(8,128)(2,1)}, u32[]{:S(2)}, u32[]{:S(2)}) collective-permute-start(bf16[384,384]{1,0:T(8,128)(2,1)} %fusion.38), channel_id=1, source_target_pairs={{0,16},{16,0},{1,17},{17,1},{2,18},{18,2},{3,19},{19,3},{4,20},{20... | collective-permute-start | bytes 884744 | tf_op jit(solution)/shard_map/ppermute | solution.py:42
  175.4 18.2 %collective-permute-start.48 = (bf16[384,384]{1,0:T(8,128)(2,1)}, bf16[384,384]{1,0:T(8,128)(2,1)}, u32[]{:S(2)}, u32[]{:S(2)}) collective-permute-start(bf16[384,384]{1,0:T(8,128)(2,1)} %fusion.39), channel_id=1, source_target_pairs={{0,16},{16,0},{1,17},{17,1},{2,18},{18,2},{3,19},{19,3},{4,20},{20... | collective-permute-start | bytes 884744 | tf_op jit(solution)/shard_map/ppermute | solution.py:42
  198.2 15.1 %all-to-all-start.4 = ((bf16[4,768,128]{2,1,0:T(8,128)(2,1)}), bf16[4,768,128]{2,1,0:T(8,128)(2,1)S(1)}, u32[]{:S(2)}, u32[]{:S(2)}) async-start(bf16[4,768,128]{2,1,0:T(8,128)(2,1)} %attend_back.1), calls=%async_computation.4 | async-start | bytes 1572864 | tf_op jit(solution)/shard_map/all_to_all | solution.py:86
  203.0 10.3 %collective-permute-start.49 = (bf16[192,384]{1,0:T(8,128)(2,1)S(1)}, bf16[192,384]{1,0:T(8,128)(2,1)S(1)}, u32[]{:S(2)}, u32[]{:S(2)}) collective-permute-start(bf16[192,384]{1,0:T(8,128)(2,1)S(1)} %broadcast_select_fusion), channel_id=1, source_target_pairs={{0,8},{8,0},{1,9},{9,1},{2,10},{10,2},{3,11},{11,3},{4,12},{12,4},... | collective-permute-start | bytes 442376 | tf_op jit(solution)/shard_map/ppermute | solution.py:42
  214.1 9.9 %collective-permute-start.51 = (bf16[192,384]{1,0:T(8,128)(2,1)}, bf16[192,384]{1,0:T(8,128)(2,1)}, u32[]{:S(2)}, u32[]{:S(2)}) collective-permute-start(bf16[192,384]{1,0:T(8,128)(2,1)} %select_bitcast_fusion.1), channel_id=1, source_target_pairs={{0,8},{8,0},{1,9},{9,1},{2,10},{10,2},{3,11},{11,3},{4,12},{12,4},... | collective-permute-start | bytes 442376 | tf_op jit(solution)/shard_map/ppermute | solution.py:42
  214.1 10.9 %collective-permute-start.50 = (bf16[192,768]{1,0:T(8,128)(2,1)S(1)}, bf16[192,768]{1,0:T(8,128)(2,1)}, u32[]{:S(2)}, u32[]{:S(2)}) collective-permute-start(bf16[192,768]{1,0:T(8,128)(2,1)S(1)} %select_bitcast_fusion), channel_id=1, source_target_pairs={{0,16},{16,0},{1,17},{17,1},{2,18},{18,2},{3,19},{19,3},{4,20},{20... | collective-permute-start | bytes 884744 | tf_op jit(solution)/shard_map/ppermute | solution.py:42
  222.2 8.2 %collective-permute-start.52 = (bf16[16,24,768]{2,1,0:T(8,128)(2,1)S(1)}, bf16[16,24,768]{2,1,0:T(8,128)(2,1)S(1)}, u32[]{:S(2)}, u32[]{:S(2)}) collective-permute-start(bf16[16,24,768]{2,1,0:T(8,128)(2,1)S(1)} %copy-done.54), channel_id=1, source_target_pairs={{0,1},{1,0},{2,3},{3,2},{4,5},{5,4},{6,7},{7,6},{8,9},{9,8},{10,11... | collective-permute-start | bytes 1769480 | tf_op jit(solution)/shard_map/ppermute | solution.py:42
  226.8 12.9 %collective-permute-start.57 = (bf16[48,1152]{1,0:T(8,128)(2,1)S(1)}, bf16[48,1152]{1,0:T(8,128)(2,1)S(1)}, u32[]{:S(2)}, u32[]{:S(2)}) collective-permute-start(bf16[48,1152]{1,0:T(8,128)(2,1)S(1)} %get-tuple-element.231), channel_id=1, source_target_pairs={{0,2},{2,0},{4,6},{6,4},{1,3},{3,1},{5,7},{7,5},{8,10},{10,8},{12,... | collective-permute-start | bytes 331784 | tf_op jit(solution)/shard_map/ppermute | solution.py:42
  228.4 12.1 %collective-permute-start.58 = (bf16[48,1152]{1,0:T(8,128)(2,1)}, bf16[48,1152]{1,0:T(8,128)(2,1)}, u32[]{:S(2)}, u32[]{:S(2)}) collective-permute-start(bf16[48,1152]{1,0:T(8,128)(2,1)} %get-tuple-element.232), channel_id=1, source_target_pairs={{0,4},{2,6},{4,0},{6,2},{1,5},{3,7},{5,1},{7,3},{8,12},{10,14},{12... | collective-permute-start | bytes 331784 | tf_op jit(solution)/shard_map/ppermute | solution.py:42
  229.3 11.2 %collective-permute-start.59 = (bf16[48,1152]{1,0:T(8,128)(2,1)S(1)}, bf16[48,1152]{1,0:T(8,128)(2,1)}, u32[]{:S(2)}, u32[]{:S(2)}) collective-permute-start(bf16[48,1152]{1,0:T(8,128)(2,1)S(1)} %get-tuple-element.233), channel_id=1, source_target_pairs={{0,6},{2,4},{4,2},{6,0},{1,7},{3,5},{5,3},{7,1},{8,14},{10,12},{12... | collective-permute-start | bytes 331784 | tf_op jit(solution)/shard_map/ppermute | solution.py:42
  231.3 31.7 %all-to-all-start.5 = ((bf16[16,24,768]{2,1,0:T(8,128)(2,1)}), bf16[16,24,768]{2,1,0:T(8,128)(2,1)S(1)}, u32[]{:S(2)}, u32[]{:S(2)}) async-start(bf16[16,24,768]{2,1,0:T(8,128)(2,1)} %add_convert_fusion.1), calls=%async_computation.5 | async-start | bytes 1179648 | tf_op jit(solution)/shard_map/all_to_all | solution.py:86
  236.3 14.3 %collective-permute-start.53 = (bf16[128,768]{1,0:T(8,128)(2,1)S(1)}, bf16[128,768]{1,0:T(8,128)(2,1)S(1)}, u32[]{:S(2)}, u32[]{:S(2)}) collective-permute-start(bf16[128,768]{1,0:T(8,128)(2,1)S(1)} %get-tuple-element.265), channel_id=1, source_target_pairs={{0,2},{2,0},{4,6},{6,4},{1,3},{3,1},{5,7},{7,5},{8,10},{10,8},{12,... | collective-permute-start | bytes 589832 | tf_op jit(solution)/shard_map/ppermute | solution.py:42
  238.3 15.7 %collective-permute-start.55 = (bf16[128,768]{1,0:T(8,128)(2,1)S(1)}, bf16[128,768]{1,0:T(8,128)(2,1)S(1)}, u32[]{:S(2)}, u32[]{:S(2)}) collective-permute-start(bf16[128,768]{1,0:T(8,128)(2,1)S(1)} %get-tuple-element.266), channel_id=1, source_target_pairs={{0,6},{2,4},{4,2},{6,0},{1,7},{3,5},{5,3},{7,1},{8,14},{10,12},{12... | collective-permute-start | bytes 589832 | tf_op jit(solution)/shard_map/ppermute | solution.py:42
  239.7 16.0 %collective-permute-start.54 = (bf16[128,768]{1,0:T(8,128)(2,1)S(1)}, bf16[128,768]{1,0:T(8,128)(2,1)S(1)}, u32[]{:S(2)}, u32[]{:S(2)}) collective-permute-start(bf16[128,768]{1,0:T(8,128)(2,1)S(1)} %get-tuple-element.267), channel_id=1, source_target_pairs={{0,4},{2,6},{4,0},{6,2},{1,5},{3,7},{5,1},{7,3},{8,12},{10,14},{12... | collective-permute-start | bytes 589832 | tf_op jit(solution)/shard_map/ppermute | solution.py:42
  240.5 18.7 %collective-permute-start.61 = (bf16[96,384]{1,0:T(8,128)(2,1)}, bf16[96,384]{1,0:T(8,128)(2,1)S(1)}, u32[]{:S(2)}, u32[]{:S(2)}) collective-permute-start(bf16[96,384]{1,0:T(8,128)(2,1)} %select_convert_fusion), channel_id=1, source_target_pairs={{0,1},{1,0},{2,3},{3,2},{4,5},{5,4},{6,7},{7,6},{8,9},{9,8},{10,11... | collective-permute-start | bytes 221192 | tf_op jit(solution)/shard_map/ppermute | solution.py:42
  242.4 16.9 %collective-permute-start.60 = (bf16[24,3456]{1,0:T(8,128)(2,1)}, bf16[24,3456]{1,0:T(8,128)(2,1)S(1)}, u32[]{:S(2)}, u32[]{:S(2)}) collective-permute-start(bf16[24,3456]{1,0:T(8,128)(2,1)} %get-tuple-element.235), channel_id=1, source_target_pairs={{0,1},{1,0},{2,3},{3,2},{4,5},{5,4},{6,7},{7,6},{8,9},{9,8},{10,11... | collective-permute-start | bytes 497672 | tf_op jit(solution)/shard_map/ppermute | solution.py:42
  255.9 6.4 %collective-permute-start.56 = (bf16[64,768]{1,0:T(8,128)(2,1)S(1)}, bf16[64,768]{1,0:T(8,128)(2,1)S(1)}, u32[]{:S(2)}, u32[]{:S(2)}) collective-permute-start(bf16[64,768]{1,0:T(8,128)(2,1)S(1)} %broadcast_select_fusion.3), channel_id=1, source_target_pairs={{0,8},{8,0},{1,9},{9,1},{2,10},{10,2},{3,11},{11,3},{4,12},{12,4},... | collective-permute-start | bytes 294920 | tf_op jit(solution)/shard_map/ppermute | solution.py:42
  (64 other events, 637.9 us)

commit v4 on v3

--- a/solution.py
+++ b/solution.py
@@ -137,7 +137,37 @@
     return low, (high + up - low) // 2
 
 
-def score_tile(qk_part, qz_part, code_part, seg_part, offset, slope):
+def score_tile(qk_part, qz_part, code_part, seg_part, tile, q_block, k_block, slope, diagonal):
+    codes = jnp.concatenate([code_part] * (BLOCK // 128), axis=1)
+    allowed = codes == seg_part
+    if diagonal:
+        distance = tile
+    else:
+        distance = tile + ((q_block - k_block) * BLOCK).astype(f32)
+    if diagonal is False:
+        fall = distance * jnp.where(q_block > k_block, slope, -slope)
+    else:
+        fall = jnp.abs(distance) * slope
+        allowed = allowed | (distance == 0.0)
+    return jnp.where(allowed, dot(qk_part, qz_part) - fall, masked_value)
+
+
+def pair_plan(index, low, high, blocks):
+    odd = (high - low) % 2
+    up = odd * (high < blocks).astype(jnp.int32)
+    low, high = low - (odd - up), high + up
+    at_low = (low == index).astype(jnp.int32)
+    partner = low + at_low
+    base = low + 1 + at_low
+
+    def member(t):
+        here = base + t
+        return here + ((here >= index) & (at_low == 0)).astype(jnp.int32)
+
+    return partner, (high - low - 2) // 2, member
+
+
+def score_tile_plain(qk_part, qz_part, code_part, seg_part, offset, slope):
     distance = distance_tile() + offset
     scores = dot(qk_part, qz_part) - slope * jnp.abs(distance)
     codes = jnp.concatenate([code_part] * (BLOCK // 128), axis=1)
@@ -167,42 +197,42 @@
         ot_ref[...] = jnp.zeros_like(ot_ref)
         lse_ref[...] = jnp.zeros_like(lse_ref)
 
+
     def query_step(i, carry):
         here = span(i)
         qz_part = qz_s[:, here]
         seg_part = seg_ref[:, here]
-        low, pairs = even_range(table_ref[0, i], table_ref[1, i], 0, blocks)
+        partner, pairs, member = pair_plan(i, table_ref[0, i], table_ref[1, i], blocks)
+
+        def scores_of(j, diagonal):
+            return score_tile(
+                nat_s[span(j), :128], qz_part, code_s[span(j), :], seg_part, distance_tile(), i, j,
+                slope, diagonal,
+            )
+
+        def mixed_of(j, probs):
+            return dot(vt_s[:, span(j)], probs.astype(bf16))
+
+        def highest(scores):
+            return jnp.maximum(*(jnp.max(values, axis=0, keepdims=True) for values in scores))
 
         def key_step(pair, state):
             top, total, mixed = state
-            keys = [low + 2 * pair, low + 2 * pair + 1]
-            scores = [
-                score_tile(
-                    nat_s[span(j), :128], qz_part, code_s[span(j), :], seg_part,
-                    ((i - j) * BLOCK).astype(f32), slope,
-                )
-                for j in keys
-            ]
-            tops = [jnp.max(values, axis=0, keepdims=True) for values in scores]
-            top_new = jnp.maximum(top, jnp.maximum(tops[0], tops[1]))
+            keys = [member(2 * pair), member(2 * pair + 1)]
+            scores = [scores_of(j, False) for j in keys]
+            top_new = jnp.maximum(top, highest(scores))
             factor = jnp.exp(top - top_new)
-            total, mixed = total * factor, mixed * factor
-            for j, values in zip(keys, scores):
-                probs = jnp.exp(values - top_new)
-                total = total + jnp.sum(probs, axis=0, keepdims=True)
-                mixed = mixed + dot(vt_s[:, span(j)], probs.astype(bf16))
+            probs = [jnp.exp(values - top_new) for values in scores]
+            total = total * factor + jnp.sum(probs[0] + probs[1], axis=0, keepdims=True)
+            mixed = mixed * factor + (mixed_of(keys[0], probs[0]) + mixed_of(keys[1], probs[1]))
             return top_new, total, mixed
 
-        top, total, mixed = lax.fori_loop(
-            0,
-            pairs,
-            key_step,
-            (
-                jnp.full((1, BLOCK), masked_value, f32),
-                jnp.zeros((1, BLOCK), f32),
-                jnp.zeros((HEAD_DIM, BLOCK), f32),
-            ),
-        )
+        scores = [scores_of(i, True), scores_of(partner, False)]
+        top = highest(scores)
+        probs = [jnp.exp(values - top) for values in scores]
+        total = jnp.sum(probs[0] + probs[1], axis=0, keepdims=True)
+        mixed = mixed_of(i, probs[0]) + mixed_of(partner, probs[1])
+        top, total, mixed = lax.fori_loop(0, pairs, key_step, (top, total, mixed))
         mixed = mixed / total
         ot_ref[:, here] = mixed
         lse_ref[:, here] = top + jnp.log(total)
@@ -261,7 +291,7 @@
             dk, dv = state
             for i in (low + 2 * pair, low + 2 * pair + 1):
                 here = span(i)
-                scores = score_tile(
+                scores = score_tile_plain(
                     qk_part, qz_s[:, here], code_part, seg_ref[:, here],
                     ((i - j) * BLOCK).astype(f32), slope,
                 )
@@ -514,7 +544,7 @@
 
 def grad_qkv_kernel(place_ref, *refs, heads, w_rows):
     token_refs = refs[:FEATS]
-    dqkv_ref, sums_ref, back_ref, kept_ref, sent_ref, wide_s, vec_s = refs[FEATS:]
+    dqkv_ref, sums_ref, w_ref, back_ref, input_ref, kept_ref, sent_ref, wide_s, vec_s = refs[FEATS:]
     first_core = place_ref[0] == 0
     head_width = heads * HEAD_DIM
     half = 2 * head_width
@@ -550,6 +580,7 @@
     grad = dot(tokens, back, 0, 0)
     grad = jnp.concatenate([grad[:, : 2 * half - 128], grad[:, 2 * half - 128 :] + vec_s[...]], axis=1)
     split_rows(first_core, grad, kept_ref, sent_ref, slice(None), w_rows)
+    input_ref[...] = dot(back, w_ref[...], 1, 1).astype(bf16)
 
 
 def place_first_kernel(place_ref, *refs, pieces, down_rows):
@@ -1039,7 +1070,8 @@
     partial_first = (dot(back_gate, full_gate, 1, 1) + dot(back_up, full_up, 1, 1)).astype(bf16)
     partial_first = partial_first.reshape(FEATS, local, width)
     partial_got = [swap(partial_first[k], "f", k) for k in range(1, FEATS)]
-    partial_got[0], back_gate, back_up, back_mixed = tie(partial_got[0], back_gate, back_up, back_mixed)
+    small = swap(partial_first[0, :16, :128], "c")
+    small, back_gate, back_up, back_mixed = tie(small, back_gate, back_up, back_mixed)
     half_width = width // 2
 
     def chosen(first, second):
@@ -1138,17 +1170,20 @@
         dqkv = dqkv[0]
     vector_sums = jnp.concatenate([sums_one, grad_down_bias, grad_gain_two, grad_shift_two], axis=0)
     attn_shape = jax.ShapeDtypeStruct((slots * FEATS, w_rows, 2 * half), bf16)
-    back_projected, attn_kept, attn_sent = call(
+    ignored, partial_input, attn_kept, attn_sent = call(
         functools.partial(grad_qkv_kernel, heads=heads, w_rows=w_rows),
-        (jax.ShapeDtypeStruct((group, 2 * half), bf16), attn_shape, attn_shape),
+        (
+            jax.ShapeDtypeStruct((group, 2 * half), bf16),
+            jax.ShapeDtypeStruct((group, width), bf16),
+            attn_shape,
+            attn_shape,
+        ),
         "grad_qkv",
-        "s" + "v" * (FEATS + 2),
+        "s" + "v" * (FEATS + 3),
         [pltpu.VMEM((128, width), f32), pltpu.VMEM((width, 128), f32)],
-    )(here, *token_parts, dqkv, vector_sums)
-    attn_sent, back_projected = tie(attn_sent, back_projected)
-    partial_input = dot(back_projected, w_attn, 1, 1).astype(bf16).reshape(FEATS, local, width)
-    grad_attn = added(attn_kept, swap(attn_sent, "c"))
-    grad_attn, partial_input = tie(grad_attn, partial_input)
+    )(here, *token_parts, dqkv, vector_sums, w_attn)
+    partial_input = partial_input.reshape(FEATS, local, width)
+    grad_attn = added(after(attn_kept, partial_input), swap(attn_sent, "c"))
     grad_attn = grad_attn.reshape(-1, 2 * half)
     grad_down = total(grad_down, down_moved).reshape(2, down_rows, half_width)
     layer_wide_low = after(layer_wide.astype(bf16), grad_attn)

time: 269 us -> 266 us (0.989)
  waiting for transfers between devices: 76 us -> 64 us
  Pallas kernels: 60.6 us -> 67 us
  local copies, waits for them, and re-layouts: 12.1 us -> 16.8 us
    ppermute x62, waiting for transfers between devices: 71.2 us -> 59.3 us  [swap(): return lax.ppermute(values, axis, [(i, i ^ step) for i in range(size)])]
    slice x4, local copies, waits for them, and re-layouts: 0.03 us -> 3.6 us  [on_device(): second_own = jnp.concatenate([piece[:, out_half:] for piece in late_feats])]
    pallas_call x1, Pallas kernels: 15.7 us -> 19 us  [attend_back(): pl.pallas_call(attend_back_kernel, out_shape=jax.ShapeDtypeStruct(qkv.sha...]
    dot_general x11 -> x10, matrix products: 12.9 us -> 12 us  [dot(): lax.dot_general(left, right, (((left_dim,), (right_dim,)), ((), ())), pre...]
    unnamed x130 -> x128, local copies, waits for them, and re-layouts: 9.01 us -> 8.53 us
  transfers between devices with their start and end apart: 68 -> 68, of which waited for: 27 -> 27; matrix products, arithmetic and copies ran while one was open for 12% -> 12% of each run, Pallas kernels for 22% -> 25%
where the time goes in v4:
time: 266 us; the launch traced here: 263 us
  starting transfers between devices  77.7 us (29%)
  Pallas kernels  67 us (25%)
  waiting for transfers between devices  64 us (24%)
  other arithmetic  24.1 us (9%)
  local copies, waits for them, and re-layouts  16.8 us (6%)
  matrix products  12 us (5%)
    ppermute x62, waiting for transfers between devices, swap(): return lax.ppermute(values, axis, [(i, i ^ step) for i in range(size)])  59.3 us
    ppermute x62, starting transfers between devices, swap(): return lax.ppermute(values, axis, [(i, i ^ step) for i in range(size)])  53 us
    all_to_all x6, starting transfers between devices, all_to_all(): return lax.all_to_all(values, axes, split_axis=0, concat_axis=0, tiled=True)  24.6 us
    pallas_call x1, Pallas kernels, attend_back(): pl.pallas_call(attend_back_kernel, out_shape=jax.ShapeDtypeStruct(qkv.sha...  19 us
    pallas_call x1, Pallas kernels, attend(): pl.pallas_call(attend_kernel, out_shape=(jax.ShapeDtypeStruct((slots * FE...  14.4 us
    dot_general x10, matrix products, dot(): lax.dot_general(left, right, (((left_dim,), (right_dim,)), ((), ())), pre...  12 us
    unnamed x128, local copies, waits for them, and re-layouts  8.53 us
    convert_element_type x4, other arithmetic, added(): return (kept.astype(f32) + got.astype(f32)).astype(bf16)  5.51 us
  transfers between devices with their start and end apart: 68, of which 27 were waited for; matrix products, arithmetic and copies ran while one was open for 12% of the time, Pallas kernels for 25%

profile of v4, /device:TPU:0, one launch (start us, length us, event | category | flops | bytes accessed | tf_op | source)
XLA Modules:
  0.0 263.3 jit_solution(4754459486824857035)
XLA Ops:
  1.7 4.1 %collective-permute-start.1 = (bf16[64,768]{1,0:T(8,128)(2,1)S(1)}, bf16[64,768]{1,0:T(8,128)(2,1)S(1)}, u32[]{:S(2)}, u32[]{:S(2)}) collective-permute-start(bf16[64,768]{1,0:T(8,128)(2,1)S(1)} %select_bitcast_fusion.7), channel_id=1, source_target_pairs={{0,8},{8,0},{1,9},{9,1},{2,10},{10,2},{3,11},{11,3},{4,12},{12,4},... | collective-permute-start | bytes 294920 | tf_op jit(solution)/shard_map/ppermute | solution.py:42
  5.8 1.7 pack_attn.1
  7.5 3.8 %all-to-all-start = ((bf16[8,24,384]{2,1,0:T(8,128)(2,1)}), bf16[8,24,384]{2,1,0:T(8,128)(2,1)S(1)}, u32[]{:S(2)}, u32[]{:S(2)}) async-start(bf16[8,24,384]{2,1,0:T(8,128)(2,1)} %bitcast.147), calls=%async_computation | async-start | bytes 294912 | tf_op jit(solution)/shard_map/all_to_all | solution.py:86
  11.9 1.9 pack_late.1
  14.7 1.9 all-to-all-done
  19.0 1.8 route_late.1
  20.8 3.2 %collective-permute-done.2.refs_9_.refs_1_ = bf16[128,768]{1,0:T(8,128)(2,1)S(1)} collective-permute-done((bf16[128,768]{1,0:T(8,128)(2,1)S(1)}, bf16[128,768]{1,0:T(8,128)(2,1)S(1)}, u32[]{:S(2)}, u32[]{:S(2)}) %collective-permute-start.2) | collective-permute-done | bytes 196640 | tf_op jit(solution)/shard_map/ppermute | solution.py:42
  25.1 1.3 collective-permute-start.4
  28.6 1.3 collective-permute-start.13
  31.1 1.8 collective-permute-done.4
  32.9 1.5 collective-permute-start.7
  35.8 1.8 collective-permute-done.14.refs_11_.refs_3_
  37.7 1.7 collective-permute-done.7.refs_2_
  39.4 1.6 collective-permute-done.8.refs_3_
  41.0 1.6 collective-permute-start.17
  44.0 3.4 %qkv.1 = (bf16[4,768,128]{2,1,0:T(8,128)(2,1)}, bf16[768,768]{1,0:T(8,128)(2,1)}, f32[8,768]{1,0:T(8,128)}, f32[1,2048]{1,0:T(1,128)}, f32[1,2048]{1,0:T(1,128)}) custom-call(s32[4]{0:T(128)} %pad_add_fusion.1.place_ref, bf16[192,384]{1,0:T(8,128)(2,1)} %bitcast.142, bf16[192,384]{1,0:T(8,128)(2,1)} %copy-done.37, bf16[192,384]{1,0:T(8,128)(2,1)} %copy-done.39, ...), custom_call_target="tpu_custom_call" | custom-call | tf_op jit(solution)/shard_map/qkv/pallas_call | solution.py:903
  47.5 3.5 %all-to-all-start.1 = ((bf16[4,768,128]{2,1,0:T(8,128)(2,1)}), bf16[4,768,128]{2,1,0:T(8,128)(2,1)S(1)}, u32[]{:S(2)}, u32[]{:S(2)}) async-start(bf16[4,768,128]{2,1,0:T(8,128)(2,1)} %get-tuple-element.140), calls=%async_computation.1 | async-start | bytes 1572864 | tf_op jit(solution)/shard_map/all_to_all | solution.py:86
  55.7 3.2 %collective-permute-done.15.refs_1_ = bf16[384,384]{1,0:T(8,128)(2,1)S(1)} collective-permute-done((bf16[384,384]{1,0:T(8,128)(2,1)S(1)}, bf16[384,384]{1,0:T(8,128)(2,1)S(1)}, u32[]{:S(2)}, u32[]{:S(2)}) %collective-permute-start.15) | collective-permute-done | bytes 294944 | tf_op jit(solution)/shard_map/ppermute | solution.py:42
  64.1 14.4 %attend.1 = (bf16[16,64,128]{2,1,0:T(8,128)(2,1)}, f32[1,2048]{1,0:T(1,128)}, f32[64,2048]{1,0:T(8,128)}) custom-call(s32[3,8]{1,0:T(4,128)} %pad_add_fusion.table_ref, f32[1,1]{1,0:T(1,128)} %bitcast.23.slope_ref, bf16[4,768,128]{2,1,0:T(8,128)(2,1)} %copy-done, f32[1,2048]{1,0:T(1,128)} %get-tuple-element.139.seg_ref, f32[1,2048]{1,0:T(1,128)} %get-tuple-element.146.code_ref), custom_call_target="tpu_custom_call" | custom-call | tf_op jit(solution)/shard_map/attend/pallas_call | solution.py:335
  78.6 4.7 %all-to-all-start.2 = ((bf16[16,64,128]{2,1,0:T(8,128)(2,1)}), bf16[16,64,128]{2,1,0:T(8,128)(2,1)S(1)}, u32[]{:S(2)}, u32[]{:S(2)}) async-start(bf16[16,64,128]{2,1,0:T(8,128)(2,1)} %get-tuple-element.149), calls=%async_computation.2 | async-start | bytes 524288 | tf_op jit(solution)/shard_map/all_to_all | solution.py:86
  84.2 1.7 collective-permute-start.27
  86.0 3.3 %place_first.1 = (bf16[768,768]{1,0:T(8,128)(2,1)}, bf16[768,768]{1,0:T(8,128)(2,1)}) custom-call(s32[4]{0:T(128)} %pad_add_fusion.1.place_ref, bf16[384,384]{1,0:T(8,128)(2,1)} %copy-done.22, bf16[384,384]{1,0:T(8,128)(2,1)} %copy-done.25, bf16[384,384]{1,0:T(8,128)(2,1)} %copy-done.24, bf16[384,384]{1,0:T(8,128)(2,1)} %collective-permute-done.23.refs_3_, ...), custom_call_target="tpu_custom_call" | custom-call | tf_op jit(solution)/shard_map/place_first/pallas_call | solution.py:970
  89.4 2.7 %all-to-all-done.2 = bf16[16,64,128]{2,1,0:T(8,128)(2,1)S(1)} async-done(((bf16[16,64,128]{2,1,0:T(8,128)(2,1)}), bf16[16,64,128]{2,1,0:T(8,128)(2,1)S(1)}, u32[]{:S(2)}, u32[]{:S(2)}) %all-to-all-start.2) | async-done | bytes 262176 | tf_op jit(solution)/shard_map/all_to_all | solution.py:86
  92.8 3.0 %join_heads.1 = (bf16[128,768]{1,0:T(8,128)(2,1)}, f32[128,768]{1,0:T(8,128)}, bf16[128,768]{1,0:T(8,128)(2,1)}, f32[128,768]{1,0:T(8,128)}, f32[128,1]{1,0:T(8,128)}) custom-call(bf16[16,64,128]{2,1,0:T(8,128)(2,1)} %copy-done.8, bf16[128,768]{1,0:T(8,128)(2,1)} %copy-done.1, bf16[768,768]{1,0:T(8,128)(2,1)} %get-tuple-element.158.w_ref, ...), custom_call_target="tpu_custom_call" | custom-call | tf_op jit(solution)/shard_map/join_heads/pallas_call | solution.py:1007
  95.9 1.5 slice_reduce_fusion.1
  97.4 2.1 collective-permute-start.31
  101.7 3.4 %place_second.1 = (bf16[768,768]{1,0:T(8,128)(2,1)}, bf16[768,768]{1,0:T(8,128)(2,1)}) custom-call(s32[4]{0:T(128)} %pad_add_fusion.1.place_ref, bf16[192,768]{1,0:T(8,128)(2,1)} %copy-done.4, bf16[192,768]{1,0:T(8,128)(2,1)} %collective-permute-done.21.refs_1_, bf16[192,768]{1,0:T(8,128)(2,1)} %collective-permute-done.22.refs_2_, ...), custom_call_target="tpu_custom_call" | custom-call | tf_op jit(solution)/shard_map/place_second/pallas_call | solution.py:1026
  106.2 3.5 %collective-permute-done.30 = bf16[128,768]{1,0:T(8,128)(2,1)S(1)} collective-permute-done((bf16[128,768]{1,0:T(8,128)(2,1)}, bf16[128,768]{1,0:T(8,128)(2,1)S(1)}, u32[]{:S(2)}, u32[]{:S(2)}) %collective-permute-start.30) | collective-permute-done | bytes 196640 | tf_op jit(solution)/shard_map/ppermute | solution.py:42
  114.7 1.5 collective-permute-start.34
  117.0 1.6 multiply_convert_fusion.2
  118.6 5.9 %collective-permute-done.32 = bf16[128,768]{1,0:T(8,128)(2,1)S(1)} collective-permute-done((bf16[128,768]{1,0:T(8,128)(2,1)S(1)}, bf16[128,768]{1,0:T(8,128)(2,1)S(1)}, u32[]{:S(2)}, u32[]{:S(2)}) %collective-permute-start.32) | collective-permute-done | bytes 196640 | tf_op jit(solution)/shard_map/ppermute | solution.py:42
  127.5 2.1 collective-permute-start.39
  131.0 5.2 %collective-permute-done.39 = bf16[128,768]{1,0:T(8,128)(2,1)S(1)} collective-permute-done((bf16[128,768]{1,0:T(8,128)(2,1)S(1)}, bf16[128,768]{1,0:T(8,128)(2,1)S(1)}, u32[]{:S(2)}, u32[]{:S(2)}) %collective-permute-start.39) | collective-permute-done | bytes 196640 | tf_op jit(solution)/shard_map/ppermute | solution.py:42
  136.2 1.8 collective-permute-done.38
  138.4 2.4 multiply_convert_fusion
  143.5 1.9 convolution_convert_fusion.1
  146.9 2.1 collective-permute-start.42
  150.4 1.4 convolution_convert_fusion.4
  151.8 1.4 convolution_convert_fusion.3
  153.2 2.4 collective-permute-done.42.got_c_ref
  155.6 2.3 collective-permute-done.41.got_b_ref
  158.6 3.9 %back_join.1 = (f32[128,768]{1,0:T(8,128)}, bf16[16,64,128]{2,1,0:T(8,128)(2,1)}, bf16[768,384]{1,0:T(8,128)(2,1)}, bf16[768,384]{1,0:T(8,128)(2,1)}, f32[3,768]{1,0:T(4,128)}) custom-call(s32[4]{0:T(128)} %pad_add_fusion.1.place_ref, f32[128,768]{1,0:T(8,128)} %get-tuple-element.248.second_ref, bf16[128,768]{1,0:T(8,128)(2,1)} %get-tuple-element.261.own_ref, ...), custom_call_target="tpu_custom_call" | custom-call | tf_op jit(solution)/shard_map/back_join/pallas_call | solution.py:1091
  163.9 3.8 %all-to-all-start.3 = ((bf16[16,64,128]{2,1,0:T(8,128)(2,1)}), bf16[16,64,128]{2,1,0:T(8,128)(2,1)S(1)}, u32[]{:S(2)}, u32[]{:S(2)}) async-start(bf16[16,64,128]{2,1,0:T(8,128)(2,1)} %get-tuple-element.194), calls=%async_computation.3 | async-start | bytes 524288 | tf_op jit(solution)/shard_map/all_to_all | solution.py:86
  168.7 2.3 collective-permute-start.44
  171.0 1.8 fusion.34
  172.8 1.9 collective-permute-start.46
  174.7 1.7 fusion.35
  178.8 19.0 %attend_back.1 = bf16[4,768,128]{2,1,0:T(8,128)(2,1)} custom-call(s32[3,8]{1,0:T(4,128)} %pad_add_fusion.table_ref, f32[1,1]{1,0:T(1,128)} %bitcast.23.slope_ref, bf16[4,768,128]{2,1,0:T(8,128)(2,1)} %copy-done, bf16[16,64,128]{2,1,0:T(8,128)(2,1)} %copy-done.7, f32[64,2048]{1,0:T(8,128)} %get-tuple-element.195.ot_ref, ...), custom_call_target="tpu_custom_call" | custom-call | tf_op jit(solution)/shard_map/attend_back/pallas_call | solution.py:360
  198.0 3.5 %all-to-all-start.4 = ((bf16[4,768,128]{2,1,0:T(8,128)(2,1)}), bf16[4,768,128]{2,1,0:T(8,128)(2,1)S(1)}, u32[]{:S(2)}, u32[]{:S(2)}) async-start(bf16[4,768,128]{2,1,0:T(8,128)(2,1)} %attend_back.1), calls=%async_computation.4 | async-start | bytes 1572864 | tf_op jit(solution)/shard_map/all_to_all | solution.py:86
  202.8 1.3 fusion.6
  205.3 7.8 %collective-permute-done.49 = bf16[192,384]{1,0:T(8,128)(2,1)} collective-permute-done((bf16[192,384]{1,0:T(8,128)(2,1)S(1)}, bf16[192,384]{1,0:T(8,128)(2,1)}, u32[]{:S(2)}, u32[]{:S(2)}) %collective-permute-start.49) | collective-permute-done | bytes 147488 | tf_op jit(solution)/shard_map/ppermute | solution.py:42
  214.4 1.7 collective-permute-start.50
  216.1 5.2 %grad_qkv.1 = (bf16[512,768]{1,0:T(8,128)(2,1)}, bf16[512,768]{1,0:T(8,128)(2,1)}, bf16[16,24,768]{2,1,0:T(8,128)(2,1)}, bf16[16,24,768]{2,1,0:T(8,128)(2,1)}) custom-call(s32[4]{0:T(128)} %pad_add_fusion.1.place_ref, bf16[128,768]{1,0:T(8,128)(2,1)} %copy-done.1, bf16[128,768]{1,0:T(8,128)(2,1)} %copy-done.9, bf16[128,768]{1,0:T(8,128)(2,1)} %copy-done.11, ...), custom_call_target="tpu_custom_call" | custom-call | tf_op jit(solution)/shard_map/grad_qkv/pallas_call | solution.py:1173
  223.3 1.7 collective-permute-start.52
  224.9 2.2 collective-permute-start.54
  228.6 5.4 %all-to-all-start.5 = ((bf16[16,24,768]{2,1,0:T(8,128)(2,1)}), bf16[16,24,768]{2,1,0:T(8,128)(2,1)S(1)}, u32[]{:S(2)}, u32[]{:S(2)}) async-start(bf16[16,24,768]{2,1,0:T(8,128)(2,1)} %add_convert_fusion.1), calls=%async_computation.5 | async-start | bytes 1179648 | tf_op jit(solution)/shard_map/all_to_all | solution.py:86
  234.7 1.9 collective-permute-start.57
  236.6 1.5 collective-permute-start.58
  239.8 2.3 collective-permute-start.55
  242.3 7.0 %collective-permute-done.58.refs_2_ = bf16[48,1152]{1,0:T(8,128)(2,1)S(1)} collective-permute-done((bf16[48,1152]{1,0:T(8,128)(2,1)S(1)}, bf16[48,1152]{1,0:T(8,128)(2,1)S(1)}, u32[]{:S(2)}, u32[]{:S(2)}) %collective-permute-start.58) | collective-permute-done | bytes 110624 | tf_op jit(solution)/shard_map/ppermute | solution.py:42
  249.3 4.2 %collective-permute-done.59.refs_3_ = bf16[48,1152]{1,0:T(8,128)(2,1)S(1)} collective-permute-done((bf16[48,1152]{1,0:T(8,128)(2,1)S(1)}, bf16[48,1152]{1,0:T(8,128)(2,1)S(1)}, u32[]{:S(2)}, u32[]{:S(2)}) %collective-permute-start.59) | collective-permute-done | bytes 110624 | tf_op jit(solution)/shard_map/ppermute | solution.py:42
  254.1 1.8 finish_late.1
  258.2 2.2 finish_wide.1
  261.2 1.9 finish.1
  (286 shorter events, 62.0 us)
Async XLA Ops:
  1.7 12.1 %collective-permute-start.1 = (bf16[64,768]{1,0:T(8,128)(2,1)S(1)}, bf16[64,768]{1,0:T(8,128)(2,1)S(1)}, u32[]{:S(2)}, u32[]{:S(2)}) collective-permute-start(bf16[64,768]{1,0:T(8,128)(2,1)S(1)} %select_bitcast_fusion.7), channel_id=1, source_target_pairs={{0,8},{8,0},{1,9},{9,1},{2,10},{10,2},{3,11},{11,3},{4,12},{12,4},... | collective-permute-start | bytes 294920 | tf_op jit(solution)/shard_map/ppermute | solution.py:42
  7.5 9.1 %all-to-all-start = ((bf16[8,24,384]{2,1,0:T(8,128)(2,1)}), bf16[8,24,384]{2,1,0:T(8,128)(2,1)S(1)}, u32[]{:S(2)}, u32[]{:S(2)}) async-start(bf16[8,24,384]{2,1,0:T(8,128)(2,1)} %bitcast.147), calls=%async_computation | async-start | bytes 294912 | tf_op jit(solution)/shard_map/all_to_all | solution.py:86
  16.6 7.4 %collective-permute-start.2 = (bf16[128,768]{1,0:T(8,128)(2,1)S(1)}, bf16[128,768]{1,0:T(8,128)(2,1)S(1)}, u32[]{:S(2)}, u32[]{:S(2)}) collective-permute-start(bf16[128,768]{1,0:T(8,128)(2,1)S(1)} %pad_maximum_fusion.2.refs_8_.tokens_ref.refs_0_), channel_id=1, source_target_pairs={{0,2},{2,0},{4,6},{6,4},{1,3},{3,1},{5,7},{7,5},{8,10},{10,8},{12,... | collective-permute-start | bytes 589832 | tf_op jit(solution)/shard_map/ppermute | solution.py:42
  17.6 11.0 %collective-permute-start.6 = (bf16[192,384]{1,0:T(8,128)(2,1)S(1)}, bf16[192,384]{1,0:T(8,128)(2,1)S(1)}, u32[]{:S(2)}, u32[]{:S(2)}) collective-permute-start(bf16[192,384]{1,0:T(8,128)(2,1)S(1)} %bitcast.139), channel_id=1, source_target_pairs={{0,8},{8,0},{1,9},{9,1},{2,10},{10,2},{3,11},{11,3},{4,12},{12,4},... | collective-permute-start | bytes 442376 | tf_op jit(solution)/shard_map/ppermute | solution.py:42
  24.0 7.1 %collective-permute-start.5 = (bf16[48,1152]{1,0:T(8,128)(2,1)}, bf16[48,1152]{1,0:T(8,128)(2,1)S(1)}, u32[]{:S(2)}, u32[]{:S(2)}) collective-permute-start(bf16[48,1152]{1,0:T(8,128)(2,1)} %get-tuple-element.137), channel_id=1, source_target_pairs={{0,6},{2,4},{4,2},{6,0},{1,7},{3,5},{5,3},{7,1},{8,14},{10,12},{12... | collective-permute-start | bytes 331784 | tf_op jit(solution)/shard_map/ppermute | solution.py:42
  25.1 7.8 %collective-permute-start.4 = (bf16[48,1152]{1,0:T(8,128)(2,1)}, bf16[48,1152]{1,0:T(8,128)(2,1)S(1)}, u32[]{:S(2)}, u32[]{:S(2)}) collective-permute-start(bf16[48,1152]{1,0:T(8,128)(2,1)} %get-tuple-element.135), channel_id=1, source_target_pairs={{0,4},{2,6},{4,0},{6,2},{1,5},{3,7},{5,1},{7,3},{8,12},{10,14},{12... | collective-permute-start | bytes 331784 | tf_op jit(solution)/shard_map/ppermute | solution.py:42
  26.4 8.0 %collective-permute-start.3 = (bf16[48,1152]{1,0:T(8,128)(2,1)}, bf16[48,1152]{1,0:T(8,128)(2,1)S(1)}, u32[]{:S(2)}, u32[]{:S(2)}) collective-permute-start(bf16[48,1152]{1,0:T(8,128)(2,1)} %get-tuple-element.133), channel_id=1, source_target_pairs={{0,2},{2,0},{4,6},{6,4},{1,3},{3,1},{5,7},{7,5},{8,10},{10,8},{12,... | collective-permute-start | bytes 331784 | tf_op jit(solution)/shard_map/ppermute | solution.py:42
  27.5 10.2 %collective-permute-start.14 = (bf16[128,768]{1,0:T(8,128)(2,1)S(1)}, bf16[128,768]{1,0:T(8,128)(2,1)S(1)}, u32[]{:S(2)}, u32[]{:S(2)}) collective-permute-start(bf16[128,768]{1,0:T(8,128)(2,1)S(1)} %pad_maximum_fusion.2.refs_8_.tokens_ref.refs_0_), channel_id=1, source_target_pairs={{0,6},{2,4},{4,2},{6,0},{1,7},{3,5},{5,3},{7,1},{8,14},{10,12},{12... | collective-permute-start | bytes 589832 | tf_op jit(solution)/shard_map/ppermute | solution.py:42
  28.6 12.3 %collective-permute-start.13 = (bf16[128,768]{1,0:T(8,128)(2,1)S(1)}, bf16[128,768]{1,0:T(8,128)(2,1)S(1)}, u32[]{:S(2)}, u32[]{:S(2)}) collective-permute-start(bf16[128,768]{1,0:T(8,128)(2,1)S(1)} %pad_maximum_fusion.2.refs_8_.tokens_ref.refs_0_), channel_id=1, source_target_pairs={{0,4},{2,6},{4,0},{6,2},{1,5},{3,7},{5,1},{7,3},{8,12},{10,14},{12... | collective-permute-start | bytes 589832 | tf_op jit(solution)/shard_map/ppermute | solution.py:42
  31.1 11.5 %collective-permute-start.9 = (bf16[192,384]{1,0:T(8,128)(2,1)S(1)}, bf16[192,384]{1,0:T(8,128)(2,1)S(1)}, u32[]{:S(2)}, u32[]{:S(2)}) collective-permute-start(bf16[192,384]{1,0:T(8,128)(2,1)S(1)} %bitcast.140), channel_id=1, source_target_pairs={{0,1},{1,0},{2,3},{3,2},{4,5},{5,4},{6,7},{7,6},{8,9},{9,8},{10,11... | collective-permute-start | bytes 442376 | tf_op jit(solution)/shard_map/ppermute | solution.py:42
  32.9 6.4 %collective-permute-start.7 = (bf16[192,384]{1,0:T(8,128)(2,1)S(1)}, bf16[192,384]{1,0:T(8,128)(2,1)S(1)}, u32[]{:S(2)}, u32[]{:S(2)}) collective-permute-start(bf16[192,384]{1,0:T(8,128)(2,1)S(1)} %bitcast.141), channel_id=1, source_target_pairs={{0,16},{16,0},{1,17},{17,1},{2,18},{18,2},{3,19},{19,3},{4,20},{20... | collective-permute-start | bytes 442376 | tf_op jit(solution)/shard_map/ppermute | solution.py:42
  34.5 6.5 %collective-permute-start.8 = (bf16[192,384]{1,0:T(8,128)(2,1)S(1)}, bf16[192,384]{1,0:T(8,128)(2,1)S(1)}, u32[]{:S(2)}, u32[]{:S(2)}) collective-permute-start(bf16[192,384]{1,0:T(8,128)(2,1)S(1)} %collective-permute-done.6.refs_1_), channel_id=1, source_target_pairs={{0,16},{16,0},{1,17},{17,1},{2,18},{18,2},{3,19},{19,3},{4,20},{20... | collective-permute-start | bytes 442376 | tf_op jit(solution)/shard_map/ppermute | solution.py:42
  37.7 4.9 %collective-permute-start.10 = (bf16[192,384]{1,0:T(8,128)(2,1)S(1)}, bf16[192,384]{1,0:T(8,128)(2,1)S(1)}, u32[]{:S(2)}, u32[]{:S(2)}) collective-permute-start(bf16[192,384]{1,0:T(8,128)(2,1)S(1)} %collective-permute-done.6.refs_1_), channel_id=1, source_target_pairs={{0,1},{1,0},{2,3},{3,2},{4,5},{5,4},{6,7},{7,6},{8,9},{9,8},{10,11... | collective-permute-start | bytes 442376 | tf_op jit(solution)/shard_map/ppermute | solution.py:42
  39.4 3.2 %collective-permute-start.11 = (bf16[192,384]{1,0:T(8,128)(2,1)S(1)}, bf16[192,384]{1,0:T(8,128)(2,1)S(1)}, u32[]{:S(2)}, u32[]{:S(2)}) collective-permute-start(bf16[192,384]{1,0:T(8,128)(2,1)S(1)} %collective-permute-done.7.refs_2_), channel_id=1, source_target_pairs={{0,1},{1,0},{2,3},{3,2},{4,5},{5,4},{6,7},{7,6},{8,9},{9,8},{10,11... | collective-permute-start | bytes 442376 | tf_op jit(solution)/shard_map/ppermute | solution.py:42
  41.0 14.2 %collective-permute-start.17 = (bf16[384,384]{1,0:T(8,128)(2,1)S(1)}, bf16[384,384]{1,0:T(8,128)(2,1)S(1)}, u32[]{:S(2)}, u32[]{:S(2)}) collective-permute-start(bf16[384,384]{1,0:T(8,128)(2,1)S(1)} %slice_dynamic-update-slice_fusion.refs_0_), channel_id=1, source_target_pairs={{0,16},{16,0},{1,17},{17,1},{2,18},{18,2},{3,19},{19,3},{4,20},{20... | collective-permute-start | bytes 884744 | tf_op jit(solution)/shard_map/ppermute | solution.py:42
  42.5 16.3 %collective-permute-start.15 = (bf16[384,384]{1,0:T(8,128)(2,1)S(1)}, bf16[384,384]{1,0:T(8,128)(2,1)S(1)}, u32[]{:S(2)}, u32[]{:S(2)}) collective-permute-start(bf16[384,384]{1,0:T(8,128)(2,1)S(1)} %slice_dynamic-update-slice_fusion.refs_0_), channel_id=1, source_target_pairs={{0,8},{8,0},{1,9},{9,1},{2,10},{10,2},{3,11},{11,3},{4,12},{12,4},... | collective-permute-start | bytes 884744 | tf_op jit(solution)/shard_map/ppermute | solution.py:42
  47.5 15.1 %all-to-all-start.1 = ((bf16[4,768,128]{2,1,0:T(8,128)(2,1)}), bf16[4,768,128]{2,1,0:T(8,128)(2,1)S(1)}, u32[]{:S(2)}, u32[]{:S(2)}) async-start(bf16[4,768,128]{2,1,0:T(8,128)(2,1)} %get-tuple-element.140), calls=%async_computation.1 | async-start | bytes 1572864 | tf_op jit(solution)/shard_map/all_to_all | solution.py:86
  54.6 6.8 %collective-permute-start.18 = (bf16[384,384]{1,0:T(8,128)(2,1)S(1)}, bf16[384,384]{1,0:T(8,128)(2,1)S(1)}, u32[]{:S(2)}, u32[]{:S(2)}) collective-permute-start(bf16[384,384]{1,0:T(8,128)(2,1)S(1)} %slice_dynamic-update-slice_fusion.refs_0_), channel_id=1, source_target_pairs={{0,1},{1,0},{2,3},{3,2},{4,5},{5,4},{6,7},{7,6},{8,9},{9,8},{10,11... | collective-permute-start | bytes 884744 | tf_op jit(solution)/shard_map/ppermute | solution.py:42
  55.1 7.5 %collective-permute-start.16 = (bf16[192,768]{1,0:T(8,128)(2,1)S(1)}, bf16[192,768]{1,0:T(8,128)(2,1)S(1)}, u32[]{:S(2)}, u32[]{:S(2)}) collective-permute-start(bf16[192,768]{1,0:T(8,128)(2,1)S(1)} %pad_maximum_fusion.1.refs_0_), channel_id=1, source_target_pairs={{0,1},{1,0},{2,3},{3,2},{4,5},{5,4},{6,7},{7,6},{8,9},{9,8},{10,11... | collective-permute-start | bytes 884744 | tf_op jit(solution)/shard_map/ppermute | solution.py:42
  55.2 7.3 %collective-permute-start.20 = (bf16[384,384]{1,0:T(8,128)(2,1)S(1)}, bf16[384,384]{1,0:T(8,128)(2,1)S(1)}, u32[]{:S(2)}, u32[]{:S(2)}) collective-permute-start(bf16[384,384]{1,0:T(8,128)(2,1)S(1)} %collective-permute-done.17.refs_2_), channel_id=1, source_target_pairs={{0,1},{1,0},{2,3},{3,2},{4,5},{5,4},{6,7},{7,6},{8,9},{9,8},{10,11... | collective-permute-start | bytes 884744 | tf_op jit(solution)/shard_map/ppermute | solution.py:42
  58.9 3.7 %collective-permute-start.19 = (bf16[384,384]{1,0:T(8,128)(2,1)S(1)}, bf16[384,384]{1,0:T(8,128)(2,1)S(1)}, u32[]{:S(2)}, u32[]{:S(2)}) collective-permute-start(bf16[384,384]{1,0:T(8,128)(2,1)S(1)} %collective-permute-done.15.refs_1_), channel_id=1, source_target_pairs={{0,1},{1,0},{2,3},{3,2},{4,5},{5,4},{6,7},{7,6},{8,9},{9,8},{10,11... | collective-permute-start | bytes 884744 | tf_op jit(solution)/shard_map/ppermute | solution.py:42
  59.6 19.0 %collective-permute-start.22 = (bf16[192,768]{1,0:T(8,128)(2,1)S(1)}, bf16[192,768]{1,0:T(8,128)(2,1)}, u32[]{:S(2)}, u32[]{:S(2)}) collective-permute-start(bf16[192,768]{1,0:T(8,128)(2,1)S(1)} %pad_maximum_fusion.1.refs_0_), channel_id=1, source_target_pairs={{0,16},{16,0},{1,17},{17,1},{2,18},{18,2},{3,19},{19,3},{4,20},{20... | collective-permute-start | bytes 884744 | tf_op jit(solution)/shard_map/ppermute | solution.py:42
  61.4 17.2 %collective-permute-start.21 = (bf16[192,768]{1,0:T(8,128)(2,1)S(1)}, bf16[192,768]{1,0:T(8,128)(2,1)}, u32[]{:S(2)}, u32[]{:S(2)}) collective-permute-start(bf16[192,768]{1,0:T(8,128)(2,1)S(1)} %pad_maximum_fusion.1.refs_0_), channel_id=1, source_target_pairs={{0,8},{8,0},{1,9},{9,1},{2,10},{10,2},{3,11},{11,3},{4,12},{12,4},... | collective-permute-start | bytes 884744 | tf_op jit(solution)/shard_map/ppermute | solution.py:42
  62.6 16.0 %collective-permute-start.23 = (bf16[384,384]{1,0:T(8,128)(2,1)S(1)}, bf16[384,384]{1,0:T(8,128)(2,1)}, u32[]{:S(2)}, u32[]{:S(2)}) collective-permute-start(bf16[384,384]{1,0:T(8,128)(2,1)S(1)} %collective-permute-done.15.refs_1_), channel_id=1, source_target_pairs={{0,16},{16,0},{1,17},{17,1},{2,18},{18,2},{3,19},{19,3},{4,20},{20... | collective-permute-start | bytes 884744 | tf_op jit(solution)/shard_map/ppermute | solution.py:42
  78.6 13.5 %all-to-all-start.2 = ((bf16[16,64,128]{2,1,0:T(8,128)(2,1)}), bf16[16,64,128]{2,1,0:T(8,128)(2,1)S(1)}, u32[]{:S(2)}, u32[]{:S(2)}) async-start(bf16[16,64,128]{2,1,0:T(8,128)(2,1)} %get-tuple-element.149), calls=%async_computation.2 | async-start | bytes 524288 | tf_op jit(solution)/shard_map/all_to_all | solution.py:86
  83.7 5.7 %collective-permute-start.25 = (bf16[192,768]{1,0:T(8,128)(2,1)}, bf16[192,768]{1,0:T(8,128)(2,1)S(1)}, u32[]{:S(2)}, u32[]{:S(2)}) collective-permute-start(bf16[192,768]{1,0:T(8,128)(2,1)} %collective-permute-done.22.refs_2_), channel_id=1, source_target_pairs={{0,1},{1,0},{2,3},{3,2},{4,5},{5,4},{6,7},{7,6},{8,9},{9,8},{10,11... | collective-permute-start | bytes 884744 | tf_op jit(solution)/shard_map/ppermute | solution.py:42
  83.8 5.5 %collective-permute-start.24 = (bf16[192,768]{1,0:T(8,128)(2,1)}, bf16[192,768]{1,0:T(8,128)(2,1)}, u32[]{:S(2)}, u32[]{:S(2)}) collective-permute-start(bf16[192,768]{1,0:T(8,128)(2,1)} %collective-permute-done.21.refs_1_), channel_id=1, source_target_pairs={{0,1},{1,0},{2,3},{3,2},{4,5},{5,4},{6,7},{7,6},{8,9},{9,8},{10,11... | collective-permute-start | bytes 884744 | tf_op jit(solution)/shard_map/ppermute | solution.py:42
  84.2 11.7 %collective-permute-start.27 = (bf16[192,768]{1,0:T(8,128)(2,1)}, bf16[192,768]{1,0:T(8,128)(2,1)}, u32[]{:S(2)}, u32[]{:S(2)}) collective-permute-start(bf16[192,768]{1,0:T(8,128)(2,1)} %collective-permute-done.21.refs_1_), channel_id=1, source_target_pairs={{0,16},{16,0},{1,17},{17,1},{2,18},{18,2},{3,19},{19,3},{4,20},{20... | collective-permute-start | bytes 884744 | tf_op jit(solution)/shard_map/ppermute | solution.py:42
  85.9 15.0 %collective-permute-start.36 = (bf16[64,768]{1,0:T(8,128)(2,1)S(1)}, bf16[64,768]{1,0:T(8,128)(2,1)S(1)}, u32[]{:S(2)}, u32[]{:S(2)}) collective-permute-start(bf16[64,768]{1,0:T(8,128)(2,1)S(1)} %select_bitcast_fusion.4), channel_id=1, source_target_pairs={{0,8},{8,0},{1,9},{9,1},{2,10},{10,2},{3,11},{11,3},{4,12},{12,4},... | collective-permute-start | bytes 294920 | tf_op jit(solution)/shard_map/ppermute | solution.py:42
  95.8 5.1 %collective-permute-start.28 = (bf16[192,768]{1,0:T(8,128)(2,1)}, bf16[192,768]{1,0:T(8,128)(2,1)S(1)}, u32[]{:S(2)}, u32[]{:S(2)}) collective-permute-start(bf16[192,768]{1,0:T(8,128)(2,1)} %collective-permute-done.27.refs_3_), channel_id=1, source_target_pairs={{0,1},{1,0},{2,3},{3,2},{4,5},{5,4},{6,7},{7,6},{8,9},{9,8},{10,11... | collective-permute-start | bytes 884744 | tf_op jit(solution)/shard_map/ppermute | solution.py:42
  97.4 8.9 %collective-permute-start.31 = (bf16[128,768]{1,0:T(8,128)(2,1)}, bf16[128,768]{1,0:T(8,128)(2,1)S(1)}, u32[]{:S(2)}, u32[]{:S(2)}) collective-permute-start(bf16[128,768]{1,0:T(8,128)(2,1)} %get-tuple-element.169), channel_id=1, source_target_pairs={{0,6},{2,4},{4,2},{6,0},{1,7},{3,5},{5,3},{7,1},{8,14},{10,12},{12... | collective-permute-start | bytes 589832 | tf_op jit(solution)/shard_map/ppermute | solution.py:42
  99.5 10.3 %collective-permute-start.30 = (bf16[128,768]{1,0:T(8,128)(2,1)}, bf16[128,768]{1,0:T(8,128)(2,1)S(1)}, u32[]{:S(2)}, u32[]{:S(2)}) collective-permute-start(bf16[128,768]{1,0:T(8,128)(2,1)} %get-tuple-element.169), channel_id=1, source_target_pairs={{0,4},{2,6},{4,0},{6,2},{1,5},{3,7},{5,1},{7,3},{8,12},{10,14},{12... | collective-permute-start | bytes 589832 | tf_op jit(solution)/shard_map/ppermute | solution.py:42
  100.0 10.0 %collective-permute-start.29 = (bf16[128,768]{1,0:T(8,128)(2,1)}, bf16[128,768]{1,0:T(8,128)(2,1)S(1)}, u32[]{:S(2)}, u32[]{:S(2)}) collective-permute-start(bf16[128,768]{1,0:T(8,128)(2,1)} %get-tuple-element.169), channel_id=1, source_target_pairs={{0,2},{2,0},{4,6},{6,4},{1,3},{3,1},{5,7},{7,5},{8,10},{10,8},{12,... | collective-permute-start | bytes 589832 | tf_op jit(solution)/shard_map/ppermute | solution.py:42
  113.5 11.1 %collective-permute-start.32 = (bf16[128,768]{1,0:T(8,128)(2,1)S(1)}, bf16[128,768]{1,0:T(8,128)(2,1)S(1)}, u32[]{:S(2)}, u32[]{:S(2)}) collective-permute-start(bf16[128,768]{1,0:T(8,128)(2,1)S(1)} %get-tuple-element.262), channel_id=1, source_target_pairs={{0,2},{2,0},{4,6},{6,4},{1,3},{3,1},{5,7},{7,5},{8,10},{10,8},{12,... | collective-permute-start | bytes 589832 | tf_op jit(solution)/shard_map/ppermute | solution.py:42
  114.7 9.9 %collective-permute-start.34 = (bf16[128,768]{1,0:T(8,128)(2,1)S(1)}, bf16[128,768]{1,0:T(8,128)(2,1)S(1)}, u32[]{:S(2)}, u32[]{:S(2)}) collective-permute-start(bf16[128,768]{1,0:T(8,128)(2,1)S(1)} %get-tuple-element.263), channel_id=1, source_target_pairs={{0,6},{2,4},{4,2},{6,0},{1,7},{3,5},{5,3},{7,1},{8,14},{10,12},{12... | collective-permute-start | bytes 589832 | tf_op jit(solution)/shard_map/ppermute | solution.py:42
  116.3 9.6 %collective-permute-start.33 = (bf16[128,768]{1,0:T(8,128)(2,1)S(1)}, bf16[128,768]{1,0:T(8,128)(2,1)S(1)}, u32[]{:S(2)}, u32[]{:S(2)}) collective-permute-start(bf16[128,768]{1,0:T(8,128)(2,1)S(1)} %get-tuple-element.264), channel_id=1, source_target_pairs={{0,4},{2,6},{4,0},{6,2},{1,5},{3,7},{5,1},{7,3},{8,12},{10,14},{12... | collective-permute-start | bytes 589832 | tf_op jit(solution)/shard_map/ppermute | solution.py:42
  127.5 8.7 %collective-permute-start.39 = (bf16[128,768]{1,0:T(8,128)(2,1)S(1)}, bf16[128,768]{1,0:T(8,128)(2,1)S(1)}, u32[]{:S(2)}, u32[]{:S(2)}) collective-permute-start(bf16[128,768]{1,0:T(8,128)(2,1)S(1)} %get-tuple-element.247), channel_id=1, source_target_pairs={{0,6},{2,4},{4,2},{6,0},{1,7},{3,5},{5,3},{7,1},{8,14},{10,12},{12... | collective-permute-start | bytes 589832 | tf_op jit(solution)/shard_map/ppermute | solution.py:42
  129.6 8.4 %collective-permute-start.38 = (bf16[128,768]{1,0:T(8,128)(2,1)S(1)}, bf16[128,768]{1,0:T(8,128)(2,1)S(1)}, u32[]{:S(2)}, u32[]{:S(2)}) collective-permute-start(bf16[128,768]{1,0:T(8,128)(2,1)S(1)} %get-tuple-element.247), channel_id=1, source_target_pairs={{0,4},{2,6},{4,0},{6,2},{1,5},{3,7},{5,1},{7,3},{8,12},{10,14},{12... | collective-permute-start | bytes 589832 | tf_op jit(solution)/shard_map/ppermute | solution.py:42
  130.1 8.3 %collective-permute-start.37 = (bf16[128,768]{1,0:T(8,128)(2,1)S(1)}, bf16[128,768]{1,0:T(8,128)(2,1)}, u32[]{:S(2)}, u32[]{:S(2)}) collective-permute-start(bf16[128,768]{1,0:T(8,128)(2,1)S(1)} %get-tuple-element.247), channel_id=1, source_target_pairs={{0,2},{2,0},{4,6},{6,4},{1,3},{3,1},{5,7},{7,5},{8,10},{10,8},{12,... | collective-permute-start | bytes 589832 | tf_op jit(solution)/shard_map/ppermute | solution.py:42
  146.9 8.7 %collective-permute-start.42 = (bf16[128,768]{1,0:T(8,128)(2,1)S(1)}, bf16[128,768]{1,0:T(8,128)(2,1)S(1)}, u32[]{:S(2)}, u32[]{:S(2)}) collective-permute-start(bf16[128,768]{1,0:T(8,128)(2,1)S(1)} %get-tuple-element.258), channel_id=1, source_target_pairs={{0,6},{2,4},{4,2},{6,0},{1,7},{3,5},{5,3},{7,1},{8,14},{10,12},{12... | collective-permute-start | bytes 589832 | tf_op jit(solution)/shard_map/ppermute | solution.py:42
  149.0 8.9 %collective-permute-start.41 = (bf16[128,768]{1,0:T(8,128)(2,1)S(1)}, bf16[128,768]{1,0:T(8,128)(2,1)S(1)}, u32[]{:S(2)}, u32[]{:S(2)}) collective-permute-start(bf16[128,768]{1,0:T(8,128)(2,1)S(1)} %get-tuple-element.259), channel_id=1, source_target_pairs={{0,4},{2,6},{4,0},{6,2},{1,5},{3,7},{5,1},{7,3},{8,12},{10,14},{12... | collective-permute-start | bytes 589832 | tf_op jit(solution)/shard_map/ppermute | solution.py:42
  149.5 8.4 %collective-permute-start.40 = (bf16[128,768]{1,0:T(8,128)(2,1)S(1)}, bf16[128,768]{1,0:T(8,128)(2,1)S(1)}, u32[]{:S(2)}, u32[]{:S(2)}) collective-permute-start(bf16[128,768]{1,0:T(8,128)(2,1)S(1)} %get-tuple-element.260), channel_id=1, source_target_pairs={{0,2},{2,0},{4,6},{6,4},{1,3},{3,1},{5,7},{7,5},{8,10},{10,8},{12,... | collective-permute-start | bytes 589832 | tf_op jit(solution)/shard_map/ppermute | solution.py:42
  158.0 9.7 %collective-permute-start.43 = (bf16[768,768]{1,0:T(8,128)(2,1)}, bf16[768,768]{1,0:T(8,128)(2,1)S(1)}, u32[]{:S(2)}, u32[]{:S(2)}) collective-permute-start(bf16[768,768]{1,0:T(8,128)(2,1)} %convolution_convert_fusion.1), channel_id=1, source_target_pairs={{0,1},{1,0},{2,3},{3,2},{4,5},{5,4},{6,7},{7,6},{8,9},{9,8},{10,11... | collective-permute-start | bytes 3538952 | tf_op jit(solution)/shard_map/ppermute | solution.py:42
  158.0 13.0 %collective-permute-start.45 = (bf16[768,384]{1,0:T(8,128)(2,1)}, bf16[768,384]{1,0:T(8,128)(2,1)}, u32[]{:S(2)}, u32[]{:S(2)}) collective-permute-start(bf16[768,384]{1,0:T(8,128)(2,1)} %convolution_convert_fusion.4), channel_id=1, source_target_pairs={{0,1},{1,0},{2,3},{3,2},{4,5},{5,4},{6,7},{7,6},{8,9},{9,8},{10,11... | collective-permute-start | bytes 1769480 | tf_op jit(solution)/shard_map/ppermute | solution.py:42
  162.5 12.2 %collective-permute-start.47 = (bf16[768,384]{1,0:T(8,128)(2,1)}, bf16[768,384]{1,0:T(8,128)(2,1)}, u32[]{:S(2)}, u32[]{:S(2)}) collective-permute-start(bf16[768,384]{1,0:T(8,128)(2,1)} %get-tuple-element.201), channel_id=1, source_target_pairs={{0,1},{1,0},{2,3},{3,2},{4,5},{5,4},{6,7},{7,6},{8,9},{9,8},{10,11... | collective-permute-start | bytes 1769480 | tf_op jit(solution)/shard_map/ppermute | solution.py:42
  163.2 13.4 %collective-permute-start.35 = (bf16[64,768]{1,0:T(8,128)(2,1)}, bf16[64,768]{1,0:T(8,128)(2,1)S(1)}, u32[]{:S(2)}, u32[]{:S(2)}) collective-permute-start(bf16[64,768]{1,0:T(8,128)(2,1)} %broadcast_select_fusion.5), channel_id=1, source_target_pairs={{0,8},{8,0},{1,9},{9,1},{2,10},{10,2},{3,11},{11,3},{4,12},{12,4},... | collective-permute-start | bytes 294920 | tf_op jit(solution)/shard_map/ppermute | solution.py:42
  163.9 14.2 %all-to-all-start.3 = ((bf16[16,64,128]{2,1,0:T(8,128)(2,1)}), bf16[16,64,128]{2,1,0:T(8,128)(2,1)S(1)}, u32[]{:S(2)}, u32[]{:S(2)}) async-start(bf16[16,64,128]{2,1,0:T(8,128)(2,1)} %get-tuple-element.194), calls=%async_computation.3 | async-start | bytes 524288 | tf_op jit(solution)/shard_map/all_to_all | solution.py:86
  168.7 29.3 %collective-permute-start.44 = (bf16[2,192,768]{2,1,0:T(8,128)(2,1)}, bf16[2,192,768]{2,1,0:T(8,128)(2,1)S(1)}, u32[]{:S(2)}, u32[]{:S(2)}) collective-permute-start(bf16[2,192,768]{2,1,0:T(8,128)(2,1)} %fusion.11), channel_id=1, source_target_pairs={{0,8},{8,0},{1,9},{9,1},{2,10},{10,2},{3,11},{11,3},{4,12},{12,4},... | collective-permute-start | bytes 1769480 | tf_op jit(solution)/shard_map/ppermute | solution.py:42
  172.8 24.9 %collective-permute-start.46 = (bf16[384,384]{1,0:T(8,128)(2,1)}, bf16[384,384]{1,0:T(8,128)(2,1)}, u32[]{:S(2)}, u32[]{:S(2)}) collective-permute-start(bf16[384,384]{1,0:T(8,128)(2,1)} %fusion.34), channel_id=1, source_target_pairs={{0,16},{16,0},{1,17},{17,1},{2,18},{18,2},{3,19},{19,3},{4,20},{20... | collective-permute-start | bytes 884744 | tf_op jit(solution)/shard_map/ppermute | solution.py:42
  176.5 21.3 %collective-permute-start.48 = (bf16[384,384]{1,0:T(8,128)(2,1)}, bf16[384,384]{1,0:T(8,128)(2,1)}, u32[]{:S(2)}, u32[]{:S(2)}) collective-permute-start(bf16[384,384]{1,0:T(8,128)(2,1)} %fusion.35), channel_id=1, source_target_pairs={{0,16},{16,0},{1,17},{17,1},{2,18},{18,2},{3,19},{19,3},{4,20},{20... | collective-permute-start | bytes 884744 | tf_op jit(solution)/shard_map/ppermute | solution.py:42
  198.0 15.2 %all-to-all-start.4 = ((bf16[4,768,128]{2,1,0:T(8,128)(2,1)}), bf16[4,768,128]{2,1,0:T(8,128)(2,1)S(1)}, u32[]{:S(2)}, u32[]{:S(2)}) async-start(bf16[4,768,128]{2,1,0:T(8,128)(2,1)} %attend_back.1), calls=%async_computation.4 | async-start | bytes 1572864 | tf_op jit(solution)/shard_map/all_to_all | solution.py:86
  202.7 10.4 %collective-permute-start.49 = (bf16[192,384]{1,0:T(8,128)(2,1)S(1)}, bf16[192,384]{1,0:T(8,128)(2,1)}, u32[]{:S(2)}, u32[]{:S(2)}) collective-permute-start(bf16[192,384]{1,0:T(8,128)(2,1)S(1)} %broadcast_select_fusion), channel_id=1, source_target_pairs={{0,8},{8,0},{1,9},{9,1},{2,10},{10,2},{3,11},{11,3},{4,12},{12,4},... | collective-permute-start | bytes 442376 | tf_op jit(solution)/shard_map/ppermute | solution.py:42
  214.3 12.9 %collective-permute-start.51 = (bf16[192,384]{1,0:T(8,128)(2,1)S(1)}, bf16[192,384]{1,0:T(8,128)(2,1)S(1)}, u32[]{:S(2)}, u32[]{:S(2)}) collective-permute-start(bf16[192,384]{1,0:T(8,128)(2,1)S(1)} %select_bitcast_fusion.1), channel_id=1, source_target_pairs={{0,8},{8,0},{1,9},{9,1},{2,10},{10,2},{3,11},{11,3},{4,12},{12,4},... | collective-permute-start | bytes 442376 | tf_op jit(solution)/shard_map/ppermute | solution.py:42
  214.4 13.1 %collective-permute-start.50 = (bf16[192,768]{1,0:T(8,128)(2,1)S(1)}, bf16[192,768]{1,0:T(8,128)(2,1)S(1)}, u32[]{:S(2)}, u32[]{:S(2)}) collective-permute-start(bf16[192,768]{1,0:T(8,128)(2,1)S(1)} %select_bitcast_fusion), channel_id=1, source_target_pairs={{0,16},{16,0},{1,17},{17,1},{2,18},{18,2},{3,19},{19,3},{4,20},{20... | collective-permute-start | bytes 884744 | tf_op jit(solution)/shard_map/ppermute | solution.py:42
  222.5 5.1 %collective-permute-start.56 = (bf16[16,24,768]{2,1,0:T(8,128)(2,1)}, bf16[16,24,768]{2,1,0:T(8,128)(2,1)S(1)}, u32[]{:S(2)}, u32[]{:S(2)}) collective-permute-start(bf16[16,24,768]{2,1,0:T(8,128)(2,1)} %get-tuple-element.214), channel_id=1, source_target_pairs={{0,1},{1,0},{2,3},{3,2},{4,5},{5,4},{6,7},{7,6},{8,9},{9,8},{10,11... | collective-permute-start | bytes 1769480 | tf_op jit(solution)/shard_map/ppermute | solution.py:42
  223.3 14.8 %collective-permute-start.52 = (bf16[128,768]{1,0:T(8,128)(2,1)S(1)}, bf16[128,768]{1,0:T(8,128)(2,1)S(1)}, u32[]{:S(2)}, u32[]{:S(2)}) collective-permute-start(bf16[128,768]{1,0:T(8,128)(2,1)S(1)} %get-tuple-element.255), channel_id=1, source_target_pairs={{0,2},{2,0},{4,6},{6,4},{1,3},{3,1},{5,7},{7,5},{8,10},{10,8},{12,... | collective-permute-start | bytes 589832 | tf_op jit(solution)/shard_map/ppermute | solution.py:42
  224.9 13.8 %collective-permute-start.54 = (bf16[128,768]{1,0:T(8,128)(2,1)S(1)}, bf16[128,768]{1,0:T(8,128)(2,1)S(1)}, u32[]{:S(2)}, u32[]{:S(2)}) collective-permute-start(bf16[128,768]{1,0:T(8,128)(2,1)S(1)} %get-tuple-element.256), channel_id=1, source_target_pairs={{0,6},{2,4},{4,2},{6,0},{1,7},{3,5},{5,3},{7,1},{8,14},{10,12},{12... | collective-permute-start | bytes 589832 | tf_op jit(solution)/shard_map/ppermute | solution.py:42
  227.2 11.6 %collective-permute-start.53 = (bf16[128,768]{1,0:T(8,128)(2,1)S(1)}, bf16[128,768]{1,0:T(8,128)(2,1)S(1)}, u32[]{:S(2)}, u32[]{:S(2)}) collective-permute-start(bf16[128,768]{1,0:T(8,128)(2,1)S(1)} %get-tuple-element.257), channel_id=1, source_target_pairs={{0,4},{2,6},{4,0},{6,2},{1,5},{3,7},{5,1},{7,3},{8,12},{10,14},{12... | collective-permute-start | bytes 589832 | tf_op jit(solution)/shard_map/ppermute | solution.py:42
  228.6 31.8 %all-to-all-start.5 = ((bf16[16,24,768]{2,1,0:T(8,128)(2,1)}), bf16[16,24,768]{2,1,0:T(8,128)(2,1)S(1)}, u32[]{:S(2)}, u32[]{:S(2)}) async-start(bf16[16,24,768]{2,1,0:T(8,128)(2,1)} %add_convert_fusion.1), calls=%async_computation.5 | async-start | bytes 1179648 | tf_op jit(solution)/shard_map/all_to_all | solution.py:86
  234.7 7.6 %collective-permute-start.57 = (bf16[48,1152]{1,0:T(8,128)(2,1)S(1)}, bf16[48,1152]{1,0:T(8,128)(2,1)S(1)}, u32[]{:S(2)}, u32[]{:S(2)}) collective-permute-start(bf16[48,1152]{1,0:T(8,128)(2,1)S(1)} %get-tuple-element.221), channel_id=1, source_target_pairs={{0,2},{2,0},{4,6},{6,4},{1,3},{3,1},{5,7},{7,5},{8,10},{10,8},{12,... | collective-permute-start | bytes 331784 | tf_op jit(solution)/shard_map/ppermute | solution.py:42
  236.6 12.7 %collective-permute-start.58 = (bf16[48,1152]{1,0:T(8,128)(2,1)S(1)}, bf16[48,1152]{1,0:T(8,128)(2,1)S(1)}, u32[]{:S(2)}, u32[]{:S(2)}) collective-permute-start(bf16[48,1152]{1,0:T(8,128)(2,1)S(1)} %get-tuple-element.222), channel_id=1, source_target_pairs={{0,4},{2,6},{4,0},{6,2},{1,5},{3,7},{5,1},{7,3},{8,12},{10,14},{12... | collective-permute-start | bytes 331784 | tf_op jit(solution)/shard_map/ppermute | solution.py:42
  238.1 15.4 %collective-permute-start.59 = (bf16[48,1152]{1,0:T(8,128)(2,1)S(1)}, bf16[48,1152]{1,0:T(8,128)(2,1)S(1)}, u32[]{:S(2)}, u32[]{:S(2)}) collective-permute-start(bf16[48,1152]{1,0:T(8,128)(2,1)S(1)} %get-tuple-element.223), channel_id=1, source_target_pairs={{0,6},{2,4},{4,2},{6,0},{1,7},{3,5},{5,3},{7,1},{8,14},{10,12},{12... | collective-permute-start | bytes 331784 | tf_op jit(solution)/shard_map/ppermute | solution.py:42
  239.8 16.1 %collective-permute-start.55 = (bf16[64,768]{1,0:T(8,128)(2,1)S(1)}, bf16[64,768]{1,0:T(8,128)(2,1)S(1)}, u32[]{:S(2)}, u32[]{:S(2)}) collective-permute-start(bf16[64,768]{1,0:T(8,128)(2,1)S(1)} %broadcast_select_fusion.3), channel_id=1, source_target_pairs={{0,8},{8,0},{1,9},{9,1},{2,10},{10,2},{3,11},{11,3},{4,12},{12,4},... | collective-permute-start | bytes 294920 | tf_op jit(solution)/shard_map/ppermute | solution.py:42
  242.2 14.5 %collective-permute-start.61 = (bf16[96,384]{1,0:T(8,128)(2,1)S(1)}, bf16[96,384]{1,0:T(8,128)(2,1)S(1)}, u32[]{:S(2)}, u32[]{:S(2)}) collective-permute-start(bf16[96,384]{1,0:T(8,128)(2,1)S(1)} %select_convert_fusion), channel_id=1, source_target_pairs={{0,1},{1,0},{2,3},{3,2},{4,5},{5,4},{6,7},{7,6},{8,9},{9,8},{10,11... | collective-permute-start | bytes 221192 | tf_op jit(solution)/shard_map/ppermute | solution.py:42
  (63 other events, 642.1 us)

commit v5 on v4

--- a/solution.py
+++ b/solution.py
@@ -1159,7 +1159,6 @@
     grad_out = total(out_own[0], out_own[1:] + out_moved).astype(bf16).reshape(2, FEATS * 2 * w_rows, -1)
     grad_down, down_moved = send(grad_down, "s")
     dqkv = all_to_all(dqkv.reshape(-1, 2 * HEAD_DIM), ("u", "c"))
-    dqkv, down_moved[0] = tie(dqkv, down_moved[0])
     grad_ff = total(ff_own[0], ff_own[1:] + ff_moved).astype(bf16)
     grad_ff, ff_moved = send(after(grad_ff, dqkv), "u")
     grad_out, out_moved = send(after(grad_out, dqkv), "s")

time: 266 us -> 264 us (level)
  Pallas kernels: 67 us -> 60.2 us
  starting transfers between devices: 77.7 us -> 81.6 us
  waiting for transfers between devices: 64 us -> 67.3 us
    ppermute x62, starting transfers between devices: 53 us -> 58.4 us  [swap(): return lax.ppermute(values, axis, [(i, i ^ step) for i in range(size)])]
    ppermute x62, waiting for transfers between devices: 59.3 us -> 64.6 us  [swap(): return lax.ppermute(values, axis, [(i, i ^ step) for i in range(size)])]
    pallas_call x1, Pallas kernels: 19 us -> 15 us  [attend_back(): pl.pallas_call(attend_back_kernel, out_shape=jax.ShapeDtypeStruct(qkv.sha...]
    pallas_call x1, Pallas kernels: 14.4 us -> 11.6 us  [attend(): pl.pallas_call(attend_kernel, out_shape=(jax.ShapeDtypeStruct((slots * FE...]
  transfers between devices with their start and end apart: 68 -> 68, of which waited for: 27 -> 25; matrix products, arithmetic and copies ran while one was open for 12% -> 12% of each run, Pallas kernels for 25% -> 22%
where the time goes in v5:
time: 264 us; the launch traced here: 263 us
  starting transfers between devices  81.6 us (31%)
  waiting for transfers between devices  67.3 us (25%)
  Pallas kernels  60.2 us (23%)
  other arithmetic  23 us (9%)
  local copies, waits for them, and re-layouts  16.8 us (6%)
  matrix products  12.1 us (5%)
    ppermute x62, waiting for transfers between devices, swap(): return lax.ppermute(values, axis, [(i, i ^ step) for i in range(size)])  64.6 us
    ppermute x62, starting transfers between devices, swap(): return lax.ppermute(values, axis, [(i, i ^ step) for i in range(size)])  58.4 us
    all_to_all x6, starting transfers between devices, all_to_all(): return lax.all_to_all(values, axes, split_axis=0, concat_axis=0, tiled=True)  23.2 us
    pallas_call x1, Pallas kernels, attend_back(): pl.pallas_call(attend_back_kernel, out_shape=jax.ShapeDtypeStruct(qkv.sha...  15 us
    dot_general x10, matrix products, dot(): lax.dot_general(left, right, (((left_dim,), (right_dim,)), ((), ())), pre...  12.1 us
    pallas_call x1, Pallas kernels, attend(): pl.pallas_call(attend_kernel, out_shape=(jax.ShapeDtypeStruct((slots * FE...  11.6 us
    unnamed x128, local copies, waits for them, and re-layouts  8.53 us
    convert_element_type x4, other arithmetic, added(): return (kept.astype(f32) + got.astype(f32)).astype(bf16)  5.49 us
  transfers between devices with their start and end apart: 68, of which 25 were waited for; matrix products, arithmetic and copies ran while one was open for 12% of the time, Pallas kernels for 22%

profile of v5, /device:TPU:0, one launch (start us, length us, event | category | flops | bytes accessed | tf_op | source)
XLA Modules:
  0.0 262.7 jit_solution(3051696733171963017)
XLA Ops:
  1.7 4.1 %collective-permute-start.1 = (bf16[64,768]{1,0:T(8,128)(2,1)S(1)}, bf16[64,768]{1,0:T(8,128)(2,1)S(1)}, u32[]{:S(2)}, u32[]{:S(2)}) collective-permute-start(bf16[64,768]{1,0:T(8,128)(2,1)S(1)} %select_bitcast_fusion.7), channel_id=1, source_target_pairs={{0,8},{8,0},{1,9},{9,1},{2,10},{10,2},{3,11},{11,3},{4,12},{12,4},... | collective-permute-start | bytes 294920 | tf_op jit(solution)/shard_map/ppermute | solution.py:42
  5.8 1.7 pack_attn.1
  7.5 3.8 %all-to-all-start = ((bf16[8,24,384]{2,1,0:T(8,128)(2,1)}), bf16[8,24,384]{2,1,0:T(8,128)(2,1)S(1)}, u32[]{:S(2)}, u32[]{:S(2)}) async-start(bf16[8,24,384]{2,1,0:T(8,128)(2,1)} %bitcast.146), calls=%async_computation | async-start | bytes 294912 | tf_op jit(solution)/shard_map/all_to_all | solution.py:86
  11.9 1.9 pack_late.1
  14.7 1.9 all-to-all-done
  19.0 1.8 route_late.1
  20.8 3.2 %collective-permute-done.2.refs_9_.refs_1_ = bf16[128,768]{1,0:T(8,128)(2,1)S(1)} collective-permute-done((bf16[128,768]{1,0:T(8,128)(2,1)S(1)}, bf16[128,768]{1,0:T(8,128)(2,1)S(1)}, u32[]{:S(2)}, u32[]{:S(2)}) %collective-permute-start.2) | collective-permute-done | bytes 196640 | tf_op jit(solution)/shard_map/ppermute | solution.py:42
  28.6 1.3 collective-permute-start.13
  31.1 1.8 collective-permute-done.4
  32.9 1.5 collective-permute-start.7
  35.8 1.8 collective-permute-done.14.refs_11_.refs_3_
  37.7 1.7 collective-permute-done.7.refs_2_
  39.4 1.6 collective-permute-done.8.refs_3_
  41.0 1.6 collective-permute-start.17
  44.0 3.4 %qkv.1 = (bf16[4,768,128]{2,1,0:T(8,128)(2,1)}, bf16[768,768]{1,0:T(8,128)(2,1)}, f32[8,768]{1,0:T(8,128)}, f32[1,2048]{1,0:T(1,128)}, f32[1,2048]{1,0:T(1,128)}) custom-call(s32[4]{0:T(128)} %pad_add_fusion.1.place_ref, bf16[192,384]{1,0:T(8,128)(2,1)} %bitcast.141, bf16[192,384]{1,0:T(8,128)(2,1)} %copy-done.37, bf16[192,384]{1,0:T(8,128)(2,1)} %copy-done.39, ...), custom_call_target="tpu_custom_call" | custom-call | tf_op jit(solution)/shard_map/qkv/pallas_call | solution.py:903
  47.4 3.5 %all-to-all-start.1 = ((bf16[4,768,128]{2,1,0:T(8,128)(2,1)}), bf16[4,768,128]{2,1,0:T(8,128)(2,1)S(1)}, u32[]{:S(2)}, u32[]{:S(2)}) async-start(bf16[4,768,128]{2,1,0:T(8,128)(2,1)} %get-tuple-element.138), calls=%async_computation.1 | async-start | bytes 1572864 | tf_op jit(solution)/shard_map/all_to_all | solution.py:86
  55.6 3.3 %collective-permute-done.15.refs_1_ = bf16[384,384]{1,0:T(8,128)(2,1)S(1)} collective-permute-done((bf16[384,384]{1,0:T(8,128)(2,1)S(1)}, bf16[384,384]{1,0:T(8,128)(2,1)S(1)}, u32[]{:S(2)}, u32[]{:S(2)}) %collective-permute-start.15) | collective-permute-done | bytes 294944 | tf_op jit(solution)/shard_map/ppermute | solution.py:42
  64.1 11.6 %attend.1 = (bf16[16,64,128]{2,1,0:T(8,128)(2,1)}, f32[1,2048]{1,0:T(1,128)}, f32[64,2048]{1,0:T(8,128)}) custom-call(s32[3,8]{1,0:T(4,128)} %pad_add_fusion.table_ref, f32[1,1]{1,0:T(1,128)} %bitcast.23.slope_ref, bf16[4,768,128]{2,1,0:T(8,128)(2,1)} %copy-done, f32[1,2048]{1,0:T(1,128)} %get-tuple-element.137.seg_ref, f32[1,2048]{1,0:T(1,128)} %get-tuple-element.144.code_ref), custom_call_target="tpu_custom_call" | custom-call | tf_op jit(solution)/shard_map/attend/pallas_call | solution.py:335
  76.2 4.2 %all-to-all-start.2 = ((bf16[16,64,128]{2,1,0:T(8,128)(2,1)}), bf16[16,64,128]{2,1,0:T(8,128)(2,1)S(1)}, u32[]{:S(2)}, u32[]{:S(2)}) async-start(bf16[16,64,128]{2,1,0:T(8,128)(2,1)} %get-tuple-element.147), calls=%async_computation.2 | async-start | bytes 524288 | tf_op jit(solution)/shard_map/all_to_all | solution.py:86
  81.3 1.7 collective-permute-start.27
  83.0 5.0 %collective-permute-start.36 = (bf16[64,768]{1,0:T(8,128)(2,1)S(1)}, bf16[64,768]{1,0:T(8,128)(2,1)S(1)}, u32[]{:S(2)}, u32[]{:S(2)}) collective-permute-start(bf16[64,768]{1,0:T(8,128)(2,1)S(1)} %select_bitcast_fusion.4), channel_id=1, source_target_pairs={{0,8},{8,0},{1,9},{9,1},{2,10},{10,2},{3,11},{11,3},{4,12},{12,4},... | collective-permute-start | bytes 294920 | tf_op jit(solution)/shard_map/ppermute | solution.py:42
  88.0 3.3 %place_first.1 = (bf16[768,768]{1,0:T(8,128)(2,1)}, bf16[768,768]{1,0:T(8,128)(2,1)}) custom-call(s32[4]{0:T(128)} %pad_add_fusion.1.place_ref, bf16[384,384]{1,0:T(8,128)(2,1)} %copy-done.22, bf16[384,384]{1,0:T(8,128)(2,1)} %copy-done.25, bf16[384,384]{1,0:T(8,128)(2,1)} %copy-done.24, bf16[384,384]{1,0:T(8,128)(2,1)} %collective-permute-done.23.refs_3_, ...), custom_call_target="tpu_custom_call" | custom-call | tf_op jit(solution)/shard_map/place_first/pallas_call | solution.py:970
  92.1 3.0 %join_heads.1 = (bf16[128,768]{1,0:T(8,128)(2,1)}, f32[128,768]{1,0:T(8,128)}, bf16[128,768]{1,0:T(8,128)(2,1)}, f32[128,768]{1,0:T(8,128)}, f32[128,1]{1,0:T(8,128)}) custom-call(bf16[16,64,128]{2,1,0:T(8,128)(2,1)} %copy-done.8, bf16[128,768]{1,0:T(8,128)(2,1)} %copy-done.1, bf16[768,768]{1,0:T(8,128)(2,1)} %get-tuple-element.156.w_ref, ...), custom_call_target="tpu_custom_call" | custom-call | tf_op jit(solution)/shard_map/join_heads/pallas_call | solution.py:1007
  95.2 1.5 slice_reduce_fusion.1
  96.7 2.4 collective-permute-start.31
  100.9 3.3 %place_second.1 = (bf16[768,768]{1,0:T(8,128)(2,1)}, bf16[768,768]{1,0:T(8,128)(2,1)}) custom-call(s32[4]{0:T(128)} %pad_add_fusion.1.place_ref, bf16[192,768]{1,0:T(8,128)(2,1)} %copy-done.4, bf16[192,768]{1,0:T(8,128)(2,1)} %collective-permute-done.21.refs_1_, bf16[192,768]{1,0:T(8,128)(2,1)} %collective-permute-done.22.refs_2_, ...), custom_call_target="tpu_custom_call" | custom-call | tf_op jit(solution)/shard_map/place_second/pallas_call | solution.py:1026
  105.5 3.8 %collective-permute-done.30 = bf16[128,768]{1,0:T(8,128)(2,1)S(1)} collective-permute-done((bf16[128,768]{1,0:T(8,128)(2,1)}, bf16[128,768]{1,0:T(8,128)(2,1)S(1)}, u32[]{:S(2)}, u32[]{:S(2)}) %collective-permute-start.30) | collective-permute-done | bytes 196640 | tf_op jit(solution)/shard_map/ppermute | solution.py:42
  112.8 1.5 collective-permute-start.32
  114.3 1.5 collective-permute-start.34
  116.4 1.7 multiply_convert_fusion.2
  118.1 5.8 %collective-permute-done.32 = bf16[128,768]{1,0:T(8,128)(2,1)S(1)} collective-permute-done((bf16[128,768]{1,0:T(8,128)(2,1)S(1)}, bf16[128,768]{1,0:T(8,128)(2,1)S(1)}, u32[]{:S(2)}, u32[]{:S(2)}) %collective-permute-start.32) | collective-permute-done | bytes 196640 | tf_op jit(solution)/shard_map/ppermute | solution.py:42
  126.8 2.4 collective-permute-start.39
  130.2 5.2 %collective-permute-done.39 = bf16[128,768]{1,0:T(8,128)(2,1)S(1)} collective-permute-done((bf16[128,768]{1,0:T(8,128)(2,1)S(1)}, bf16[128,768]{1,0:T(8,128)(2,1)S(1)}, u32[]{:S(2)}, u32[]{:S(2)}) %collective-permute-start.39) | collective-permute-done | bytes 196640 | tf_op jit(solution)/shard_map/ppermute | solution.py:42
  135.4 2.2 collective-permute-done.38
  137.6 2.4 multiply_convert_fusion
  142.7 1.9 convolution_convert_fusion.1
  146.1 2.4 collective-permute-start.42
  149.6 1.5 convolution_convert_fusion.4
  151.1 1.5 convolution_convert_fusion.3
  152.5 2.3 collective-permute-done.42.got_c_ref
  154.8 2.8 %collective-permute-done.41.got_b_ref = bf16[128,768]{1,0:T(8,128)(2,1)S(1)} collective-permute-done((bf16[128,768]{1,0:T(8,128)(2,1)S(1)}, bf16[128,768]{1,0:T(8,128)(2,1)S(1)}, u32[]{:S(2)}, u32[]{:S(2)}) %collective-permute-start.41) | collective-permute-done | bytes 196640 | tf_op jit(solution)/shard_map/ppermute | solution.py:42
  158.3 3.9 %back_join.1 = (f32[128,768]{1,0:T(8,128)}, bf16[16,64,128]{2,1,0:T(8,128)(2,1)}, bf16[768,384]{1,0:T(8,128)(2,1)}, bf16[768,384]{1,0:T(8,128)(2,1)}, f32[3,768]{1,0:T(4,128)}) custom-call(s32[4]{0:T(128)} %pad_add_fusion.1.place_ref, f32[128,768]{1,0:T(8,128)} %get-tuple-element.244.second_ref, bf16[128,768]{1,0:T(8,128)(2,1)} %get-tuple-element.257.own_ref, ...), custom_call_target="tpu_custom_call" | custom-call | tf_op jit(solution)/shard_map/back_join/pallas_call | solution.py:1091
  162.9 2.5 collective-permute-start.35
  165.4 3.8 %all-to-all-start.3 = ((bf16[16,64,128]{2,1,0:T(8,128)(2,1)}), bf16[16,64,128]{2,1,0:T(8,128)(2,1)S(1)}, u32[]{:S(2)}, u32[]{:S(2)}) async-start(bf16[16,64,128]{2,1,0:T(8,128)(2,1)} %get-tuple-element.192), calls=%async_computation.3 | async-start | bytes 524288 | tf_op jit(solution)/shard_map/all_to_all | solution.py:86
  170.6 1.8 fusion.34
  172.4 1.8 collective-permute-start.46
  174.2 1.7 fusion.35
  178.6 15.0 %attend_back.1 = bf16[4,768,128]{2,1,0:T(8,128)(2,1)} custom-call(s32[3,8]{1,0:T(4,128)} %pad_add_fusion.table_ref, f32[1,1]{1,0:T(1,128)} %bitcast.23.slope_ref, bf16[4,768,128]{2,1,0:T(8,128)(2,1)} %copy-done, bf16[16,64,128]{2,1,0:T(8,128)(2,1)} %copy-done.7, f32[64,2048]{1,0:T(8,128)} %get-tuple-element.193.ot_ref, ...), custom_call_target="tpu_custom_call" | custom-call | tf_op jit(solution)/shard_map/attend_back/pallas_call | solution.py:360
  193.6 5.8 %collective-permute-done.44 = bf16[2,192,768]{2,1,0:T(8,128)(2,1)S(1)} collective-permute-done((bf16[2,192,768]{2,1,0:T(8,128)(2,1)}, bf16[2,192,768]{2,1,0:T(8,128)(2,1)S(1)}, u32[]{:S(2)}, u32[]{:S(2)}) %collective-permute-start.44) | collective-permute-done | bytes 589856 | tf_op jit(solution)/shard_map/ppermute | solution.py:42
  199.4 3.5 %all-to-all-start.4 = ((bf16[4,768,128]{2,1,0:T(8,128)(2,1)}), bf16[4,768,128]{2,1,0:T(8,128)(2,1)S(1)}, u32[]{:S(2)}, u32[]{:S(2)}) async-start(bf16[4,768,128]{2,1,0:T(8,128)(2,1)} %attend_back.1), calls=%async_computation.4 | async-start | bytes 1572864 | tf_op jit(solution)/shard_map/all_to_all | solution.py:86
  204.5 1.3 fusion.6
  207.0 6.4 %collective-permute-done.60 = bf16[192,384]{1,0:T(8,128)(2,1)S(1)} collective-permute-done((bf16[192,384]{1,0:T(8,128)(2,1)S(1)}, bf16[192,384]{1,0:T(8,128)(2,1)S(1)}, u32[]{:S(2)}, u32[]{:S(2)}) %collective-permute-start.60) | collective-permute-done | bytes 147488 | tf_op jit(solution)/shard_map/ppermute | solution.py:42
  216.0 5.2 %grad_qkv.1 = (bf16[512,768]{1,0:T(8,128)(2,1)}, bf16[512,768]{1,0:T(8,128)(2,1)}, bf16[16,24,768]{2,1,0:T(8,128)(2,1)}, bf16[16,24,768]{2,1,0:T(8,128)(2,1)}) custom-call(s32[4]{0:T(128)} %pad_add_fusion.1.place_ref, bf16[128,768]{1,0:T(8,128)(2,1)} %copy-done.1, bf16[128,768]{1,0:T(8,128)(2,1)} %copy-done.9, bf16[128,768]{1,0:T(8,128)(2,1)} %copy-done.11, ...), custom_call_target="tpu_custom_call" | custom-call | tf_op jit(solution)/shard_map/grad_qkv/pallas_call | solution.py:1172
  222.5 1.5 collective-permute-start.51
  224.0 2.8 %collective-permute-start.53 = (bf16[128,768]{1,0:T(8,128)(2,1)S(1)}, bf16[128,768]{1,0:T(8,128)(2,1)S(1)}, u32[]{:S(2)}, u32[]{:S(2)}) collective-permute-start(bf16[128,768]{1,0:T(8,128)(2,1)S(1)} %get-tuple-element.252), channel_id=1, source_target_pairs={{0,6},{2,4},{4,2},{6,0},{1,7},{3,5},{5,3},{7,1},{8,14},{10,12},{12... | collective-permute-start | bytes 589832 | tf_op jit(solution)/shard_map/ppermute | solution.py:42
  228.3 4.4 %all-to-all-start.5 = ((bf16[16,24,768]{2,1,0:T(8,128)(2,1)}), bf16[16,24,768]{2,1,0:T(8,128)(2,1)S(1)}, u32[]{:S(2)}, u32[]{:S(2)}) async-start(bf16[16,24,768]{2,1,0:T(8,128)(2,1)} %add_convert_fusion.1), calls=%async_computation.5 | async-start | bytes 1179648 | tf_op jit(solution)/shard_map/all_to_all | solution.py:86
  233.5 1.9 collective-permute-start.56
  235.4 1.5 collective-permute-start.57
  236.9 2.0 collective-permute-start.58
  241.1 10.0 %collective-permute-done.57.refs_2_ = bf16[48,1152]{1,0:T(8,128)(2,1)S(1)} collective-permute-done((bf16[48,1152]{1,0:T(8,128)(2,1)S(1)}, bf16[48,1152]{1,0:T(8,128)(2,1)S(1)}, u32[]{:S(2)}, u32[]{:S(2)}) %collective-permute-start.57) | collective-permute-done | bytes 110624 | tf_op jit(solution)/shard_map/ppermute | solution.py:42
  251.1 1.7 collective-permute-done.58.refs_3_
  253.4 1.8 finish_late.1
  257.5 2.2 finish_wide.1
  260.6 1.9 finish.1
  (286 shorter events, 61.7 us)
Async XLA Ops:
  1.7 12.1 %collective-permute-start.1 = (bf16[64,768]{1,0:T(8,128)(2,1)S(1)}, bf16[64,768]{1,0:T(8,128)(2,1)S(1)}, u32[]{:S(2)}, u32[]{:S(2)}) collective-permute-start(bf16[64,768]{1,0:T(8,128)(2,1)S(1)} %select_bitcast_fusion.7), channel_id=1, source_target_pairs={{0,8},{8,0},{1,9},{9,1},{2,10},{10,2},{3,11},{11,3},{4,12},{12,4},... | collective-permute-start | bytes 294920 | tf_op jit(solution)/shard_map/ppermute | solution.py:42
  7.5 9.1 %all-to-all-start = ((bf16[8,24,384]{2,1,0:T(8,128)(2,1)}), bf16[8,24,384]{2,1,0:T(8,128)(2,1)S(1)}, u32[]{:S(2)}, u32[]{:S(2)}) async-start(bf16[8,24,384]{2,1,0:T(8,128)(2,1)} %bitcast.146), calls=%async_computation | async-start | bytes 294912 | tf_op jit(solution)/shard_map/all_to_all | solution.py:86
  16.6 7.4 %collective-permute-start.2 = (bf16[128,768]{1,0:T(8,128)(2,1)S(1)}, bf16[128,768]{1,0:T(8,128)(2,1)S(1)}, u32[]{:S(2)}, u32[]{:S(2)}) collective-permute-start(bf16[128,768]{1,0:T(8,128)(2,1)S(1)} %pad_maximum_fusion.2.refs_8_.tokens_ref.refs_0_), channel_id=1, source_target_pairs={{0,2},{2,0},{4,6},{6,4},{1,3},{3,1},{5,7},{7,5},{8,10},{10,8},{12,... | collective-permute-start | bytes 589832 | tf_op jit(solution)/shard_map/ppermute | solution.py:42
  17.6 11.0 %collective-permute-start.6 = (bf16[192,384]{1,0:T(8,128)(2,1)S(1)}, bf16[192,384]{1,0:T(8,128)(2,1)S(1)}, u32[]{:S(2)}, u32[]{:S(2)}) collective-permute-start(bf16[192,384]{1,0:T(8,128)(2,1)S(1)} %bitcast.138), channel_id=1, source_target_pairs={{0,8},{8,0},{1,9},{9,1},{2,10},{10,2},{3,11},{11,3},{4,12},{12,4},... | collective-permute-start | bytes 442376 | tf_op jit(solution)/shard_map/ppermute | solution.py:42
  24.0 7.1 %collective-permute-start.5 = (bf16[48,1152]{1,0:T(8,128)(2,1)}, bf16[48,1152]{1,0:T(8,128)(2,1)S(1)}, u32[]{:S(2)}, u32[]{:S(2)}) collective-permute-start(bf16[48,1152]{1,0:T(8,128)(2,1)} %get-tuple-element.135), channel_id=1, source_target_pairs={{0,6},{2,4},{4,2},{6,0},{1,7},{3,5},{5,3},{7,1},{8,14},{10,12},{12... | collective-permute-start | bytes 331784 | tf_op jit(solution)/shard_map/ppermute | solution.py:42
  25.1 7.8 %collective-permute-start.4 = (bf16[48,1152]{1,0:T(8,128)(2,1)}, bf16[48,1152]{1,0:T(8,128)(2,1)S(1)}, u32[]{:S(2)}, u32[]{:S(2)}) collective-permute-start(bf16[48,1152]{1,0:T(8,128)(2,1)} %get-tuple-element.133), channel_id=1, source_target_pairs={{0,4},{2,6},{4,0},{6,2},{1,5},{3,7},{5,1},{7,3},{8,12},{10,14},{12... | collective-permute-start | bytes 331784 | tf_op jit(solution)/shard_map/ppermute | solution.py:42
  26.4 8.0 %collective-permute-start.3 = (bf16[48,1152]{1,0:T(8,128)(2,1)}, bf16[48,1152]{1,0:T(8,128)(2,1)S(1)}, u32[]{:S(2)}, u32[]{:S(2)}) collective-permute-start(bf16[48,1152]{1,0:T(8,128)(2,1)} %get-tuple-element.131), channel_id=1, source_target_pairs={{0,2},{2,0},{4,6},{6,4},{1,3},{3,1},{5,7},{7,5},{8,10},{10,8},{12,... | collective-permute-start | bytes 331784 | tf_op jit(solution)/shard_map/ppermute | solution.py:42
  27.5 10.2 %collective-permute-start.14 = (bf16[128,768]{1,0:T(8,128)(2,1)S(1)}, bf16[128,768]{1,0:T(8,128)(2,1)S(1)}, u32[]{:S(2)}, u32[]{:S(2)}) collective-permute-start(bf16[128,768]{1,0:T(8,128)(2,1)S(1)} %pad_maximum_fusion.2.refs_8_.tokens_ref.refs_0_), channel_id=1, source_target_pairs={{0,6},{2,4},{4,2},{6,0},{1,7},{3,5},{5,3},{7,1},{8,14},{10,12},{12... | collective-permute-start | bytes 589832 | tf_op jit(solution)/shard_map/ppermute | solution.py:42
  28.6 12.3 %collective-permute-start.13 = (bf16[128,768]{1,0:T(8,128)(2,1)S(1)}, bf16[128,768]{1,0:T(8,128)(2,1)S(1)}, u32[]{:S(2)}, u32[]{:S(2)}) collective-permute-start(bf16[128,768]{1,0:T(8,128)(2,1)S(1)} %pad_maximum_fusion.2.refs_8_.tokens_ref.refs_0_), channel_id=1, source_target_pairs={{0,4},{2,6},{4,0},{6,2},{1,5},{3,7},{5,1},{7,3},{8,12},{10,14},{12... | collective-permute-start | bytes 589832 | tf_op jit(solution)/shard_map/ppermute | solution.py:42
  31.1 11.5 %collective-permute-start.9 = (bf16[192,384]{1,0:T(8,128)(2,1)S(1)}, bf16[192,384]{1,0:T(8,128)(2,1)S(1)}, u32[]{:S(2)}, u32[]{:S(2)}) collective-permute-start(bf16[192,384]{1,0:T(8,128)(2,1)S(1)} %bitcast.139), channel_id=1, source_target_pairs={{0,1},{1,0},{2,3},{3,2},{4,5},{5,4},{6,7},{7,6},{8,9},{9,8},{10,11... | collective-permute-start | bytes 442376 | tf_op jit(solution)/shard_map/ppermute | solution.py:42
  32.9 6.4 %collective-permute-start.7 = (bf16[192,384]{1,0:T(8,128)(2,1)S(1)}, bf16[192,384]{1,0:T(8,128)(2,1)S(1)}, u32[]{:S(2)}, u32[]{:S(2)}) collective-permute-start(bf16[192,384]{1,0:T(8,128)(2,1)S(1)} %bitcast.140), channel_id=1, source_target_pairs={{0,16},{16,0},{1,17},{17,1},{2,18},{18,2},{3,19},{19,3},{4,20},{20... | collective-permute-start | bytes 442376 | tf_op jit(solution)/shard_map/ppermute | solution.py:42
  34.5 6.5 %collective-permute-start.8 = (bf16[192,384]{1,0:T(8,128)(2,1)S(1)}, bf16[192,384]{1,0:T(8,128)(2,1)S(1)}, u32[]{:S(2)}, u32[]{:S(2)}) collective-permute-start(bf16[192,384]{1,0:T(8,128)(2,1)S(1)} %collective-permute-done.6.refs_1_), channel_id=1, source_target_pairs={{0,16},{16,0},{1,17},{17,1},{2,18},{18,2},{3,19},{19,3},{4,20},{20... | collective-permute-start | bytes 442376 | tf_op jit(solution)/shard_map/ppermute | solution.py:42
  37.7 4.9 %collective-permute-start.10 = (bf16[192,384]{1,0:T(8,128)(2,1)S(1)}, bf16[192,384]{1,0:T(8,128)(2,1)S(1)}, u32[]{:S(2)}, u32[]{:S(2)}) collective-permute-start(bf16[192,384]{1,0:T(8,128)(2,1)S(1)} %collective-permute-done.6.refs_1_), channel_id=1, source_target_pairs={{0,1},{1,0},{2,3},{3,2},{4,5},{5,4},{6,7},{7,6},{8,9},{9,8},{10,11... | collective-permute-start | bytes 442376 | tf_op jit(solution)/shard_map/ppermute | solution.py:42
  41.0 14.2 %collective-permute-start.17 = (bf16[384,384]{1,0:T(8,128)(2,1)S(1)}, bf16[384,384]{1,0:T(8,128)(2,1)S(1)}, u32[]{:S(2)}, u32[]{:S(2)}) collective-permute-start(bf16[384,384]{1,0:T(8,128)(2,1)S(1)} %slice_dynamic-update-slice_fusion.refs_0_), channel_id=1, source_target_pairs={{0,16},{16,0},{1,17},{17,1},{2,18},{18,2},{3,19},{19,3},{4,20},{20... | collective-permute-start | bytes 884744 | tf_op jit(solution)/shard_map/ppermute | solution.py:42
  42.5 16.3 %collective-permute-start.15 = (bf16[384,384]{1,0:T(8,128)(2,1)S(1)}, bf16[384,384]{1,0:T(8,128)(2,1)S(1)}, u32[]{:S(2)}, u32[]{:S(2)}) collective-permute-start(bf16[384,384]{1,0:T(8,128)(2,1)S(1)} %slice_dynamic-update-slice_fusion.refs_0_), channel_id=1, source_target_pairs={{0,8},{8,0},{1,9},{9,1},{2,10},{10,2},{3,11},{11,3},{4,12},{12,4},... | collective-permute-start | bytes 884744 | tf_op jit(solution)/shard_map/ppermute | solution.py:42
  47.4 15.1 %all-to-all-start.1 = ((bf16[4,768,128]{2,1,0:T(8,128)(2,1)}), bf16[4,768,128]{2,1,0:T(8,128)(2,1)S(1)}, u32[]{:S(2)}, u32[]{:S(2)}) async-start(bf16[4,768,128]{2,1,0:T(8,128)(2,1)} %get-tuple-element.138), calls=%async_computation.1 | async-start | bytes 1572864 | tf_op jit(solution)/shard_map/all_to_all | solution.py:86
  54.5 6.8 %collective-permute-start.18 = (bf16[384,384]{1,0:T(8,128)(2,1)S(1)}, bf16[384,384]{1,0:T(8,128)(2,1)S(1)}, u32[]{:S(2)}, u32[]{:S(2)}) collective-permute-start(bf16[384,384]{1,0:T(8,128)(2,1)S(1)} %slice_dynamic-update-slice_fusion.refs_0_), channel_id=1, source_target_pairs={{0,1},{1,0},{2,3},{3,2},{4,5},{5,4},{6,7},{7,6},{8,9},{9,8},{10,11... | collective-permute-start | bytes 884744 | tf_op jit(solution)/shard_map/ppermute | solution.py:42
  55.0 7.5 %collective-permute-start.16 = (bf16[192,768]{1,0:T(8,128)(2,1)S(1)}, bf16[192,768]{1,0:T(8,128)(2,1)S(1)}, u32[]{:S(2)}, u32[]{:S(2)}) collective-permute-start(bf16[192,768]{1,0:T(8,128)(2,1)S(1)} %pad_maximum_fusion.1.refs_0_), channel_id=1, source_target_pairs={{0,1},{1,0},{2,3},{3,2},{4,5},{5,4},{6,7},{7,6},{8,9},{9,8},{10,11... | collective-permute-start | bytes 884744 | tf_op jit(solution)/shard_map/ppermute | solution.py:42
  55.1 7.3 %collective-permute-start.20 = (bf16[384,384]{1,0:T(8,128)(2,1)S(1)}, bf16[384,384]{1,0:T(8,128)(2,1)S(1)}, u32[]{:S(2)}, u32[]{:S(2)}) collective-permute-start(bf16[384,384]{1,0:T(8,128)(2,1)S(1)} %collective-permute-done.17.refs_2_), channel_id=1, source_target_pairs={{0,1},{1,0},{2,3},{3,2},{4,5},{5,4},{6,7},{7,6},{8,9},{9,8},{10,11... | collective-permute-start | bytes 884744 | tf_op jit(solution)/shard_map/ppermute | solution.py:42
  58.9 3.6 %collective-permute-start.19 = (bf16[384,384]{1,0:T(8,128)(2,1)S(1)}, bf16[384,384]{1,0:T(8,128)(2,1)S(1)}, u32[]{:S(2)}, u32[]{:S(2)}) collective-permute-start(bf16[384,384]{1,0:T(8,128)(2,1)S(1)} %collective-permute-done.15.refs_1_), channel_id=1, source_target_pairs={{0,1},{1,0},{2,3},{3,2},{4,5},{5,4},{6,7},{7,6},{8,9},{9,8},{10,11... | collective-permute-start | bytes 884744 | tf_op jit(solution)/shard_map/ppermute | solution.py:42
  59.6 16.1 %collective-permute-start.22 = (bf16[192,768]{1,0:T(8,128)(2,1)S(1)}, bf16[192,768]{1,0:T(8,128)(2,1)}, u32[]{:S(2)}, u32[]{:S(2)}) collective-permute-start(bf16[192,768]{1,0:T(8,128)(2,1)S(1)} %pad_maximum_fusion.1.refs_0_), channel_id=1, source_target_pairs={{0,16},{16,0},{1,17},{17,1},{2,18},{18,2},{3,19},{19,3},{4,20},{20... | collective-permute-start | bytes 884744 | tf_op jit(solution)/shard_map/ppermute | solution.py:42
  61.4 14.8 %collective-permute-start.21 = (bf16[192,768]{1,0:T(8,128)(2,1)S(1)}, bf16[192,768]{1,0:T(8,128)(2,1)}, u32[]{:S(2)}, u32[]{:S(2)}) collective-permute-start(bf16[192,768]{1,0:T(8,128)(2,1)S(1)} %pad_maximum_fusion.1.refs_0_), channel_id=1, source_target_pairs={{0,8},{8,0},{1,9},{9,1},{2,10},{10,2},{3,11},{11,3},{4,12},{12,4},... | collective-permute-start | bytes 884744 | tf_op jit(solution)/shard_map/ppermute | solution.py:42
  62.5 13.6 %collective-permute-start.23 = (bf16[384,384]{1,0:T(8,128)(2,1)S(1)}, bf16[384,384]{1,0:T(8,128)(2,1)}, u32[]{:S(2)}, u32[]{:S(2)}) collective-permute-start(bf16[384,384]{1,0:T(8,128)(2,1)S(1)} %collective-permute-done.15.refs_1_), channel_id=1, source_target_pairs={{0,16},{16,0},{1,17},{17,1},{2,18},{18,2},{3,19},{19,3},{4,20},{20... | collective-permute-start | bytes 884744 | tf_op jit(solution)/shard_map/ppermute | solution.py:42
  76.2 15.2 %all-to-all-start.2 = ((bf16[16,64,128]{2,1,0:T(8,128)(2,1)}), bf16[16,64,128]{2,1,0:T(8,128)(2,1)S(1)}, u32[]{:S(2)}, u32[]{:S(2)}) async-start(bf16[16,64,128]{2,1,0:T(8,128)(2,1)} %get-tuple-element.147), calls=%async_computation.2 | async-start | bytes 524288 | tf_op jit(solution)/shard_map/all_to_all | solution.py:86
  80.3 7.7 %collective-permute-start.26 = (bf16[384,384]{1,0:T(8,128)(2,1)}, bf16[384,384]{1,0:T(8,128)(2,1)}, u32[]{:S(2)}, u32[]{:S(2)}) collective-permute-start(bf16[384,384]{1,0:T(8,128)(2,1)} %collective-permute-done.23.refs_3_), channel_id=1, source_target_pairs={{0,1},{1,0},{2,3},{3,2},{4,5},{5,4},{6,7},{7,6},{8,9},{9,8},{10,11... | collective-permute-start | bytes 884744 | tf_op jit(solution)/shard_map/ppermute | solution.py:42
  80.7 10.6 %collective-permute-start.25 = (bf16[192,768]{1,0:T(8,128)(2,1)}, bf16[192,768]{1,0:T(8,128)(2,1)S(1)}, u32[]{:S(2)}, u32[]{:S(2)}) collective-permute-start(bf16[192,768]{1,0:T(8,128)(2,1)} %collective-permute-done.22.refs_2_), channel_id=1, source_target_pairs={{0,1},{1,0},{2,3},{3,2},{4,5},{5,4},{6,7},{7,6},{8,9},{9,8},{10,11... | collective-permute-start | bytes 884744 | tf_op jit(solution)/shard_map/ppermute | solution.py:42
  80.9 10.4 %collective-permute-start.24 = (bf16[192,768]{1,0:T(8,128)(2,1)}, bf16[192,768]{1,0:T(8,128)(2,1)}, u32[]{:S(2)}, u32[]{:S(2)}) collective-permute-start(bf16[192,768]{1,0:T(8,128)(2,1)} %collective-permute-done.21.refs_1_), channel_id=1, source_target_pairs={{0,1},{1,0},{2,3},{3,2},{4,5},{5,4},{6,7},{7,6},{8,9},{9,8},{10,11... | collective-permute-start | bytes 884744 | tf_op jit(solution)/shard_map/ppermute | solution.py:42
  81.3 13.9 %collective-permute-start.27 = (bf16[192,768]{1,0:T(8,128)(2,1)}, bf16[192,768]{1,0:T(8,128)(2,1)}, u32[]{:S(2)}, u32[]{:S(2)}) collective-permute-start(bf16[192,768]{1,0:T(8,128)(2,1)} %collective-permute-done.21.refs_1_), channel_id=1, source_target_pairs={{0,16},{16,0},{1,17},{17,1},{2,18},{18,2},{3,19},{19,3},{4,20},{20... | collective-permute-start | bytes 884744 | tf_op jit(solution)/shard_map/ppermute | solution.py:42
  83.0 17.2 %collective-permute-start.36 = (bf16[64,768]{1,0:T(8,128)(2,1)S(1)}, bf16[64,768]{1,0:T(8,128)(2,1)S(1)}, u32[]{:S(2)}, u32[]{:S(2)}) collective-permute-start(bf16[64,768]{1,0:T(8,128)(2,1)S(1)} %select_bitcast_fusion.4), channel_id=1, source_target_pairs={{0,8},{8,0},{1,9},{9,1},{2,10},{10,2},{3,11},{11,3},{4,12},{12,4},... | collective-permute-start | bytes 294920 | tf_op jit(solution)/shard_map/ppermute | solution.py:42
  95.1 5.1 %collective-permute-start.28 = (bf16[192,768]{1,0:T(8,128)(2,1)}, bf16[192,768]{1,0:T(8,128)(2,1)S(1)}, u32[]{:S(2)}, u32[]{:S(2)}) collective-permute-start(bf16[192,768]{1,0:T(8,128)(2,1)} %collective-permute-done.27.refs_3_), channel_id=1, source_target_pairs={{0,1},{1,0},{2,3},{3,2},{4,5},{5,4},{6,7},{7,6},{8,9},{9,8},{10,11... | collective-permute-start | bytes 884744 | tf_op jit(solution)/shard_map/ppermute | solution.py:42
  96.7 8.9 %collective-permute-start.31 = (bf16[128,768]{1,0:T(8,128)(2,1)}, bf16[128,768]{1,0:T(8,128)(2,1)S(1)}, u32[]{:S(2)}, u32[]{:S(2)}) collective-permute-start(bf16[128,768]{1,0:T(8,128)(2,1)} %get-tuple-element.167), channel_id=1, source_target_pairs={{0,6},{2,4},{4,2},{6,0},{1,7},{3,5},{5,3},{7,1},{8,14},{10,12},{12... | collective-permute-start | bytes 589832 | tf_op jit(solution)/shard_map/ppermute | solution.py:42
  99.0 10.3 %collective-permute-start.30 = (bf16[128,768]{1,0:T(8,128)(2,1)}, bf16[128,768]{1,0:T(8,128)(2,1)S(1)}, u32[]{:S(2)}, u32[]{:S(2)}) collective-permute-start(bf16[128,768]{1,0:T(8,128)(2,1)} %get-tuple-element.167), channel_id=1, source_target_pairs={{0,4},{2,6},{4,0},{6,2},{1,5},{3,7},{5,1},{7,3},{8,12},{10,14},{12... | collective-permute-start | bytes 589832 | tf_op jit(solution)/shard_map/ppermute | solution.py:42
  99.6 9.7 %collective-permute-start.29 = (bf16[128,768]{1,0:T(8,128)(2,1)}, bf16[128,768]{1,0:T(8,128)(2,1)S(1)}, u32[]{:S(2)}, u32[]{:S(2)}) collective-permute-start(bf16[128,768]{1,0:T(8,128)(2,1)} %get-tuple-element.167), channel_id=1, source_target_pairs={{0,2},{2,0},{4,6},{6,4},{1,3},{3,1},{5,7},{7,5},{8,10},{10,8},{12,... | collective-permute-start | bytes 589832 | tf_op jit(solution)/shard_map/ppermute | solution.py:42
  112.8 11.1 %collective-permute-start.32 = (bf16[128,768]{1,0:T(8,128)(2,1)S(1)}, bf16[128,768]{1,0:T(8,128)(2,1)S(1)}, u32[]{:S(2)}, u32[]{:S(2)}) collective-permute-start(bf16[128,768]{1,0:T(8,128)(2,1)S(1)} %get-tuple-element.258), channel_id=1, source_target_pairs={{0,2},{2,0},{4,6},{6,4},{1,3},{3,1},{5,7},{7,5},{8,10},{10,8},{12,... | collective-permute-start | bytes 589832 | tf_op jit(solution)/shard_map/ppermute | solution.py:42
  114.3 9.6 %collective-permute-start.34 = (bf16[128,768]{1,0:T(8,128)(2,1)S(1)}, bf16[128,768]{1,0:T(8,128)(2,1)S(1)}, u32[]{:S(2)}, u32[]{:S(2)}) collective-permute-start(bf16[128,768]{1,0:T(8,128)(2,1)S(1)} %get-tuple-element.259), channel_id=1, source_target_pairs={{0,6},{2,4},{4,2},{6,0},{1,7},{3,5},{5,3},{7,1},{8,14},{10,12},{12... | collective-permute-start | bytes 589832 | tf_op jit(solution)/shard_map/ppermute | solution.py:42
  115.8 9.3 %collective-permute-start.33 = (bf16[128,768]{1,0:T(8,128)(2,1)S(1)}, bf16[128,768]{1,0:T(8,128)(2,1)S(1)}, u32[]{:S(2)}, u32[]{:S(2)}) collective-permute-start(bf16[128,768]{1,0:T(8,128)(2,1)S(1)} %get-tuple-element.260), channel_id=1, source_target_pairs={{0,4},{2,6},{4,0},{6,2},{1,5},{3,7},{5,1},{7,3},{8,12},{10,14},{12... | collective-permute-start | bytes 589832 | tf_op jit(solution)/shard_map/ppermute | solution.py:42
  126.8 8.7 %collective-permute-start.39 = (bf16[128,768]{1,0:T(8,128)(2,1)S(1)}, bf16[128,768]{1,0:T(8,128)(2,1)S(1)}, u32[]{:S(2)}, u32[]{:S(2)}) collective-permute-start(bf16[128,768]{1,0:T(8,128)(2,1)S(1)} %get-tuple-element.243), channel_id=1, source_target_pairs={{0,6},{2,4},{4,2},{6,0},{1,7},{3,5},{5,3},{7,1},{8,14},{10,12},{12... | collective-permute-start | bytes 589832 | tf_op jit(solution)/shard_map/ppermute | solution.py:42
  129.1 8.5 %collective-permute-start.38 = (bf16[128,768]{1,0:T(8,128)(2,1)S(1)}, bf16[128,768]{1,0:T(8,128)(2,1)S(1)}, u32[]{:S(2)}, u32[]{:S(2)}) collective-permute-start(bf16[128,768]{1,0:T(8,128)(2,1)S(1)} %get-tuple-element.243), channel_id=1, source_target_pairs={{0,4},{2,6},{4,0},{6,2},{1,5},{3,7},{5,1},{7,3},{8,12},{10,14},{12... | collective-permute-start | bytes 589832 | tf_op jit(solution)/shard_map/ppermute | solution.py:42
  129.7 7.9 %collective-permute-start.37 = (bf16[128,768]{1,0:T(8,128)(2,1)S(1)}, bf16[128,768]{1,0:T(8,128)(2,1)}, u32[]{:S(2)}, u32[]{:S(2)}) collective-permute-start(bf16[128,768]{1,0:T(8,128)(2,1)S(1)} %get-tuple-element.243), channel_id=1, source_target_pairs={{0,2},{2,0},{4,6},{6,4},{1,3},{3,1},{5,7},{7,5},{8,10},{10,8},{12,... | collective-permute-start | bytes 589832 | tf_op jit(solution)/shard_map/ppermute | solution.py:42
  146.1 8.7 %collective-permute-start.42 = (bf16[128,768]{1,0:T(8,128)(2,1)S(1)}, bf16[128,768]{1,0:T(8,128)(2,1)S(1)}, u32[]{:S(2)}, u32[]{:S(2)}) collective-permute-start(bf16[128,768]{1,0:T(8,128)(2,1)S(1)} %get-tuple-element.254), channel_id=1, source_target_pairs={{0,6},{2,4},{4,2},{6,0},{1,7},{3,5},{5,3},{7,1},{8,14},{10,12},{12... | collective-permute-start | bytes 589832 | tf_op jit(solution)/shard_map/ppermute | solution.py:42
  148.5 9.1 %collective-permute-start.41 = (bf16[128,768]{1,0:T(8,128)(2,1)S(1)}, bf16[128,768]{1,0:T(8,128)(2,1)S(1)}, u32[]{:S(2)}, u32[]{:S(2)}) collective-permute-start(bf16[128,768]{1,0:T(8,128)(2,1)S(1)} %get-tuple-element.255), channel_id=1, source_target_pairs={{0,4},{2,6},{4,0},{6,2},{1,5},{3,7},{5,1},{7,3},{8,12},{10,14},{12... | collective-permute-start | bytes 589832 | tf_op jit(solution)/shard_map/ppermute | solution.py:42
  149.1 8.5 %collective-permute-start.40 = (bf16[128,768]{1,0:T(8,128)(2,1)S(1)}, bf16[128,768]{1,0:T(8,128)(2,1)S(1)}, u32[]{:S(2)}, u32[]{:S(2)}) collective-permute-start(bf16[128,768]{1,0:T(8,128)(2,1)S(1)} %get-tuple-element.256), channel_id=1, source_target_pairs={{0,2},{2,0},{4,6},{6,4},{1,3},{3,1},{5,7},{7,5},{8,10},{10,8},{12,... | collective-permute-start | bytes 589832 | tf_op jit(solution)/shard_map/ppermute | solution.py:42
  157.6 11.6 %collective-permute-start.43 = (bf16[768,768]{1,0:T(8,128)(2,1)}, bf16[768,768]{1,0:T(8,128)(2,1)S(1)}, u32[]{:S(2)}, u32[]{:S(2)}) collective-permute-start(bf16[768,768]{1,0:T(8,128)(2,1)} %convolution_convert_fusion.1), channel_id=1, source_target_pairs={{0,1},{1,0},{2,3},{3,2},{4,5},{5,4},{6,7},{7,6},{8,9},{9,8},{10,11... | collective-permute-start | bytes 3538952 | tf_op jit(solution)/shard_map/ppermute | solution.py:42
  157.7 12.9 %collective-permute-start.45 = (bf16[768,384]{1,0:T(8,128)(2,1)}, bf16[768,384]{1,0:T(8,128)(2,1)}, u32[]{:S(2)}, u32[]{:S(2)}) collective-permute-start(bf16[768,384]{1,0:T(8,128)(2,1)} %convolution_convert_fusion.4), channel_id=1, source_target_pairs={{0,1},{1,0},{2,3},{3,2},{4,5},{5,4},{6,7},{7,6},{8,9},{9,8},{10,11... | collective-permute-start | bytes 1769480 | tf_op jit(solution)/shard_map/ppermute | solution.py:42
  162.2 12.0 %collective-permute-start.47 = (bf16[768,384]{1,0:T(8,128)(2,1)}, bf16[768,384]{1,0:T(8,128)(2,1)}, u32[]{:S(2)}, u32[]{:S(2)}) collective-permute-start(bf16[768,384]{1,0:T(8,128)(2,1)} %get-tuple-element.199), channel_id=1, source_target_pairs={{0,1},{1,0},{2,3},{3,2},{4,5},{5,4},{6,7},{7,6},{8,9},{9,8},{10,11... | collective-permute-start | bytes 1769480 | tf_op jit(solution)/shard_map/ppermute | solution.py:42
  162.9 13.3 %collective-permute-start.35 = (bf16[64,768]{1,0:T(8,128)(2,1)}, bf16[64,768]{1,0:T(8,128)(2,1)S(1)}, u32[]{:S(2)}, u32[]{:S(2)}) collective-permute-start(bf16[64,768]{1,0:T(8,128)(2,1)} %broadcast_select_fusion.5), channel_id=1, source_target_pairs={{0,8},{8,0},{1,9},{9,1},{2,10},{10,2},{3,11},{11,3},{4,12},{12,4},... | collective-permute-start | bytes 294920 | tf_op jit(solution)/shard_map/ppermute | solution.py:42
  165.4 12.5 %all-to-all-start.3 = ((bf16[16,64,128]{2,1,0:T(8,128)(2,1)}), bf16[16,64,128]{2,1,0:T(8,128)(2,1)S(1)}, u32[]{:S(2)}, u32[]{:S(2)}) async-start(bf16[16,64,128]{2,1,0:T(8,128)(2,1)} %get-tuple-element.192), calls=%async_computation.3 | async-start | bytes 524288 | tf_op jit(solution)/shard_map/all_to_all | solution.py:86
  170.2 29.3 %collective-permute-start.44 = (bf16[2,192,768]{2,1,0:T(8,128)(2,1)}, bf16[2,192,768]{2,1,0:T(8,128)(2,1)S(1)}, u32[]{:S(2)}, u32[]{:S(2)}) collective-permute-start(bf16[2,192,768]{2,1,0:T(8,128)(2,1)} %fusion.11), channel_id=1, source_target_pairs={{0,8},{8,0},{1,9},{9,1},{2,10},{10,2},{3,11},{11,3},{4,12},{12,4},... | collective-permute-start | bytes 1769480 | tf_op jit(solution)/shard_map/ppermute | solution.py:42
  172.4 21.2 %collective-permute-start.46 = (bf16[384,384]{1,0:T(8,128)(2,1)}, bf16[384,384]{1,0:T(8,128)(2,1)}, u32[]{:S(2)}, u32[]{:S(2)}) collective-permute-start(bf16[384,384]{1,0:T(8,128)(2,1)} %fusion.34), channel_id=1, source_target_pairs={{0,16},{16,0},{1,17},{17,1},{2,18},{18,2},{3,19},{19,3},{4,20},{20... | collective-permute-start | bytes 884744 | tf_op jit(solution)/shard_map/ppermute | solution.py:42
  176.0 17.7 %collective-permute-start.48 = (bf16[384,384]{1,0:T(8,128)(2,1)}, bf16[384,384]{1,0:T(8,128)(2,1)}, u32[]{:S(2)}, u32[]{:S(2)}) collective-permute-start(bf16[384,384]{1,0:T(8,128)(2,1)} %fusion.35), channel_id=1, source_target_pairs={{0,16},{16,0},{1,17},{17,1},{2,18},{18,2},{3,19},{19,3},{4,20},{20... | collective-permute-start | bytes 884744 | tf_op jit(solution)/shard_map/ppermute | solution.py:42
  199.4 15.1 %all-to-all-start.4 = ((bf16[4,768,128]{2,1,0:T(8,128)(2,1)}), bf16[4,768,128]{2,1,0:T(8,128)(2,1)S(1)}, u32[]{:S(2)}, u32[]{:S(2)}) async-start(bf16[4,768,128]{2,1,0:T(8,128)(2,1)} %attend_back.1), calls=%async_computation.4 | async-start | bytes 1572864 | tf_op jit(solution)/shard_map/all_to_all | solution.py:86
  204.2 9.2 %collective-permute-start.60 = (bf16[192,384]{1,0:T(8,128)(2,1)S(1)}, bf16[192,384]{1,0:T(8,128)(2,1)S(1)}, u32[]{:S(2)}, u32[]{:S(2)}) collective-permute-start(bf16[192,384]{1,0:T(8,128)(2,1)S(1)} %broadcast_select_fusion), channel_id=1, source_target_pairs={{0,8},{8,0},{1,9},{9,1},{2,10},{10,2},{3,11},{11,3},{4,12},{12,4},... | collective-permute-start | bytes 442376 | tf_op jit(solution)/shard_map/ppermute | solution.py:42
  214.6 12.3 %collective-permute-start.50 = (bf16[192,384]{1,0:T(8,128)(2,1)S(1)}, bf16[192,384]{1,0:T(8,128)(2,1)S(1)}, u32[]{:S(2)}, u32[]{:S(2)}) collective-permute-start(bf16[192,384]{1,0:T(8,128)(2,1)S(1)} %select_bitcast_fusion.1), channel_id=1, source_target_pairs={{0,8},{8,0},{1,9},{9,1},{2,10},{10,2},{3,11},{11,3},{4,12},{12,4},... | collective-permute-start | bytes 442376 | tf_op jit(solution)/shard_map/ppermute | solution.py:42
  215.0 12.2 %collective-permute-start.49 = (bf16[192,768]{1,0:T(8,128)(2,1)S(1)}, bf16[192,768]{1,0:T(8,128)(2,1)S(1)}, u32[]{:S(2)}, u32[]{:S(2)}) collective-permute-start(bf16[192,768]{1,0:T(8,128)(2,1)S(1)} %select_bitcast_fusion), channel_id=1, source_target_pairs={{0,16},{16,0},{1,17},{17,1},{2,18},{18,2},{3,19},{19,3},{4,20},{20... | collective-permute-start | bytes 884744 | tf_op jit(solution)/shard_map/ppermute | solution.py:42
  221.3 6.1 %collective-permute-start.55 = (bf16[16,24,768]{2,1,0:T(8,128)(2,1)}, bf16[16,24,768]{2,1,0:T(8,128)(2,1)S(1)}, u32[]{:S(2)}, u32[]{:S(2)}) collective-permute-start(bf16[16,24,768]{2,1,0:T(8,128)(2,1)} %get-tuple-element.210), channel_id=1, source_target_pairs={{0,1},{1,0},{2,3},{3,2},{4,5},{5,4},{6,7},{7,6},{8,9},{9,8},{10,11... | collective-permute-start | bytes 1769480 | tf_op jit(solution)/shard_map/ppermute | solution.py:42
  222.5 14.4 %collective-permute-start.51 = (bf16[128,768]{1,0:T(8,128)(2,1)S(1)}, bf16[128,768]{1,0:T(8,128)(2,1)S(1)}, u32[]{:S(2)}, u32[]{:S(2)}) collective-permute-start(bf16[128,768]{1,0:T(8,128)(2,1)S(1)} %get-tuple-element.251), channel_id=1, source_target_pairs={{0,2},{2,0},{4,6},{6,4},{1,3},{3,1},{5,7},{7,5},{8,10},{10,8},{12,... | collective-permute-start | bytes 589832 | tf_op jit(solution)/shard_map/ppermute | solution.py:42
  224.0 14.9 %collective-permute-start.53 = (bf16[128,768]{1,0:T(8,128)(2,1)S(1)}, bf16[128,768]{1,0:T(8,128)(2,1)S(1)}, u32[]{:S(2)}, u32[]{:S(2)}) collective-permute-start(bf16[128,768]{1,0:T(8,128)(2,1)S(1)} %get-tuple-element.252), channel_id=1, source_target_pairs={{0,6},{2,4},{4,2},{6,0},{1,7},{3,5},{5,3},{7,1},{8,14},{10,12},{12... | collective-permute-start | bytes 589832 | tf_op jit(solution)/shard_map/ppermute | solution.py:42
  226.9 12.1 %collective-permute-start.52 = (bf16[128,768]{1,0:T(8,128)(2,1)S(1)}, bf16[128,768]{1,0:T(8,128)(2,1)S(1)}, u32[]{:S(2)}, u32[]{:S(2)}) collective-permute-start(bf16[128,768]{1,0:T(8,128)(2,1)S(1)} %get-tuple-element.253), channel_id=1, source_target_pairs={{0,4},{2,6},{4,0},{6,2},{1,5},{3,7},{5,1},{7,3},{8,12},{10,14},{12... | collective-permute-start | bytes 589832 | tf_op jit(solution)/shard_map/ppermute | solution.py:42
  228.3 31.4 %all-to-all-start.5 = ((bf16[16,24,768]{2,1,0:T(8,128)(2,1)}), bf16[16,24,768]{2,1,0:T(8,128)(2,1)S(1)}, u32[]{:S(2)}, u32[]{:S(2)}) async-start(bf16[16,24,768]{2,1,0:T(8,128)(2,1)} %add_convert_fusion.1), calls=%async_computation.5 | async-start | bytes 1179648 | tf_op jit(solution)/shard_map/all_to_all | solution.py:86
  233.5 7.6 %collective-permute-start.56 = (bf16[48,1152]{1,0:T(8,128)(2,1)S(1)}, bf16[48,1152]{1,0:T(8,128)(2,1)S(1)}, u32[]{:S(2)}, u32[]{:S(2)}) collective-permute-start(bf16[48,1152]{1,0:T(8,128)(2,1)S(1)} %get-tuple-element.217), channel_id=1, source_target_pairs={{0,2},{2,0},{4,6},{6,4},{1,3},{3,1},{5,7},{7,5},{8,10},{10,8},{12,... | collective-permute-start | bytes 331784 | tf_op jit(solution)/shard_map/ppermute | solution.py:42
  235.4 15.7 %collective-permute-start.57 = (bf16[48,1152]{1,0:T(8,128)(2,1)S(1)}, bf16[48,1152]{1,0:T(8,128)(2,1)S(1)}, u32[]{:S(2)}, u32[]{:S(2)}) collective-permute-start(bf16[48,1152]{1,0:T(8,128)(2,1)S(1)} %get-tuple-element.218), channel_id=1, source_target_pairs={{0,4},{2,6},{4,0},{6,2},{1,5},{3,7},{5,1},{7,3},{8,12},{10,14},{12... | collective-permute-start | bytes 331784 | tf_op jit(solution)/shard_map/ppermute | solution.py:42
  236.9 15.9 %collective-permute-start.58 = (bf16[48,1152]{1,0:T(8,128)(2,1)S(1)}, bf16[48,1152]{1,0:T(8,128)(2,1)S(1)}, u32[]{:S(2)}, u32[]{:S(2)}) collective-permute-start(bf16[48,1152]{1,0:T(8,128)(2,1)S(1)} %get-tuple-element.219), channel_id=1, source_target_pairs={{0,6},{2,4},{4,2},{6,0},{1,7},{3,5},{5,3},{7,1},{8,14},{10,12},{12... | collective-permute-start | bytes 331784 | tf_op jit(solution)/shard_map/ppermute | solution.py:42
  240.0 15.3 %collective-permute-start.54 = (bf16[64,768]{1,0:T(8,128)(2,1)S(1)}, bf16[64,768]{1,0:T(8,128)(2,1)S(1)}, u32[]{:S(2)}, u32[]{:S(2)}) collective-permute-start(bf16[64,768]{1,0:T(8,128)(2,1)S(1)} %broadcast_select_fusion.3), channel_id=1, source_target_pairs={{0,8},{8,0},{1,9},{9,1},{2,10},{10,2},{3,11},{11,3},{4,12},{12,4},... | collective-permute-start | bytes 294920 | tf_op jit(solution)/shard_map/ppermute | solution.py:42
  241.0 15.0 %collective-permute-start.61 = (bf16[96,384]{1,0:T(8,128)(2,1)S(1)}, bf16[96,384]{1,0:T(8,128)(2,1)S(1)}, u32[]{:S(2)}, u32[]{:S(2)}) collective-permute-start(bf16[96,384]{1,0:T(8,128)(2,1)S(1)} %select_convert_fusion), channel_id=1, source_target_pairs={{0,1},{1,0},{2,3},{3,2},{4,5},{5,4},{6,7},{7,6},{8,9},{9,8},{10,11... | collective-permute-start | bytes 221192 | tf_op jit(solution)/shard_map/ppermute | solution.py:42
  (63 other events, 641.2 us)
